TPU v7x, 32 devices: a whole 2x2x4 slice. The times are simulated.
32 devices in a mesh: groups: 2 (over y), tok: 4 (over z), head: 2 (over x), rep: 2 (over core).
Axes of the slice: x: 2, y: 2, z: 4, core: 2. Of those that a mesh axis runs over, the one named last changes fastest.
Arguments:
- keys: bfloat16 [1024, 1024], P(('groups', 'tok'), 'head'), parts along dimension 0, may hold values from -6 to 6
- values: bfloat16 [1024, 1024], P(('groups', 'tok'), 'head'), parts along dimension 0, may hold values from -6 to 6
- rates: float32 [1024, 2], P(('groups', 'tok'), 'head'), parts along dimension 0, may hold values from 0.0003 to 0.006
- queries: bfloat16 [1024, 1024], P(('groups', 'tok'), 'head'), parts along dimension 0, may hold values from -6 to 6
- stream: bfloat16 [1024, 1024], P(('groups', 'tok'), 'head'), parts along dimension 0, may hold values from -16 to 16
- gain: float32 [1024], P('head'), may hold values from 0.1 to 1.9
- counts: int32 [8], P(('groups', 'tok')), parts along dimension 0, may hold values from 1 to 128, 307 in all
- fw_one: float32 [2, 512, 1024], P('head', None, 'rep'), may hold values from -0.25 to 0.25
- fw_three: float32 [2, 512, 1024], P('head', None, 'rep'), may hold values from -0.25 to 0.25
- fw_two: float32 [2, 1024, 512], P('head', 'rep'), may hold values from -1 to 1
- mlp_up: bfloat16 [1024, 4096], P('tok', ('head', 'rep')), may hold values from -0.1875 to 0.1875
- mlp_down: bfloat16 [4096, 1024], P(('head', 'rep'), 'tok'), may hold values from -0.09375 to 0.09375
Outputs:
- result: bfloat16 [1024, 1024], P(('groups', 'tok'), ('head', 'rep')), parts along dimension 0
There are 2 independent parts, one for each index of `groups`. A program takes and returns all parts, laid end to end along the dimension named above; an argument that names none is the same for every part. Nothing has to cross between parts.
Inputs may be any that keep to these rules, and one draw needn't show every extreme that they name: counts sum to 307, and one index of tok is full.
All inputs are finite; a program needn't handle non-finite values. No bound on the sum of `counts` on one device may be relied on, other than what follows from the above.
Results may differ from a plain program's by a relative error of at most 0.04.
Values may be sent and summed in bfloat16 or wider, within the bound.
No kernel may reach another device: no remote copies, remote signals or barrier semaphores. Data moves between devices by JAX's collectives and lax.ppermute only.
A program may use at most 64 MiB of HBM per device.

v0:
```python
import jax
import jax.numpy as jnp
from jax import lax
from jax.sharding import PartitionSpec as P


def swish_parts(pre_act):
    sigmoid_val = jax.nn.sigmoid(pre_act)
    return (pre_act * sigmoid_val, sigmoid_val * (1.0 + pre_act * (1.0 - sigmoid_val)))


def column_squares(former, updated, gate_cols):
    left_old = former[:, :gate_cols]
    left_new = updated[:, :gate_cols]
    return (jnp.sum(left_old * left_old, axis=0), jnp.sum(left_new * left_new, axis=0))


def rescale(former, updated, col_former, col_updated):
    gate_cols = col_former.shape[0]
    right_old = former[:, gate_cols:]
    right_new = updated[:, gate_cols:]
    row_sums = lax.psum(
        (jnp.sum(right_old * right_old, axis=1), jnp.sum(right_new * right_new, axis=1)), "rep"
    )
    left_part = updated[:, :gate_cols] * jnp.sqrt(col_former) * lax.rsqrt(col_updated + 1e-06)
    row_factor = jnp.sqrt(row_sums[0]) * lax.rsqrt(row_sums[1] + 1e-06)
    right_part = right_new * row_factor[:, None]
    return jnp.concatenate([left_part, right_part], axis=1).astype(jnp.bfloat16)


def on_device(
    keys, values, rates, queries, stream, gain, counts, fw_one, fw_three, fw_two, mlp_up, mlp_down
):
    head_width = keys.shape[1]
    local_hidden = fw_one.shape[2]
    gate_cols = 2 * local_hidden
    packed_old = jnp.concatenate([fw_one[0], fw_three[0], fw_two[0].T], axis=1)
    first_pre = jnp.dot(keys, fw_one[0].astype(jnp.bfloat16), preferred_element_type=jnp.float32)
    third_pre = jnp.dot(keys, fw_three[0].astype(jnp.bfloat16), preferred_element_type=jnp.float32)
    act_first, slope_first = swish_parts(first_pre)
    hidden_in = (act_first * third_pre).astype(jnp.bfloat16)
    scaled_val = (rates * values.astype(jnp.float32)).astype(jnp.bfloat16)
    second_t = fw_two[0].T.astype(jnp.bfloat16)
    back_hidden = jnp.dot(scaled_val, second_t, preferred_element_type=jnp.float32)
    err_first = (back_hidden * third_pre * slope_first).astype(jnp.bfloat16)
    err_third = (back_hidden * act_first).astype(jnp.bfloat16)
    grad_first = jnp.einsum("nd,nf->df", keys, err_first, preferred_element_type=jnp.float32)
    grad_third = jnp.einsum("nd,nf->df", keys, err_third, preferred_element_type=jnp.float32)
    grad_second = jnp.einsum("nd,nf->df", scaled_val, hidden_in, preferred_element_type=jnp.float32)
    grad_all = lax.psum(
        jnp.concatenate([grad_first, grad_third, grad_second], axis=1).astype(jnp.bfloat16), "tok"
    ).astype(jnp.float32)
    packed_new = packed_old + grad_all
    col_former, col_updated = column_squares(packed_old, packed_new, gate_cols)
    fast = rescale(packed_old, packed_new, col_former, col_updated)
    query_first = jnp.dot(queries, fast[:, :local_hidden], preferred_element_type=jnp.float32)
    query_third = jnp.dot(
        queries, fast[:, local_hidden:gate_cols], preferred_element_type=jnp.float32
    )
    query_act, unused_slope = swish_parts(query_first)
    query_hidden = (query_act * query_third).astype(jnp.bfloat16)
    head_part = jnp.einsum(
        "tf,df->td", query_hidden, fast[:, gate_cols:], preferred_element_type=jnp.float32
    )
    head_out = lax.psum(head_part.astype(jnp.bfloat16), "rep").astype(jnp.float32)
    mixed_rows = stream.astype(jnp.float32) + head_out
    row_total = lax.psum(jnp.sum(mixed_rows * mixed_rows, axis=1), "head")
    model_width = head_width * lax.axis_size("head")
    inv_rms = lax.rsqrt(row_total / model_width + 1e-06)
    normed = (mixed_rows * inv_rms[:, None] * gain).astype(jnp.bfloat16)
    features = lax.all_gather(normed, "head", axis=1, tiled=True)
    up_total = jnp.dot(
        features,
        lax.all_gather(mlp_up, "tok", axis=0, tiled=True),
        preferred_element_type=jnp.float32,
    )
    expanded = jax.nn.gelu(up_total, approximate=False).astype(jnp.bfloat16)
    partial_terms = jnp.dot(
        expanded,
        lax.all_gather(mlp_down, "tok", axis=1, tiled=True),
        preferred_element_type=jnp.float32,
    )
    summed = lax.psum_scatter(
        partial_terms.astype(jnp.bfloat16), ("head", "rep"), scatter_dimension=1, tiled=True
    ).astype(jnp.float32)
    out_width = summed.shape[1]
    stream_cols = lax.dynamic_slice_in_dim(
        mixed_rows, lax.axis_index("rep") * out_width, out_width, 1
    )
    slot_index = jnp.arange(mixed_rows.shape[0], dtype=jnp.int32)
    live_rows = slot_index < counts[0]
    return jnp.where(live_rows[:, None], stream_cols + summed, 0.0).astype(jnp.bfloat16)


def solution(mesh):
    placed = (
        P(("groups", "tok"), "head"),
        P(("groups", "tok"), "head"),
        P(("groups", "tok"), "head"),
        P(("groups", "tok"), "head"),
        P(("groups", "tok"), "head"),
        P("head"),
        P(("groups", "tok")),
        P("head", None, "rep"),
        P("head", None, "rep"),
        P("head", "rep", None),
        P("tok", ("head", "rep")),
        P(("head", "rep"), "tok"),
    )
    return jax.shard_map(
        on_device,
        mesh=mesh,
        in_specs=placed,
        out_specs=P(("groups", "tok"), ("head", "rep")),
        check_vma=False,
    )
```

profile of v0, /device:TPU:0, one launch (start us, length us, event | category | flops | bytes accessed | tf_op | source)
XLA Modules:
  0.0 239.5 jit_solution(2878484344632137081)
XLA Ops:
  6.5 0.0 copy-start
  6.5 0.0 all-reduce.4.cloned.1.call-start
  6.5 1.6 copy.13
  8.1 0.0 copy-start.1
  8.1 0.0 copy-start.3
  8.2 0.0 copy-start.7
  8.2 0.0 copy-start.9
  8.2 2.0 copy.14
  10.1 0.0 copy-done
  10.2 0.0 copy-start.2
  10.2 0.3 fusion.111
  10.5 0.3 fusion.109
  10.8 0.0 copy-done.3
  10.8 0.0 copy-done.7
  10.8 0.0 copy-done.9
  10.8 0.3 fusion.22
  11.1 0.4 convolution_convert_fusion
  11.5 0.4 fusion.1
  11.9 0.3 fusion.2
  12.2 1.2 pad_maximum_fusion
  13.5 0.0 all-reduce.4.cloned.1.call-update
  13.5 0.0 all-reduce.6.cloned.1.call-start
  13.5 0.0 copy-done.1
  13.6 0.0 copy-done.2
  13.6 0.2 fusion
  13.8 0.1 multiply_reduce_fusion.2
  13.9 71.5 %all-reduce.4.cloned.1.call-done = bf16[512,1536]{0,1:T(8,128)(2,1)} async-done(((bf16[512,1536]{0,1:T(8,128)(2,1)}), bf16[512,1536]{0,1:T(8,128)(2,1)}) %all-reduce.4.cloned.1.call-update) | async-done | bytes 1572880 | tf_op jit(solution)/shard_map/psum | solution.py:50
  85.5 2.9 %maximum_add_fusion = f32[512,1536]{0,1:T(8,128)S(1)} fusion(f32[512,512]{0,1:T(8,128)} %bitcast.75, f32[512,512]{0,1:T(8,128)} %bitcast.74, f32[512,512]{0,1:T(8,128)} %bitcast.72, bf16[512,1536]{0,1:T(8,128)(2,1)} %all-reduce.4.cloned.1.call-done), kind=kLoop, calls=%fused_computation | loop fusion | flops 3145728 | bytes 7864320 | tf_op jit(solution)/shard_map/add | solution.py:53
  88.3 0.2 multiply_reduce_fusion
  88.5 0.0 copy-start.6
  88.5 0.1 multiply_reduce_fusion.1
  88.7 0.3 multiply_convert_fusion
  89.0 0.0 copy-start.4
  89.0 1.0 copy-done.4
  90.0 0.0 copy-done.6
  90.0 1.0 convolution_bitcast_fusion.1
  91.0 0.0 copy-start.5
  91.0 2.6 %all-reduce = (f32[512]{0:T(512)S(1)}, f32[512]{0:T(512)S(1)}) all-reduce(f32[512]{0:T(512)S(1)} %multiply_reduce_fusion.1, f32[512]{0:T(512)S(1)} %multiply_reduce_fusion.2), channel_id=1, replica_groups=mesh['groups'=2,'tok'=4,'head'=2,'rep'=2] {'rep'}, use_global_device_ids=true, to_apply=%region_6.0 | all-reduce | flops 1024 | bytes 8192 | tf_op jit(solution)/shard_map/psum | solution.py:22
  93.6 0.0 copy-start.8
  93.6 2.2 convolution_convert_fusion.4
  95.9 0.0 all-reduce.6.cloned.1.call-update
  95.9 0.0 all-gather.3.cloned.1.call-start
  96.0 0.7 all-gather.3.cloned.1.call-update
  96.6 0.0 all-gather.5.cloned.1.call-start
  96.7 0.5 all-gather.5.cloned.1.call-update
  97.2 0.0 reduce-scatter.2.cloned.1.call-start
  97.3 15.8 %all-reduce.6.cloned.1.call-done = bf16[128,512]{1,0:T(8,128)(2,1)} async-done(((bf16[128,512]{1,0:T(8,128)(2,1)}), bf16[128,512]{1,0:T(8,128)(2,1)}) %all-reduce.6.cloned.1.call-update) | async-done | bytes 131088 | tf_op jit(solution)/shard_map/psum | solution.py:65
  113.0 0.0 copy-done.5
  113.0 1.0 convert_add_fusion
  114.1 4.9 %psum.39 = f32[128]{0:T(128)S(1)} all-reduce(f32[128]{0:T(128)S(1)} %get-tuple-element.8), channel_id=1, replica_groups=mesh['groups'=2,'tok'=4,'head'=2,'rep'=2] {'head'}, use_global_device_ids=true, to_apply=%region_9.0 | all-reduce | flops 128 | bytes 1024 | tf_op jit(solution)/shard_map/psum | solution.py:67
  119.0 0.0 copy-done.8
  119.0 1.0 multiply_convert_fusion.3
  120.0 5.6 %all_gather.9 = bf16[128,1024]{1,0:T(8,128)(2,1)S(1)} all-gather(bf16[128,512]{1,0:T(8,128)(2,1)S(1)} %multiply_convert_fusion.3), channel_id=1, replica_groups=mesh['groups'=2,'tok'=4,'head'=2,'rep'=2] {'head'}, dimensions={1}, use_global_device_ids=true | all-gather | bytes 393216 | tf_op jit(solution)/shard_map/all_gather | solution.py:71
  125.7 36.1 %all-gather.3.cloned.1.call-done = bf16[1024,1024]{1,0:T(8,128)(2,1)} async-done(((bf16[256,1024]{1,0:T(8,128)(2,1)}), bf16[1024,1024]{1,0:T(8,128)(2,1)}) %all-gather.3.cloned.1.call-update) | async-done | bytes 2097168 | tf_op jit(solution)/shard_map/all_gather | solution.py:74
  161.7 46.4 %all-gather.5.cloned.1.call-done = bf16[1024,1024]{1,0:T(8,128)(2,1)} async-done(((bf16[1024,256]{1,0:T(8,128)(2,1)}), bf16[1024,1024]{1,0:T(8,128)(2,1)}) %all-gather.5.cloned.1.call-update) | async-done | bytes 2097168 | tf_op jit(solution)/shard_map/all_gather | solution.py:80
  208.1 4.8 %convolution_convert_fusion.3 = bf16[128,1024]{1,0:T(8,128)(2,1)} fusion(bf16[1024,1024]{1,0:T(8,128)(2,1)} %all-gather.5.cloned.1.call-done, bf16[128,1024]{1,0:T(8,128)(2,1)S(1)} %all_gather.9, bf16[1024,1024]{1,0:T(8,128)(2,1)} %all-gather.3.cloned.1.call-done), kind=kOutput, calls=%fused_computation.11 | convolution fusion | flops 545521664 | bytes 4718592 | tf_op jit(solution)/shard_map/dot_general | solution.py:78
  212.9 0.0 reduce-scatter.2.cloned.1.call-update
  213.6 17.8 %reduce-scatter.2.cloned.1.call-done = bf16[128,256]{1,0:T(8,128)(2,1)} async-done(((bf16[128,1024]{1,0:T(8,128)(2,1)}), bf16[128,256]{1,0:T(8,128)(2,1)}) %reduce-scatter.2.cloned.1.call-update) | async-done | bytes 65552 | tf_op jit(solution)/shard_map/reduce_scatter | solution.py:83
  231.4 1.6 select_convert_fusion
  (5 shorter events, 0.0 us)
Async XLA Ops:
  6.5 3.6 %copy-start = (bf16[128,512]{1,0:T(8,128)(2,1)S(1)}, bf16[128,512]{1,0:T(8,128)(2,1)}, u32[]{:S(2)}) copy-start(bf16[128,512]{1,0:T(8,128)(2,1)} %param.12) | copy-start | bytes 393220
  6.5 78.9 %all-reduce.4.cloned.1.call-start = ((), (), s32[]{:S(2)}) async-start(), calls=%async_computation.1 | async-start | bytes 3145728 | tf_op jit(solution)/shard_map/psum | solution.py:50
  8.1 5.4 %copy-start.1 = (f32[1,512,512]{1,2,0:T(8,128)}, f32[1,512,512]{1,2,0:T(8,128)S(1)}, u32[]{:S(2)}) copy-start(f32[1,512,512]{1,2,0:T(8,128)S(1)} %copy.13) | copy-start | bytes 3145732
  8.1 2.6 %copy-start.3 = (f32[1,512,512]{2,1,0:T(8,128)S(1)}, f32[1,512,512]{2,1,0:T(8,128)}, u32[]{:S(2)}) copy-start(f32[1,512,512]{2,1,0:T(8,128)} %param.21) | copy-start | bytes 3145732
  8.2 2.6 %copy-start.7 = (bf16[128,512]{1,0:T(8,128)(2,1)S(1)}, bf16[128,512]{1,0:T(8,128)(2,1)}, u32[]{:S(2)}) copy-start(bf16[128,512]{1,0:T(8,128)(2,1)} %param.13) | copy-start | bytes 393220
  8.2 2.6 %copy-start.9 = (f32[128,1]{0,1:T(1,128)S(1)}, f32[128,1]{0,1:T(1,128)}, u32[]{:S(2)}) copy-start(f32[128,1]{0,1:T(1,128)} %param.14) | copy-start | bytes 1540
  10.2 3.4 %copy-start.2 = (f32[1,512,512]{1,2,0:T(8,128)}, f32[1,512,512]{1,2,0:T(8,128)S(1)}, u32[]{:S(2)}) copy-start(f32[1,512,512]{1,2,0:T(8,128)S(1)} %copy.14) | copy-start | bytes 3145732
  13.5 99.5 %all-reduce.6.cloned.1.call-start = ((), (), s32[]{:S(2)}) async-start(), calls=%async_computation.2 | async-start | bytes 262144 | tf_op jit(solution)/shard_map/psum | solution.py:65
  88.5 1.5 copy-start.6
  89.0 1.0 copy-start.4
  91.0 22.0 %copy-start.5 = (bf16[128,512]{1,0:T(8,128)(2,1)S(1)}, bf16[128,512]{1,0:T(8,128)(2,1)}, u32[]{:S(2)}) copy-start(bf16[128,512]{1,0:T(8,128)(2,1)} %param.16) | copy-start | bytes 393220
  93.6 25.4 %copy-start.8 = (f32[512]{0:T(512)S(1)}, f32[512]{0:T(512)}, u32[]{:S(2)}) copy-start(f32[512]{0:T(512)} %param.17) | copy-start | bytes 6148
  95.9 65.8 %all-gather.3.cloned.1.call-start = ((), (), s32[]{:S(2)}) async-start(), calls=%async_computation.3 | async-start | bytes 2621440 | tf_op jit(solution)/shard_map/all_gather | solution.py:74
  96.6 111.5 %all-gather.5.cloned.1.call-start = ((), (), s32[]{:S(2)}) async-start(), calls=%async_computation.4 | async-start | bytes 2621440 | tf_op jit(solution)/shard_map/all_gather | solution.py:80
  97.2 134.2 %reduce-scatter.2.cloned.1.call-start = ((), (), s32[]{:S(2)}) async-start(), calls=%async_computation.5 | async-start | bytes 327680 | tf_op jit(solution)/shard_map/reduce_scatter | solution.py:83
Sparse Core Ops, SparseCore 0:
  13.6 71.7 all-reduce.3
  96.0 16.9 all-reduce.5
  114.6 47.0 all-gather.2
  163.2 44.9 all-gather.4
  213.1 18.2 reduce-scatter.1
where the time goes:
time: 240 us; the launch traced here: 239 us
  waiting for transfers between devices  189 us (79%)
  between operations  14 us (6%)
  blocking collectives  13.2 us (6%)
  matrix products  10 us (4%)
  other arithmetic  8.71 us (4%)
  local copies, waits for them, and re-layouts  4.58 us (2%)
    psum x1, waiting for transfers between devices, on_device(): lax.psum(jnp.concatenate([grad_first, grad_third, grad_second], axis=1).a...  71.5 us
    all_gather x1, waiting for transfers between devices, on_device(): lax.all_gather(mlp_down, 'tok', axis=1, tiled=True)  46.4 us
    all_gather x1, waiting for transfers between devices, on_device(): lax.all_gather(mlp_up, 'tok', axis=0, tiled=True)  36.1 us
    reduce_scatter x1, waiting for transfers between devices, on_device(): lax.psum_scatter(partial_terms.astype(jnp.bfloat16), ('head', 'rep'), sca...  17.8 us
    psum x1, waiting for transfers between devices, on_device(): lax.psum(head_part.astype(jnp.bfloat16), 'rep').astype(jnp.float32)  15.8 us
    all_gather x1, blocking collectives, on_device(): features = lax.all_gather(normed, 'head', axis=1, tiled=True)  5.64 us
    psum x1, blocking collectives, on_device(): row_total = lax.psum(jnp.sum(mixed_rows * mixed_rows, axis=1), 'head')  4.93 us
  transfers between devices with their start and end apart: 5, of which 5 were waited for; matrix products, arithmetic and copies ran while one was open for 1% of the time, Pallas kernels for 0%

commit v1 on v0

v1 whole, which is shorter than its diff:
```python
import functools

import jax
import jax.numpy as jnp
import numpy as np
from jax import lax
from jax.experimental import pallas as pl
from jax.experimental.pallas import tpu as pltpu
from jax.sharding import PartitionSpec as P

BF, F32 = jnp.bfloat16, jnp.float32
VMEM_BYTES = 48 << 20


def dot(a, b, dims=((1,), (0,))):
    return lax.dot_general(a, b, (dims, ((), ())), preferred_element_type=F32)


def shifted(x, axes, shifts):
    sizes = [lax.axis_size(a) for a in axes]
    pairs = []
    for here in range(int(np.prod(sizes))):
        at = np.unravel_index(here, sizes)
        there = [(a + s) % n for a, s, n in zip(at, shifts, sizes)]
        pairs.append((int(np.ravel_multi_index(there, sizes)), here))
    return lax.ppermute(x, axes, pairs)


def call(kernel, outs, args, scratch=(), flops=0):
    moved = sum(int(np.prod(x.shape)) * x.dtype.itemsize for x in (*args, *outs))
    return pl.pallas_call(
        kernel,
        out_shape=outs,
        in_specs=[pl.BlockSpec(memory_space=pltpu.VMEM)] * len(args),
        out_specs=[pl.BlockSpec(memory_space=pltpu.VMEM)] * len(outs),
        scratch_shapes=list(scratch),
        compiler_params=pltpu.CompilerParams(vmem_limit_bytes=VMEM_BYTES),
        cost_estimate=pl.CostEstimate(flops=flops, bytes_accessed=moved, transcendentals=0),
    )(*args)


def shape(dims, dtype):
    return jax.ShapeDtypeStruct(dims, dtype)


def half(ref_width):
    return ref_width // lax.axis_size("rep")


def fast_kernel(n_pieces, *refs):
    pieces, refs = refs[:n_pieces], refs[n_pieces:]
    w1, w3, w2, q, own_out, own_sq, send, ks, es, hp = refs
    dh, hidden = w1.shape
    at = 0
    for p in pieces:
        n = p.shape[0]
        ks[at : at + n, :] = p[:, :dh]
        es[at : at + n, :] = p[:, dh:]
        at += n
    tokens, step, block = at, min(at, 512), min(hidden, 256)
    old_sq = jnp.zeros((1, dh), F32)
    new_sq = jnp.zeros((1, dh), F32)
    for j in range(0, hidden, block):
        w1j, w3j, w2j = w1[:, j : j + block], w3[:, j : j + block], w2[j : j + block, :]
        w1b, w3b, w2b = w1j.astype(BF), w3j.astype(BF), w2j.astype(BF)

        def grads(i, sums):
            rows = pl.ds(pl.multiple_of(i * step, step), step)
            k, e = ks[rows, :], es[rows, :]
            a1, a3, b = dot(k, w1b), dot(k, w3b), dot(e, w2b, ((1,), (1,)))
            sig = jax.nn.sigmoid(a1)
            act = a1 * sig
            g = (act * a3).astype(BF)
            r1 = (b * a3 * (sig * (1.0 + a1 * (1.0 - sig)))).astype(BF)
            r3 = (b * act).astype(BF)
            first = ((0,), (0,))
            return sums[0] + dot(k, r1, first), sums[1] + dot(k, r3, first), sums[2] + dot(g, e, first)

        sums = (w1j, w3j, w2j)
        if tokens == step:
            u1, u3, u2 = grads(0, sums)
        else:
            u1, u3, u2 = lax.fori_loop(0, tokens // step, grads, sums)

        def normed(old, new):
            top = jnp.sqrt(jnp.sum(old * old, axis=0, keepdims=True))
            return (new * (top * lax.rsqrt(jnp.sum(new * new, axis=0, keepdims=True) + 1e-06))).astype(BF)

        old_sq = old_sq + jnp.sum(w2j * w2j, axis=0, keepdims=True)
        new_sq = new_sq + jnp.sum(u2 * u2, axis=0, keepdims=True)
        qa, qc = dot(q[...], normed(w1j, u1)), dot(q[...], normed(w3j, u3))
        part = dot((qa * jax.nn.sigmoid(qa) * qc).astype(BF), u2.astype(BF))
        hp[...] = part if j == 0 else hp[...] + part
    wide = half(dh)
    me = lax.axis_index("rep")
    mine = pl.ds(pl.multiple_of(me * wide, wide), wide)
    other = pl.ds(pl.multiple_of((1 - me) * wide, wide), wide)
    n = q.shape[0]
    own_out[...] = hp[:, mine]
    send[:n, :] = hp[:, other].astype(BF)
    row = lax.broadcasted_iota(jnp.int32, (8, dh), 0)
    hp[:8, :] = jnp.where(row == 0, old_sq, jnp.where(row == 1, new_sq, 0.0))
    own_sq[...] = hp[:8, mine]
    sq = hp[:8, other]
    top = sq.astype(BF).astype(F32)
    send[n:, :] = jnp.concatenate([top, sq - top], axis=0).astype(BF)


def mix_kernel(own, own_sq, got, stream, mixed, mixed_low):
    n, wide = own.shape
    mine = pl.ds(pl.multiple_of(lax.axis_index("rep") * wide, wide), wide)
    tail = got[n:, :].astype(F32)
    sq = own_sq[...] + tail[:8] + tail[8:]
    scale = jnp.sqrt(sq[0:1]) * lax.rsqrt(sq[1:2] + 1e-06)
    y = stream[:, mine].astype(F32) + (own[...] + got[:n, :].astype(F32)) * scale
    mixed[...] = y
    mixed_low[...] = y.astype(BF)


def take(parts, step):
    if len(parts) == 1:
        return parts[0][...]
    me, n = lax.axis_index("tok"), lax.axis_size("tok")
    direct = me >= step if step == 1 else me < step
    return jnp.where(direct, parts[0][...], parts[1][...])


def split(refs, counts):
    out = []
    for c in counts:
        out.append(refs[:c])
        refs = refs[c:]
    return out, refs


def up_kernel(places, counts, *refs):
    pieces, refs = refs[: len(places)], refs[len(places) :]
    n_head = lax.axis_size("head")
    gains, refs = refs[:n_head], refs[n_head:]
    blocks, (out, zs) = split(refs, counts)
    me_h, me_r, me_t = lax.axis_index("head"), lax.axis_index("rep"), lax.axis_index("tok")
    n, wide = pieces[0].shape
    groups = lax.axis_size("groups")
    width = zs.shape[1]
    for dg in range(groups):
        here = [(p, dh, dr) for p, (g, dh, dr) in zip(pieces, places) if g == dg]
        total = jnp.zeros((n, 1), F32)
        for p, _, _ in here:
            x = p[...].astype(F32)
            total = total + jnp.sum(x * x, axis=1, keepdims=True)
        inv = lax.rsqrt(total / width + 1e-06)
        for p, dh, dr in here:
            r = lax.rem(me_r + dr, 2)
            head = lax.rem(me_h + dh, n_head)
            cols = pl.ds(pl.multiple_of(head * 2 * wide + r * wide, wide), wide)
            gain = gains[dh][:, pl.ds(pl.multiple_of(r * wide, wide), wide)]
            zs[dg * n : (dg + 1) * n, cols] = (p[...].astype(F32) * inv * gain).astype(BF)
    total = None
    for s, parts in enumerate(blocks):
        deep = parts[0].shape[0]
        if len(blocks) == 1:
            z = zs[...]
        else:
            z = zs[:, pl.ds(pl.multiple_of(lax.rem(me_t + len(blocks) - s, len(blocks)) * deep, deep), deep)]
        term = dot(z, take(parts, s))
        total = term if total is None else total + term
    out[...] = (0.5 * total * (1.0 + lax.erf(total * np.float32(0.5**0.5)))).astype(BF)


def down_kernel(counts, h, *refs):
    blocks, (own, send, os) = split(refs, counts)
    me_h, me_r, me_t = lax.axis_index("head"), lax.axis_index("rep"), lax.axis_index("tok")
    n_head = lax.axis_size("head")
    for s, parts in enumerate(blocks):
        wide = parts[0].shape[1]
        term = dot(h[...], take(parts, s))
        if len(blocks) == 1:
            os[...] = term
        else:
            os[:, pl.ds(pl.multiple_of(lax.rem(me_t + len(blocks) - s, len(blocks)) * wide, wide), wide)] = term
    wide = own.shape[1] // n_head
    for dh in range(n_head):
        at = lax.rem(me_h + dh, n_head) * 2 * wide
        there = slice(dh * wide, (dh + 1) * wide)
        own[:, there] = os[:, pl.ds(pl.multiple_of(at + me_r * wide, wide), wide)]
        send[:, there] = os[:, pl.ds(pl.multiple_of(at + (1 - me_r) * wide, wide), wide)].astype(BF)


def pair_kernel(own, got, mixed, *outs):
    n, wide = mixed.shape
    n_head = lax.axis_size("head")
    for i, out in enumerate(outs):
        dg, dh = divmod(i, n_head)
        rows, cols = slice(dg * n, (dg + 1) * n), slice(dh * wide, (dh + 1) * wide)
        total = own[rows, cols] + got[rows, cols].astype(F32)
        out[...] = mixed[...] + total if i == 0 else total.astype(BF)


def spread(x):
    def along(y, pairs):
        return lax.ppermute(y, "tok", pairs)

    up = along(x, [(0, 1), (1, 2), (2, 3)])
    down = along(x, [(1, 0), (2, 1), (3, 2)])
    far = along(x, [(0, 2), (1, 3), (2, 0), (3, 1)])
    last = along(far, [(2, 3), (1, 0)])
    return [[x], [up, last], [far], [down, last]]


def on_device(
    keys, values, rates, queries, stream, gain, counts, fw_one, fw_three, fw_two, mlp_up, mlp_down
):
    n_tok, n_head = lax.axis_size("tok"), lax.axis_size("head")
    groups, reps = lax.axis_size("groups"), lax.axis_size("rep")
    me_g, me_r = lax.axis_index("groups"), lax.axis_index("rep")
    dh, n_key, n = keys.shape[1], keys.shape[0], queries.shape[0]
    wide = dh // reps
    scaled = (rates * values.astype(F32)).astype(BF)
    pair = jnp.concatenate([keys, scaled], axis=1)
    units = mlp_up.shape[1] // groups
    up_own = lax.dynamic_slice_in_dim(mlp_up, me_g * units, units, 1)
    down_own = lax.dynamic_slice_in_dim(mlp_down, me_g * units, units, 0)
    if n_tok == 4:
        piece = lax.dynamic_slice_in_dim(pair, me_r * (n_key // reps), n_key // reps, 0)
        near = [shifted(piece, ("tok",), (s,)) for s in range(1, n_tok)]
        near, up_own, down_own, gain = lax.optimization_barrier((near, up_own, down_own, gain))
        tokens = [pair, *near, *[shifted(x, ("rep",), (1,)) for x in near]]
        up_blocks, down_blocks = spread(up_own), spread(down_own)
    else:
        tokens = [lax.all_gather(pair, "tok", axis=0, tiled=True)]
        up_blocks = [[lax.all_gather(up_own, "tok", axis=0, tiled=True)]]
        down_blocks = [[lax.all_gather(down_own, "tok", axis=1, tiled=True)]]
    gain = gain[None, :]
    gains = [gain] + [shifted(gain, ("head",), (s,)) for s in range(1, n_head)]

    n_all = sum(x.shape[0] for x in tokens)
    hidden = fw_one.shape[2]
    own, own_sq, send = call(
        functools.partial(fast_kernel, len(tokens)),
        [shape((n, wide), F32), shape((8, wide), F32), shape((n + 16, wide), BF)],
        [*tokens, fw_one[0], fw_three[0], fw_two[0], queries],
        [pltpu.VMEM((n_all, dh), BF), pltpu.VMEM((n_all, dh), BF), pltpu.VMEM((n, dh), F32)],
        flops=12 * n_all * dh * hidden + 6 * n * dh * hidden,
    )
    got = shifted(send, ("rep",), (1,))
    mixed, low = call(
        mix_kernel, [shape((n, wide), F32), shape((n, wide), BF)], [own, own_sq, got, stream]
    )
    moves = [(dg, h) for dg in range(groups) for h in range(n_head)]
    across = {m: low if m == (0, 0) else shifted(low, ("groups", "head"), m) for m in moves}
    pieces, places = [], []
    for m, x in across.items():
        pieces += [x, shifted(x, ("rep",), (1,))]
        places += [(*m, 0), (*m, 1)]
    up_counts, down_counts = [len(b) for b in up_blocks], [len(b) for b in down_blocks]
    rows, model = groups * n, n_head * dh
    (act,) = call(
        functools.partial(up_kernel, places, up_counts),
        [shape((rows, units), BF)],
        [*pieces, *gains, *[x for b in up_blocks for x in b]],
        [pltpu.VMEM((rows, model), BF)],
        flops=2 * rows * units * model,
    )
    own, send = call(
        functools.partial(down_kernel, down_counts),
        [shape((rows, n_head * wide), F32), shape((rows, n_head * wide), BF)],
        [act, *[x for b in down_blocks for x in b]],
        [pltpu.VMEM((rows, model), F32)],
        flops=2 * rows * units * model,
    )
    got = shifted(send, ("rep",), (1,))
    total, *parts = call(
        pair_kernel,
        [shape((n, wide), F32 if m == (0, 0) else BF) for m in moves],
        [own, got, mixed],
    )
    for m, x in zip(moves[1:], parts):
        back = (groups - m[0], n_head - m[1])
        total = total + shifted(x, ("groups", "head"), back).astype(F32)
    live = jnp.arange(n, dtype=jnp.int32) < counts[0]
    return jnp.where(live[:, None], total, 0.0).astype(BF)


def solution(mesh):
    placed = (
        P(("groups", "tok"), "head"),
        P(("groups", "tok"), "head"),
        P(("groups", "tok"), "head"),
        P(("groups", "tok"), "head"),
        P(("groups", "tok"), "head"),
        P("head"),
        P(("groups", "tok")),
        P("head", None, "rep"),
        P("head", None, "rep"),
        P("head", "rep", None),
        P("tok", ("head", "rep")),
        P(("head", "rep"), "tok"),
    )
    return jax.shard_map(
        on_device,
        mesh=mesh,
        in_specs=placed,
        out_specs=P(("groups", "tok"), ("head", "rep")),
        check_vma=False,
    )
```

time: 240 us -> 84.5 us (0.35)
  waiting for transfers between devices: 189 us -> 39.2 us
  starting transfers between devices: 0.16 us -> 32.9 us
  blocking collectives: 13.2 us -> 0 us
  between operations: 14 us -> 0.9 us
  matrix products: 10 us -> 0 us
  other arithmetic: 8.71 us -> 3.66 us
  Pallas kernels: 0 us -> 4.42 us
    psum x2 -> x0, waiting for transfers between devices: 87.3 us -> none  [the longest x1 71.5 us: on_device(): lax.psum(jnp.concatenate([grad_first, grad_third, grad_second], axis=1).a...]
    all_gather x2 -> x0, waiting for transfers between devices: 82.5 us -> none  [the longest x1 46.4 us: on_device(): lax.all_gather(mlp_down, 'tok', axis=1, tiled=True)]
    ppermute x0 -> x27, waiting for transfers between devices: none -> 39.2 us  [the longest x19 21.5 us: shifted(): return lax.ppermute(x, axes, pairs)]
    ppermute x0 -> x27, starting transfers between devices: none -> 32.9 us  [the longest x8 17.3 us: along(): return lax.ppermute(y, 'tok', pairs)]
    reduce_scatter x1 -> x0, waiting for transfers between devices: 17.8 us -> none  [on_device(): lax.psum_scatter(partial_terms.astype(jnp.bfloat16), ('head', 'rep'), sca...]
    dot_general x9 -> x0, matrix products: 10 us -> none  [the longest x1 4.77 us: on_device(): jnp.dot(expanded, lax.all_gather(mlp_down, 'tok', axis=1, tiled=True), pr...]
    psum x2 -> x0, blocking collectives: 7.51 us -> none  [the longest x1 4.93 us: on_device(): row_total = lax.psum(jnp.sum(mixed_rows * mixed_rows, axis=1), 'head')]
    all_gather x1 -> x0, blocking collectives: 5.64 us -> none  [on_device(): features = lax.all_gather(normed, 'head', axis=1, tiled=True)]
  transfers between devices with their start and end apart: 5 -> 27, of which waited for: 5 -> 14; matrix products, arithmetic and copies ran while one was open for 1% -> 2% of each run, Pallas kernels for 0% -> 5%
where the time goes in v1:
time: 84.5 us; the launch traced here: 84.1 us
  waiting for transfers between devices  39.2 us (46%)
  starting transfers between devices  32.9 us (39%)
  Pallas kernels  4.42 us (5%)
  other arithmetic  3.66 us (4%)
  local copies, waits for them, and re-layouts  2.96 us (4%)
  between operations  0.9 us (1%)
    ppermute x19, waiting for transfers between devices, shifted(): return lax.ppermute(x, axes, pairs)  21.5 us
    ppermute x8, waiting for transfers between devices, along(): return lax.ppermute(y, 'tok', pairs)  17.7 us
    ppermute x8, starting transfers between devices, along(): return lax.ppermute(y, 'tok', pairs)  17.3 us
    ppermute x19, starting transfers between devices, shifted(): return lax.ppermute(x, axes, pairs)  15.7 us
    pallas_call x5, Pallas kernels, call(): pl.pallas_call(kernel, out_shape=outs, in_specs=[pl.BlockSpec(memory_spac...  4.42 us
    unnamed x16, local copies, waits for them, and re-layouts  1.96 us
    concatenate x2, other arithmetic, on_device(): pair = jnp.concatenate([keys, scaled], axis=1)  1.87 us
  transfers between devices with their start and end apart: 27, of which 14 were waited for; matrix products, arithmetic and copies ran while one was open for 2% of the time, Pallas kernels for 5%

profile of v1, /device:TPU:0, one launch (start us, length us, event | category | flops | bytes accessed | tf_op | source)
XLA Modules:
  0.0 84.1 jit_solution(2204948543356997015)
XLA Ops:
  0.0 0.7 copy-done.7
  0.7 1.1 %multiply_convert_fusion = bf16[128,512]{1,0:T(8,128)(2,1)S(1)} fusion(bf16[128,512]{1,0:T(8,128)(2,1)} %param.13, f32[128]{0:T(128)S(1)} %bitcast.12), kind=kLoop, calls=%fused_computation.3 | loop fusion | flops 196608 | bytes 262656 | tf_op jit(solution)/shard_map/convert_element_type | solution.py:218
  1.8 0.0 copy-start.3
  1.8 0.9 %fusion = bf16[64,1024]{1,0:T(8,128)(2,1)S(1)} fusion(s32[]{:T(128)S(6)} %select_n.11, bf16[128,512]{1,0:T(8,128)(2,1)} %param.12, bf16[128,512]{1,0:T(8,128)(2,1)S(1)} %multiply_convert_fusion), kind=kLoop, calls=%fused_computation.4 | loop fusion | flops 262144 | bytes 393220 | tf_op jit(solution)/shard_map/concatenate | solution.py:219
  2.8 5.1 %collective-permute-start = (bf16[64,1024]{1,0:T(8,128)(2,1)S(1)}, bf16[64,1024]{1,0:T(8,128)(2,1)S(1)}, u32[]{:S(2)}, u32[]{:S(2)}) collective-permute-start(bf16[64,1024]{1,0:T(8,128)(2,1)S(1)} %fusion), channel_id=1, source_target_pairs={{4,0},{8,4},{12,8},{0,12},{5,1},{9,5},{13,9},{1,13},{6,2},{10,6},{... | collective-permute-start | bytes 393224 | tf_op jit(solution)/shard_map/ppermute | solution.py:26
  7.9 0.0 collective-permute-start.1
  7.9 1.0 %collective-permute-start.2 = (bf16[64,1024]{1,0:T(8,128)(2,1)S(1)}, bf16[64,1024]{1,0:T(8,128)(2,1)S(1)}, u32[]{:S(2)}, u32[]{:S(2)}) collective-permute-start(bf16[64,1024]{1,0:T(8,128)(2,1)S(1)} %fusion), channel_id=1, source_target_pairs={{12,0},{0,4},{4,8},{8,12},{13,1},{1,5},{5,9},{9,13},{14,2},{2,6},{... | collective-permute-start | bytes 393224 | tf_op jit(solution)/shard_map/ppermute | solution.py:26
  8.9 1.0 %constant_dynamic-slice_fusion.1.refs_10_ = bf16[256,512]{1,0:T(8,128)(2,1)S(1)} fusion(bf16[256,1024]{1,0:T(8,128)(2,1)} %param.22, s32[]{:T(128)S(6)} %select_n.12), kind=kLoop, calls=%fused_computation.7 | loop fusion | bytes 524292 | tf_op jit(solution)/shard_map/dynamic_slice | solution.py:221
  9.9 0.0 copy-start.6
  9.9 1.9 %collective-permute-done.refs_1_ = bf16[64,1024]{1,0:T(8,128)(2,1)S(1)} collective-permute-done((bf16[64,1024]{1,0:T(8,128)(2,1)S(1)}, bf16[64,1024]{1,0:T(8,128)(2,1)S(1)}, u32[]{:S(2)}, u32[]{:S(2)}) %collective-permute-start) | collective-permute-done | bytes 131104 | tf_op jit(solution)/shard_map/ppermute | solution.py:26
  11.8 7.3 %collective-permute-done.1.refs_2_ = bf16[64,1024]{1,0:T(8,128)(2,1)S(1)} collective-permute-done((bf16[64,1024]{1,0:T(8,128)(2,1)S(1)}, bf16[64,1024]{1,0:T(8,128)(2,1)S(1)}, u32[]{:S(2)}, u32[]{:S(2)}) %collective-permute-start.1) | collective-permute-done | bytes 131104 | tf_op jit(solution)/shard_map/ppermute | solution.py:26
  19.1 0.0 collective-permute-done.2.refs_3_
  19.1 0.0 collective-permute-start.3
  19.1 0.5 collective-permute-start.4
  19.6 0.0 collective-permute-start.5
  19.6 2.6 %collective-permute-start.16 = (bf16[256,512]{1,0:T(8,128)(2,1)S(1)}, bf16[256,512]{1,0:T(8,128)(2,1)S(1)}, u32[]{:S(2)}, u32[]{:S(2)}) collective-permute-start(bf16[256,512]{1,0:T(8,128)(2,1)S(1)} %constant_dynamic-slice_fusion.1.refs_10_), channel_id=1, source_target_pairs={{0,8},{4,12},{8,0},{12,4},{1,9},{5,13},{9,1},{13,5},{2,10},{6,14},... | collective-permute-start | bytes 786440 | tf_op jit(solution)/shard_map/ppermute | solution.py:201
  22.2 1.4 %collective-permute-start.15 = (bf16[256,512]{1,0:T(8,128)(2,1)S(1)}, bf16[256,512]{1,0:T(8,128)(2,1)S(1)}, u32[]{:S(2)}, u32[]{:S(2)}) collective-permute-start(bf16[256,512]{1,0:T(8,128)(2,1)S(1)} %constant_dynamic-slice_fusion.1.refs_10_), channel_id=1, source_target_pairs={{0,4},{4,8},{8,12},{1,5},{5,9},{9,13},{2,6},{6,10},{10,14},{3,7},{... | collective-permute-start | bytes 786440 | tf_op jit(solution)/shard_map/ppermute | solution.py:201
  23.7 0.9 %pad_maximum_fusion.refs_0_ = bf16[128,1024]{1,0:T(8,128)(2,1)S(1)} fusion(bf16[128,512]{1,0:T(8,128)(2,1)S(1)} %multiply_convert_fusion, bf16[128,512]{1,0:T(8,128)(2,1)} %param.12), kind=kLoop, calls=%fused_computation.1 | loop fusion | flops 524288 | bytes 524288 | tf_op jit(solution)/shard_map/concatenate | solution.py:219
  24.6 0.0 collective-permute-done.3.refs_4_
  24.6 1.3 %collective-permute-start.18 = (bf16[256,512]{1,0:T(8,128)(2,1)S(1)}, bf16[256,512]{1,0:T(8,128)(2,1)S(1)}, u32[]{:S(2)}, u32[]{:S(2)}) collective-permute-start(bf16[256,512]{1,0:T(8,128)(2,1)S(1)} %constant_dynamic-slice_fusion.1.refs_10_), channel_id=1, source_target_pairs={{4,0},{8,4},{12,8},{5,1},{9,5},{13,9},{6,2},{10,6},{14,10},{7,3},{... | collective-permute-start | bytes 786440 | tf_op jit(solution)/shard_map/ppermute | solution.py:201
  25.9 0.0 collective-permute-done.4.refs_5_
  25.9 3.5 %collective-permute-start.20 = (bf16[512,256]{1,0:T(8,128)(2,1)S(1)}, bf16[512,256]{1,0:T(8,128)(2,1)S(1)}, u32[]{:S(2)}, u32[]{:S(2)}) collective-permute-start(bf16[512,256]{1,0:T(8,128)(2,1)S(1)} %constant_dynamic-slice_fusion.refs_0_), channel_id=1, source_target_pairs={{0,8},{4,12},{8,0},{12,4},{1,9},{5,13},{9,1},{13,5},{2,10},{6,14},... | collective-permute-start | bytes 786440 | tf_op jit(solution)/shard_map/ppermute | solution.py:201
  29.4 0.0 collective-permute-done.5.refs_6_
  29.4 0.0 copy-start.5
  29.4 1.2 %copy-done.5 = f32[1,512,512]{2,1,0:T(8,128)S(1)} copy-done((f32[1,512,512]{2,1,0:T(8,128)S(1)}, f32[1,512,512]{2,1,0:T(8,128)}, u32[]{:S(2)}) %copy-start.5) | copy-done | bytes 1048600
  30.6 3.1 %shard_map.118 = (f32[128,256]{1,0:T(8,128)S(1)}, f32[8,256]{1,0:T(8,128)S(1)}, bf16[144,256]{1,0:T(8,128)(2,1)S(1)}) custom-call(bf16[128,1024]{1,0:T(8,128)(2,1)S(1)} %pad_maximum_fusion.refs_0_, bf16[64,1024]{1,0:T(8,128)(2,1)S(1)} %collective-permute-done.refs_1_, bf16[64,1024]{1,0:T(8,128)(2,1)S(1)} %collective-permute-done.1.refs_2_, ...), custom_call_target="tpu_custom_call" | custom-call | flops 1811939328 | bytes 4538368 | tf_op jit(solution)/shard_map/pallas_call | solution.py:31
  33.7 0.0 copy-start.2
  33.7 0.1 collective-permute-start.6
  33.8 1.3 %collective-permute-done.6.got = bf16[144,256]{1,0:T(8,128)(2,1)S(1)} collective-permute-done((bf16[144,256]{1,0:T(8,128)(2,1)S(1)}, bf16[144,256]{1,0:T(8,128)(2,1)S(1)}, u32[]{:S(2)}, u32[]{:S(2)}) %collective-permute-start.6) | collective-permute-done | bytes 73760 | tf_op jit(solution)/shard_map/ppermute | solution.py:26
  35.1 1.5 %collective-permute-start.14 = (f32[1,512]{1,0:T(1,128)S(1)}, f32[1,512]{1,0:T(1,128)S(1)}, u32[]{:S(2)}, u32[]{:S(2)}) collective-permute-start(f32[1,512]{1,0:T(1,128)S(1)} %bitcast.7), channel_id=1, source_target_pairs={{2,0},{0,2},{3,1},{1,3},{6,4},{4,6},{7,5},{5,7},{10,8},{8,10},{11,... | collective-permute-start | bytes 6152 | tf_op jit(solution)/shard_map/ppermute | solution.py:26
  36.6 2.1 %collective-permute-done.14.refs_9_ = f32[1,512]{1,0:T(1,128)S(1)} collective-permute-done((f32[1,512]{1,0:T(1,128)S(1)}, f32[1,512]{1,0:T(1,128)S(1)}, u32[]{:S(2)}, u32[]{:S(2)}) %collective-permute-start.14) | collective-permute-done | bytes 2080 | tf_op jit(solution)/shard_map/ppermute | solution.py:26
  38.7 1.5 %collective-permute-start.10 = (bf16[128,256]{1,0:T(8,128)(2,1)S(1)}, bf16[128,256]{1,0:T(8,128)(2,1)S(1)}, u32[]{:S(2)}, u32[]{:S(2)}) collective-permute-start(bf16[128,256]{1,0:T(8,128)(2,1)S(1)} %get-tuple-element.28.refs_0_), channel_id=1, source_target_pairs={{16,0},{18,2},{0,16},{2,18},{17,1},{19,3},{1,17},{3,19},{20,4},{22... | collective-permute-start | bytes 196616 | tf_op jit(solution)/shard_map/ppermute | solution.py:26
  40.2 0.0 collective-permute-done.16.refs_13_
  40.2 1.4 %collective-permute-start.12 = (bf16[128,256]{1,0:T(8,128)(2,1)S(1)}, bf16[128,256]{1,0:T(8,128)(2,1)S(1)}, u32[]{:S(2)}, u32[]{:S(2)}) collective-permute-start(bf16[128,256]{1,0:T(8,128)(2,1)S(1)} %get-tuple-element.28.refs_0_), channel_id=1, source_target_pairs={{18,0},{16,2},{2,16},{0,18},{19,1},{17,3},{3,17},{1,19},{22,4},{20... | collective-permute-start | bytes 196616 | tf_op jit(solution)/shard_map/ppermute | solution.py:26
  41.6 0.0 collective-permute-done.15.refs_11_
  41.6 0.5 collective-permute-start.8
  42.2 9.6 %collective-permute-done.20.refs_3_ = bf16[512,256]{1,0:T(8,128)(2,1)S(1)} collective-permute-done((bf16[512,256]{1,0:T(8,128)(2,1)S(1)}, bf16[512,256]{1,0:T(8,128)(2,1)S(1)}, u32[]{:S(2)}, u32[]{:S(2)}) %collective-permute-start.20) | collective-permute-done | bytes 262176 | tf_op jit(solution)/shard_map/ppermute | solution.py:201
  51.7 1.3 %collective-permute-start.17 = (bf16[256,512]{1,0:T(8,128)(2,1)S(1)}, bf16[256,512]{1,0:T(8,128)(2,1)S(1)}, u32[]{:S(2)}, u32[]{:S(2)}) collective-permute-start(bf16[256,512]{1,0:T(8,128)(2,1)S(1)} %collective-permute-done.16.refs_13_), channel_id=1, source_target_pairs={{8,12},{4,0},{9,13},{5,1},{10,14},{6,2},{11,15},{7,3},{24,28},{20,... | collective-permute-start | bytes 786440 | tf_op jit(solution)/shard_map/ppermute | solution.py:201
  53.0 4.6 %collective-permute-start.19 = (bf16[512,256]{1,0:T(8,128)(2,1)S(1)}, bf16[512,256]{1,0:T(8,128)(2,1)S(1)}, u32[]{:S(2)}, u32[]{:S(2)}) collective-permute-start(bf16[512,256]{1,0:T(8,128)(2,1)S(1)} %constant_dynamic-slice_fusion.refs_0_), channel_id=1, source_target_pairs={{0,4},{4,8},{8,12},{1,5},{5,9},{9,13},{2,6},{6,10},{10,14},{3,7},{... | collective-permute-start | bytes 786440 | tf_op jit(solution)/shard_map/ppermute | solution.py:201
  57.6 0.0 collective-permute-done.12.refs_6_
  57.6 1.3 %collective-permute-start.22 = (bf16[512,256]{1,0:T(8,128)(2,1)S(1)}, bf16[512,256]{1,0:T(8,128)(2,1)S(1)}, u32[]{:S(2)}, u32[]{:S(2)}) collective-permute-start(bf16[512,256]{1,0:T(8,128)(2,1)S(1)} %constant_dynamic-slice_fusion.refs_0_), channel_id=1, source_target_pairs={{4,0},{8,4},{12,8},{5,1},{9,5},{13,9},{6,2},{10,6},{14,10},{7,3},{... | collective-permute-start | bytes 786440 | tf_op jit(solution)/shard_map/ppermute | solution.py:201
  58.9 0.0 collective-permute-done.8.refs_2_
  58.9 1.3 %collective-permute-start.21 = (bf16[512,256]{1,0:T(8,128)(2,1)S(1)}, bf16[512,256]{1,0:T(8,128)(2,1)S(1)}, u32[]{:S(2)}, u32[]{:S(2)}) collective-permute-start(bf16[512,256]{1,0:T(8,128)(2,1)S(1)} %collective-permute-done.20.refs_3_), channel_id=1, source_target_pairs={{8,12},{4,0},{9,13},{5,1},{10,14},{6,2},{11,15},{7,3},{24,28},{20,... | collective-permute-start | bytes 786440 | tf_op jit(solution)/shard_map/ppermute | solution.py:201
  60.2 0.1 collective-permute-start.11
  60.3 1.2 %collective-permute-done.11.refs_5_ = bf16[128,256]{1,0:T(8,128)(2,1)S(1)} collective-permute-done((bf16[128,256]{1,0:T(8,128)(2,1)S(1)}, bf16[128,256]{1,0:T(8,128)(2,1)S(1)}, u32[]{:S(2)}, u32[]{:S(2)}) %collective-permute-start.11) | collective-permute-done | bytes 65568 | tf_op jit(solution)/shard_map/ppermute | solution.py:26
  61.6 0.2 collective-permute-start.13
  61.7 1.1 %collective-permute-done.13.refs_7_ = bf16[128,256]{1,0:T(8,128)(2,1)S(1)} collective-permute-done((bf16[128,256]{1,0:T(8,128)(2,1)S(1)}, bf16[128,256]{1,0:T(8,128)(2,1)S(1)}, u32[]{:S(2)}, u32[]{:S(2)}) %collective-permute-start.13) | collective-permute-done | bytes 65568 | tf_op jit(solution)/shard_map/ppermute | solution.py:26
  62.8 0.2 collective-permute-start.9
  63.0 1.1 %collective-permute-done.9.refs_3_ = bf16[128,256]{1,0:T(8,128)(2,1)S(1)} collective-permute-done((bf16[128,256]{1,0:T(8,128)(2,1)S(1)}, bf16[128,256]{1,0:T(8,128)(2,1)S(1)}, u32[]{:S(2)}, u32[]{:S(2)}) %collective-permute-start.9) | collective-permute-done | bytes 65568 | tf_op jit(solution)/shard_map/ppermute | solution.py:26
  64.1 0.7 shard_map.120.h
  64.7 0.0 collective-permute-done.19.refs_1_
  64.8 4.0 %collective-permute-done.22.refs_4_ = bf16[512,256]{1,0:T(8,128)(2,1)S(1)} collective-permute-done((bf16[512,256]{1,0:T(8,128)(2,1)S(1)}, bf16[512,256]{1,0:T(8,128)(2,1)S(1)}, u32[]{:S(2)}, u32[]{:S(2)}) %collective-permute-start.22) | collective-permute-done | bytes 262176 | tf_op jit(solution)/shard_map/ppermute | solution.py:201
  68.7 4.2 %collective-permute-done.21.refs_2_.refs_5_ = bf16[512,256]{1,0:T(8,128)(2,1)S(1)} collective-permute-done((bf16[512,256]{1,0:T(8,128)(2,1)S(1)}, bf16[512,256]{1,0:T(8,128)(2,1)S(1)}, u32[]{:S(2)}, u32[]{:S(2)}) %collective-permute-start.21) | collective-permute-done | bytes 262176 | tf_op jit(solution)/shard_map/ppermute | solution.py:201
  72.9 0.6 shard_map.121
  73.5 0.1 collective-permute-start.23
  74.2 0.9 %collective-permute-done.23.got = bf16[256,512]{1,0:T(8,128)(2,1)S(1)} collective-permute-done((bf16[256,512]{1,0:T(8,128)(2,1)S(1)}, bf16[256,512]{1,0:T(8,128)(2,1)S(1)}, u32[]{:S(2)}, u32[]{:S(2)}) %collective-permute-start.23) | collective-permute-done | bytes 262176 | tf_op jit(solution)/shard_map/ppermute | solution.py:26
  75.1 0.1 shard_map.122
  75.2 1.6 %collective-permute-start.24 = (bf16[128,256]{1,0:T(8,128)(2,1)S(1)}, bf16[128,256]{1,0:T(8,128)(2,1)S(1)}, u32[]{:S(2)}, u32[]{:S(2)}) collective-permute-start(bf16[128,256]{1,0:T(8,128)(2,1)S(1)} %get-tuple-element.36), channel_id=1, source_target_pairs={{2,0},{0,2},{18,16},{16,18},{3,1},{1,3},{19,17},{17,19},{6,4},{4,6... | collective-permute-start | bytes 196616 | tf_op jit(solution)/shard_map/ppermute | solution.py:26
  76.7 1.5 %collective-permute-start.25 = (bf16[128,256]{1,0:T(8,128)(2,1)S(1)}, bf16[128,256]{1,0:T(8,128)(2,1)S(1)}, u32[]{:S(2)}, u32[]{:S(2)}) collective-permute-start(bf16[128,256]{1,0:T(8,128)(2,1)S(1)} %get-tuple-element.37), channel_id=1, source_target_pairs={{16,0},{18,2},{0,16},{2,18},{17,1},{19,3},{1,17},{3,19},{20,4},{22... | collective-permute-start | bytes 196616 | tf_op jit(solution)/shard_map/ppermute | solution.py:26
  78.2 0.5 collective-permute-start.26
  78.7 0.8 collective-permute-done.24
  79.5 1.5 %collective-permute-done.25 = bf16[128,256]{1,0:T(8,128)(2,1)S(1)} collective-permute-done((bf16[128,256]{1,0:T(8,128)(2,1)S(1)}, bf16[128,256]{1,0:T(8,128)(2,1)S(1)}, u32[]{:S(2)}, u32[]{:S(2)}) %collective-permute-start.25) | collective-permute-done | bytes 65568 | tf_op jit(solution)/shard_map/ppermute | solution.py:26
  81.0 2.4 %collective-permute-done.26 = bf16[128,256]{1,0:T(8,128)(2,1)S(1)} collective-permute-done((bf16[128,256]{1,0:T(8,128)(2,1)S(1)}, bf16[128,256]{1,0:T(8,128)(2,1)S(1)}, u32[]{:S(2)}, u32[]{:S(2)}) %collective-permute-start.26) | collective-permute-done | bytes 65568 | tf_op jit(solution)/shard_map/ppermute | solution.py:26
  83.4 0.7 select_convert_fusion
  (18 shorter events, 0.1 us)
Async XLA Ops:
  0.0 8.9 %copy-start = (bf16[1024,256]{1,0:T(8,128)(2,1)S(1)}, bf16[1024,256]{1,0:T(8,128)(2,1)}, u32[]{:S(2)}) copy-start(bf16[1024,256]{1,0:T(8,128)(2,1)} %param.23) | copy-start | bytes 1572868
  0.0 0.7 copy-start.7
  0.7 28.7 %copy-start.4 = (f32[1,512,512]{2,1,0:T(8,128)S(1)}, f32[1,512,512]{2,1,0:T(8,128)}, u32[]{:S(2)}) copy-start(f32[1,512,512]{2,1,0:T(8,128)} %param.20) | copy-start | bytes 3145732
  1.8 27.6 %copy-start.3 = (f32[1,512,512]{2,1,0:T(8,128)S(1)}, f32[1,512,512]{2,1,0:T(8,128)}, u32[]{:S(2)}) copy-start(f32[1,512,512]{2,1,0:T(8,128)} %param.19) | copy-start | bytes 3145732
  2.8 9.0 %collective-permute-start = (bf16[64,1024]{1,0:T(8,128)(2,1)S(1)}, bf16[64,1024]{1,0:T(8,128)(2,1)S(1)}, u32[]{:S(2)}, u32[]{:S(2)}) collective-permute-start(bf16[64,1024]{1,0:T(8,128)(2,1)S(1)} %fusion), channel_id=1, source_target_pairs={{4,0},{8,4},{12,8},{0,12},{5,1},{9,5},{13,9},{1,13},{6,2},{10,6},{... | collective-permute-start | bytes 393224 | tf_op jit(solution)/shard_map/ppermute | solution.py:26
  7.9 11.2 %collective-permute-start.1 = (bf16[64,1024]{1,0:T(8,128)(2,1)S(1)}, bf16[64,1024]{1,0:T(8,128)(2,1)S(1)}, u32[]{:S(2)}, u32[]{:S(2)}) collective-permute-start(bf16[64,1024]{1,0:T(8,128)(2,1)S(1)} %fusion), channel_id=1, source_target_pairs={{8,0},{12,4},{0,8},{4,12},{9,1},{13,5},{1,9},{5,13},{10,2},{14,6},... | collective-permute-start | bytes 393224 | tf_op jit(solution)/shard_map/ppermute | solution.py:26
  7.9 11.2 %collective-permute-start.2 = (bf16[64,1024]{1,0:T(8,128)(2,1)S(1)}, bf16[64,1024]{1,0:T(8,128)(2,1)S(1)}, u32[]{:S(2)}, u32[]{:S(2)}) collective-permute-start(bf16[64,1024]{1,0:T(8,128)(2,1)S(1)} %fusion), channel_id=1, source_target_pairs={{12,0},{0,4},{4,8},{8,12},{13,1},{1,5},{5,9},{9,13},{14,2},{2,6},{... | collective-permute-start | bytes 393224 | tf_op jit(solution)/shard_map/ppermute | solution.py:26
  9.9 19.5 %copy-start.6 = (bf16[128,512]{1,0:T(8,128)(2,1)S(1)}, bf16[128,512]{1,0:T(8,128)(2,1)}, u32[]{:S(2)}) copy-start(bf16[128,512]{1,0:T(8,128)(2,1)} %refs_10_.1) | copy-start | bytes 393220
  19.1 5.5 %collective-permute-start.3 = (bf16[64,1024]{1,0:T(8,128)(2,1)S(1)}, bf16[64,1024]{1,0:T(8,128)(2,1)S(1)}, u32[]{:S(2)}, u32[]{:S(2)}) collective-permute-start(bf16[64,1024]{1,0:T(8,128)(2,1)S(1)} %collective-permute-done.refs_1_), channel_id=1, source_target_pairs={{1,0},{0,1},{3,2},{2,3},{5,4},{4,5},{7,6},{6,7},{9,8},{8,9},{11,10... | collective-permute-start | bytes 393224 | tf_op jit(solution)/shard_map/ppermute | solution.py:26
  19.1 6.8 %collective-permute-start.4 = (bf16[64,1024]{1,0:T(8,128)(2,1)S(1)}, bf16[64,1024]{1,0:T(8,128)(2,1)S(1)}, u32[]{:S(2)}, u32[]{:S(2)}) collective-permute-start(bf16[64,1024]{1,0:T(8,128)(2,1)S(1)} %collective-permute-done.1.refs_2_), channel_id=1, source_target_pairs={{1,0},{0,1},{3,2},{2,3},{5,4},{4,5},{7,6},{6,7},{9,8},{8,9},{11,10... | collective-permute-start | bytes 393224 | tf_op jit(solution)/shard_map/ppermute | solution.py:26
  19.6 9.8 %collective-permute-start.5 = (bf16[64,1024]{1,0:T(8,128)(2,1)S(1)}, bf16[64,1024]{1,0:T(8,128)(2,1)S(1)}, u32[]{:S(2)}, u32[]{:S(2)}) collective-permute-start(bf16[64,1024]{1,0:T(8,128)(2,1)S(1)} %collective-permute-done.2.refs_3_), channel_id=1, source_target_pairs={{1,0},{0,1},{3,2},{2,3},{5,4},{4,5},{7,6},{6,7},{9,8},{8,9},{11,10... | collective-permute-start | bytes 393224 | tf_op jit(solution)/shard_map/ppermute | solution.py:26
  19.6 20.6 %collective-permute-start.16 = (bf16[256,512]{1,0:T(8,128)(2,1)S(1)}, bf16[256,512]{1,0:T(8,128)(2,1)S(1)}, u32[]{:S(2)}, u32[]{:S(2)}) collective-permute-start(bf16[256,512]{1,0:T(8,128)(2,1)S(1)} %constant_dynamic-slice_fusion.1.refs_10_), channel_id=1, source_target_pairs={{0,8},{4,12},{8,0},{12,4},{1,9},{5,13},{9,1},{13,5},{2,10},{6,14},... | collective-permute-start | bytes 786440 | tf_op jit(solution)/shard_map/ppermute | solution.py:201
  22.2 19.4 %collective-permute-start.15 = (bf16[256,512]{1,0:T(8,128)(2,1)S(1)}, bf16[256,512]{1,0:T(8,128)(2,1)S(1)}, u32[]{:S(2)}, u32[]{:S(2)}) collective-permute-start(bf16[256,512]{1,0:T(8,128)(2,1)S(1)} %constant_dynamic-slice_fusion.1.refs_10_), channel_id=1, source_target_pairs={{0,4},{4,8},{8,12},{1,5},{5,9},{9,13},{2,6},{6,10},{10,14},{3,7},{... | collective-permute-start | bytes 786440 | tf_op jit(solution)/shard_map/ppermute | solution.py:201
  24.6 17.5 %collective-permute-start.18 = (bf16[256,512]{1,0:T(8,128)(2,1)S(1)}, bf16[256,512]{1,0:T(8,128)(2,1)S(1)}, u32[]{:S(2)}, u32[]{:S(2)}) collective-permute-start(bf16[256,512]{1,0:T(8,128)(2,1)S(1)} %constant_dynamic-slice_fusion.1.refs_10_), channel_id=1, source_target_pairs={{4,0},{8,4},{12,8},{5,1},{9,5},{13,9},{6,2},{10,6},{14,10},{7,3},{... | collective-permute-start | bytes 786440 | tf_op jit(solution)/shard_map/ppermute | solution.py:201
  25.9 25.8 %collective-permute-start.20 = (bf16[512,256]{1,0:T(8,128)(2,1)S(1)}, bf16[512,256]{1,0:T(8,128)(2,1)S(1)}, u32[]{:S(2)}, u32[]{:S(2)}) collective-permute-start(bf16[512,256]{1,0:T(8,128)(2,1)S(1)} %constant_dynamic-slice_fusion.refs_0_), channel_id=1, source_target_pairs={{0,8},{4,12},{8,0},{12,4},{1,9},{5,13},{9,1},{13,5},{2,10},{6,14},... | collective-permute-start | bytes 786440 | tf_op jit(solution)/shard_map/ppermute | solution.py:201
  29.4 1.2 %copy-start.5 = (f32[1,512,512]{2,1,0:T(8,128)S(1)}, f32[1,512,512]{2,1,0:T(8,128)}, u32[]{:S(2)}) copy-start(f32[1,512,512]{2,1,0:T(8,128)} %param.21) | copy-start | bytes 3145732
  30.6 5.9 %copy-start.1 = (bf16[128,512]{1,0:T(8,128)(2,1)S(1)}, bf16[128,512]{1,0:T(8,128)(2,1)}, u32[]{:S(2)}) copy-start(bf16[128,512]{1,0:T(8,128)(2,1)} %stream.1) | copy-start | bytes 393220
  33.7 1.3 %copy-start.2 = (f32[512]{0:T(512)S(1)}, f32[512]{0:T(512)}, u32[]{:S(2)}) copy-start(f32[512]{0:T(512)} %param.17) | copy-start | bytes 6148
  33.7 1.3 %collective-permute-start.6 = (bf16[144,256]{1,0:T(8,128)(2,1)S(1)}, bf16[144,256]{1,0:T(8,128)(2,1)S(1)}, u32[]{:S(2)}, u32[]{:S(2)}) collective-permute-start(bf16[144,256]{1,0:T(8,128)(2,1)S(1)} %get-tuple-element.27), channel_id=1, source_target_pairs={{1,0},{0,1},{3,2},{2,3},{5,4},{4,5},{7,6},{6,7},{9,8},{8,9},{11,10... | collective-permute-start | bytes 221192 | tf_op jit(solution)/shard_map/ppermute | solution.py:26
  35.1 3.6 %collective-permute-start.14 = (f32[1,512]{1,0:T(1,128)S(1)}, f32[1,512]{1,0:T(1,128)S(1)}, u32[]{:S(2)}, u32[]{:S(2)}) collective-permute-start(f32[1,512]{1,0:T(1,128)S(1)} %bitcast.7), channel_id=1, source_target_pairs={{2,0},{0,2},{3,1},{1,3},{6,4},{4,6},{7,5},{5,7},{10,8},{8,10},{11,... | collective-permute-start | bytes 6152 | tf_op jit(solution)/shard_map/ppermute | solution.py:26
  38.7 14.4 %collective-permute-start.10 = (bf16[128,256]{1,0:T(8,128)(2,1)S(1)}, bf16[128,256]{1,0:T(8,128)(2,1)S(1)}, u32[]{:S(2)}, u32[]{:S(2)}) collective-permute-start(bf16[128,256]{1,0:T(8,128)(2,1)S(1)} %get-tuple-element.28.refs_0_), channel_id=1, source_target_pairs={{16,0},{18,2},{0,16},{2,18},{17,1},{19,3},{1,17},{3,19},{20,4},{22... | collective-permute-start | bytes 196616 | tf_op jit(solution)/shard_map/ppermute | solution.py:26
  40.2 17.4 %collective-permute-start.12 = (bf16[128,256]{1,0:T(8,128)(2,1)S(1)}, bf16[128,256]{1,0:T(8,128)(2,1)S(1)}, u32[]{:S(2)}, u32[]{:S(2)}) collective-permute-start(bf16[128,256]{1,0:T(8,128)(2,1)S(1)} %get-tuple-element.28.refs_0_), channel_id=1, source_target_pairs={{18,0},{16,2},{2,16},{0,18},{19,1},{17,3},{3,17},{1,19},{22,4},{20... | collective-permute-start | bytes 196616 | tf_op jit(solution)/shard_map/ppermute | solution.py:26
  41.6 17.3 %collective-permute-start.8 = (bf16[128,256]{1,0:T(8,128)(2,1)S(1)}, bf16[128,256]{1,0:T(8,128)(2,1)S(1)}, u32[]{:S(2)}, u32[]{:S(2)}) collective-permute-start(bf16[128,256]{1,0:T(8,128)(2,1)S(1)} %get-tuple-element.28.refs_0_), channel_id=1, source_target_pairs={{2,0},{0,2},{18,16},{16,18},{3,1},{1,3},{19,17},{17,19},{6,4},{4,6... | collective-permute-start | bytes 196616 | tf_op jit(solution)/shard_map/ppermute | solution.py:26
  42.2 18.1 %collective-permute-start.7 = (bf16[128,256]{1,0:T(8,128)(2,1)S(1)}, bf16[128,256]{1,0:T(8,128)(2,1)S(1)}, u32[]{:S(2)}, u32[]{:S(2)}) collective-permute-start(bf16[128,256]{1,0:T(8,128)(2,1)S(1)} %get-tuple-element.28.refs_0_), channel_id=1, source_target_pairs={{1,0},{0,1},{3,2},{2,3},{5,4},{4,5},{7,6},{6,7},{9,8},{8,9},{11,10... | collective-permute-start | bytes 196616 | tf_op jit(solution)/shard_map/ppermute | solution.py:26
  51.7 12.3 %collective-permute-start.17 = (bf16[256,512]{1,0:T(8,128)(2,1)S(1)}, bf16[256,512]{1,0:T(8,128)(2,1)S(1)}, u32[]{:S(2)}, u32[]{:S(2)}) collective-permute-start(bf16[256,512]{1,0:T(8,128)(2,1)S(1)} %collective-permute-done.16.refs_13_), channel_id=1, source_target_pairs={{8,12},{4,0},{9,13},{5,1},{10,14},{6,2},{11,15},{7,3},{24,28},{20,... | collective-permute-start | bytes 786440 | tf_op jit(solution)/shard_map/ppermute | solution.py:201
  53.0 11.7 %collective-permute-start.19 = (bf16[512,256]{1,0:T(8,128)(2,1)S(1)}, bf16[512,256]{1,0:T(8,128)(2,1)S(1)}, u32[]{:S(2)}, u32[]{:S(2)}) collective-permute-start(bf16[512,256]{1,0:T(8,128)(2,1)S(1)} %constant_dynamic-slice_fusion.refs_0_), channel_id=1, source_target_pairs={{0,4},{4,8},{8,12},{1,5},{5,9},{9,13},{2,6},{6,10},{10,14},{3,7},{... | collective-permute-start | bytes 786440 | tf_op jit(solution)/shard_map/ppermute | solution.py:201
  57.6 11.1 %collective-permute-start.22 = (bf16[512,256]{1,0:T(8,128)(2,1)S(1)}, bf16[512,256]{1,0:T(8,128)(2,1)S(1)}, u32[]{:S(2)}, u32[]{:S(2)}) collective-permute-start(bf16[512,256]{1,0:T(8,128)(2,1)S(1)} %constant_dynamic-slice_fusion.refs_0_), channel_id=1, source_target_pairs={{4,0},{8,4},{12,8},{5,1},{9,5},{13,9},{6,2},{10,6},{14,10},{7,3},{... | collective-permute-start | bytes 786440 | tf_op jit(solution)/shard_map/ppermute | solution.py:201
  58.9 14.0 %collective-permute-start.21 = (bf16[512,256]{1,0:T(8,128)(2,1)S(1)}, bf16[512,256]{1,0:T(8,128)(2,1)S(1)}, u32[]{:S(2)}, u32[]{:S(2)}) collective-permute-start(bf16[512,256]{1,0:T(8,128)(2,1)S(1)} %collective-permute-done.20.refs_3_), channel_id=1, source_target_pairs={{8,12},{4,0},{9,13},{5,1},{10,14},{6,2},{11,15},{7,3},{24,28},{20,... | collective-permute-start | bytes 786440 | tf_op jit(solution)/shard_map/ppermute | solution.py:201
  60.2 1.3 %collective-permute-start.11 = (bf16[128,256]{1,0:T(8,128)(2,1)S(1)}, bf16[128,256]{1,0:T(8,128)(2,1)S(1)}, u32[]{:S(2)}, u32[]{:S(2)}) collective-permute-start(bf16[128,256]{1,0:T(8,128)(2,1)S(1)} %collective-permute-done.10.refs_4_), channel_id=1, source_target_pairs={{1,0},{0,1},{3,2},{2,3},{5,4},{4,5},{7,6},{6,7},{9,8},{8,9},{11,10... | collective-permute-start | bytes 196616 | tf_op jit(solution)/shard_map/ppermute | solution.py:26
  61.6 1.3 %collective-permute-start.13 = (bf16[128,256]{1,0:T(8,128)(2,1)S(1)}, bf16[128,256]{1,0:T(8,128)(2,1)S(1)}, u32[]{:S(2)}, u32[]{:S(2)}) collective-permute-start(bf16[128,256]{1,0:T(8,128)(2,1)S(1)} %collective-permute-done.12.refs_6_), channel_id=1, source_target_pairs={{1,0},{0,1},{3,2},{2,3},{5,4},{4,5},{7,6},{6,7},{9,8},{8,9},{11,10... | collective-permute-start | bytes 196616 | tf_op jit(solution)/shard_map/ppermute | solution.py:26
  62.8 1.3 %collective-permute-start.9 = (bf16[128,256]{1,0:T(8,128)(2,1)S(1)}, bf16[128,256]{1,0:T(8,128)(2,1)S(1)}, u32[]{:S(2)}, u32[]{:S(2)}) collective-permute-start(bf16[128,256]{1,0:T(8,128)(2,1)S(1)} %collective-permute-done.8.refs_2_), channel_id=1, source_target_pairs={{1,0},{0,1},{3,2},{2,3},{5,4},{4,5},{7,6},{6,7},{9,8},{8,9},{11,10... | collective-permute-start | bytes 196616 | tf_op jit(solution)/shard_map/ppermute | solution.py:26
  73.5 1.6 %collective-permute-start.23 = (bf16[256,512]{1,0:T(8,128)(2,1)S(1)}, bf16[256,512]{1,0:T(8,128)(2,1)S(1)}, u32[]{:S(2)}, u32[]{:S(2)}) collective-permute-start(bf16[256,512]{1,0:T(8,128)(2,1)S(1)} %get-tuple-element.33), channel_id=1, source_target_pairs={{1,0},{0,1},{3,2},{2,3},{5,4},{4,5},{7,6},{6,7},{9,8},{8,9},{11,10... | collective-permute-start | bytes 786440 | tf_op jit(solution)/shard_map/ppermute | solution.py:26
  75.2 4.3 %collective-permute-start.24 = (bf16[128,256]{1,0:T(8,128)(2,1)S(1)}, bf16[128,256]{1,0:T(8,128)(2,1)S(1)}, u32[]{:S(2)}, u32[]{:S(2)}) collective-permute-start(bf16[128,256]{1,0:T(8,128)(2,1)S(1)} %get-tuple-element.36), channel_id=1, source_target_pairs={{2,0},{0,2},{18,16},{16,18},{3,1},{1,3},{19,17},{17,19},{6,4},{4,6... | collective-permute-start | bytes 196616 | tf_op jit(solution)/shard_map/ppermute | solution.py:26
  76.7 4.3 %collective-permute-start.25 = (bf16[128,256]{1,0:T(8,128)(2,1)S(1)}, bf16[128,256]{1,0:T(8,128)(2,1)S(1)}, u32[]{:S(2)}, u32[]{:S(2)}) collective-permute-start(bf16[128,256]{1,0:T(8,128)(2,1)S(1)} %get-tuple-element.37), channel_id=1, source_target_pairs={{16,0},{18,2},{0,16},{2,18},{17,1},{19,3},{1,17},{3,19},{20,4},{22... | collective-permute-start | bytes 196616 | tf_op jit(solution)/shard_map/ppermute | solution.py:26
  78.2 5.2 %collective-permute-start.26 = (bf16[128,256]{1,0:T(8,128)(2,1)S(1)}, bf16[128,256]{1,0:T(8,128)(2,1)S(1)}, u32[]{:S(2)}, u32[]{:S(2)}) collective-permute-start(bf16[128,256]{1,0:T(8,128)(2,1)S(1)} %get-tuple-element.38), channel_id=1, source_target_pairs={{18,0},{16,2},{2,16},{0,18},{19,1},{17,3},{3,17},{1,19},{22,4},{20... | collective-permute-start | bytes 196616 | tf_op jit(solution)/shard_map/ppermute | solution.py:26

commit v2 on v1

--- a/solution.py
+++ b/solution.py
@@ -9,7 +9,6 @@
 from jax.sharding import PartitionSpec as P
 
 BF, F32 = jnp.bfloat16, jnp.float32
-VMEM_BYTES = 48 << 20
 
 
 def dot(a, b, dims=((1,), (0,))):
@@ -26,15 +25,16 @@
     return lax.ppermute(x, axes, pairs)
 
 
-def call(kernel, outs, args, scratch=(), flops=0):
+def call(kernel, outs, args, scratch=(), flops=0, far=()):
     moved = sum(int(np.prod(x.shape)) * x.dtype.itemsize for x in (*args, *outs))
+    kept = sum(int(np.prod(x.shape)) * 4 for x in scratch if x.dtype in (BF, F32))
     return pl.pallas_call(
         kernel,
         out_shape=outs,
-        in_specs=[pl.BlockSpec(memory_space=pltpu.VMEM)] * len(args),
+        in_specs=[pl.BlockSpec(memory_space=pltpu.HBM if i in far else pltpu.VMEM) for i in range(len(args))],
         out_specs=[pl.BlockSpec(memory_space=pltpu.VMEM)] * len(outs),
         scratch_shapes=list(scratch),
-        compiler_params=pltpu.CompilerParams(vmem_limit_bytes=VMEM_BYTES),
+        compiler_params=pltpu.CompilerParams(vmem_limit_bytes=moved + kept + (10 << 20)),
         cost_estimate=pl.CostEstimate(flops=flops, bytes_accessed=moved, transcendentals=0),
     )(*args)
 
@@ -47,9 +47,22 @@
     return ref_width // lax.axis_size("rep")
 
 
+def pair_up_kernel(keys, values, rates, pair, *message):
+    n, dh = keys.shape
+    rate = jnp.broadcast_to(rates[...], (128, n)).T
+    pair[:, :dh] = keys[...]
+    for c in range(0, dh, 128):
+        pair[:, dh + c : dh + c + 128] = (values[:, c : c + 128].astype(F32) * rate).astype(BF)
+    for m in message:
+        rows = m.shape[0]
+        m[...] = pair[pl.ds(pl.multiple_of(lax.axis_index("rep") * rows, rows), rows), :]
+
+
 def fast_kernel(n_pieces, *refs):
     pieces, refs = refs[:n_pieces], refs[n_pieces:]
-    w1, w3, w2, q, own_out, own_sq, send, ks, es, hp = refs
+    w1, w3, w2_far, q, own_out, own_sq, send, ks, es, hp, w2, sem = refs
+    fetch = pltpu.make_async_copy(w2_far, w2, sem)
+    fetch.start()
     dh, hidden = w1.shape
     at = 0
     for p in pieces:
@@ -58,6 +71,7 @@
         es[at : at + n, :] = p[:, dh:]
         at += n
     tokens, step, block = at, min(at, 512), min(hidden, 256)
+    fetch.wait()
     old_sq = jnp.zeros((1, dh), F32)
     new_sq = jnp.zeros((1, dh), F32)
     for j in range(0, hidden, block):
@@ -117,12 +131,14 @@
     mixed_low[...] = y.astype(BF)
 
 
-def take(parts, step):
-    if len(parts) == 1:
-        return parts[0][...]
-    me, n = lax.axis_index("tok"), lax.axis_size("tok")
-    direct = me >= step if step == 1 else me < step
-    return jnp.where(direct, parts[0][...], parts[1][...])
+def take(parts, rows=None):
+    x = [p[...] if rows is None else p[rows, :] for p in parts]
+    return x[0] if len(x) == 1 else jnp.where(inner(), *x)
+
+
+def inner():
+    me = lax.axis_index("tok")
+    return jnp.logical_and(me > 0, me < lax.axis_size("tok") - 1)
 
 
 def split(refs, counts):
@@ -157,12 +173,12 @@
             zs[dg * n : (dg + 1) * n, cols] = (p[...].astype(F32) * inv * gain).astype(BF)
     total = None
     for s, parts in enumerate(blocks):
-        deep = parts[0].shape[0]
         if len(blocks) == 1:
-            z = zs[...]
+            term = dot(zs[...], take(parts))
         else:
-            z = zs[:, pl.ds(pl.multiple_of(lax.rem(me_t + len(blocks) - s, len(blocks)) * deep, deep), deep)]
-        term = dot(z, take(parts, s))
+            deep = width // len(blocks)
+            z = zs[:, pl.ds(pl.multiple_of(lax.bitwise_xor(me_t, s) * deep, deep), deep)]
+            term = dot(z, take(parts, slice(0, deep)))
         total = term if total is None else total + term
     out[...] = (0.5 * total * (1.0 + lax.erf(total * np.float32(0.5**0.5)))).astype(BF)
 
@@ -172,12 +188,16 @@
     me_h, me_r, me_t = lax.axis_index("head"), lax.axis_index("rep"), lax.axis_index("tok")
     n_head = lax.axis_size("head")
     for s, parts in enumerate(blocks):
-        wide = parts[0].shape[1]
-        term = dot(h[...], take(parts, s))
         if len(blocks) == 1:
-            os[...] = term
+            os[...] = dot(h[...], take(parts))
         else:
-            os[:, pl.ds(pl.multiple_of(lax.rem(me_t + len(blocks) - s, len(blocks)) * wide, wide), wide)] = term
+            wide = os.shape[1] // len(blocks)
+            x = take(parts, slice(wide, parts[0].shape[0]))
+            term = None
+            for at in range(0, h.shape[1], wide):
+                part = dot(h[:, at : at + wide], x[:, at : at + wide])
+                term = part if term is None else term + part
+            os[:, pl.ds(pl.multiple_of(lax.bitwise_xor(me_t, s) * wide, wide), wide)] = term
     wide = own.shape[1] // n_head
     for dh in range(n_head):
         at = lax.rem(me_h + dh, n_head) * 2 * wide
@@ -196,15 +216,16 @@
         out[...] = mixed[...] + total if i == 0 else total.astype(BF)
 
 
-def spread(x):
-    def along(y, pairs):
-        return lax.ppermute(y, "tok", pairs)
-
-    up = along(x, [(0, 1), (1, 2), (2, 3)])
-    down = along(x, [(1, 0), (2, 1), (3, 2)])
-    far = along(x, [(0, 2), (1, 3), (2, 0), (3, 1)])
-    last = along(far, [(2, 3), (1, 0)])
-    return [[x], [up, last], [far], [down, last]]
+def along(x, pairs):
+    return lax.ppermute(x, "tok", pairs)
+
+
+def first_phase(x):
+    return along(x, [(0, 1), (1, 0), (2, 3), (3, 2)]), along(x, [(0, 2), (2, 0), (1, 3), (3, 1)])
+
+
+def second_phase(x, far):
+    return along(x, [(1, 2), (2, 1)]), along(far, [(1, 0), (2, 3)])
 
 
 def on_device(
@@ -215,23 +236,32 @@
     me_g, me_r = lax.axis_index("groups"), lax.axis_index("rep")
     dh, n_key, n = keys.shape[1], keys.shape[0], queries.shape[0]
     wide = dh // reps
-    scaled = (rates * values.astype(F32)).astype(BF)
-    pair = jnp.concatenate([keys, scaled], axis=1)
     units = mlp_up.shape[1] // groups
     up_own = lax.dynamic_slice_in_dim(mlp_up, me_g * units, units, 1)
     down_own = lax.dynamic_slice_in_dim(mlp_down, me_g * units, units, 0)
+    share = [shape((n_key // reps, 2 * dh), BF)] if n_tok == 4 else []
+    pair, *message = call(
+        pair_up_kernel, [shape((n_key, 2 * dh), BF), *share], [keys, values, rates.reshape(1, n_key)]
+    )
+    gain = gain[None, :]
     if n_tok == 4:
-        piece = lax.dynamic_slice_in_dim(pair, me_r * (n_key // reps), n_key // reps, 0)
-        near = [shifted(piece, ("tok",), (s,)) for s in range(1, n_tok)]
-        near, up_own, down_own, gain = lax.optimization_barrier((near, up_own, down_own, gain))
-        tokens = [pair, *near, *[shifted(x, ("rep",), (1,)) for x in near]]
-        up_blocks, down_blocks = spread(up_own), spread(down_own)
+        flip = functools.partial(shifted, axes=("rep",), shifts=(1,))
+        near, far = first_phase(message[0])
+        wide_down = down_own.shape[1]
+        low_rows = [down_own[i : i + wide_down] for i in range(0, units, wide_down)]
+        packed = jnp.concatenate([up_own, jnp.concatenate(low_rows, axis=1)], axis=0)
+        near, far, own, gain, packed = lax.optimization_barrier((near, far, message[0], gain, packed))
+        middle, end = second_phase(own, far)
+        w_near, w_far = first_phase(packed)
+        gains = [gain] + [shifted(gain, ("head",), (s,)) for s in range(1, n_head)]
+        late = jnp.where(inner(), middle, end)
+        tokens = [pair, near, far, late, flip(near), flip(far), flip(late)]
+        tokens, gains = lax.optimization_barrier((tokens, gains))
     else:
         tokens = [lax.all_gather(pair, "tok", axis=0, tiled=True)]
         up_blocks = [[lax.all_gather(up_own, "tok", axis=0, tiled=True)]]
         down_blocks = [[lax.all_gather(down_own, "tok", axis=1, tiled=True)]]
-    gain = gain[None, :]
-    gains = [gain] + [shifted(gain, ("head",), (s,)) for s in range(1, n_head)]
+        gains = [gain] + [shifted(gain, ("head",), (s,)) for s in range(1, n_head)]
 
     n_all = sum(x.shape[0] for x in tokens)
     hidden = fw_one.shape[2]
@@ -239,8 +269,15 @@
         functools.partial(fast_kernel, len(tokens)),
         [shape((n, wide), F32), shape((8, wide), F32), shape((n + 16, wide), BF)],
         [*tokens, fw_one[0], fw_three[0], fw_two[0], queries],
-        [pltpu.VMEM((n_all, dh), BF), pltpu.VMEM((n_all, dh), BF), pltpu.VMEM((n, dh), F32)],
+        [
+            pltpu.VMEM((n_all, dh), BF),
+            pltpu.VMEM((n_all, dh), BF),
+            pltpu.VMEM((n, dh), F32),
+            pltpu.VMEM((hidden, dh), F32),
+            pltpu.SemaphoreType.DMA,
+        ],
         flops=12 * n_all * dh * hidden + 6 * n * dh * hidden,
+        far=(len(tokens) + 2,),
     )
     got = shifted(send, ("rep",), (1,))
     mixed, low = call(
@@ -248,6 +285,9 @@
     )
     moves = [(dg, h) for dg in range(groups) for h in range(n_head)]
     across = {m: low if m == (0, 0) else shifted(low, ("groups", "head"), m) for m in moves}
+    if n_tok == 4:
+        w_own, w_there, w_near, _ = lax.optimization_barrier((packed, w_far, w_near, list(across.values())))
+        up_blocks = down_blocks = [[packed], [w_near], [w_far], list(second_phase(w_own, w_there))]
     pieces, places = [], []
     for m, x in across.items():
         pieces += [x, shifted(x, ("rep",), (1,))]

time: 84.5 us -> 85.1 us (level)
  starting transfers between devices: 32.9 us -> 25.7 us
  waiting for transfers between devices: 39.2 us -> 45.4 us
  other arithmetic: 3.66 us -> 1.68 us
  local copies, waits for them, and re-layouts: 2.96 us -> 4.92 us
  Pallas kernels: 4.42 us -> 6.3 us
    ppermute x8, waiting for transfers between devices: 17.7 us -> 31.7 us  [along(): return lax.ppermute(x, 'tok', pairs)]
    ppermute x19 -> x16, waiting for transfers between devices: 21.5 us -> 13.8 us  [shifted(): return lax.ppermute(x, axes, pairs)]
    ppermute x19 -> x16, starting transfers between devices: 15.7 us -> 9.79 us  [shifted(): return lax.ppermute(x, axes, pairs)]
    pallas_call x5 -> x6, Pallas kernels: 4.42 us -> 6.3 us  [call(): pl.pallas_call(kernel, out_shape=outs, in_specs=[pl.BlockSpec(memory_spac...]
    concatenate x2 -> x1, other arithmetic: 1.87 us -> 0.04 us  [on_device(): jnp.concatenate([up_own, jnp.concatenate(low_rows, axis=1)], axis=0)]
    unnamed x16 -> x20, local copies, waits for them, and re-layouts: 1.96 us -> 3.77 us
    ppermute x8, starting transfers between devices: 17.3 us -> 15.9 us  [along(): return lax.ppermute(x, 'tok', pairs)]
    slice x0 -> x1, local copies, waits for them, and re-layouts: none -> 1.14 us  [on_device(): low_rows = [down_own[i:i + wide_down] for i in range(0, units, wide_down)]]
  transfers between devices with their start and end apart: 27 -> 24, of which waited for: 14 -> 17; matrix products, arithmetic and copies ran while one was open for 2% -> 2% of each run, Pallas kernels for 5% -> 5%
where the time goes in v2:
time: 85.1 us; the launch traced here: 84.8 us
  waiting for transfers between devices  45.4 us (53%)
  starting transfers between devices  25.7 us (30%)
  Pallas kernels  6.3 us (7%)
  local copies, waits for them, and re-layouts  4.92 us (6%)
  other arithmetic  1.68 us (2%)
    ppermute x8, waiting for transfers between devices, along(): return lax.ppermute(x, 'tok', pairs)  31.7 us
    ppermute x8, starting transfers between devices, along(): return lax.ppermute(x, 'tok', pairs)  15.9 us
    ppermute x16, waiting for transfers between devices, shifted(): return lax.ppermute(x, axes, pairs)  13.8 us
    ppermute x16, starting transfers between devices, shifted(): return lax.ppermute(x, axes, pairs)  9.79 us
    pallas_call x6, Pallas kernels, call(): pl.pallas_call(kernel, out_shape=outs, in_specs=[pl.BlockSpec(memory_spac...  6.3 us
    unnamed x20, local copies, waits for them, and re-layouts  3.77 us
  transfers between devices with their start and end apart: 24, of which 17 were waited for; matrix products, arithmetic and copies ran while one was open for 2% of the time, Pallas kernels for 5%

profile of v2, /device:TPU:0, one launch (start us, length us, event | category | flops | bytes accessed | tf_op | source)
XLA Modules:
  0.0 84.8 jit_solution(13262276181287597294)
XLA Ops:
  0.0 0.0 copy-start
  0.0 0.7 copy-done.5
  0.7 0.9 %copy-done.1 = bf16[128,512]{1,0:T(8,128)(2,1)S(1)} copy-done((bf16[128,512]{1,0:T(8,128)(2,1)S(1)}, bf16[128,512]{1,0:T(8,128)(2,1)}, u32[]{:S(2)}) %copy-start.1) | copy-done | bytes 131096
  1.6 0.9 %copy-done.2 = bf16[128,512]{1,0:T(8,128)(2,1)S(1)} copy-done((bf16[128,512]{1,0:T(8,128)(2,1)S(1)}, bf16[128,512]{1,0:T(8,128)(2,1)}, u32[]{:S(2)}) %copy-start.2) | copy-done | bytes 131096
  2.5 0.8 shard_map.118
  3.3 3.0 %collective-permute-start = (bf16[64,1024]{1,0:T(8,128)(2,1)}, bf16[64,1024]{1,0:T(8,128)(2,1)S(1)}, u32[]{:S(2)}, u32[]{:S(2)}) collective-permute-start(bf16[64,1024]{1,0:T(8,128)(2,1)} %get-tuple-element.39), channel_id=1, source_target_pairs={{0,4},{4,0},{8,12},{12,8},{1,5},{5,1},{9,13},{13,9},{2,6},{6,2},{1... | collective-permute-start | bytes 393224 | tf_op jit(solution)/shard_map/ppermute | solution.py:220
  6.3 2.6 %collective-permute-start.1 = (bf16[64,1024]{1,0:T(8,128)(2,1)}, bf16[64,1024]{1,0:T(8,128)(2,1)}, u32[]{:S(2)}, u32[]{:S(2)}) collective-permute-start(bf16[64,1024]{1,0:T(8,128)(2,1)} %get-tuple-element.39), channel_id=1, source_target_pairs={{0,8},{8,0},{4,12},{12,4},{1,9},{9,1},{5,13},{13,5},{2,10},{10,2},... | collective-permute-start | bytes 393224 | tf_op jit(solution)/shard_map/ppermute | solution.py:220
  8.9 0.0 copy-start.6
  8.9 1.1 %constant_dynamic-slice_fusion = (bf16[256,256]{1,0:T(8,128)(2,1)S(1)}, bf16[256,256]{1,0:T(8,128)(2,1)S(1)}) fusion(bf16[1024,256]{1,0:T(8,128)(2,1)} %param.23, s32[]{:T(128)S(6)} %select_n.16, s32[]{:T(128)S(6)} %add.17), kind=kLoop, calls=%fused_computation.3 | loop fusion | bytes 524296 | tf_op jit(solution)/shard_map/slice | solution.py:251
  10.1 1.7 %collective-permute-done.refs_1_ = bf16[64,1024]{1,0:T(8,128)(2,1)S(1)} collective-permute-done((bf16[64,1024]{1,0:T(8,128)(2,1)}, bf16[64,1024]{1,0:T(8,128)(2,1)S(1)}, u32[]{:S(2)}, u32[]{:S(2)}) %collective-permute-start) | collective-permute-done | bytes 131104 | tf_op jit(solution)/shard_map/ppermute | solution.py:220
  11.8 3.5 %collective-permute-done.1.refs_2_ = bf16[64,1024]{1,0:T(8,128)(2,1)} collective-permute-done((bf16[64,1024]{1,0:T(8,128)(2,1)}, bf16[64,1024]{1,0:T(8,128)(2,1)}, u32[]{:S(2)}, u32[]{:S(2)}) %collective-permute-start.1) | collective-permute-done | bytes 131104 | tf_op jit(solution)/shard_map/ppermute | solution.py:220
  15.4 1.3 %collective-permute-start.3 = (bf16[64,1024]{1,0:T(8,128)(2,1)}, bf16[64,1024]{1,0:T(8,128)(2,1)}, u32[]{:S(2)}, u32[]{:S(2)}) collective-permute-start(bf16[64,1024]{1,0:T(8,128)(2,1)} %collective-permute-done.1.refs_2_), channel_id=1, source_target_pairs={{4,0},{8,12},{5,1},{9,13},{6,2},{10,14},{7,3},{11,15},{20,16},{24,... | collective-permute-start | bytes 393224 | tf_op jit(solution)/shard_map/ppermute | solution.py:220
  16.7 1.3 %collective-permute-start.2 = (bf16[64,1024]{1,0:T(8,128)(2,1)}, bf16[64,1024]{1,0:T(8,128)(2,1)}, u32[]{:S(2)}, u32[]{:S(2)}) collective-permute-start(bf16[64,1024]{1,0:T(8,128)(2,1)} %get-tuple-element.39), channel_id=1, source_target_pairs={{4,8},{8,4},{5,9},{9,5},{6,10},{10,6},{7,11},{11,7},{20,24},{24,20... | collective-permute-start | bytes 393224 | tf_op jit(solution)/shard_map/ppermute | solution.py:220
  18.0 0.0 collective-permute-start.5
  18.0 5.5 %collective-permute-start.16 = (bf16[512,512]{1,0:T(8,128)(2,1)S(1)}, bf16[512,512]{1,0:T(8,128)(2,1)S(1)}, u32[]{:S(2)}, u32[]{:S(2)}) collective-permute-start(bf16[512,512]{1,0:T(8,128)(2,1)S(1)} %maximum_maximum_fusion.refs_10_.refs_0_), channel_id=1, source_target_pairs={{0,8},{8,0},{4,12},{12,4},{1,9},{9,1},{5,13},{13,5},{2,10},{10,2},... | collective-permute-start | bytes 1572872 | tf_op jit(solution)/shard_map/ppermute | solution.py:220
  23.5 0.2 collective-permute-start.17
  23.7 0.0 collective-permute-done.3
  23.7 0.1 collective-permute-start.4
  23.7 0.0 collective-permute-done.2
  23.7 1.5 %collective-permute-start.7 = (f32[1,512]{1,0:T(1,128)S(1)}, f32[1,512]{1,0:T(1,128)S(1)}, u32[]{:S(2)}, u32[]{:S(2)}) collective-permute-start(f32[1,512]{1,0:T(1,128)S(1)} %bitcast.7), channel_id=1, source_target_pairs={{2,0},{0,2},{3,1},{1,3},{6,4},{4,6},{7,5},{5,7},{10,8},{8,10},{11,... | collective-permute-start | bytes 6152 | tf_op jit(solution)/shard_map/ppermute | solution.py:25
  25.2 0.9 %broadcast_select_fusion.refs_3_ = bf16[64,1024]{1,0:T(8,128)(2,1)S(1)} fusion(bf16[64,1024]{1,0:T(8,128)(2,1)} %collective-permute-done.2, bf16[64,1024]{1,0:T(8,128)(2,1)} %collective-permute-done.3, pred[]{:T(512)S(6)} %and.5), kind=kLoop, calls=%fused_computation.2 | loop fusion | flops 65536 | bytes 393217 | tf_op jit(solution)/shard_map/jit(_where)/select_n | solution.py:257
  26.2 1.2 %collective-permute-done.7.refs_9_ = f32[1,512]{1,0:T(1,128)S(1)} collective-permute-done((f32[1,512]{1,0:T(1,128)S(1)}, f32[1,512]{1,0:T(1,128)S(1)}, u32[]{:S(2)}, u32[]{:S(2)}) %collective-permute-start.7) | collective-permute-done | bytes 2080 | tf_op jit(solution)/shard_map/ppermute | solution.py:25
  27.3 0.0 collective-permute-start.6
  27.3 0.0 collective-permute-done.5.refs_5_
  27.4 0.0 collective-permute-done.4.refs_4_
  27.4 1.3 %collective-permute-done.6.refs_6_ = bf16[64,1024]{1,0:T(8,128)(2,1)S(1)} collective-permute-done((bf16[64,1024]{1,0:T(8,128)(2,1)S(1)}, bf16[64,1024]{1,0:T(8,128)(2,1)S(1)}, u32[]{:S(2)}, u32[]{:S(2)}) %collective-permute-start.6) | collective-permute-done | bytes 131104 | tf_op jit(solution)/shard_map/ppermute | solution.py:25
  28.7 0.0 copy-done.7
  28.7 0.0 copy-start.8
  28.7 1.2 %copy-done.8 = f32[1,512,512]{2,1,0:T(8,128)S(1)} copy-done((f32[1,512,512]{2,1,0:T(8,128)S(1)}, f32[1,512,512]{2,1,0:T(8,128)}, u32[]{:S(2)}) %copy-start.8) | copy-done | bytes 1048600
  29.9 4.2 %shard_map.119 = (f32[128,256]{1,0:T(8,128)S(1)}, f32[8,256]{1,0:T(8,128)S(1)}, bf16[144,256]{1,0:T(8,128)(2,1)S(1)}) custom-call(bf16[128,1024]{1,0:T(8,128)(2,1)S(1)} %get-tuple-element.41.refs_0_, bf16[64,1024]{1,0:T(8,128)(2,1)S(1)} %collective-permute-done.refs_1_, bf16[64,1024]{1,0:T(8,128)(2,1)} %collective-permute-done.1.refs_2_, ...), custom_call_target="tpu_custom_call" | custom-call | flops 1811939328 | bytes 4538368 | tf_op jit(solution)/shard_map/pallas_call | solution.py:31
  34.1 0.2 collective-permute-start.8
  34.4 1.1 %collective-permute-done.8.got = bf16[144,256]{1,0:T(8,128)(2,1)S(1)} collective-permute-done((bf16[144,256]{1,0:T(8,128)(2,1)S(1)}, bf16[144,256]{1,0:T(8,128)(2,1)S(1)}, u32[]{:S(2)}, u32[]{:S(2)}) %collective-permute-start.8) | collective-permute-done | bytes 73760 | tf_op jit(solution)/shard_map/ppermute | solution.py:25
  35.5 1.6 %collective-permute-start.10 = (bf16[128,256]{1,0:T(8,128)(2,1)S(1)}, bf16[128,256]{1,0:T(8,128)(2,1)S(1)}, u32[]{:S(2)}, u32[]{:S(2)}) collective-permute-start(bf16[128,256]{1,0:T(8,128)(2,1)S(1)} %get-tuple-element.51.refs_0_), channel_id=1, source_target_pairs={{2,0},{0,2},{18,16},{16,18},{3,1},{1,3},{19,17},{17,19},{6,4},{4,6... | collective-permute-start | bytes 196616 | tf_op jit(solution)/shard_map/ppermute | solution.py:25
  37.1 1.5 %collective-permute-start.12 = (bf16[128,256]{1,0:T(8,128)(2,1)S(1)}, bf16[128,256]{1,0:T(8,128)(2,1)S(1)}, u32[]{:S(2)}, u32[]{:S(2)}) collective-permute-start(bf16[128,256]{1,0:T(8,128)(2,1)S(1)} %get-tuple-element.51.refs_0_), channel_id=1, source_target_pairs={{16,0},{18,2},{0,16},{2,18},{17,1},{19,3},{1,17},{3,19},{20,4},{22... | collective-permute-start | bytes 196616 | tf_op jit(solution)/shard_map/ppermute | solution.py:25
  38.6 0.5 collective-permute-start.14
  39.1 0.8 collective-permute-done.10.refs_2_
  39.9 1.5 %collective-permute-done.12.refs_4_ = bf16[128,256]{1,0:T(8,128)(2,1)S(1)} collective-permute-done((bf16[128,256]{1,0:T(8,128)(2,1)S(1)}, bf16[128,256]{1,0:T(8,128)(2,1)S(1)}, u32[]{:S(2)}, u32[]{:S(2)}) %collective-permute-start.12) | collective-permute-done | bytes 65568 | tf_op jit(solution)/shard_map/ppermute | solution.py:25
  41.3 2.4 %collective-permute-done.14.refs_6_ = bf16[128,256]{1,0:T(8,128)(2,1)S(1)} collective-permute-done((bf16[128,256]{1,0:T(8,128)(2,1)S(1)}, bf16[128,256]{1,0:T(8,128)(2,1)S(1)}, u32[]{:S(2)}, u32[]{:S(2)}) %collective-permute-start.14) | collective-permute-done | bytes 65568 | tf_op jit(solution)/shard_map/ppermute | solution.py:25
  43.8 4.9 %collective-permute-done.16.refs_12_.refs_2_ = bf16[512,512]{1,0:T(8,128)(2,1)S(1)} collective-permute-done((bf16[512,512]{1,0:T(8,128)(2,1)S(1)}, bf16[512,512]{1,0:T(8,128)(2,1)S(1)}, u32[]{:S(2)}, u32[]{:S(2)}) %collective-permute-start.16) | collective-permute-done | bytes 524320 | tf_op jit(solution)/shard_map/ppermute | solution.py:220
  48.6 0.0 collective-permute-done.17.refs_11_.refs_1_
  48.6 0.7 collective-permute-start.18
  49.3 1.3 %collective-permute-start.19 = (bf16[512,512]{1,0:T(8,128)(2,1)S(1)}, bf16[512,512]{1,0:T(8,128)(2,1)S(1)}, u32[]{:S(2)}, u32[]{:S(2)}) collective-permute-start(bf16[512,512]{1,0:T(8,128)(2,1)S(1)} %collective-permute-done.16.refs_12_.refs_2_), channel_id=1, source_target_pairs={{4,0},{8,12},{5,1},{9,13},{6,2},{10,14},{7,3},{11,15},{20,16},{24,... | collective-permute-start | bytes 1572872 | tf_op jit(solution)/shard_map/ppermute | solution.py:220
  50.6 0.1 collective-permute-start.9
  50.7 0.5 collective-permute-start.11
  51.2 0.1 collective-permute-start.13
  51.3 0.7 collective-permute-done.9.refs_1_
  52.0 0.2 collective-permute-start.15
  52.1 0.0 collective-permute-done.11.refs_3_
  52.1 0.3 collective-permute-done.13.refs_5_
  52.5 0.7 collective-permute-done.15.refs_7_
  53.2 0.0 collective-permute-done.18.refs_13_.refs_3_
  53.2 21.5 %collective-permute-done.19.refs_14_.refs_4_ = bf16[512,512]{1,0:T(8,128)(2,1)S(1)} collective-permute-done((bf16[512,512]{1,0:T(8,128)(2,1)S(1)}, bf16[512,512]{1,0:T(8,128)(2,1)S(1)}, u32[]{:S(2)}, u32[]{:S(2)}) %collective-permute-start.19) | collective-permute-done | bytes 524320 | tf_op jit(solution)/shard_map/ppermute | solution.py:220
  74.8 0.7 shard_map.121.h
  75.5 0.5 shard_map.122
  76.0 0.1 collective-permute-start.20
  76.7 0.9 %collective-permute-done.20.got = bf16[256,512]{1,0:T(8,128)(2,1)S(1)} collective-permute-done((bf16[256,512]{1,0:T(8,128)(2,1)S(1)}, bf16[256,512]{1,0:T(8,128)(2,1)S(1)}, u32[]{:S(2)}, u32[]{:S(2)}) %collective-permute-start.20) | collective-permute-done | bytes 262176 | tf_op jit(solution)/shard_map/ppermute | solution.py:25
  77.6 0.1 shard_map.123
  77.7 0.7 collective-permute-start.21
  78.4 0.6 collective-permute-start.22
  78.9 2.3 %collective-permute-start.23 = (bf16[128,256]{1,0:T(8,128)(2,1)S(1)}, bf16[128,256]{1,0:T(8,128)(2,1)S(1)}, u32[]{:S(2)}, u32[]{:S(2)}) collective-permute-start(bf16[128,256]{1,0:T(8,128)(2,1)S(1)} %get-tuple-element.64), channel_id=1, source_target_pairs={{18,0},{16,2},{2,16},{0,18},{19,1},{17,3},{3,17},{1,19},{22,4},{20... | collective-permute-start | bytes 196616 | tf_op jit(solution)/shard_map/ppermute | solution.py:25
  81.2 0.8 collective-permute-done.21
  82.1 1.2 %collective-permute-done.22 = bf16[128,256]{1,0:T(8,128)(2,1)S(1)} collective-permute-done((bf16[128,256]{1,0:T(8,128)(2,1)S(1)}, bf16[128,256]{1,0:T(8,128)(2,1)S(1)}, u32[]{:S(2)}, u32[]{:S(2)}) %collective-permute-start.22) | collective-permute-done | bytes 65568 | tf_op jit(solution)/shard_map/ppermute | solution.py:25
  83.3 0.8 collective-permute-done.23
  84.1 0.7 select_convert_fusion
  (16 shorter events, 0.1 us)
Async XLA Ops:
  0.0 8.9 %copy-start = (bf16[256,1024]{1,0:T(8,128)(2,1)S(1)}, bf16[256,1024]{1,0:T(8,128)(2,1)}, u32[]{:S(2)}) copy-start(bf16[256,1024]{1,0:T(8,128)(2,1)} %param.22) | copy-start | bytes 1572868
  0.0 0.7 copy-start.5
  0.7 0.9 %copy-start.1 = (bf16[128,512]{1,0:T(8,128)(2,1)S(1)}, bf16[128,512]{1,0:T(8,128)(2,1)}, u32[]{:S(2)}) copy-start(bf16[128,512]{1,0:T(8,128)(2,1)} %keys.1) | copy-start | bytes 393220
  1.6 0.9 %copy-start.2 = (bf16[128,512]{1,0:T(8,128)(2,1)S(1)}, bf16[128,512]{1,0:T(8,128)(2,1)}, u32[]{:S(2)}) copy-start(bf16[128,512]{1,0:T(8,128)(2,1)} %values.1) | copy-start | bytes 393220
  3.3 8.6 %collective-permute-start = (bf16[64,1024]{1,0:T(8,128)(2,1)}, bf16[64,1024]{1,0:T(8,128)(2,1)S(1)}, u32[]{:S(2)}, u32[]{:S(2)}) collective-permute-start(bf16[64,1024]{1,0:T(8,128)(2,1)} %get-tuple-element.39), channel_id=1, source_target_pairs={{0,4},{4,0},{8,12},{12,8},{1,5},{5,1},{9,13},{13,9},{2,6},{6,2},{1... | collective-permute-start | bytes 393224 | tf_op jit(solution)/shard_map/ppermute | solution.py:220
  6.3 9.1 %collective-permute-start.1 = (bf16[64,1024]{1,0:T(8,128)(2,1)}, bf16[64,1024]{1,0:T(8,128)(2,1)}, u32[]{:S(2)}, u32[]{:S(2)}) collective-permute-start(bf16[64,1024]{1,0:T(8,128)(2,1)} %get-tuple-element.39), channel_id=1, source_target_pairs={{0,8},{8,0},{4,12},{12,4},{1,9},{9,1},{5,13},{13,5},{2,10},{10,2},... | collective-permute-start | bytes 393224 | tf_op jit(solution)/shard_map/ppermute | solution.py:220
  8.9 19.8 %copy-start.7 = (f32[1,512,512]{2,1,0:T(8,128)S(1)}, f32[1,512,512]{2,1,0:T(8,128)}, u32[]{:S(2)}) copy-start(f32[1,512,512]{2,1,0:T(8,128)} %param.20) | copy-start | bytes 3145732
  8.9 19.8 %copy-start.6 = (f32[1,512,512]{2,1,0:T(8,128)S(1)}, f32[1,512,512]{2,1,0:T(8,128)}, u32[]{:S(2)}) copy-start(f32[1,512,512]{2,1,0:T(8,128)} %param.19) | copy-start | bytes 3145732
  15.4 8.3 %collective-permute-start.3 = (bf16[64,1024]{1,0:T(8,128)(2,1)}, bf16[64,1024]{1,0:T(8,128)(2,1)}, u32[]{:S(2)}, u32[]{:S(2)}) collective-permute-start(bf16[64,1024]{1,0:T(8,128)(2,1)} %collective-permute-done.1.refs_2_), channel_id=1, source_target_pairs={{4,0},{8,12},{5,1},{9,13},{6,2},{10,14},{7,3},{11,15},{20,16},{24,... | collective-permute-start | bytes 393224 | tf_op jit(solution)/shard_map/ppermute | solution.py:220
  16.7 7.1 %collective-permute-start.2 = (bf16[64,1024]{1,0:T(8,128)(2,1)}, bf16[64,1024]{1,0:T(8,128)(2,1)}, u32[]{:S(2)}, u32[]{:S(2)}) collective-permute-start(bf16[64,1024]{1,0:T(8,128)(2,1)} %get-tuple-element.39), channel_id=1, source_target_pairs={{4,8},{8,4},{5,9},{9,5},{6,10},{10,6},{7,11},{11,7},{20,24},{24,20... | collective-permute-start | bytes 393224 | tf_op jit(solution)/shard_map/ppermute | solution.py:220
  18.0 5.8 %copy-start.4 = (f32[512]{0:T(512)S(1)}, f32[512]{0:T(512)}, u32[]{:S(2)}) copy-start(f32[512]{0:T(512)} %param.17) | copy-start | bytes 6148
  18.0 10.7 %copy-start.9 = (bf16[128,512]{1,0:T(8,128)(2,1)S(1)}, bf16[128,512]{1,0:T(8,128)(2,1)}, u32[]{:S(2)}) copy-start(bf16[128,512]{1,0:T(8,128)(2,1)} %refs_10_.1) | copy-start | bytes 393220
  18.0 9.4 %collective-permute-start.5 = (bf16[64,1024]{1,0:T(8,128)(2,1)}, bf16[64,1024]{1,0:T(8,128)(2,1)S(1)}, u32[]{:S(2)}, u32[]{:S(2)}) collective-permute-start(bf16[64,1024]{1,0:T(8,128)(2,1)} %collective-permute-done.1.refs_2_), channel_id=1, source_target_pairs={{1,0},{0,1},{3,2},{2,3},{5,4},{4,5},{7,6},{6,7},{9,8},{8,9},{11,10... | collective-permute-start | bytes 393224 | tf_op jit(solution)/shard_map/ppermute | solution.py:25
  18.0 30.6 %collective-permute-start.16 = (bf16[512,512]{1,0:T(8,128)(2,1)S(1)}, bf16[512,512]{1,0:T(8,128)(2,1)S(1)}, u32[]{:S(2)}, u32[]{:S(2)}) collective-permute-start(bf16[512,512]{1,0:T(8,128)(2,1)S(1)} %maximum_maximum_fusion.refs_10_.refs_0_), channel_id=1, source_target_pairs={{0,8},{8,0},{4,12},{12,4},{1,9},{9,1},{5,13},{13,5},{2,10},{10,2},... | collective-permute-start | bytes 1572872 | tf_op jit(solution)/shard_map/ppermute | solution.py:220
  23.5 25.2 %collective-permute-start.17 = (bf16[512,512]{1,0:T(8,128)(2,1)S(1)}, bf16[512,512]{1,0:T(8,128)(2,1)S(1)}, u32[]{:S(2)}, u32[]{:S(2)}) collective-permute-start(bf16[512,512]{1,0:T(8,128)(2,1)S(1)} %maximum_maximum_fusion.refs_10_.refs_0_), channel_id=1, source_target_pairs={{0,4},{4,0},{8,12},{12,8},{1,5},{5,1},{9,13},{13,9},{2,6},{6,2},{1... | collective-permute-start | bytes 1572872 | tf_op jit(solution)/shard_map/ppermute | solution.py:220
  23.7 3.7 %collective-permute-start.4 = (bf16[64,1024]{1,0:T(8,128)(2,1)S(1)}, bf16[64,1024]{1,0:T(8,128)(2,1)S(1)}, u32[]{:S(2)}, u32[]{:S(2)}) collective-permute-start(bf16[64,1024]{1,0:T(8,128)(2,1)S(1)} %collective-permute-done.refs_1_), channel_id=1, source_target_pairs={{1,0},{0,1},{3,2},{2,3},{5,4},{4,5},{7,6},{6,7},{9,8},{8,9},{11,10... | collective-permute-start | bytes 393224 | tf_op jit(solution)/shard_map/ppermute | solution.py:25
  23.7 3.6 %collective-permute-start.7 = (f32[1,512]{1,0:T(1,128)S(1)}, f32[1,512]{1,0:T(1,128)S(1)}, u32[]{:S(2)}, u32[]{:S(2)}) collective-permute-start(f32[1,512]{1,0:T(1,128)S(1)} %bitcast.7), channel_id=1, source_target_pairs={{2,0},{0,2},{3,1},{1,3},{6,4},{4,6},{7,5},{5,7},{10,8},{8,10},{11,... | collective-permute-start | bytes 6152 | tf_op jit(solution)/shard_map/ppermute | solution.py:25
  27.3 1.3 %collective-permute-start.6 = (bf16[64,1024]{1,0:T(8,128)(2,1)S(1)}, bf16[64,1024]{1,0:T(8,128)(2,1)S(1)}, u32[]{:S(2)}, u32[]{:S(2)}) collective-permute-start(bf16[64,1024]{1,0:T(8,128)(2,1)S(1)} %broadcast_select_fusion.refs_3_), channel_id=1, source_target_pairs={{1,0},{0,1},{3,2},{2,3},{5,4},{4,5},{7,6},{6,7},{9,8},{8,9},{11,10... | collective-permute-start | bytes 393224 | tf_op jit(solution)/shard_map/ppermute | solution.py:25
  28.7 1.2 %copy-start.8 = (f32[1,512,512]{2,1,0:T(8,128)S(1)}, f32[1,512,512]{2,1,0:T(8,128)}, u32[]{:S(2)}) copy-start(f32[1,512,512]{2,1,0:T(8,128)} %param.21) | copy-start | bytes 3145732
  29.9 5.6 %copy-start.3 = (bf16[128,512]{1,0:T(8,128)(2,1)S(1)}, bf16[128,512]{1,0:T(8,128)(2,1)}, u32[]{:S(2)}) copy-start(bf16[128,512]{1,0:T(8,128)(2,1)} %stream.1) | copy-start | bytes 393220
  34.1 1.3 %collective-permute-start.8 = (bf16[144,256]{1,0:T(8,128)(2,1)S(1)}, bf16[144,256]{1,0:T(8,128)(2,1)S(1)}, u32[]{:S(2)}, u32[]{:S(2)}) collective-permute-start(bf16[144,256]{1,0:T(8,128)(2,1)S(1)} %get-tuple-element.50), channel_id=1, source_target_pairs={{1,0},{0,1},{3,2},{2,3},{5,4},{4,5},{7,6},{6,7},{9,8},{8,9},{11,10... | collective-permute-start | bytes 221192 | tf_op jit(solution)/shard_map/ppermute | solution.py:25
  35.5 4.3 %collective-permute-start.10 = (bf16[128,256]{1,0:T(8,128)(2,1)S(1)}, bf16[128,256]{1,0:T(8,128)(2,1)S(1)}, u32[]{:S(2)}, u32[]{:S(2)}) collective-permute-start(bf16[128,256]{1,0:T(8,128)(2,1)S(1)} %get-tuple-element.51.refs_0_), channel_id=1, source_target_pairs={{2,0},{0,2},{18,16},{16,18},{3,1},{1,3},{19,17},{17,19},{6,4},{4,6... | collective-permute-start | bytes 196616 | tf_op jit(solution)/shard_map/ppermute | solution.py:25
  37.1 4.3 %collective-permute-start.12 = (bf16[128,256]{1,0:T(8,128)(2,1)S(1)}, bf16[128,256]{1,0:T(8,128)(2,1)S(1)}, u32[]{:S(2)}, u32[]{:S(2)}) collective-permute-start(bf16[128,256]{1,0:T(8,128)(2,1)S(1)} %get-tuple-element.51.refs_0_), channel_id=1, source_target_pairs={{16,0},{18,2},{0,16},{2,18},{17,1},{19,3},{1,17},{3,19},{20,4},{22... | collective-permute-start | bytes 196616 | tf_op jit(solution)/shard_map/ppermute | solution.py:25
  38.6 5.2 %collective-permute-start.14 = (bf16[128,256]{1,0:T(8,128)(2,1)S(1)}, bf16[128,256]{1,0:T(8,128)(2,1)S(1)}, u32[]{:S(2)}, u32[]{:S(2)}) collective-permute-start(bf16[128,256]{1,0:T(8,128)(2,1)S(1)} %get-tuple-element.51.refs_0_), channel_id=1, source_target_pairs={{18,0},{16,2},{2,16},{0,18},{19,1},{17,3},{3,17},{1,19},{22,4},{20... | collective-permute-start | bytes 196616 | tf_op jit(solution)/shard_map/ppermute | solution.py:25
  48.6 4.6 %collective-permute-start.18 = (bf16[512,512]{1,0:T(8,128)(2,1)S(1)}, bf16[512,512]{1,0:T(8,128)(2,1)S(1)}, u32[]{:S(2)}, u32[]{:S(2)}) collective-permute-start(bf16[512,512]{1,0:T(8,128)(2,1)S(1)} %maximum_maximum_fusion.refs_10_.refs_0_), channel_id=1, source_target_pairs={{4,8},{8,4},{5,9},{9,5},{6,10},{10,6},{7,11},{11,7},{20,24},{24,20... | collective-permute-start | bytes 1572872 | tf_op jit(solution)/shard_map/ppermute | solution.py:220
  49.3 25.4 %collective-permute-start.19 = (bf16[512,512]{1,0:T(8,128)(2,1)S(1)}, bf16[512,512]{1,0:T(8,128)(2,1)S(1)}, u32[]{:S(2)}, u32[]{:S(2)}) collective-permute-start(bf16[512,512]{1,0:T(8,128)(2,1)S(1)} %collective-permute-done.16.refs_12_.refs_2_), channel_id=1, source_target_pairs={{4,0},{8,12},{5,1},{9,13},{6,2},{10,14},{7,3},{11,15},{20,16},{24,... | collective-permute-start | bytes 1572872 | tf_op jit(solution)/shard_map/ppermute | solution.py:220
  50.6 1.3 %collective-permute-start.9 = (bf16[128,256]{1,0:T(8,128)(2,1)S(1)}, bf16[128,256]{1,0:T(8,128)(2,1)S(1)}, u32[]{:S(2)}, u32[]{:S(2)}) collective-permute-start(bf16[128,256]{1,0:T(8,128)(2,1)S(1)} %get-tuple-element.51.refs_0_), channel_id=1, source_target_pairs={{1,0},{0,1},{3,2},{2,3},{5,4},{4,5},{7,6},{6,7},{9,8},{8,9},{11,10... | collective-permute-start | bytes 196616 | tf_op jit(solution)/shard_map/ppermute | solution.py:25
  50.7 1.4 %collective-permute-start.11 = (bf16[128,256]{1,0:T(8,128)(2,1)S(1)}, bf16[128,256]{1,0:T(8,128)(2,1)S(1)}, u32[]{:S(2)}, u32[]{:S(2)}) collective-permute-start(bf16[128,256]{1,0:T(8,128)(2,1)S(1)} %collective-permute-done.10.refs_2_), channel_id=1, source_target_pairs={{1,0},{0,1},{3,2},{2,3},{5,4},{4,5},{7,6},{6,7},{9,8},{8,9},{11,10... | collective-permute-start | bytes 196616 | tf_op jit(solution)/shard_map/ppermute | solution.py:25
  51.2 1.3 %collective-permute-start.13 = (bf16[128,256]{1,0:T(8,128)(2,1)S(1)}, bf16[128,256]{1,0:T(8,128)(2,1)S(1)}, u32[]{:S(2)}, u32[]{:S(2)}) collective-permute-start(bf16[128,256]{1,0:T(8,128)(2,1)S(1)} %collective-permute-done.12.refs_4_), channel_id=1, source_target_pairs={{1,0},{0,1},{3,2},{2,3},{5,4},{4,5},{7,6},{6,7},{9,8},{8,9},{11,10... | collective-permute-start | bytes 196616 | tf_op jit(solution)/shard_map/ppermute | solution.py:25
  52.0 1.3 %collective-permute-start.15 = (bf16[128,256]{1,0:T(8,128)(2,1)S(1)}, bf16[128,256]{1,0:T(8,128)(2,1)S(1)}, u32[]{:S(2)}, u32[]{:S(2)}) collective-permute-start(bf16[128,256]{1,0:T(8,128)(2,1)S(1)} %collective-permute-done.14.refs_6_), channel_id=1, source_target_pairs={{1,0},{0,1},{3,2},{2,3},{5,4},{4,5},{7,6},{6,7},{9,8},{8,9},{11,10... | collective-permute-start | bytes 196616 | tf_op jit(solution)/shard_map/ppermute | solution.py:25
  76.0 1.6 %collective-permute-start.20 = (bf16[256,512]{1,0:T(8,128)(2,1)S(1)}, bf16[256,512]{1,0:T(8,128)(2,1)S(1)}, u32[]{:S(2)}, u32[]{:S(2)}) collective-permute-start(bf16[256,512]{1,0:T(8,128)(2,1)S(1)} %get-tuple-element.59), channel_id=1, source_target_pairs={{1,0},{0,1},{3,2},{2,3},{5,4},{4,5},{7,6},{6,7},{9,8},{8,9},{11,10... | collective-permute-start | bytes 786440 | tf_op jit(solution)/shard_map/ppermute | solution.py:25
  77.7 4.4 %collective-permute-start.21 = (bf16[128,256]{1,0:T(8,128)(2,1)S(1)}, bf16[128,256]{1,0:T(8,128)(2,1)S(1)}, u32[]{:S(2)}, u32[]{:S(2)}) collective-permute-start(bf16[128,256]{1,0:T(8,128)(2,1)S(1)} %get-tuple-element.62), channel_id=1, source_target_pairs={{2,0},{0,2},{18,16},{16,18},{3,1},{1,3},{19,17},{17,19},{6,4},{4,6... | collective-permute-start | bytes 196616 | tf_op jit(solution)/shard_map/ppermute | solution.py:25
  78.4 5.0 %collective-permute-start.22 = (bf16[128,256]{1,0:T(8,128)(2,1)S(1)}, bf16[128,256]{1,0:T(8,128)(2,1)S(1)}, u32[]{:S(2)}, u32[]{:S(2)}) collective-permute-start(bf16[128,256]{1,0:T(8,128)(2,1)S(1)} %get-tuple-element.63), channel_id=1, source_target_pairs={{16,0},{18,2},{0,16},{2,18},{17,1},{19,3},{1,17},{3,19},{20,4},{22... | collective-permute-start | bytes 196616 | tf_op jit(solution)/shard_map/ppermute | solution.py:25
  78.9 5.2 %collective-permute-start.23 = (bf16[128,256]{1,0:T(8,128)(2,1)S(1)}, bf16[128,256]{1,0:T(8,128)(2,1)S(1)}, u32[]{:S(2)}, u32[]{:S(2)}) collective-permute-start(bf16[128,256]{1,0:T(8,128)(2,1)S(1)} %get-tuple-element.64), channel_id=1, source_target_pairs={{18,0},{16,2},{2,16},{0,18},{19,1},{17,3},{3,17},{1,19},{22,4},{20... | collective-permute-start | bytes 196616 | tf_op jit(solution)/shard_map/ppermute | solution.py:25

commit v3 on v1

v3 whole, which is shorter than its diff:
```python
import functools
import itertools

import jax
import jax.numpy as jnp
import numpy as np
from jax import lax
from jax.experimental import pallas as pl
from jax.experimental.pallas import tpu as pltpu
from jax.sharding import PartitionSpec as P

BF, F32 = jnp.bfloat16, jnp.float32


def dot(a, b, dims=((1,), (0,))):
    return lax.dot_general(a, b, (dims, ((), ())), preferred_element_type=F32)


def moved(x, groups=0, tok=0, head=0, rep=0):
    shifts = {"groups": groups, "tok": tok, "head": head, "rep": rep}
    axes = [a for a, s in shifts.items() if s]
    if not axes:
        return x
    sizes = [lax.axis_size(a) for a in axes]
    pairs = []
    for here in range(int(np.prod(sizes))):
        at = np.unravel_index(here, sizes)
        there = [i ^ tok if a == "tok" else (i + shifts[a]) % n for a, i, n in zip(axes, at, sizes)]
        pairs.append((int(np.ravel_multi_index(there, sizes)), here))
    return lax.ppermute(x, tuple(axes), pairs)


def shape(dims, dtype):
    return jax.ShapeDtypeStruct(dims, dtype)


def call(kernel, outs, args, scratch=(), flops=0):
    touched = sum(int(np.prod(x.shape)) * x.dtype.itemsize for x in (*args, *outs))
    kept = sum(int(np.prod(x.shape)) * 4 for x in scratch)
    return pl.pallas_call(
        kernel,
        out_shape=outs,
        in_specs=[pl.BlockSpec(memory_space=pltpu.VMEM)] * len(args),
        out_specs=[pl.BlockSpec(memory_space=pltpu.VMEM)] * len(outs),
        scratch_shapes=list(scratch),
        compiler_params=pltpu.CompilerParams(vmem_limit_bytes=touched + kept + (10 << 20)),
        cost_estimate=pl.CostEstimate(flops=1, bytes_accessed=1, transcendentals=0),
    )(*args)


def window(index, size):
    return pl.ds(pl.multiple_of(index * size, size), size)


def message_kernel(keys, values, rates, queries, stream, pair, *messages):
    n, dh = keys.shape
    me = lax.axis_index("rep")
    rate = jnp.broadcast_to(rates[...], (128, n)).T
    pair[:, :dh] = keys[...]
    for c in range(0, dh, 128):
        pair[:, dh + c : dh + c + 128] = (values[:, c : c + 128].astype(F32) * rate).astype(BF)
    if messages:
        share, ask = messages
        share[...] = pair[window(me, share.shape[0]), :]
        ask[:, :dh] = queries[...]
        ask[:, dh:] = stream[:, window(me, ask.shape[1] - dh)]


def pack_kernel(up, down, same, other):
    deep, wide = up.shape[0], same.shape[1]
    bit = lax.bitwise_and(lax.axis_index("tok"), 1)
    for out, b in ((same, bit), (other, 1 - bit)):
        part = window(lax.axis_index("groups") * 2 + b, wide)
        out[:deep, :] = up[:, part]
        out[deep:, :] = down[part, :]


def gradients(k, e, w1b, w3b, w2b):
    a1, a3, b = dot(k, w1b), dot(k, w3b), dot(e, w2b, ((1,), (1,)))
    sig = jax.nn.sigmoid(a1)
    act = a1 * sig
    g = (act * a3).astype(BF)
    r1 = (b * a3 * (sig * (1.0 + a1 * (1.0 - sig)))).astype(BF)
    r3 = (b * act).astype(BF)
    first = ((0,), (0,))
    return dot(k, r1, first), dot(k, r3, first), dot(g, e, first)


def squares(x):
    return jnp.sum(x * x, axis=0, keepdims=True)


def own_kernel(take_own, pair, w1, w3, w2, b1, b3, b2, u1, u3, u2, sq13, sq2):
    dh, hidden = w1.shape
    block = min(hidden, 256)
    sq2[...] = jnp.broadcast_to(squares(w2[...]), sq2.shape)
    for j in range(0, hidden, block):
        js = slice(j, j + block)
        x1, x3, x2 = w1[:, js], w3[:, js], w2[js, :]
        b1[:, js], b3[:, js], b2[js, :] = x1.astype(BF), x3.astype(BF), x2.astype(BF)
        sq13[0:8, js] = jnp.broadcast_to(squares(x1), (8, block))
        sq13[8:16, js] = jnp.broadcast_to(squares(x3), (8, block))
        if take_own:
            d1, d3, d2 = gradients(pair[:, :dh], pair[:, dh:], b1[:, js], b3[:, js], b2[js, :])
            x1, x3, x2 = x1 + d1, x3 + d3, x2 + d2
        u1[:, js], u3[:, js], u2[js, :] = x1, x3, x2


def fast_kernel(n_pieces, n_ask, *refs):
    pieces, refs = refs[:n_pieces], refs[n_pieces:]
    asks, refs = refs[:n_ask], refs[n_ask:]
    b1, b3, b2, u1, u3, u2, sq13, sq2, own_out, own_sq, send, ks, es, hp = refs
    dh, hidden = b1.shape
    at = 0
    for p in pieces:
        n = p.shape[0]
        ks[at : at + n, :] = p[:, :dh]
        es[at : at + n, :] = p[:, dh:]
        at += n
    tokens, step, block = at, min(at, 512), min(hidden, 256)
    asked = [q[:, :dh] for q in asks]
    asked = asked[0] if n_ask == 1 else jnp.concatenate(asked, axis=0)
    new_sq = jnp.zeros((1, dh), F32)
    for j in range(0, hidden, block):
        js = slice(j, j + block)

        def add(i, sums):
            rows = pl.ds(pl.multiple_of(i * step, step), step)
            parts = gradients(ks[rows, :], es[rows, :], b1[:, js], b3[:, js], b2[js, :])
            return tuple(s + p for s, p in zip(sums, parts))

        sums = (u1[:, js], u3[:, js], u2[js, :])
        sums = add(0, sums) if tokens == step else lax.fori_loop(0, tokens // step, add, sums)

        def normed(old_sq, new):
            return (new * (jnp.sqrt(old_sq) * lax.rsqrt(squares(new) + 1e-06))).astype(BF)

        new_sq = new_sq + squares(sums[2])
        qa = dot(asked, normed(sq13[0:1, js], sums[0]))
        qc = dot(asked, normed(sq13[8:9, js], sums[1]))
        part = dot((qa * jax.nn.sigmoid(qa) * qc).astype(BF), sums[2].astype(BF))
        hp[...] = part if j == 0 else hp[...] + part
    me, wide = lax.axis_index("rep"), own_out.shape[1]
    n = own_out.shape[0]
    own_out[...] = hp[:, window(me, wide)]
    send[:n, :] = hp[:, window(1 - me, wide)].astype(BF)
    row = lax.broadcasted_iota(jnp.int32, (8, dh), 0)
    hp[:8, :] = jnp.where(row == 0, sq2[...], jnp.where(row == 1, new_sq, 0.0))
    own_sq[...] = hp[:8, window(me, wide)]
    sq = hp[:8, window(1 - me, wide)]
    top = sq.astype(BF).astype(F32)
    send[n:, :] = jnp.concatenate([top, sq - top], axis=0).astype(BF)


def mix_kernel(own, own_sq, got, stream, gain, *refs):
    *asks, mixed, low = refs
    n, wide = mixed.shape
    rows = own.shape[0]
    tail = got[rows:, :].astype(F32)
    sq = own_sq[...] + tail[:8] + tail[8:]
    scale = jnp.sqrt(sq[0:1]) * lax.rsqrt(sq[1:2] + 1e-06)
    for z in range(rows // n):
        part = slice(z * n, (z + 1) * n)
        base = stream[:, window(lax.axis_index("rep"), wide)] if z == 0 else asks[0][:, asks[0].shape[1] - wide :]
        y = base.astype(F32) + (own[part, :] + got[part, :].astype(F32)) * scale
        low[part, :] = y.astype(BF)
        if z == 0:
            mixed[...] = y
    g = jnp.broadcast_to(gain[:, window(lax.axis_index("rep"), wide)], (16, wide))
    row = lax.broadcasted_iota(jnp.int32, (16, wide), 0)
    top = g.astype(BF).astype(F32)
    mid = (g - top).astype(BF).astype(F32)
    low[rows:, :] = jnp.where(row == 0, top, jnp.where(row == 1, mid, jnp.where(row == 2, g - top - mid, 0.0))).astype(BF)


def up_kernel(places, n_blocks, *refs):
    pieces, refs = refs[: len(places)], refs[len(places) :]
    n_head = lax.axis_size("head")
    blocks, (out, zs) = refs[:n_blocks], refs[n_blocks:]
    me_h, me_r, me_t = lax.axis_index("head"), lax.axis_index("rep"), lax.axis_index("tok")
    n, wide = pieces[0].shape[0] - 16, pieces[0].shape[1]
    width = zs.shape[1]
    for dg in range(lax.axis_size("groups")):
        here = [(p, dh, dr) for p, (g, dh, dr) in zip(pieces, places) if g == dg]
        total = jnp.zeros((n, 1), F32)
        for p, _, _ in here:
            x = p[:n, :].astype(F32)
            total = total + jnp.sum(x * x, axis=1, keepdims=True)
        inv = lax.rsqrt(total / width + 1e-06)
        for p, dh, dr in here:
            r = lax.rem(me_r + dr, 2)
            head = lax.rem(me_h + dh, n_head)
            gain = jnp.sum(p[n:, :].astype(F32), axis=0, keepdims=True)
            zs[dg * n : (dg + 1) * n, window(head * 2 + r, wide)] = (p[:n, :].astype(F32) * inv * gain).astype(BF)
    total = None
    deep = width // n_blocks
    for s, x in enumerate(blocks):
        z = zs[...] if n_blocks == 1 else zs[:, window(lax.bitwise_xor(me_t, s), deep)]
        term = dot(z, x[:deep, :])
        total = term if total is None else total + term
    out[...] = (0.5 * total * (1.0 + lax.erf(total * np.float32(0.5**0.5)))).astype(BF)


def down_kernel(n_blocks, h, *refs):
    blocks, (own, send, os) = refs[:n_blocks], refs[n_blocks:]
    me_h, me_r, me_t = lax.axis_index("head"), lax.axis_index("rep"), lax.axis_index("tok")
    n_head = lax.axis_size("head")
    units = h.shape[1]
    for s, x in enumerate(blocks):
        term = dot(h[...], x[x.shape[0] - units :, :])
        if n_blocks == 1:
            os[...] = term
        else:
            os[:, window(lax.bitwise_xor(me_t, s), term.shape[1])] = term
    wide = own.shape[1] // n_head
    for dh in range(n_head):
        at = lax.rem(me_h + dh, n_head) * 2
        there = slice(dh * wide, (dh + 1) * wide)
        own[:, there] = os[:, window(at + me_r, wide)]
        send[:, there] = os[:, window(at + 1 - me_r, wide)].astype(BF)


def pair_kernel(moves, near, own, got, mixed, *outs):
    n, wide = mixed.shape
    for (dg, dz, dh), out in zip(moves, outs):
        at = (dg * near + dz) * n
        rows, cols = slice(at, at + n), slice(dh * wide, (dh + 1) * wide)
        total = own[rows, cols] + got[rows, cols].astype(F32)
        out[...] = mixed[...] + total if (dg, dz, dh) == (0, 0, 0) else total.astype(BF)


def on_device(
    keys, values, rates, queries, stream, gain, counts, fw_one, fw_three, fw_two, mlp_up, mlp_down
):
    n_tok, n_head = lax.axis_size("tok"), lax.axis_size("head")
    groups, reps = lax.axis_size("groups"), lax.axis_size("rep")
    dh, n_key, n = keys.shape[1], keys.shape[0], queries.shape[0]
    hidden = fw_one.shape[2]
    wide = dh // reps
    paired = n_tok == 4
    near = 2 if paired else 1
    units = mlp_up.shape[1] // groups // near
    barrier = lax.optimization_barrier

    messages = [shape((n_key // reps, 2 * dh), BF), shape((n, dh + wide), BF)] if paired else []
    pair, *messages = call(
        message_kernel,
        [shape((n_key, 2 * dh), BF), *messages],
        [keys, values, rates.reshape(1, n_key), queries, stream],
    )
    asks = []
    if paired:
        share, ask = messages
        others = [moved(share, tok=s) for s in (1, 2, 3)]
        same, other = call(
            pack_kernel, [shape((mlp_up.shape[0] + units, units), BF)] * 2, [mlp_up, mlp_down]
        )
        first, ask, other_1 = barrier((others[0], ask, other))
        asks = [moved(ask, tok=1)]
        w_first = moved(other_1, tok=1)
        far, same_2 = barrier((others[1:], same))
        w_second = moved(same_2, tok=2)
        w_third = moved(barrier((other, w_second))[0], tok=3)
        tokens = [first, *far]
        tokens = tokens + [moved(x, rep=1) for x in tokens]
    else:
        me_g = lax.axis_index("groups")
        up_own = lax.dynamic_slice_in_dim(mlp_up, me_g * units, units, 1)
        down_own = lax.dynamic_slice_in_dim(mlp_down, me_g * units, units, 0)
        tokens = [lax.all_gather(pair, "tok", axis=0, tiled=True)]
        up_blocks = [lax.all_gather(up_own, "tok", axis=0, tiled=True)]
        down_blocks = [lax.all_gather(down_own, "tok", axis=1, tiled=True)]
    square = [shape((dh, hidden), F32), shape((dh, hidden), F32), shape((hidden, dh), F32)]
    prepared = call(
        functools.partial(own_kernel, paired),
        [
            *[shape(x.shape, BF) for x in square],
            *square,
            shape((16, hidden), F32),
            shape((8, dh), F32),
        ],
        [pair, fw_one[0], fw_three[0], fw_two[0]],
        flops=12 * n_key * dh * hidden,
    )
    n_all = sum(x.shape[0] for x in tokens)
    tokens, asks = barrier((tokens, asks))
    own, own_sq, send = call(
        functools.partial(fast_kernel, len(tokens), near),
        [shape((near * n, wide), F32), shape((8, wide), F32), shape((near * n + 16, wide), BF)],
        [*tokens, queries, *asks, *prepared],
        [pltpu.VMEM((n_all, dh), BF), pltpu.VMEM((n_all, dh), BF), pltpu.VMEM((near * n, dh), F32)],
        flops=12 * n_all * dh * hidden + 6 * near * n * dh * hidden,
    )
    got = moved(send, rep=1)
    if paired:
        got, w_first, w_second = barrier((got, w_first, w_second))
    mixed, low = call(
        mix_kernel,
        [shape((n, wide), F32), shape((near * n + 16, wide), BF)],
        [own, own_sq, got, stream, gain[None, :], *asks],
    )
    pieces, places = [], []
    for dg, h in itertools.product(range(groups), range(n_head)):
        x = moved(low, groups=dg, head=h)
        pieces += [x, moved(x, rep=1)]
        places += [(dg, h, 0), (dg, h, 1)]
    if paired:
        up_blocks = down_blocks = [same, w_first, w_second, w_third]
    rows, model = groups * near * n, n_head * dh
    (act,) = call(
        functools.partial(up_kernel, places, len(up_blocks)),
        [shape((rows, units), BF)],
        [*pieces, *up_blocks],
        [pltpu.VMEM((rows, model), BF)],
        flops=2 * rows * units * model,
    )
    own, send = call(
        functools.partial(down_kernel, len(down_blocks)),
        [shape((rows, n_head * wide), F32), shape((rows, n_head * wide), BF)],
        [act, *down_blocks],
        [pltpu.VMEM((rows, model), F32)],
        flops=2 * rows * units * model,
    )
    got = moved(send, rep=1)
    moves = list(itertools.product(range(groups), range(near), range(n_head)))
    total, *parts = call(
        functools.partial(pair_kernel, moves, near),
        [shape((n, wide), F32), *[shape((n, wide), BF)] * (len(moves) - 1)],
        [own, got, mixed],
    )
    for (dg, dz, h), x in zip(moves[1:], parts):
        total = total + moved(x, groups=(groups - dg) % groups, tok=dz, head=(n_head - h) % n_head).astype(F32)
    live = jnp.arange(n, dtype=jnp.int32) < counts[0]
    return jnp.where(live[:, None], total, 0.0).astype(BF)


def solution(mesh):
    placed = (
        P(("groups", "tok"), "head"),
        P(("groups", "tok"), "head"),
        P(("groups", "tok"), "head"),
        P(("groups", "tok"), "head"),
        P(("groups", "tok"), "head"),
        P("head"),
        P(("groups", "tok")),
        P("head", None, "rep"),
        P("head", None, "rep"),
        P("head", "rep", None),
        P("tok", ("head", "rep")),
        P(("head", "rep"), "tok"),
    )
    return jax.shard_map(
        on_device,
        mesh=mesh,
        in_specs=placed,
        out_specs=P(("groups", "tok"), ("head", "rep")),
        check_vma=False,
    )
```

time: 84.5 us -> 76.7 us (0.908)
  waiting for transfers between devices: 39.2 us -> 24.8 us
  local copies, waits for them, and re-layouts: 2.96 us -> 9.58 us
  other arithmetic: 3.66 us -> 0.72 us
  Pallas kernels: 4.42 us -> 6.38 us
  starting transfers between devices: 32.9 us -> 34 us
    ppermute x27 -> x26, waiting for transfers between devices: 39.2 us -> 24.8 us  [moved(): return lax.ppermute(x, tuple(axes), pairs)]
    unnamed x16 -> x26, local copies, waits for them, and re-layouts: 1.96 us -> 9.58 us
    pallas_call x5 -> x8, Pallas kernels: 4.42 us -> 6.38 us  [call(): pl.pallas_call(kernel, out_shape=outs, in_specs=[pl.BlockSpec(memory_spac...]
    concatenate x2 -> x0, other arithmetic: 1.87 us -> none  [on_device(): pair = jnp.concatenate([keys, scaled], axis=1)]
    ppermute x27 -> x26, starting transfers between devices: 32.9 us -> 34 us  [moved(): return lax.ppermute(x, tuple(axes), pairs)]
    convert_element_type x1 -> x0, other arithmetic: 1.07 us -> none  [on_device(): scaled = (rates * values.astype(F32)).astype(BF)]
    dynamic_slice x2 -> x0, local copies, waits for them, and re-layouts: 0.99 us -> none  [the longest x1 0.98 us: on_device(): up_own = lax.dynamic_slice_in_dim(mlp_up, me_g * units, units, 1)]
  transfers between devices with their start and end apart: 27 -> 26, of which waited for: 14 -> 11; matrix products, arithmetic and copies ran while one was open for 2% -> 0% of each run, Pallas kernels for 5% -> 6%
where the time goes in v3:
time: 76.7 us; the launch traced here: 76.3 us
  starting transfers between devices  34 us (44%)
  waiting for transfers between devices  24.8 us (32%)
  local copies, waits for them, and re-layouts  9.58 us (12%)
  Pallas kernels  6.38 us (8%)
  between operations  0.78 us (1%)
    ppermute x26, starting transfers between devices, moved(): return lax.ppermute(x, tuple(axes), pairs)  34 us
    ppermute x26, waiting for transfers between devices, moved(): return lax.ppermute(x, tuple(axes), pairs)  24.8 us
    unnamed x26, local copies, waits for them, and re-layouts  9.58 us
    pallas_call x8, Pallas kernels, call(): pl.pallas_call(kernel, out_shape=outs, in_specs=[pl.BlockSpec(memory_spac...  6.38 us
  transfers between devices with their start and end apart: 26, of which 11 were waited for; matrix products, arithmetic and copies ran while one was open for 0% of the time, Pallas kernels for 6%

profile of v3, /device:TPU:0, one launch (start us, length us, event | category | flops | bytes accessed | tf_op | source)
XLA Modules:
  0.0 76.3 jit_solution(16330499248517880192)
XLA Ops:
  0.0 1.0 %copy-done.3 = bf16[128,512]{1,0:T(8,128)(2,1)S(1)} copy-done((bf16[128,512]{1,0:T(8,128)(2,1)S(1)}, bf16[128,512]{1,0:T(8,128)(2,1)}, u32[]{:S(2)}) %copy-start.3) | copy-done | bytes 131096
  1.0 0.9 %copy-done.7 = bf16[128,512]{1,0:T(8,128)(2,1)S(1)} copy-done((bf16[128,512]{1,0:T(8,128)(2,1)S(1)}, bf16[128,512]{1,0:T(8,128)(2,1)}, u32[]{:S(2)}) %copy-start.7) | copy-done | bytes 131096
  1.9 0.9 %copy-done.9 = bf16[128,512]{1,0:T(8,128)(2,1)S(1)} copy-done((bf16[128,512]{1,0:T(8,128)(2,1)S(1)}, bf16[128,512]{1,0:T(8,128)(2,1)}, u32[]{:S(2)}) %copy-start.9) | copy-done | bytes 131096
  2.8 0.9 %copy-done.10 = bf16[128,512]{1,0:T(8,128)(2,1)S(1)} copy-done((bf16[128,512]{1,0:T(8,128)(2,1)S(1)}, bf16[128,512]{1,0:T(8,128)(2,1)}, u32[]{:S(2)}) %copy-start.10) | copy-done | bytes 131096
  3.7 0.7 copy-done.12
  4.4 0.1 shard_map.118
  4.5 4.1 %collective-permute-start.1 = (bf16[64,1024]{1,0:T(8,128)(2,1)S(1)}, bf16[64,1024]{1,0:T(8,128)(2,1)S(1)}, u32[]{:S(2)}, u32[]{:S(2)}) collective-permute-start(bf16[64,1024]{1,0:T(8,128)(2,1)S(1)} %get-tuple-element.50), channel_id=1, source_target_pairs={{8,0},{12,4},{0,8},{4,12},{9,1},{13,5},{1,9},{5,13},{10,2},{14,6},... | collective-permute-start | bytes 393224 | tf_op jit(solution)/shard_map/ppermute | solution.py:30
  8.6 1.3 %collective-permute-start.2 = (bf16[64,1024]{1,0:T(8,128)(2,1)S(1)}, bf16[64,1024]{1,0:T(8,128)(2,1)S(1)}, u32[]{:S(2)}, u32[]{:S(2)}) collective-permute-start(bf16[64,1024]{1,0:T(8,128)(2,1)S(1)} %get-tuple-element.50), channel_id=1, source_target_pairs={{12,0},{8,4},{4,8},{0,12},{13,1},{9,5},{5,9},{1,13},{14,2},{10,6},... | collective-permute-start | bytes 393224 | tf_op jit(solution)/shard_map/ppermute | solution.py:30
  9.9 0.2 collective-permute-start
  10.2 1.0 %copy-done.5 = bf16[256,1024]{1,0:T(8,128)(2,1)S(1)} copy-done((bf16[256,1024]{1,0:T(8,128)(2,1)S(1)}, bf16[256,1024]{1,0:T(8,128)(2,1)}, u32[]{:S(2)}) %copy-start.5) | copy-done | bytes 524312
  11.2 1.0 %copy-done.6 = bf16[1024,256]{1,0:T(8,128)(2,1)S(1)} copy-done((bf16[1024,256]{1,0:T(8,128)(2,1)S(1)}, bf16[1024,256]{1,0:T(8,128)(2,1)}, u32[]{:S(2)}) %copy-start.6) | copy-done | bytes 524312
  12.3 6.3 %collective-permute-done.1.refs_1_ = bf16[64,1024]{1,0:T(8,128)(2,1)S(1)} collective-permute-done((bf16[64,1024]{1,0:T(8,128)(2,1)S(1)}, bf16[64,1024]{1,0:T(8,128)(2,1)S(1)}, u32[]{:S(2)}, u32[]{:S(2)}) %collective-permute-start.1) | collective-permute-done | bytes 131104 | tf_op jit(solution)/shard_map/ppermute | solution.py:30
  18.6 0.0 collective-permute-done.2.refs_2_
  18.6 0.5 collective-permute-done.refs_0_
  19.1 2.2 %collective-permute-start.6 = (bf16[128,768]{1,0:T(8,128)(2,1)S(1)}, bf16[128,768]{1,0:T(8,128)(2,1)S(1)}, u32[]{:S(2)}, u32[]{:S(2)}) collective-permute-start(bf16[128,768]{1,0:T(8,128)(2,1)S(1)} %get-tuple-element.57), channel_id=1, source_target_pairs={{4,0},{0,4},{12,8},{8,12},{5,1},{1,5},{13,9},{9,13},{6,2},{2,6},{1... | collective-permute-start | bytes 589832 | tf_op jit(solution)/shard_map/ppermute | solution.py:30
  21.3 0.2 collective-permute-start.5
  21.5 0.3 collective-permute-start.3
  21.8 2.0 %collective-permute-start.9 = (bf16[512,256]{1,0:T(8,128)(2,1)S(1)}, bf16[512,256]{1,0:T(8,128)(2,1)S(1)}, u32[]{:S(2)}, u32[]{:S(2)}) collective-permute-start(bf16[512,256]{1,0:T(8,128)(2,1)S(1)} %get-tuple-element.78.refs_8_.refs_0_), channel_id=1, source_target_pairs={{8,0},{12,4},{0,8},{4,12},{9,1},{13,5},{1,9},{5,13},{10,2},{14,6},... | collective-permute-start | bytes 786440 | tf_op jit(solution)/shard_map/ppermute | solution.py:30
  23.8 2.0 %collective-permute-start.8 = (bf16[512,256]{1,0:T(8,128)(2,1)S(1)}, bf16[512,256]{1,0:T(8,128)(2,1)S(1)}, u32[]{:S(2)}, u32[]{:S(2)}) collective-permute-start(bf16[512,256]{1,0:T(8,128)(2,1)S(1)} %get-tuple-element.83), channel_id=1, source_target_pairs={{4,0},{0,4},{12,8},{8,12},{5,1},{1,5},{13,9},{9,13},{6,2},{2,6},{1... | collective-permute-start | bytes 786440 | tf_op jit(solution)/shard_map/ppermute | solution.py:30
  25.8 1.2 %copy-done.1 = f32[1,512,512]{2,1,0:T(8,128)S(1)} copy-done((f32[1,512,512]{2,1,0:T(8,128)S(1)}, f32[1,512,512]{2,1,0:T(8,128)}, u32[]{:S(2)}) %copy-start.1) | copy-done | bytes 1048600
  27.0 1.2 %copy-done.2 = f32[1,512,512]{2,1,0:T(8,128)S(1)} copy-done((f32[1,512,512]{2,1,0:T(8,128)S(1)}, f32[1,512,512]{2,1,0:T(8,128)}, u32[]{:S(2)}) %copy-start.2) | copy-done | bytes 1048600
  28.2 1.4 %shard_map.120 = (bf16[512,512]{1,0:T(8,128)(2,1)S(1)}, bf16[512,512]{1,0:T(8,128)(2,1)S(1)}, bf16[512,512]{1,0:T(8,128)(2,1)S(1)}, f32[512,512]{1,0:T(8,128)S(1...) custom-call(bf16[128,1024]{1,0:T(8,128)(2,1)S(1)} %get-tuple-element.65.pair,, ...), custom_call_target="tpu_custom_call" | custom-call | flops 1 | bytes 1 | tf_op jit(solution)/shard_map/pallas_call | solution.py:40
  29.6 0.0 collective-permute-done.5.refs_5_
  29.7 0.0 collective-permute-done.3.refs_3_
  29.7 1.9 %collective-permute-done.6.refs_7_.refs_0_ = bf16[128,768]{1,0:T(8,128)(2,1)S(1)} collective-permute-done((bf16[128,768]{1,0:T(8,128)(2,1)S(1)}, bf16[128,768]{1,0:T(8,128)(2,1)S(1)}, u32[]{:S(2)}, u32[]{:S(2)}) %collective-permute-start.6) | collective-permute-done | bytes 196640 | tf_op jit(solution)/shard_map/ppermute | solution.py:30
  31.5 3.0 %shard_map.121 = (f32[256,256]{1,0:T(8,128)S(1)}, f32[8,256]{1,0:T(8,128)S(1)}, bf16[272,256]{1,0:T(8,128)(2,1)S(1)}) custom-call(bf16[64,1024]{1,0:T(8,128)(2,1)S(1)} %collective-permute-done.refs_0_, bf16[64,1024]{1,0:T(8,128)(2,1)S(1)} %collective-permute-done.1.refs_1_, bf16[64,1024]{1,0:T(8,128)(2,1)S(1)} %collective-permute-done.2.refs_2_, ...), custom_call_target="tpu_custom_call" | custom-call | flops 1 | bytes 1 | tf_op jit(solution)/shard_map/pallas_call | solution.py:40
  34.6 0.1 collective-permute-start.7
  34.6 2.3 %collective-permute-done.9.refs_10_.refs_2_ = bf16[512,256]{1,0:T(8,128)(2,1)S(1)} collective-permute-done((bf16[512,256]{1,0:T(8,128)(2,1)S(1)}, bf16[512,256]{1,0:T(8,128)(2,1)S(1)}, u32[]{:S(2)}, u32[]{:S(2)}) %collective-permute-start.9) | collective-permute-done | bytes 262176 | tf_op jit(solution)/shard_map/ppermute | solution.py:30
  36.9 1.2 %collective-permute-done.8.refs_9_.refs_1_ = bf16[512,256]{1,0:T(8,128)(2,1)S(1)} collective-permute-done((bf16[512,256]{1,0:T(8,128)(2,1)S(1)}, bf16[512,256]{1,0:T(8,128)(2,1)S(1)}, u32[]{:S(2)}, u32[]{:S(2)}) %collective-permute-start.8) | collective-permute-done | bytes 262176 | tf_op jit(solution)/shard_map/ppermute | solution.py:30
  38.1 0.0 collective-permute-done.7.got
  38.1 0.7 copy-done.11
  38.8 0.1 shard_map.122
  38.8 1.6 %collective-permute-start.11 = (bf16[272,256]{1,0:T(8,128)(2,1)S(1)}, bf16[272,256]{1,0:T(8,128)(2,1)S(1)}, u32[]{:S(2)}, u32[]{:S(2)}) collective-permute-start(bf16[272,256]{1,0:T(8,128)(2,1)S(1)} %get-tuple-element.80.refs_0_), channel_id=1, source_target_pairs={{2,0},{0,2},{3,1},{1,3},{6,4},{4,6},{7,5},{5,7},{10,8},{8,10},{11,... | collective-permute-start | bytes 417800 | tf_op jit(solution)/shard_map/ppermute | solution.py:30
  40.4 1.5 %collective-permute-start.13 = (bf16[272,256]{1,0:T(8,128)(2,1)S(1)}, bf16[272,256]{1,0:T(8,128)(2,1)S(1)}, u32[]{:S(2)}, u32[]{:S(2)}) collective-permute-start(bf16[272,256]{1,0:T(8,128)(2,1)S(1)} %get-tuple-element.80.refs_0_), channel_id=1, source_target_pairs={{16,0},{0,16},{17,1},{1,17},{18,2},{2,18},{19,3},{3,19},{20,4},{4,... | collective-permute-start | bytes 417800 | tf_op jit(solution)/shard_map/ppermute | solution.py:30
  41.9 0.5 collective-permute-start.15
  42.4 3.4 %collective-permute-start.17 = (bf16[512,256]{1,0:T(8,128)(2,1)S(1)}, bf16[512,256]{1,0:T(8,128)(2,1)S(1)}, u32[]{:S(2)}, u32[]{:S(2)}) collective-permute-start(bf16[512,256]{1,0:T(8,128)(2,1)S(1)} %get-tuple-element.83), channel_id=1, source_target_pairs={{12,0},{8,4},{4,8},{0,12},{13,1},{9,5},{5,9},{1,13},{14,2},{10,6},... | collective-permute-start | bytes 786440 | tf_op jit(solution)/shard_map/ppermute | solution.py:30
  45.8 0.0 collective-permute-start.10
  45.8 0.0 collective-permute-done.11.refs_2_
  45.8 0.5 collective-permute-start.12
  46.3 2.3 %collective-permute-done.13.refs_4_ = bf16[272,256]{1,0:T(8,128)(2,1)S(1)} collective-permute-done((bf16[272,256]{1,0:T(8,128)(2,1)S(1)}, bf16[272,256]{1,0:T(8,128)(2,1)S(1)}, u32[]{:S(2)}, u32[]{:S(2)}) %collective-permute-start.13) | collective-permute-done | bytes 139296 | tf_op jit(solution)/shard_map/ppermute | solution.py:30
  48.6 0.5 collective-permute-start.16
  49.1 2.5 %collective-permute-done.17.refs_11_.refs_3_ = bf16[512,256]{1,0:T(8,128)(2,1)S(1)} collective-permute-done((bf16[512,256]{1,0:T(8,128)(2,1)S(1)}, bf16[512,256]{1,0:T(8,128)(2,1)S(1)}, u32[]{:S(2)}, u32[]{:S(2)}) %collective-permute-start.17) | collective-permute-done | bytes 262176 | tf_op jit(solution)/shard_map/ppermute | solution.py:30
  51.6 0.0 collective-permute-done.14.refs_5_
  51.6 0.0 collective-permute-done.16.refs_7_
  51.6 0.9 %shard_map.123.h = bf16[512,256]{1,0:T(8,128)(2,1)S(1)} custom-call(bf16[272,256]{1,0:T(8,128)(2,1)S(1)} %get-tuple-element.80.refs_0_, bf16[272,256]{1,0:T(8,128)(2,1)S(1)} %collective-permute-done.10.refs_1_, bf16[272,256]{1,0:T(8,128)(2,1)S(1)} %collective-permute-done.11.refs_2_, bf16[272,256]{1,0:T(8,128)(2,1)S(1)} %collective-permute-done.12.refs_3_, ...), custom_call_target="tpu_custom_call" | custom-call | flops 1 | bytes 1 | tf_op jit(solution)/shard_map/pallas_call | solution.py:40
  52.6 0.7 shard_map.124
  53.2 0.1 collective-permute-start.18
  53.3 1.9 %collective-permute-done.18.got = bf16[512,512]{1,0:T(8,128)(2,1)S(1)} collective-permute-done((bf16[512,512]{1,0:T(8,128)(2,1)S(1)}, bf16[512,512]{1,0:T(8,128)(2,1)S(1)}, u32[]{:S(2)}, u32[]{:S(2)}) %collective-permute-start.18) | collective-permute-done | bytes 524320 | tf_op jit(solution)/shard_map/ppermute | solution.py:30
  55.2 0.1 shard_map.125
  55.3 1.6 %collective-permute-start.19 = (bf16[128,256]{1,0:T(8,128)(2,1)S(1)}, bf16[128,256]{1,0:T(8,128)(2,1)S(1)}, u32[]{:S(2)}, u32[]{:S(2)}) collective-permute-start(bf16[128,256]{1,0:T(8,128)(2,1)S(1)} %get-tuple-element.88), channel_id=1, source_target_pairs={{2,0},{0,2},{3,1},{1,3},{6,4},{4,6},{7,5},{5,7},{10,8},{8,10},{11,... | collective-permute-start | bytes 196616 | tf_op jit(solution)/shard_map/ppermute | solution.py:30
  56.9 6.0 %collective-permute-start.20 = (bf16[128,256]{1,0:T(8,128)(2,1)S(1)}, bf16[128,256]{1,0:T(8,128)(2,1)S(1)}, u32[]{:S(2)}, u32[]{:S(2)}) collective-permute-start(bf16[128,256]{1,0:T(8,128)(2,1)S(1)} %get-tuple-element.89), channel_id=1, source_target_pairs={{4,0},{0,4},{12,8},{8,12},{5,1},{1,5},{13,9},{9,13},{6,2},{2,6},{1... | collective-permute-start | bytes 196616 | tf_op jit(solution)/shard_map/ppermute | solution.py:30
  63.6 0.1 collective-permute-start.21
  63.6 1.6 %collective-permute-start.22 = (bf16[128,256]{1,0:T(8,128)(2,1)S(1)}, bf16[128,256]{1,0:T(8,128)(2,1)S(1)}, u32[]{:S(2)}, u32[]{:S(2)}) collective-permute-start(bf16[128,256]{1,0:T(8,128)(2,1)S(1)} %get-tuple-element.91), channel_id=1, source_target_pairs={{16,0},{0,16},{17,1},{1,17},{18,2},{2,18},{19,3},{3,19},{20,4},{4,... | collective-permute-start | bytes 196616 | tf_op jit(solution)/shard_map/ppermute | solution.py:30
  65.2 1.3 %collective-permute-start.23 = (bf16[128,256]{1,0:T(8,128)(2,1)S(1)}, bf16[128,256]{1,0:T(8,128)(2,1)S(1)}, u32[]{:S(2)}, u32[]{:S(2)}) collective-permute-start(bf16[128,256]{1,0:T(8,128)(2,1)S(1)} %get-tuple-element.92), channel_id=1, source_target_pairs={{18,0},{16,2},{2,16},{0,18},{19,1},{17,3},{3,17},{1,19},{22,4},{20... | collective-permute-start | bytes 196616 | tf_op jit(solution)/shard_map/ppermute | solution.py:30
  66.6 0.0 collective-permute-done.19
  66.6 3.0 %collective-permute-start.24 = (bf16[128,256]{1,0:T(8,128)(2,1)S(1)}, bf16[128,256]{1,0:T(8,128)(2,1)S(1)}, u32[]{:S(2)}, u32[]{:S(2)}) collective-permute-start(bf16[128,256]{1,0:T(8,128)(2,1)S(1)} %get-tuple-element.93), channel_id=1, source_target_pairs={{20,0},{16,4},{28,8},{24,12},{4,16},{0,20},{12,24},{8,28},{21,1},{... | collective-permute-start | bytes 196616 | tf_op jit(solution)/shard_map/ppermute | solution.py:30
  69.5 0.0 collective-permute-done.20
  69.5 0.0 collective-permute-start.25
  69.6 0.0 collective-permute-done.21
  69.6 0.0 collective-permute-done.22
  69.6 1.1 %collective-permute-done.23 = bf16[128,256]{1,0:T(8,128)(2,1)S(1)} collective-permute-done((bf16[128,256]{1,0:T(8,128)(2,1)S(1)}, bf16[128,256]{1,0:T(8,128)(2,1)S(1)}, u32[]{:S(2)}, u32[]{:S(2)}) %collective-permute-start.23) | collective-permute-done | bytes 65568 | tf_op jit(solution)/shard_map/ppermute | solution.py:30
  70.7 1.5 %collective-permute-done.24 = bf16[128,256]{1,0:T(8,128)(2,1)S(1)} collective-permute-done((bf16[128,256]{1,0:T(8,128)(2,1)S(1)}, bf16[128,256]{1,0:T(8,128)(2,1)S(1)}, u32[]{:S(2)}, u32[]{:S(2)}) %collective-permute-start.24) | collective-permute-done | bytes 65568 | tf_op jit(solution)/shard_map/ppermute | solution.py:30
  72.2 3.4 %collective-permute-done.25 = bf16[128,256]{1,0:T(8,128)(2,1)S(1)} collective-permute-done((bf16[128,256]{1,0:T(8,128)(2,1)S(1)}, bf16[128,256]{1,0:T(8,128)(2,1)S(1)}, u32[]{:S(2)}, u32[]{:S(2)}) %collective-permute-start.25) | collective-permute-done | bytes 65568 | tf_op jit(solution)/shard_map/ppermute | solution.py:30
  75.6 0.7 select_convert_fusion
  (24 shorter events, 0.1 us)
Async XLA Ops:
  0.0 25.8 %copy-start = (f32[1,512,512]{2,1,0:T(8,128)S(1)}, f32[1,512,512]{2,1,0:T(8,128)}, u32[]{:S(2)}) copy-start(f32[1,512,512]{2,1,0:T(8,128)} %param.19) | copy-start | bytes 3145732
  0.0 1.0 %copy-start.3 = (bf16[128,512]{1,0:T(8,128)(2,1)S(1)}, bf16[128,512]{1,0:T(8,128)(2,1)}, u32[]{:S(2)}) copy-start(bf16[128,512]{1,0:T(8,128)(2,1)} %refs_6_.1) | copy-start | bytes 393220
  1.0 0.9 %copy-start.7 = (bf16[128,512]{1,0:T(8,128)(2,1)S(1)}, bf16[128,512]{1,0:T(8,128)(2,1)}, u32[]{:S(2)}) copy-start(bf16[128,512]{1,0:T(8,128)(2,1)} %stream.3) | copy-start | bytes 393220
  1.9 0.9 %copy-start.9 = (bf16[128,512]{1,0:T(8,128)(2,1)S(1)}, bf16[128,512]{1,0:T(8,128)(2,1)}, u32[]{:S(2)}) copy-start(bf16[128,512]{1,0:T(8,128)(2,1)} %keys.1) | copy-start | bytes 393220
  2.8 0.9 %copy-start.10 = (bf16[128,512]{1,0:T(8,128)(2,1)S(1)}, bf16[128,512]{1,0:T(8,128)(2,1)}, u32[]{:S(2)}) copy-start(bf16[128,512]{1,0:T(8,128)(2,1)} %values.1) | copy-start | bytes 393220
  3.7 0.7 copy-start.12
  4.5 14.1 %collective-permute-start.1 = (bf16[64,1024]{1,0:T(8,128)(2,1)S(1)}, bf16[64,1024]{1,0:T(8,128)(2,1)S(1)}, u32[]{:S(2)}, u32[]{:S(2)}) collective-permute-start(bf16[64,1024]{1,0:T(8,128)(2,1)S(1)} %get-tuple-element.50), channel_id=1, source_target_pairs={{8,0},{12,4},{0,8},{4,12},{9,1},{13,5},{1,9},{5,13},{10,2},{14,6},... | collective-permute-start | bytes 393224 | tf_op jit(solution)/shard_map/ppermute | solution.py:30
  8.6 10.0 %collective-permute-start.2 = (bf16[64,1024]{1,0:T(8,128)(2,1)S(1)}, bf16[64,1024]{1,0:T(8,128)(2,1)S(1)}, u32[]{:S(2)}, u32[]{:S(2)}) collective-permute-start(bf16[64,1024]{1,0:T(8,128)(2,1)S(1)} %get-tuple-element.50), channel_id=1, source_target_pairs={{12,0},{8,4},{4,8},{0,12},{13,1},{9,5},{5,9},{1,13},{14,2},{10,6},... | collective-permute-start | bytes 393224 | tf_op jit(solution)/shard_map/ppermute | solution.py:30
  9.9 9.2 %collective-permute-start = (bf16[64,1024]{1,0:T(8,128)(2,1)S(1)}, bf16[64,1024]{1,0:T(8,128)(2,1)S(1)}, u32[]{:S(2)}, u32[]{:S(2)}) collective-permute-start(bf16[64,1024]{1,0:T(8,128)(2,1)S(1)} %get-tuple-element.50), channel_id=1, source_target_pairs={{4,0},{0,4},{12,8},{8,12},{5,1},{1,5},{13,9},{9,13},{6,2},{2,6},{1... | collective-permute-start | bytes 393224 | tf_op jit(solution)/shard_map/ppermute | solution.py:30
  10.2 1.0 %copy-start.5 = (bf16[256,1024]{1,0:T(8,128)(2,1)S(1)}, bf16[256,1024]{1,0:T(8,128)(2,1)}, u32[]{:S(2)}) copy-start(bf16[256,1024]{1,0:T(8,128)(2,1)} %up.1) | copy-start | bytes 1572868
  11.2 1.0 %copy-start.6 = (bf16[1024,256]{1,0:T(8,128)(2,1)S(1)}, bf16[1024,256]{1,0:T(8,128)(2,1)}, u32[]{:S(2)}) copy-start(bf16[1024,256]{1,0:T(8,128)(2,1)} %down.1) | copy-start | bytes 1572868
  18.6 5.2 %collective-permute-start.4 = (bf16[64,1024]{1,0:T(8,128)(2,1)S(1)}, bf16[64,1024]{1,0:T(8,128)(2,1)S(1)}, u32[]{:S(2)}, u32[]{:S(2)}) collective-permute-start(bf16[64,1024]{1,0:T(8,128)(2,1)S(1)} %collective-permute-done.1.refs_1_), channel_id=1, source_target_pairs={{1,0},{0,1},{3,2},{2,3},{5,4},{4,5},{7,6},{6,7},{9,8},{8,9},{11,10... | collective-permute-start | bytes 393224 | tf_op jit(solution)/shard_map/ppermute | solution.py:30
  19.1 12.4 %collective-permute-start.6 = (bf16[128,768]{1,0:T(8,128)(2,1)S(1)}, bf16[128,768]{1,0:T(8,128)(2,1)S(1)}, u32[]{:S(2)}, u32[]{:S(2)}) collective-permute-start(bf16[128,768]{1,0:T(8,128)(2,1)S(1)} %get-tuple-element.57), channel_id=1, source_target_pairs={{4,0},{0,4},{12,8},{8,12},{5,1},{1,5},{13,9},{9,13},{6,2},{2,6},{1... | collective-permute-start | bytes 589832 | tf_op jit(solution)/shard_map/ppermute | solution.py:30
  21.3 8.3 %collective-permute-start.5 = (bf16[64,1024]{1,0:T(8,128)(2,1)S(1)}, bf16[64,1024]{1,0:T(8,128)(2,1)S(1)}, u32[]{:S(2)}, u32[]{:S(2)}) collective-permute-start(bf16[64,1024]{1,0:T(8,128)(2,1)S(1)} %collective-permute-done.2.refs_2_), channel_id=1, source_target_pairs={{1,0},{0,1},{3,2},{2,3},{5,4},{4,5},{7,6},{6,7},{9,8},{8,9},{11,10... | collective-permute-start | bytes 393224 | tf_op jit(solution)/shard_map/ppermute | solution.py:30
  21.5 8.1 %collective-permute-start.3 = (bf16[64,1024]{1,0:T(8,128)(2,1)S(1)}, bf16[64,1024]{1,0:T(8,128)(2,1)S(1)}, u32[]{:S(2)}, u32[]{:S(2)}) collective-permute-start(bf16[64,1024]{1,0:T(8,128)(2,1)S(1)} %collective-permute-done.refs_0_), channel_id=1, source_target_pairs={{1,0},{0,1},{3,2},{2,3},{5,4},{4,5},{7,6},{6,7},{9,8},{8,9},{11,10... | collective-permute-start | bytes 393224 | tf_op jit(solution)/shard_map/ppermute | solution.py:30
  21.8 15.1 %collective-permute-start.9 = (bf16[512,256]{1,0:T(8,128)(2,1)S(1)}, bf16[512,256]{1,0:T(8,128)(2,1)S(1)}, u32[]{:S(2)}, u32[]{:S(2)}) collective-permute-start(bf16[512,256]{1,0:T(8,128)(2,1)S(1)} %get-tuple-element.78.refs_8_.refs_0_), channel_id=1, source_target_pairs={{8,0},{12,4},{0,8},{4,12},{9,1},{13,5},{1,9},{5,13},{10,2},{14,6},... | collective-permute-start | bytes 786440 | tf_op jit(solution)/shard_map/ppermute | solution.py:30
  23.8 14.3 %collective-permute-start.8 = (bf16[512,256]{1,0:T(8,128)(2,1)S(1)}, bf16[512,256]{1,0:T(8,128)(2,1)S(1)}, u32[]{:S(2)}, u32[]{:S(2)}) collective-permute-start(bf16[512,256]{1,0:T(8,128)(2,1)S(1)} %get-tuple-element.83), channel_id=1, source_target_pairs={{4,0},{0,4},{12,8},{8,12},{5,1},{1,5},{13,9},{9,13},{6,2},{2,6},{1... | collective-permute-start | bytes 786440 | tf_op jit(solution)/shard_map/ppermute | solution.py:30
  25.8 1.2 %copy-start.1 = (f32[1,512,512]{2,1,0:T(8,128)S(1)}, f32[1,512,512]{2,1,0:T(8,128)}, u32[]{:S(2)}) copy-start(f32[1,512,512]{2,1,0:T(8,128)} %param.20) | copy-start | bytes 3145732
  27.0 1.2 %copy-start.2 = (f32[1,512,512]{2,1,0:T(8,128)S(1)}, f32[1,512,512]{2,1,0:T(8,128)}, u32[]{:S(2)}) copy-start(f32[1,512,512]{2,1,0:T(8,128)} %param.21) | copy-start | bytes 3145732
  28.2 3.3 %copy-start.4 = (bf16[128,512]{1,0:T(8,128)(2,1)S(1)}, bf16[128,512]{1,0:T(8,128)(2,1)}, u32[]{:S(2)}) copy-start(bf16[128,512]{1,0:T(8,128)(2,1)} %refs_6_.1) | copy-start | bytes 393220
  31.5 6.6 %copy-start.8 = (bf16[128,512]{1,0:T(8,128)(2,1)S(1)}, bf16[128,512]{1,0:T(8,128)(2,1)}, u32[]{:S(2)}) copy-start(bf16[128,512]{1,0:T(8,128)(2,1)} %stream.3) | copy-start | bytes 393220
  34.6 3.5 %collective-permute-start.7 = (bf16[272,256]{1,0:T(8,128)(2,1)S(1)}, bf16[272,256]{1,0:T(8,128)(2,1)S(1)}, u32[]{:S(2)}, u32[]{:S(2)}) collective-permute-start(bf16[272,256]{1,0:T(8,128)(2,1)S(1)} %get-tuple-element.76), channel_id=1, source_target_pairs={{1,0},{0,1},{3,2},{2,3},{5,4},{4,5},{7,6},{6,7},{9,8},{8,9},{11,10... | collective-permute-start | bytes 417800 | tf_op jit(solution)/shard_map/ppermute | solution.py:30
  38.1 0.7 copy-start.11
  38.8 6.9 %collective-permute-start.11 = (bf16[272,256]{1,0:T(8,128)(2,1)S(1)}, bf16[272,256]{1,0:T(8,128)(2,1)S(1)}, u32[]{:S(2)}, u32[]{:S(2)}) collective-permute-start(bf16[272,256]{1,0:T(8,128)(2,1)S(1)} %get-tuple-element.80.refs_0_), channel_id=1, source_target_pairs={{2,0},{0,2},{3,1},{1,3},{6,4},{4,6},{7,5},{5,7},{10,8},{8,10},{11,... | collective-permute-start | bytes 417800 | tf_op jit(solution)/shard_map/ppermute | solution.py:30
  40.4 8.2 %collective-permute-start.13 = (bf16[272,256]{1,0:T(8,128)(2,1)S(1)}, bf16[272,256]{1,0:T(8,128)(2,1)S(1)}, u32[]{:S(2)}, u32[]{:S(2)}) collective-permute-start(bf16[272,256]{1,0:T(8,128)(2,1)S(1)} %get-tuple-element.80.refs_0_), channel_id=1, source_target_pairs={{16,0},{0,16},{17,1},{1,17},{18,2},{2,18},{19,3},{3,19},{20,4},{4,... | collective-permute-start | bytes 417800 | tf_op jit(solution)/shard_map/ppermute | solution.py:30
  41.9 6.7 %collective-permute-start.15 = (bf16[272,256]{1,0:T(8,128)(2,1)S(1)}, bf16[272,256]{1,0:T(8,128)(2,1)S(1)}, u32[]{:S(2)}, u32[]{:S(2)}) collective-permute-start(bf16[272,256]{1,0:T(8,128)(2,1)S(1)} %get-tuple-element.80.refs_0_), channel_id=1, source_target_pairs={{18,0},{16,2},{2,16},{0,18},{19,1},{17,3},{3,17},{1,19},{22,4},{20... | collective-permute-start | bytes 417800 | tf_op jit(solution)/shard_map/ppermute | solution.py:30
  42.4 9.2 %collective-permute-start.17 = (bf16[512,256]{1,0:T(8,128)(2,1)S(1)}, bf16[512,256]{1,0:T(8,128)(2,1)S(1)}, u32[]{:S(2)}, u32[]{:S(2)}) collective-permute-start(bf16[512,256]{1,0:T(8,128)(2,1)S(1)} %get-tuple-element.83), channel_id=1, source_target_pairs={{12,0},{8,4},{4,8},{0,12},{13,1},{9,5},{5,9},{1,13},{14,2},{10,6},... | collective-permute-start | bytes 786440 | tf_op jit(solution)/shard_map/ppermute | solution.py:30
  45.8 3.3 %collective-permute-start.10 = (bf16[272,256]{1,0:T(8,128)(2,1)S(1)}, bf16[272,256]{1,0:T(8,128)(2,1)S(1)}, u32[]{:S(2)}, u32[]{:S(2)}) collective-permute-start(bf16[272,256]{1,0:T(8,128)(2,1)S(1)} %get-tuple-element.80.refs_0_), channel_id=1, source_target_pairs={{1,0},{0,1},{3,2},{2,3},{5,4},{4,5},{7,6},{6,7},{9,8},{8,9},{11,10... | collective-permute-start | bytes 417800 | tf_op jit(solution)/shard_map/ppermute | solution.py:30
  45.8 5.8 %collective-permute-start.12 = (bf16[272,256]{1,0:T(8,128)(2,1)S(1)}, bf16[272,256]{1,0:T(8,128)(2,1)S(1)}, u32[]{:S(2)}, u32[]{:S(2)}) collective-permute-start(bf16[272,256]{1,0:T(8,128)(2,1)S(1)} %collective-permute-done.11.refs_2_), channel_id=1, source_target_pairs={{1,0},{0,1},{3,2},{2,3},{5,4},{4,5},{7,6},{6,7},{9,8},{8,9},{11,10... | collective-permute-start | bytes 417800 | tf_op jit(solution)/shard_map/ppermute | solution.py:30
  48.6 3.0 %collective-permute-start.14 = (bf16[272,256]{1,0:T(8,128)(2,1)S(1)}, bf16[272,256]{1,0:T(8,128)(2,1)S(1)}, u32[]{:S(2)}, u32[]{:S(2)}) collective-permute-start(bf16[272,256]{1,0:T(8,128)(2,1)S(1)} %collective-permute-done.13.refs_4_), channel_id=1, source_target_pairs={{1,0},{0,1},{3,2},{2,3},{5,4},{4,5},{7,6},{6,7},{9,8},{8,9},{11,10... | collective-permute-start | bytes 417800 | tf_op jit(solution)/shard_map/ppermute | solution.py:30
  48.6 3.0 %collective-permute-start.16 = (bf16[272,256]{1,0:T(8,128)(2,1)S(1)}, bf16[272,256]{1,0:T(8,128)(2,1)S(1)}, u32[]{:S(2)}, u32[]{:S(2)}) collective-permute-start(bf16[272,256]{1,0:T(8,128)(2,1)S(1)} %collective-permute-done.15.refs_6_), channel_id=1, source_target_pairs={{1,0},{0,1},{3,2},{2,3},{5,4},{4,5},{7,6},{6,7},{9,8},{8,9},{11,10... | collective-permute-start | bytes 417800 | tf_op jit(solution)/shard_map/ppermute | solution.py:30
  53.2 2.0 %collective-permute-start.18 = (bf16[512,512]{1,0:T(8,128)(2,1)S(1)}, bf16[512,512]{1,0:T(8,128)(2,1)S(1)}, u32[]{:S(2)}, u32[]{:S(2)}) collective-permute-start(bf16[512,512]{1,0:T(8,128)(2,1)S(1)} %get-tuple-element.85), channel_id=1, source_target_pairs={{1,0},{0,1},{3,2},{2,3},{5,4},{4,5},{7,6},{6,7},{9,8},{8,9},{11,10... | collective-permute-start | bytes 1572872 | tf_op jit(solution)/shard_map/ppermute | solution.py:30
  55.3 11.2 %collective-permute-start.19 = (bf16[128,256]{1,0:T(8,128)(2,1)S(1)}, bf16[128,256]{1,0:T(8,128)(2,1)S(1)}, u32[]{:S(2)}, u32[]{:S(2)}) collective-permute-start(bf16[128,256]{1,0:T(8,128)(2,1)S(1)} %get-tuple-element.88), channel_id=1, source_target_pairs={{2,0},{0,2},{3,1},{1,3},{6,4},{4,6},{7,5},{5,7},{10,8},{8,10},{11,... | collective-permute-start | bytes 196616 | tf_op jit(solution)/shard_map/ppermute | solution.py:30
  56.9 12.7 %collective-permute-start.20 = (bf16[128,256]{1,0:T(8,128)(2,1)S(1)}, bf16[128,256]{1,0:T(8,128)(2,1)S(1)}, u32[]{:S(2)}, u32[]{:S(2)}) collective-permute-start(bf16[128,256]{1,0:T(8,128)(2,1)S(1)} %get-tuple-element.89), channel_id=1, source_target_pairs={{4,0},{0,4},{12,8},{8,12},{5,1},{1,5},{13,9},{9,13},{6,2},{2,6},{1... | collective-permute-start | bytes 196616 | tf_op jit(solution)/shard_map/ppermute | solution.py:30
  63.6 6.0 %collective-permute-start.21 = (bf16[128,256]{1,0:T(8,128)(2,1)S(1)}, bf16[128,256]{1,0:T(8,128)(2,1)S(1)}, u32[]{:S(2)}, u32[]{:S(2)}) collective-permute-start(bf16[128,256]{1,0:T(8,128)(2,1)S(1)} %get-tuple-element.90), channel_id=1, source_target_pairs={{6,0},{4,2},{2,4},{0,6},{14,8},{12,10},{10,12},{8,14},{7,1},{5,3},... | collective-permute-start | bytes 196616 | tf_op jit(solution)/shard_map/ppermute | solution.py:30
  63.6 6.0 %collective-permute-start.22 = (bf16[128,256]{1,0:T(8,128)(2,1)S(1)}, bf16[128,256]{1,0:T(8,128)(2,1)S(1)}, u32[]{:S(2)}, u32[]{:S(2)}) collective-permute-start(bf16[128,256]{1,0:T(8,128)(2,1)S(1)} %get-tuple-element.91), channel_id=1, source_target_pairs={{16,0},{0,16},{17,1},{1,17},{18,2},{2,18},{19,3},{3,19},{20,4},{4,... | collective-permute-start | bytes 196616 | tf_op jit(solution)/shard_map/ppermute | solution.py:30
  65.2 5.5 %collective-permute-start.23 = (bf16[128,256]{1,0:T(8,128)(2,1)S(1)}, bf16[128,256]{1,0:T(8,128)(2,1)S(1)}, u32[]{:S(2)}, u32[]{:S(2)}) collective-permute-start(bf16[128,256]{1,0:T(8,128)(2,1)S(1)} %get-tuple-element.92), channel_id=1, source_target_pairs={{18,0},{16,2},{2,16},{0,18},{19,1},{17,3},{3,17},{1,19},{22,4},{20... | collective-permute-start | bytes 196616 | tf_op jit(solution)/shard_map/ppermute | solution.py:30
  66.6 5.6 %collective-permute-start.24 = (bf16[128,256]{1,0:T(8,128)(2,1)S(1)}, bf16[128,256]{1,0:T(8,128)(2,1)S(1)}, u32[]{:S(2)}, u32[]{:S(2)}) collective-permute-start(bf16[128,256]{1,0:T(8,128)(2,1)S(1)} %get-tuple-element.93), channel_id=1, source_target_pairs={{20,0},{16,4},{28,8},{24,12},{4,16},{0,20},{12,24},{8,28},{21,1},{... | collective-permute-start | bytes 196616 | tf_op jit(solution)/shard_map/ppermute | solution.py:30
  69.5 6.1 %collective-permute-start.25 = (bf16[128,256]{1,0:T(8,128)(2,1)S(1)}, bf16[128,256]{1,0:T(8,128)(2,1)S(1)}, u32[]{:S(2)}, u32[]{:S(2)}) collective-permute-start(bf16[128,256]{1,0:T(8,128)(2,1)S(1)} %get-tuple-element.94), channel_id=1, source_target_pairs={{22,0},{20,2},{18,4},{16,6},{30,8},{28,10},{26,12},{24,14},{6,16},... | collective-permute-start | bytes 196616 | tf_op jit(solution)/shard_map/ppermute | solution.py:30

commit v4 on v3

--- a/solution.py
+++ b/solution.py
@@ -34,13 +34,14 @@
     return jax.ShapeDtypeStruct(dims, dtype)
 
 
-def call(kernel, outs, args, scratch=(), flops=0):
+def call(kernel, outs, args, scratch=(), fetched=0):
     touched = sum(int(np.prod(x.shape)) * x.dtype.itemsize for x in (*args, *outs))
-    kept = sum(int(np.prod(x.shape)) * 4 for x in scratch)
+    kept = sum(int(np.prod(x.shape)) * 4 for x in scratch if hasattr(x, "shape"))
+    args = [pltpu.with_memory_space_constraint(x, pltpu.HBM) if i < fetched else x for i, x in enumerate(args)]
     return pl.pallas_call(
         kernel,
         out_shape=outs,
-        in_specs=[pl.BlockSpec(memory_space=pltpu.VMEM)] * len(args),
+        in_specs=[pl.BlockSpec(memory_space=pltpu.HBM if i < fetched else pltpu.VMEM) for i in range(len(args))],
         out_specs=[pl.BlockSpec(memory_space=pltpu.VMEM)] * len(outs),
         scratch_shapes=list(scratch),
         compiler_params=pltpu.CompilerParams(vmem_limit_bytes=touched + kept + (10 << 20)),
@@ -52,18 +53,41 @@
     return pl.ds(pl.multiple_of(index * size, size), size)
 
 
-def message_kernel(keys, values, rates, queries, stream, pair, *messages):
+def fetch(pairs, sems):
+    copies = [pltpu.make_async_copy(src, dst, sems.at[i]) for i, (src, dst) in enumerate(pairs)]
+    for c in copies:
+        c.start()
+    return copies
+
+
+def message_kernel(keys, values, rates, *refs):
     n, dh = keys.shape
+    n_far = 2 if len(refs) > 4 else 0
+    far, (pair, *messages) = refs[:n_far], refs[n_far:]
+    *messages, v, rate_row, sems = messages
     me = lax.axis_index("rep")
-    rate = jnp.broadcast_to(rates[...], (128, n)).T
-    pair[:, :dh] = keys[...]
+    pairs = [(keys, pair.at[:, :dh]), (values, v), (rates, rate_row)]
+    if n_far:
+        share, full, *messages = messages
+        q, s = messages
+        pairs += [(far[0], q), (far[1], s)]
+    copies = fetch(pairs, sems)
+    for c in copies:
+        c.wait()
+    rate = jnp.broadcast_to(rate_row[...], (128, n)).T
     for c in range(0, dh, 128):
-        pair[:, dh + c : dh + c + 128] = (values[:, c : c + 128].astype(F32) * rate).astype(BF)
-    if messages:
-        share, ask = messages
-        share[...] = pair[window(me, share.shape[0]), :]
-        ask[:, :dh] = queries[...]
-        ask[:, dh:] = stream[:, window(me, ask.shape[1] - dh)]
+        pair[:, dh + c : dh + c + 128] = (v[:, c : c + 128].astype(F32) * rate).astype(BF)
+    if n_far:
+        rows = share.shape[0]
+        wide = dh // 2
+        part = pair[window(me, rows), :]
+        share[...] = part
+        full[:, : 2 * dh] = part
+        for i in range(n // rows):
+            at = 2 * dh + i * (dh + wide)
+            there = slice(i * rows, (i + 1) * rows)
+            full[:, at : at + dh] = q[there, :]
+            full[:, at + dh : at + dh + wide] = s[there, window(me, wide)]
 
 
 def pack_kernel(up, down, same, other):
@@ -106,20 +130,27 @@
         u1[:, js], u3[:, js], u2[js, :] = x1, x3, x2
 
 
-def fast_kernel(n_pieces, n_ask, *refs):
+def asked_part(message, dh, wide, i):
+    at = 2 * dh + i * (dh + wide)
+    return message[:, at : at + dh], message[:, at + dh : at + dh + wide]
+
+
+def fast_kernel(n_pieces, near, *refs):
     pieces, refs = refs[:n_pieces], refs[n_pieces:]
-    asks, refs = refs[:n_ask], refs[n_ask:]
-    b1, b3, b2, u1, u3, u2, sq13, sq2, own_out, own_sq, send, ks, es, hp = refs
+    q, b1, b3, b2, u1, u3, u2, sq13, sq2, own_out, own_sq, send, ks, es, hp = refs
     dh, hidden = b1.shape
+    wide = own_out.shape[1]
     at = 0
     for p in pieces:
         n = p.shape[0]
         ks[at : at + n, :] = p[:, :dh]
-        es[at : at + n, :] = p[:, dh:]
+        es[at : at + n, :] = p[:, dh : 2 * dh]
         at += n
     tokens, step, block = at, min(at, 512), min(hidden, 256)
-    asked = [q[:, :dh] for q in asks]
-    asked = asked[0] if n_ask == 1 else jnp.concatenate(asked, axis=0)
+    asked = q[...]
+    if near > 1:
+        times = q.shape[0] // pieces[0].shape[0]
+        asked = jnp.concatenate([asked, *[asked_part(pieces[0], dh, wide, i)[0] for i in range(times)]], axis=0)
     new_sq = jnp.zeros((1, dh), F32)
     for j in range(0, hidden, block):
         js = slice(j, j + block)
@@ -140,8 +171,7 @@
         qc = dot(asked, normed(sq13[8:9, js], sums[1]))
         part = dot((qa * jax.nn.sigmoid(qa) * qc).astype(BF), sums[2].astype(BF))
         hp[...] = part if j == 0 else hp[...] + part
-    me, wide = lax.axis_index("rep"), own_out.shape[1]
-    n = own_out.shape[0]
+    me, n = lax.axis_index("rep"), own_out.shape[0]
     own_out[...] = hp[:, window(me, wide)]
     send[:n, :] = hp[:, window(1 - me, wide)].astype(BF)
     row = lax.broadcasted_iota(jnp.int32, (8, dh), 0)
@@ -159,13 +189,15 @@
     tail = got[rows:, :].astype(F32)
     sq = own_sq[...] + tail[:8] + tail[8:]
     scale = jnp.sqrt(sq[0:1]) * lax.rsqrt(sq[1:2] + 1e-06)
-    for z in range(rows // n):
-        part = slice(z * n, (z + 1) * n)
-        base = stream[:, window(lax.axis_index("rep"), wide)] if z == 0 else asks[0][:, asks[0].shape[1] - wide :]
-        y = base.astype(F32) + (own[part, :] + got[part, :].astype(F32)) * scale
-        low[part, :] = y.astype(BF)
-        if z == 0:
-            mixed[...] = y
+    dh = stream.shape[1]
+    y = (own[...] + got[:rows, :].astype(F32)) * scale
+    mixed[...] = y[:n] + stream[:, window(lax.axis_index("rep"), wide)].astype(F32)
+    low[:n, :] = mixed[...].astype(BF)
+    if asks:
+        rest = asks[0].shape[0]
+        for i in range(n // rest):
+            part = slice(n + i * rest, n + (i + 1) * rest)
+            low[part, :] = (y[part] + asked_part(asks[0], dh, wide, i)[1].astype(F32)).astype(BF)
     g = jnp.broadcast_to(gain[:, window(lax.axis_index("rep"), wide)], (16, wide))
     row = lax.broadcasted_iota(jnp.int32, (16, wide), 0)
     top = g.astype(BF).astype(F32)
@@ -242,34 +274,19 @@
     units = mlp_up.shape[1] // groups // near
     barrier = lax.optimization_barrier
 
-    messages = [shape((n_key // reps, 2 * dh), BF), shape((n, dh + wide), BF)] if paired else []
+    rows = n_key // reps
+    messages, far, fetches = [], [], [pltpu.VMEM((n_key, dh), BF), pltpu.VMEM((1, n_key), F32)]
+    if paired:
+        messages = [shape((rows, 2 * dh), BF), shape((rows, 2 * dh + (n // rows) * (dh + wide)), BF)]
+        far = [queries, stream]
+        fetches = [pltpu.VMEM((n, dh), BF), pltpu.VMEM((n, dh), BF), *fetches]
     pair, *messages = call(
         message_kernel,
         [shape((n_key, 2 * dh), BF), *messages],
-        [keys, values, rates.reshape(1, n_key), queries, stream],
-    )
-    asks = []
-    if paired:
-        share, ask = messages
-        others = [moved(share, tok=s) for s in (1, 2, 3)]
-        same, other = call(
-            pack_kernel, [shape((mlp_up.shape[0] + units, units), BF)] * 2, [mlp_up, mlp_down]
-        )
-        first, ask, other_1 = barrier((others[0], ask, other))
-        asks = [moved(ask, tok=1)]
-        w_first = moved(other_1, tok=1)
-        far, same_2 = barrier((others[1:], same))
-        w_second = moved(same_2, tok=2)
-        w_third = moved(barrier((other, w_second))[0], tok=3)
-        tokens = [first, *far]
-        tokens = tokens + [moved(x, rep=1) for x in tokens]
-    else:
-        me_g = lax.axis_index("groups")
-        up_own = lax.dynamic_slice_in_dim(mlp_up, me_g * units, units, 1)
-        down_own = lax.dynamic_slice_in_dim(mlp_down, me_g * units, units, 0)
-        tokens = [lax.all_gather(pair, "tok", axis=0, tiled=True)]
-        up_blocks = [lax.all_gather(up_own, "tok", axis=0, tiled=True)]
-        down_blocks = [lax.all_gather(down_own, "tok", axis=1, tiled=True)]
+        [keys, values, rates.reshape(1, n_key), *far],
+        [*fetches, pltpu.SemaphoreType.DMA((5,))],
+        fetched=3 + len(far),
+    )
     square = [shape((dh, hidden), F32), shape((dh, hidden), F32), shape((hidden, dh), F32)]
     prepared = call(
         functools.partial(own_kernel, paired),
@@ -280,16 +297,37 @@
             shape((8, dh), F32),
         ],
         [pair, fw_one[0], fw_three[0], fw_two[0]],
-        flops=12 * n_key * dh * hidden,
-    )
+    )
+    asks = []
+    if paired:
+        share, full = messages
+        others = [moved(full, tok=1), moved(share, tok=2), moved(share, tok=3)]
+        same, other = call(
+            pack_kernel, [shape((mlp_up.shape[0] + units, units), BF)] * 2, [mlp_up, mlp_down]
+        )
+        same_2, _ = barrier((same, prepared))
+        w_second = moved(same_2, tok=2)
+        others, other_1, prepared = barrier((others, other, prepared))
+        first = others[0]
+        w_first = moved(other_1, tok=1)
+        tokens = [first, *others[1:]]
+        tokens = tokens + [moved(x, rep=1) for x in (first[:, : 2 * dh], *others[1:])]
+        asks = [first]
+        w_third = moved(barrier((other, w_second))[0], tok=3)
+    else:
+        me_g = lax.axis_index("groups")
+        up_own = lax.dynamic_slice_in_dim(mlp_up, me_g * units, units, 1)
+        down_own = lax.dynamic_slice_in_dim(mlp_down, me_g * units, units, 0)
+        tokens = [lax.all_gather(pair, "tok", axis=0, tiled=True)]
+        up_blocks = [lax.all_gather(up_own, "tok", axis=0, tiled=True)]
+        down_blocks = [lax.all_gather(down_own, "tok", axis=1, tiled=True)]
     n_all = sum(x.shape[0] for x in tokens)
-    tokens, asks = barrier((tokens, asks))
+    tokens = barrier(tokens)
     own, own_sq, send = call(
         functools.partial(fast_kernel, len(tokens), near),
         [shape((near * n, wide), F32), shape((8, wide), F32), shape((near * n + 16, wide), BF)],
-        [*tokens, queries, *asks, *prepared],
+        [*tokens, queries, *prepared],
         [pltpu.VMEM((n_all, dh), BF), pltpu.VMEM((n_all, dh), BF), pltpu.VMEM((near * n, dh), F32)],
-        flops=12 * n_all * dh * hidden + 6 * near * n * dh * hidden,
     )
     got = moved(send, rep=1)
     if paired:
@@ -312,14 +350,12 @@
         [shape((rows, units), BF)],
         [*pieces, *up_blocks],
         [pltpu.VMEM((rows, model), BF)],
-        flops=2 * rows * units * model,
     )
     own, send = call(
         functools.partial(down_kernel, len(down_blocks)),
         [shape((rows, n_head * wide), F32), shape((rows, n_head * wide), BF)],
         [act, *down_blocks],
         [pltpu.VMEM((rows, model), F32)],
-        flops=2 * rows * units * model,
     )
     got = moved(send, rep=1)
     moves = list(itertools.product(range(groups), range(near), range(n_head)))

time: 76.7 us -> 71.4 us (0.931)
  starting transfers between devices: 34 us -> 26.7 us
  waiting for transfers between devices: 24.8 us -> 31 us
  local copies, waits for them, and re-layouts: 9.58 us -> 4.19 us
  Pallas kernels: 6.38 us -> 7.68 us
    ppermute x26 -> x25, starting transfers between devices: 34 us -> 26.7 us  [moved(): return lax.ppermute(x, tuple(axes), pairs)]
    ppermute x26 -> x25, waiting for transfers between devices: 24.8 us -> 31 us  [moved(): return lax.ppermute(x, tuple(axes), pairs)]
    unnamed x26 -> x16, local copies, waits for them, and re-layouts: 9.58 us -> 4.18 us
    pallas_call x8, Pallas kernels: 6.38 us -> 7.68 us  [call(): pl.pallas_call(kernel, out_shape=outs, in_specs=[pl.BlockSpec(memory_spac...]
  transfers between devices with their start and end apart: 26 -> 25, of which waited for: 11 -> 11; matrix products, arithmetic and copies ran while one was open for 0% -> 0% of each run, Pallas kernels for 6% -> 6%
where the time goes in v4:
time: 71.4 us; the launch traced here: 71.2 us
  waiting for transfers between devices  31 us (43%)
  starting transfers between devices  26.7 us (37%)
  Pallas kernels  7.68 us (11%)
  local copies, waits for them, and re-layouts  4.19 us (6%)
  between operations  0.8 us (1%)
  other arithmetic  0.72 us (1%)
    ppermute x25, waiting for transfers between devices, moved(): return lax.ppermute(x, tuple(axes), pairs)  31 us
    ppermute x25, starting transfers between devices, moved(): return lax.ppermute(x, tuple(axes), pairs)  26.7 us
    pallas_call x8, Pallas kernels, call(): pl.pallas_call(kernel, out_shape=outs, in_specs=[pl.BlockSpec(memory_spac...  7.68 us
    unnamed x16, local copies, waits for them, and re-layouts  4.18 us
  transfers between devices with their start and end apart: 25, of which 11 were waited for; matrix products, arithmetic and copies ran while one was open for 0% of the time, Pallas kernels for 6%

profile of v4, /device:TPU:0, one launch (start us, length us, event | category | flops | bytes accessed | tf_op | source)
XLA Modules:
  0.0 71.2 jit_solution(3151428489281787471)
XLA Ops:
  0.0 1.4 %shard_map.118 = (bf16[128,1024]{1,0:T(8,128)(2,1)S(1)}, bf16[64,1024]{1,0:T(8,128)(2,1)S(1)}, bf16[64,2560]{1,0:T(8,128)(2,1)S(1)}) custom-call(bf16[128,512]{1,0:T(8,128)(2,1)} %keys.1, bf16[128,512]{1,0:T(8,128)(2,1)} %values.1, f32[1,128]{1,0:T(1,128)} %bitcast.11, bf16[128,512]{1,0:T(8,128)(2,1)} %refs_6_.1, bf16[128,512]{1,0:T(8,128)(2,1)} %stream.1), custom_call_target="tpu_custom_call" | custom-call | flops 1 | bytes 1 | tf_op jit(solution)/shard_map/pallas_call | solution.py:41
  1.4 3.1 %collective-permute-start = (bf16[64,2560]{1,0:T(8,128)(2,1)S(1)}, bf16[64,2560]{1,0:T(8,128)(2,1)S(1)}, u32[]{:S(2)}, u32[]{:S(2)}) collective-permute-start(bf16[64,2560]{1,0:T(8,128)(2,1)S(1)} %get-tuple-element.56), channel_id=1, source_target_pairs={{4,0},{0,4},{12,8},{8,12},{5,1},{1,5},{13,9},{9,13},{6,2},{2,6},{1... | collective-permute-start | bytes 983048 | tf_op jit(solution)/shard_map/ppermute | solution.py:30
  4.5 2.6 %collective-permute-start.1 = (bf16[64,1024]{1,0:T(8,128)(2,1)S(1)}, bf16[64,1024]{1,0:T(8,128)(2,1)S(1)}, u32[]{:S(2)}, u32[]{:S(2)}) collective-permute-start(bf16[64,1024]{1,0:T(8,128)(2,1)S(1)} %get-tuple-element.57), channel_id=1, source_target_pairs={{8,0},{12,4},{0,8},{4,12},{9,1},{13,5},{1,9},{5,13},{10,2},{14,6},... | collective-permute-start | bytes 393224 | tf_op jit(solution)/shard_map/ppermute | solution.py:30
  7.1 0.0 collective-permute-start.2
  7.1 0.0 copy-done.4
  7.1 1.0 %copy-done.5 = bf16[1024,256]{1,0:T(8,128)(2,1)S(1)} copy-done((bf16[1024,256]{1,0:T(8,128)(2,1)S(1)}, bf16[1024,256]{1,0:T(8,128)(2,1)}, u32[]{:S(2)}) %copy-start.5) | copy-done | bytes 524312
  8.2 0.0 copy-start.1
  8.2 1.2 %copy-done.1 = f32[1,512,512]{2,1,0:T(8,128)S(1)} copy-done((f32[1,512,512]{2,1,0:T(8,128)S(1)}, f32[1,512,512]{2,1,0:T(8,128)}, u32[]{:S(2)}) %copy-start.1) | copy-done | bytes 1048600
  9.4 1.2 %copy-done.2 = f32[1,512,512]{2,1,0:T(8,128)S(1)} copy-done((f32[1,512,512]{2,1,0:T(8,128)S(1)}, f32[1,512,512]{2,1,0:T(8,128)}, u32[]{:S(2)}) %copy-start.2) | copy-done | bytes 1048600
  10.6 1.4 %shard_map.120 = (bf16[512,512]{1,0:T(8,128)(2,1)S(1)}, bf16[512,512]{1,0:T(8,128)(2,1)S(1)}, bf16[512,512]{1,0:T(8,128)(2,1)S(1)}, f32[512,512]{1,0:T(8,128)S(1...) custom-call(bf16[128,1024]{1,0:T(8,128)(2,1)S(1)} %get-tuple-element.59.pair,, ...), custom_call_target="tpu_custom_call" | custom-call | flops 1 | bytes 1 | tf_op jit(solution)/shard_map/pallas_call | solution.py:41
  12.1 3.4 %collective-permute-done.1.refs_1_ = bf16[64,1024]{1,0:T(8,128)(2,1)S(1)} collective-permute-done((bf16[64,1024]{1,0:T(8,128)(2,1)S(1)}, bf16[64,1024]{1,0:T(8,128)(2,1)S(1)}, u32[]{:S(2)}, u32[]{:S(2)}) %collective-permute-start.1) | collective-permute-done | bytes 131104 | tf_op jit(solution)/shard_map/ppermute | solution.py:30
  15.4 4.6 %collective-permute-done.2.refs_2_ = bf16[64,1024]{1,0:T(8,128)(2,1)S(1)} collective-permute-done((bf16[64,1024]{1,0:T(8,128)(2,1)S(1)}, bf16[64,1024]{1,0:T(8,128)(2,1)S(1)}, u32[]{:S(2)}, u32[]{:S(2)}) %collective-permute-start.2) | collective-permute-done | bytes 131104 | tf_op jit(solution)/shard_map/ppermute | solution.py:30
  20.0 0.0 collective-permute-done.refs_0_
  20.0 0.1 collective-permute-start.3
  20.1 0.5 collective-permute-start.4
  20.6 0.1 collective-permute-start.5
  20.7 0.0 collective-permute-start.8
  20.7 2.1 %collective-permute-start.7 = (bf16[512,256]{1,0:T(8,128)(2,1)S(1)}, bf16[512,256]{1,0:T(8,128)(2,1)S(1)}, u32[]{:S(2)}, u32[]{:S(2)}) collective-permute-start(bf16[512,256]{1,0:T(8,128)(2,1)S(1)} %get-tuple-element.95), channel_id=1, source_target_pairs={{4,0},{0,4},{12,8},{8,12},{5,1},{1,5},{13,9},{9,13},{6,2},{2,6},{1... | collective-permute-start | bytes 786440 | tf_op jit(solution)/shard_map/ppermute | solution.py:30
  22.8 0.0 collective-permute-done.3.refs_3_
  22.8 0.0 collective-permute-done.4.refs_4_
  22.8 0.0 collective-permute-done.5.refs_5_
  22.9 3.0 %shard_map.121 = (f32[256,256]{1,0:T(8,128)S(1)}, f32[8,256]{1,0:T(8,128)S(1)}, bf16[272,256]{1,0:T(8,128)(2,1)S(1)}) custom-call(bf16[64,2560]{1,0:T(8,128)(2,1)S(1)} %collective-permute-done.refs_0_, bf16[64,1024]{1,0:T(8,128)(2,1)S(1)} %collective-permute-done.1.refs_1_, bf16[64,1024]{1,0:T(8,128)(2,1)S(1)} %collective-permute-done.2.refs_2_, ...), custom_call_target="tpu_custom_call" | custom-call | flops 1 | bytes 1 | tf_op jit(solution)/shard_map/pallas_call | solution.py:41
  25.9 0.1 collective-permute-start.6
  26.0 8.9 %collective-permute-done.8.refs_10_.refs_2_ = bf16[512,256]{1,0:T(8,128)(2,1)S(1)} collective-permute-done((bf16[512,256]{1,0:T(8,128)(2,1)S(1)}, bf16[512,256]{1,0:T(8,128)(2,1)S(1)}, u32[]{:S(2)}, u32[]{:S(2)}) %collective-permute-start.8) | collective-permute-done | bytes 262176 | tf_op jit(solution)/shard_map/ppermute | solution.py:30
  34.9 0.2 collective-permute-done.7.refs_9_.refs_1_
  35.1 0.0 collective-permute-done.6.got
  35.1 0.7 copy-done.7
  35.8 0.1 shard_map.122
  35.9 1.6 %collective-permute-start.10 = (bf16[272,256]{1,0:T(8,128)(2,1)S(1)}, bf16[272,256]{1,0:T(8,128)(2,1)S(1)}, u32[]{:S(2)}, u32[]{:S(2)}) collective-permute-start(bf16[272,256]{1,0:T(8,128)(2,1)S(1)} %get-tuple-element.92.refs_0_), channel_id=1, source_target_pairs={{2,0},{0,2},{3,1},{1,3},{6,4},{4,6},{7,5},{5,7},{10,8},{8,10},{11,... | collective-permute-start | bytes 417800 | tf_op jit(solution)/shard_map/ppermute | solution.py:30
  37.4 1.5 %collective-permute-start.12 = (bf16[272,256]{1,0:T(8,128)(2,1)S(1)}, bf16[272,256]{1,0:T(8,128)(2,1)S(1)}, u32[]{:S(2)}, u32[]{:S(2)}) collective-permute-start(bf16[272,256]{1,0:T(8,128)(2,1)S(1)} %get-tuple-element.92.refs_0_), channel_id=1, source_target_pairs={{16,0},{0,16},{17,1},{1,17},{18,2},{2,18},{19,3},{3,19},{20,4},{4,... | collective-permute-start | bytes 417800 | tf_op jit(solution)/shard_map/ppermute | solution.py:30
  38.9 0.5 collective-permute-start.14
  39.4 2.3 %collective-permute-start.16 = (bf16[512,256]{1,0:T(8,128)(2,1)S(1)}, bf16[512,256]{1,0:T(8,128)(2,1)S(1)}, u32[]{:S(2)}, u32[]{:S(2)}) collective-permute-start(bf16[512,256]{1,0:T(8,128)(2,1)S(1)} %get-tuple-element.95), channel_id=1, source_target_pairs={{12,0},{8,4},{4,8},{0,12},{13,1},{9,5},{5,9},{1,13},{14,2},{10,6},... | collective-permute-start | bytes 786440 | tf_op jit(solution)/shard_map/ppermute | solution.py:30
  41.7 0.0 collective-permute-start.9
  41.7 0.2 collective-permute-done.10.refs_2_
  41.9 0.3 collective-permute-start.11
  42.2 3.3 %collective-permute-done.12.refs_4_ = bf16[272,256]{1,0:T(8,128)(2,1)S(1)} collective-permute-done((bf16[272,256]{1,0:T(8,128)(2,1)S(1)}, bf16[272,256]{1,0:T(8,128)(2,1)S(1)}, u32[]{:S(2)}, u32[]{:S(2)}) %collective-permute-start.12) | collective-permute-done | bytes 139296 | tf_op jit(solution)/shard_map/ppermute | solution.py:30
  45.5 0.0 collective-permute-start.13
  45.5 0.0 collective-permute-done.14.refs_6_
  45.5 0.5 collective-permute-start.15
  46.0 2.5 %collective-permute-done.16.refs_11_.refs_3_ = bf16[512,256]{1,0:T(8,128)(2,1)S(1)} collective-permute-done((bf16[512,256]{1,0:T(8,128)(2,1)S(1)}, bf16[512,256]{1,0:T(8,128)(2,1)S(1)}, u32[]{:S(2)}, u32[]{:S(2)}) %collective-permute-start.16) | collective-permute-done | bytes 262176 | tf_op jit(solution)/shard_map/ppermute | solution.py:30
  48.5 0.0 collective-permute-done.9.refs_1_
  48.5 0.0 collective-permute-done.11.refs_3_
  48.5 0.0 collective-permute-done.13.refs_5_
  48.5 0.0 collective-permute-done.15.refs_7_
  48.5 0.9 %shard_map.123.h = bf16[512,256]{1,0:T(8,128)(2,1)S(1)} custom-call(bf16[272,256]{1,0:T(8,128)(2,1)S(1)} %get-tuple-element.92.refs_0_, bf16[272,256]{1,0:T(8,128)(2,1)S(1)} %collective-permute-done.9.refs_1_, bf16[272,256]{1,0:T(8,128)(2,1)S(1)} %collective-permute-done.10.refs_2_, bf16[272,256]{1,0:T(8,128)(2,1)S(1)} %collective-permute-done.11.refs_3_, ...), custom_call_target="tpu_custom_call" | custom-call | flops 1 | bytes 1 | tf_op jit(solution)/shard_map/pallas_call | solution.py:41
  49.5 0.7 shard_map.124
  50.2 0.1 collective-permute-start.17
  50.2 1.9 %collective-permute-done.17.got = bf16[512,512]{1,0:T(8,128)(2,1)S(1)} collective-permute-done((bf16[512,512]{1,0:T(8,128)(2,1)S(1)}, bf16[512,512]{1,0:T(8,128)(2,1)S(1)}, u32[]{:S(2)}, u32[]{:S(2)}) %collective-permute-start.17) | collective-permute-done | bytes 524320 | tf_op jit(solution)/shard_map/ppermute | solution.py:30
  52.1 0.1 shard_map.125
  52.2 1.6 %collective-permute-start.18 = (bf16[128,256]{1,0:T(8,128)(2,1)S(1)}, bf16[128,256]{1,0:T(8,128)(2,1)S(1)}, u32[]{:S(2)}, u32[]{:S(2)}) collective-permute-start(bf16[128,256]{1,0:T(8,128)(2,1)S(1)} %get-tuple-element.100), channel_id=1, source_target_pairs={{2,0},{0,2},{3,1},{1,3},{6,4},{4,6},{7,5},{5,7},{10,8},{8,10},{11,... | collective-permute-start | bytes 196616 | tf_op jit(solution)/shard_map/ppermute | solution.py:30
  53.8 4.0 %collective-permute-start.19 = (bf16[128,256]{1,0:T(8,128)(2,1)S(1)}, bf16[128,256]{1,0:T(8,128)(2,1)S(1)}, u32[]{:S(2)}, u32[]{:S(2)}) collective-permute-start(bf16[128,256]{1,0:T(8,128)(2,1)S(1)} %get-tuple-element.101), channel_id=1, source_target_pairs={{4,0},{0,4},{12,8},{8,12},{5,1},{1,5},{13,9},{9,13},{6,2},{2,6},{1... | collective-permute-start | bytes 196616 | tf_op jit(solution)/shard_map/ppermute | solution.py:30
  58.4 0.1 collective-permute-start.20
  58.5 1.6 %collective-permute-start.21 = (bf16[128,256]{1,0:T(8,128)(2,1)S(1)}, bf16[128,256]{1,0:T(8,128)(2,1)S(1)}, u32[]{:S(2)}, u32[]{:S(2)}) collective-permute-start(bf16[128,256]{1,0:T(8,128)(2,1)S(1)} %get-tuple-element.103), channel_id=1, source_target_pairs={{16,0},{0,16},{17,1},{1,17},{18,2},{2,18},{19,3},{3,19},{20,4},{4,... | collective-permute-start | bytes 196616 | tf_op jit(solution)/shard_map/ppermute | solution.py:30
  60.1 1.3 %collective-permute-start.22 = (bf16[128,256]{1,0:T(8,128)(2,1)S(1)}, bf16[128,256]{1,0:T(8,128)(2,1)S(1)}, u32[]{:S(2)}, u32[]{:S(2)}) collective-permute-start(bf16[128,256]{1,0:T(8,128)(2,1)S(1)} %get-tuple-element.104), channel_id=1, source_target_pairs={{18,0},{16,2},{2,16},{0,18},{19,1},{17,3},{3,17},{1,19},{22,4},{20... | collective-permute-start | bytes 196616 | tf_op jit(solution)/shard_map/ppermute | solution.py:30
  61.4 0.0 collective-permute-done.18
  61.4 3.0 %collective-permute-start.23 = (bf16[128,256]{1,0:T(8,128)(2,1)S(1)}, bf16[128,256]{1,0:T(8,128)(2,1)S(1)}, u32[]{:S(2)}, u32[]{:S(2)}) collective-permute-start(bf16[128,256]{1,0:T(8,128)(2,1)S(1)} %get-tuple-element.105), channel_id=1, source_target_pairs={{20,0},{16,4},{28,8},{24,12},{4,16},{0,20},{12,24},{8,28},{21,1},{... | collective-permute-start | bytes 196616 | tf_op jit(solution)/shard_map/ppermute | solution.py:30
  64.4 0.0 collective-permute-done.19
  64.4 0.0 collective-permute-start.24
  64.4 0.0 collective-permute-done.20
  64.4 0.0 collective-permute-done.21
  64.4 1.1 %collective-permute-done.22 = bf16[128,256]{1,0:T(8,128)(2,1)S(1)} collective-permute-done((bf16[128,256]{1,0:T(8,128)(2,1)S(1)}, bf16[128,256]{1,0:T(8,128)(2,1)S(1)}, u32[]{:S(2)}, u32[]{:S(2)}) %collective-permute-start.22) | collective-permute-done | bytes 65568 | tf_op jit(solution)/shard_map/ppermute | solution.py:30
  65.6 1.5 %collective-permute-done.23 = bf16[128,256]{1,0:T(8,128)(2,1)S(1)} collective-permute-done((bf16[128,256]{1,0:T(8,128)(2,1)S(1)}, bf16[128,256]{1,0:T(8,128)(2,1)S(1)}, u32[]{:S(2)}, u32[]{:S(2)}) %collective-permute-start.23) | collective-permute-done | bytes 65568 | tf_op jit(solution)/shard_map/ppermute | solution.py:30
  67.0 3.4 %collective-permute-done.24 = bf16[128,256]{1,0:T(8,128)(2,1)S(1)} collective-permute-done((bf16[128,256]{1,0:T(8,128)(2,1)S(1)}, bf16[128,256]{1,0:T(8,128)(2,1)S(1)}, u32[]{:S(2)}, u32[]{:S(2)}) %collective-permute-start.24) | collective-permute-done | bytes 65568 | tf_op jit(solution)/shard_map/ppermute | solution.py:30
  70.4 0.7 %select_convert_fusion = bf16[128,256]{1,0:T(8,128)(2,1)} fusion(bf16[128,256]{1,0:T(8,128)(2,1)S(1)} %collective-permute-done.24, bf16[128,256]{1,0:T(8,128)(2,1)S(1)} %collective-permute-done.23, bf16[128,256]{1,0:T(8,128)(2,1)S(1)} %collective-permute-done.22, bf16[128,256]{1,0:T(8,128)(2,1)S(1)} %collective-permute-done.21, ...), kind=kLoop, calls=%fused_computation | loop fusion | flops 524288 | bytes 655488 | tf_op jit(solution)/shard_map/convert_element_type | solution.py:370
  (13 shorter events, 0.1 us)
Async XLA Ops:
  0.0 7.1 %copy-start.4 = (bf16[256,1024]{1,0:T(8,128)(2,1)S(1)}, bf16[256,1024]{1,0:T(8,128)(2,1)}, u32[]{:S(2)}) copy-start(bf16[256,1024]{1,0:T(8,128)(2,1)} %up.1) | copy-start | bytes 1572868
  0.0 8.2 %copy-start = (f32[1,512,512]{2,1,0:T(8,128)S(1)}, f32[1,512,512]{2,1,0:T(8,128)}, u32[]{:S(2)}) copy-start(f32[1,512,512]{2,1,0:T(8,128)} %param.19) | copy-start | bytes 3145732
  1.4 18.6 %collective-permute-start = (bf16[64,2560]{1,0:T(8,128)(2,1)S(1)}, bf16[64,2560]{1,0:T(8,128)(2,1)S(1)}, u32[]{:S(2)}, u32[]{:S(2)}) collective-permute-start(bf16[64,2560]{1,0:T(8,128)(2,1)S(1)} %get-tuple-element.56), channel_id=1, source_target_pairs={{4,0},{0,4},{12,8},{8,12},{5,1},{1,5},{13,9},{9,13},{6,2},{2,6},{1... | collective-permute-start | bytes 983048 | tf_op jit(solution)/shard_map/ppermute | solution.py:30
  4.5 10.9 %collective-permute-start.1 = (bf16[64,1024]{1,0:T(8,128)(2,1)S(1)}, bf16[64,1024]{1,0:T(8,128)(2,1)S(1)}, u32[]{:S(2)}, u32[]{:S(2)}) collective-permute-start(bf16[64,1024]{1,0:T(8,128)(2,1)S(1)} %get-tuple-element.57), channel_id=1, source_target_pairs={{8,0},{12,4},{0,8},{4,12},{9,1},{13,5},{1,9},{5,13},{10,2},{14,6},... | collective-permute-start | bytes 393224 | tf_op jit(solution)/shard_map/ppermute | solution.py:30
  7.1 12.9 %collective-permute-start.2 = (bf16[64,1024]{1,0:T(8,128)(2,1)S(1)}, bf16[64,1024]{1,0:T(8,128)(2,1)S(1)}, u32[]{:S(2)}, u32[]{:S(2)}) collective-permute-start(bf16[64,1024]{1,0:T(8,128)(2,1)S(1)} %get-tuple-element.57), channel_id=1, source_target_pairs={{12,0},{8,4},{4,8},{0,12},{13,1},{9,5},{5,9},{1,13},{14,2},{10,6},... | collective-permute-start | bytes 393224 | tf_op jit(solution)/shard_map/ppermute | solution.py:30
  7.1 1.0 %copy-start.5 = (bf16[1024,256]{1,0:T(8,128)(2,1)S(1)}, bf16[1024,256]{1,0:T(8,128)(2,1)}, u32[]{:S(2)}) copy-start(bf16[1024,256]{1,0:T(8,128)(2,1)} %down.1) | copy-start | bytes 1572868
  8.2 1.2 %copy-start.1 = (f32[1,512,512]{2,1,0:T(8,128)S(1)}, f32[1,512,512]{2,1,0:T(8,128)}, u32[]{:S(2)}) copy-start(f32[1,512,512]{2,1,0:T(8,128)} %param.20) | copy-start | bytes 3145732
  9.4 1.2 %copy-start.2 = (f32[1,512,512]{2,1,0:T(8,128)S(1)}, f32[1,512,512]{2,1,0:T(8,128)}, u32[]{:S(2)}) copy-start(f32[1,512,512]{2,1,0:T(8,128)} %param.21) | copy-start | bytes 3145732
  20.0 2.8 %copy-start.3 = (bf16[128,512]{1,0:T(8,128)(2,1)S(1)}, bf16[128,512]{1,0:T(8,128)(2,1)}, u32[]{:S(2)}) copy-start(bf16[128,512]{1,0:T(8,128)(2,1)} %refs_6_.1) | copy-start | bytes 393220
  20.0 2.8 %collective-permute-start.3 = (bf16[64,1024]{1,0:T(8,128)(2,1)S(1)}, bf16[64,1024]{1,0:T(8,128)(2,1)S(1)}, u32[]{:S(2)}, u32[]{:S(2)}) collective-permute-start(bf16[64,1024]{1,0:T(8,128)(2,1)S(1)} %slice.3), channel_id=1, source_target_pairs={{1,0},{0,1},{3,2},{2,3},{5,4},{4,5},{7,6},{6,7},{9,8},{8,9},{11,10... | collective-permute-start | bytes 393224 | tf_op jit(solution)/shard_map/ppermute | solution.py:30
  20.1 2.7 %collective-permute-start.4 = (bf16[64,1024]{1,0:T(8,128)(2,1)S(1)}, bf16[64,1024]{1,0:T(8,128)(2,1)S(1)}, u32[]{:S(2)}, u32[]{:S(2)}) collective-permute-start(bf16[64,1024]{1,0:T(8,128)(2,1)S(1)} %collective-permute-done.1.refs_1_), channel_id=1, source_target_pairs={{1,0},{0,1},{3,2},{2,3},{5,4},{4,5},{7,6},{6,7},{9,8},{8,9},{11,10... | collective-permute-start | bytes 393224 | tf_op jit(solution)/shard_map/ppermute | solution.py:30
  20.6 2.2 %collective-permute-start.5 = (bf16[64,1024]{1,0:T(8,128)(2,1)S(1)}, bf16[64,1024]{1,0:T(8,128)(2,1)S(1)}, u32[]{:S(2)}, u32[]{:S(2)}) collective-permute-start(bf16[64,1024]{1,0:T(8,128)(2,1)S(1)} %collective-permute-done.2.refs_2_), channel_id=1, source_target_pairs={{1,0},{0,1},{3,2},{2,3},{5,4},{4,5},{7,6},{6,7},{9,8},{8,9},{11,10... | collective-permute-start | bytes 393224 | tf_op jit(solution)/shard_map/ppermute | solution.py:30
  20.7 14.4 %copy-start.6 = (bf16[128,512]{1,0:T(8,128)(2,1)S(1)}, bf16[128,512]{1,0:T(8,128)(2,1)}, u32[]{:S(2)}) copy-start(bf16[128,512]{1,0:T(8,128)(2,1)} %stream.1) | copy-start | bytes 393220
  20.7 14.2 %collective-permute-start.8 = (bf16[512,256]{1,0:T(8,128)(2,1)S(1)}, bf16[512,256]{1,0:T(8,128)(2,1)S(1)}, u32[]{:S(2)}, u32[]{:S(2)}) collective-permute-start(bf16[512,256]{1,0:T(8,128)(2,1)S(1)} %get-tuple-element.90.refs_8_.refs_0_), channel_id=1, source_target_pairs={{8,0},{12,4},{0,8},{4,12},{9,1},{13,5},{1,9},{5,13},{10,2},{14,6},... | collective-permute-start | bytes 786440 | tf_op jit(solution)/shard_map/ppermute | solution.py:30
  20.7 14.4 %collective-permute-start.7 = (bf16[512,256]{1,0:T(8,128)(2,1)S(1)}, bf16[512,256]{1,0:T(8,128)(2,1)S(1)}, u32[]{:S(2)}, u32[]{:S(2)}) collective-permute-start(bf16[512,256]{1,0:T(8,128)(2,1)S(1)} %get-tuple-element.95), channel_id=1, source_target_pairs={{4,0},{0,4},{12,8},{8,12},{5,1},{1,5},{13,9},{9,13},{6,2},{2,6},{1... | collective-permute-start | bytes 786440 | tf_op jit(solution)/shard_map/ppermute | solution.py:30
  25.9 9.2 %collective-permute-start.6 = (bf16[272,256]{1,0:T(8,128)(2,1)S(1)}, bf16[272,256]{1,0:T(8,128)(2,1)S(1)}, u32[]{:S(2)}, u32[]{:S(2)}) collective-permute-start(bf16[272,256]{1,0:T(8,128)(2,1)S(1)} %get-tuple-element.87), channel_id=1, source_target_pairs={{1,0},{0,1},{3,2},{2,3},{5,4},{4,5},{7,6},{6,7},{9,8},{8,9},{11,10... | collective-permute-start | bytes 417800 | tf_op jit(solution)/shard_map/ppermute | solution.py:30
  35.1 0.7 copy-start.7
  35.9 6.0 %collective-permute-start.10 = (bf16[272,256]{1,0:T(8,128)(2,1)S(1)}, bf16[272,256]{1,0:T(8,128)(2,1)S(1)}, u32[]{:S(2)}, u32[]{:S(2)}) collective-permute-start(bf16[272,256]{1,0:T(8,128)(2,1)S(1)} %get-tuple-element.92.refs_0_), channel_id=1, source_target_pairs={{2,0},{0,2},{3,1},{1,3},{6,4},{4,6},{7,5},{5,7},{10,8},{8,10},{11,... | collective-permute-start | bytes 417800 | tf_op jit(solution)/shard_map/ppermute | solution.py:30
  37.4 8.1 %collective-permute-start.12 = (bf16[272,256]{1,0:T(8,128)(2,1)S(1)}, bf16[272,256]{1,0:T(8,128)(2,1)S(1)}, u32[]{:S(2)}, u32[]{:S(2)}) collective-permute-start(bf16[272,256]{1,0:T(8,128)(2,1)S(1)} %get-tuple-element.92.refs_0_), channel_id=1, source_target_pairs={{16,0},{0,16},{17,1},{1,17},{18,2},{2,18},{19,3},{3,19},{20,4},{4,... | collective-permute-start | bytes 417800 | tf_op jit(solution)/shard_map/ppermute | solution.py:30
  38.9 6.6 %collective-permute-start.14 = (bf16[272,256]{1,0:T(8,128)(2,1)S(1)}, bf16[272,256]{1,0:T(8,128)(2,1)S(1)}, u32[]{:S(2)}, u32[]{:S(2)}) collective-permute-start(bf16[272,256]{1,0:T(8,128)(2,1)S(1)} %get-tuple-element.92.refs_0_), channel_id=1, source_target_pairs={{18,0},{16,2},{2,16},{0,18},{19,1},{17,3},{3,17},{1,19},{22,4},{20... | collective-permute-start | bytes 417800 | tf_op jit(solution)/shard_map/ppermute | solution.py:30
  39.4 9.1 %collective-permute-start.16 = (bf16[512,256]{1,0:T(8,128)(2,1)S(1)}, bf16[512,256]{1,0:T(8,128)(2,1)S(1)}, u32[]{:S(2)}, u32[]{:S(2)}) collective-permute-start(bf16[512,256]{1,0:T(8,128)(2,1)S(1)} %get-tuple-element.95), channel_id=1, source_target_pairs={{12,0},{8,4},{4,8},{0,12},{13,1},{9,5},{5,9},{1,13},{14,2},{10,6},... | collective-permute-start | bytes 786440 | tf_op jit(solution)/shard_map/ppermute | solution.py:30
  41.7 6.8 %collective-permute-start.9 = (bf16[272,256]{1,0:T(8,128)(2,1)S(1)}, bf16[272,256]{1,0:T(8,128)(2,1)S(1)}, u32[]{:S(2)}, u32[]{:S(2)}) collective-permute-start(bf16[272,256]{1,0:T(8,128)(2,1)S(1)} %get-tuple-element.92.refs_0_), channel_id=1, source_target_pairs={{1,0},{0,1},{3,2},{2,3},{5,4},{4,5},{7,6},{6,7},{9,8},{8,9},{11,10... | collective-permute-start | bytes 417800 | tf_op jit(solution)/shard_map/ppermute | solution.py:30
  41.9 6.6 %collective-permute-start.11 = (bf16[272,256]{1,0:T(8,128)(2,1)S(1)}, bf16[272,256]{1,0:T(8,128)(2,1)S(1)}, u32[]{:S(2)}, u32[]{:S(2)}) collective-permute-start(bf16[272,256]{1,0:T(8,128)(2,1)S(1)} %collective-permute-done.10.refs_2_), channel_id=1, source_target_pairs={{1,0},{0,1},{3,2},{2,3},{5,4},{4,5},{7,6},{6,7},{9,8},{8,9},{11,10... | collective-permute-start | bytes 417800 | tf_op jit(solution)/shard_map/ppermute | solution.py:30
  45.5 3.0 %collective-permute-start.13 = (bf16[272,256]{1,0:T(8,128)(2,1)S(1)}, bf16[272,256]{1,0:T(8,128)(2,1)S(1)}, u32[]{:S(2)}, u32[]{:S(2)}) collective-permute-start(bf16[272,256]{1,0:T(8,128)(2,1)S(1)} %collective-permute-done.12.refs_4_), channel_id=1, source_target_pairs={{1,0},{0,1},{3,2},{2,3},{5,4},{4,5},{7,6},{6,7},{9,8},{8,9},{11,10... | collective-permute-start | bytes 417800 | tf_op jit(solution)/shard_map/ppermute | solution.py:30
  45.5 3.0 %collective-permute-start.15 = (bf16[272,256]{1,0:T(8,128)(2,1)S(1)}, bf16[272,256]{1,0:T(8,128)(2,1)S(1)}, u32[]{:S(2)}, u32[]{:S(2)}) collective-permute-start(bf16[272,256]{1,0:T(8,128)(2,1)S(1)} %collective-permute-done.14.refs_6_), channel_id=1, source_target_pairs={{1,0},{0,1},{3,2},{2,3},{5,4},{4,5},{7,6},{6,7},{9,8},{8,9},{11,10... | collective-permute-start | bytes 417800 | tf_op jit(solution)/shard_map/ppermute | solution.py:30
  50.2 2.0 %collective-permute-start.17 = (bf16[512,512]{1,0:T(8,128)(2,1)S(1)}, bf16[512,512]{1,0:T(8,128)(2,1)S(1)}, u32[]{:S(2)}, u32[]{:S(2)}) collective-permute-start(bf16[512,512]{1,0:T(8,128)(2,1)S(1)} %get-tuple-element.97), channel_id=1, source_target_pairs={{1,0},{0,1},{3,2},{2,3},{5,4},{4,5},{7,6},{6,7},{9,8},{8,9},{11,10... | collective-permute-start | bytes 1572872 | tf_op jit(solution)/shard_map/ppermute | solution.py:30
  52.2 9.2 %collective-permute-start.18 = (bf16[128,256]{1,0:T(8,128)(2,1)S(1)}, bf16[128,256]{1,0:T(8,128)(2,1)S(1)}, u32[]{:S(2)}, u32[]{:S(2)}) collective-permute-start(bf16[128,256]{1,0:T(8,128)(2,1)S(1)} %get-tuple-element.100), channel_id=1, source_target_pairs={{2,0},{0,2},{3,1},{1,3},{6,4},{4,6},{7,5},{5,7},{10,8},{8,10},{11,... | collective-permute-start | bytes 196616 | tf_op jit(solution)/shard_map/ppermute | solution.py:30
  53.8 10.6 %collective-permute-start.19 = (bf16[128,256]{1,0:T(8,128)(2,1)S(1)}, bf16[128,256]{1,0:T(8,128)(2,1)S(1)}, u32[]{:S(2)}, u32[]{:S(2)}) collective-permute-start(bf16[128,256]{1,0:T(8,128)(2,1)S(1)} %get-tuple-element.101), channel_id=1, source_target_pairs={{4,0},{0,4},{12,8},{8,12},{5,1},{1,5},{13,9},{9,13},{6,2},{2,6},{1... | collective-permute-start | bytes 196616 | tf_op jit(solution)/shard_map/ppermute | solution.py:30
  58.4 6.0 %collective-permute-start.20 = (bf16[128,256]{1,0:T(8,128)(2,1)S(1)}, bf16[128,256]{1,0:T(8,128)(2,1)S(1)}, u32[]{:S(2)}, u32[]{:S(2)}) collective-permute-start(bf16[128,256]{1,0:T(8,128)(2,1)S(1)} %get-tuple-element.102), channel_id=1, source_target_pairs={{6,0},{4,2},{2,4},{0,6},{14,8},{12,10},{10,12},{8,14},{7,1},{5,3},... | collective-permute-start | bytes 196616 | tf_op jit(solution)/shard_map/ppermute | solution.py:30
  58.5 6.0 %collective-permute-start.21 = (bf16[128,256]{1,0:T(8,128)(2,1)S(1)}, bf16[128,256]{1,0:T(8,128)(2,1)S(1)}, u32[]{:S(2)}, u32[]{:S(2)}) collective-permute-start(bf16[128,256]{1,0:T(8,128)(2,1)S(1)} %get-tuple-element.103), channel_id=1, source_target_pairs={{16,0},{0,16},{17,1},{1,17},{18,2},{2,18},{19,3},{3,19},{20,4},{4,... | collective-permute-start | bytes 196616 | tf_op jit(solution)/shard_map/ppermute | solution.py:30
  60.1 5.5 %collective-permute-start.22 = (bf16[128,256]{1,0:T(8,128)(2,1)S(1)}, bf16[128,256]{1,0:T(8,128)(2,1)S(1)}, u32[]{:S(2)}, u32[]{:S(2)}) collective-permute-start(bf16[128,256]{1,0:T(8,128)(2,1)S(1)} %get-tuple-element.104), channel_id=1, source_target_pairs={{18,0},{16,2},{2,16},{0,18},{19,1},{17,3},{3,17},{1,19},{22,4},{20... | collective-permute-start | bytes 196616 | tf_op jit(solution)/shard_map/ppermute | solution.py:30
  61.4 5.6 %collective-permute-start.23 = (bf16[128,256]{1,0:T(8,128)(2,1)S(1)}, bf16[128,256]{1,0:T(8,128)(2,1)S(1)}, u32[]{:S(2)}, u32[]{:S(2)}) collective-permute-start(bf16[128,256]{1,0:T(8,128)(2,1)S(1)} %get-tuple-element.105), channel_id=1, source_target_pairs={{20,0},{16,4},{28,8},{24,12},{4,16},{0,20},{12,24},{8,28},{21,1},{... | collective-permute-start | bytes 196616 | tf_op jit(solution)/shard_map/ppermute | solution.py:30
  64.4 6.1 %collective-permute-start.24 = (bf16[128,256]{1,0:T(8,128)(2,1)S(1)}, bf16[128,256]{1,0:T(8,128)(2,1)S(1)}, u32[]{:S(2)}, u32[]{:S(2)}) collective-permute-start(bf16[128,256]{1,0:T(8,128)(2,1)S(1)} %get-tuple-element.106), channel_id=1, source_target_pairs={{22,0},{20,2},{18,4},{16,6},{30,8},{28,10},{26,12},{24,14},{6,16},... | collective-permute-start | bytes 196616 | tf_op jit(solution)/shard_map/ppermute | solution.py:30

commit v5 on v4

v5 whole, which is shorter than its diff:
```python
import functools
import itertools

import jax
import jax.numpy as jnp
import numpy as np
from jax import lax
from jax.experimental import pallas as pl
from jax.experimental.pallas import tpu as pltpu
from jax.sharding import PartitionSpec as P

BF, F32 = jnp.bfloat16, jnp.float32


def dot(a, b, dims=((1,), (0,))):
    return lax.dot_general(a, b, (dims, ((), ())), preferred_element_type=F32)


def moved(x, groups=0, tok=0, head=0, rep=0):
    shifts = {"groups": groups, "tok": tok, "head": head, "rep": rep}
    axes = [a for a, s in shifts.items() if s]
    if not axes:
        return x
    sizes = [lax.axis_size(a) for a in axes]
    pairs = []
    for here in range(int(np.prod(sizes))):
        at = np.unravel_index(here, sizes)
        there = [i ^ tok if a == "tok" else (i + shifts[a]) % n for a, i, n in zip(axes, at, sizes)]
        pairs.append((int(np.ravel_multi_index(there, sizes)), here))
    return lax.ppermute(x, tuple(axes), pairs)


def shape(dims, dtype):
    return jax.ShapeDtypeStruct(dims, dtype)


def call(kernel, outs, args, scratch=(), fetched=0):
    touched = sum(int(np.prod(x.shape)) * x.dtype.itemsize for x in (*args, *outs))
    kept = sum(int(np.prod(x.shape)) * 4 for x in scratch if hasattr(x, "shape"))
    args = [pltpu.with_memory_space_constraint(x, pltpu.HBM) if i < fetched else x for i, x in enumerate(args)]
    return pl.pallas_call(
        kernel,
        out_shape=outs,
        in_specs=[pl.BlockSpec(memory_space=pltpu.HBM if i < fetched else pltpu.VMEM) for i in range(len(args))],
        out_specs=[pl.BlockSpec(memory_space=pltpu.VMEM)] * len(outs),
        scratch_shapes=list(scratch),
        compiler_params=pltpu.CompilerParams(vmem_limit_bytes=touched + kept + (10 << 20)),
        cost_estimate=pl.CostEstimate(flops=1, bytes_accessed=1, transcendentals=0),
    )(*args)


def window(index, size):
    return pl.ds(pl.multiple_of(index * size, size), size)


def fetch(pairs, sems):
    copies = [pltpu.make_async_copy(src, dst, sems.at[i]) for i, (src, dst) in enumerate(pairs)]
    for c in copies:
        c.start()
    return copies


def message_kernel(keys, values, rates, stream, gain, *refs):
    n, dh = keys.shape
    *_, v, rate_row, s, g, sems = refs
    copies = [(keys, None), (values, v), (rates, rate_row), (stream, s), (gain, g)]
    if len(refs) == 8:
        pair, base, gains = refs[:3]
    else:
        queries, pair, base, gains, share, full, q = refs[:7]
        copies.append((queries, q))
    copies[0] = (keys, pair.at[:, :dh])
    for c in fetch(copies, sems):
        c.wait()
    me, wide = lax.axis_index("rep"), base.shape[1]
    rate = jnp.broadcast_to(rate_row[...], (128, n)).T
    for c in range(0, dh, 128):
        pair[:, dh + c : dh + c + 128] = (v[:, c : c + 128].astype(F32) * rate).astype(BF)
    base[...] = s[:, window(me, wide)]
    x = jnp.broadcast_to(g[:, window(me, wide)], gains.shape)
    row = lax.broadcasted_iota(jnp.int32, gains.shape, 0)
    top = x.astype(BF).astype(F32)
    mid = (x - top).astype(BF).astype(F32)
    gains[...] = jnp.where(row == 0, top, jnp.where(row == 1, mid, jnp.where(row == 2, x - top - mid, 0.0))).astype(BF)
    if len(refs) > 8:
        rows = share.shape[0]
        part = pair[window(me, rows), :]
        share[...] = part
        full[:, : 2 * dh] = part
        full[:, 2 * dh : 3 * dh] = q[window(me, rows), :]
        for i in range(n // rows):
            full[:, 3 * dh + i * wide : 3 * dh + (i + 1) * wide] = base[i * rows : (i + 1) * rows, :]


def pack_kernel(up, down, same, other):
    deep, wide = up.shape[0], same.shape[1]
    bit = lax.bitwise_and(lax.axis_index("tok"), 1)
    for out, b in ((same, bit), (other, 1 - bit)):
        part = window(lax.axis_index("groups") * 2 + b, wide)
        out[:deep, :] = up[:, part]
        out[deep:, :] = down[part, :]


def gradients(k, e, w1b, w3b, w2b):
    a1, a3, b = dot(k, w1b), dot(k, w3b), dot(e, w2b, ((1,), (1,)))
    sig = jax.nn.sigmoid(a1)
    act = a1 * sig
    g = (act * a3).astype(BF)
    r1 = (b * a3 * (sig * (1.0 + a1 * (1.0 - sig)))).astype(BF)
    r3 = (b * act).astype(BF)
    first = ((0,), (0,))
    return dot(k, r1, first), dot(k, r3, first), dot(g, e, first)


def squares(x):
    return jnp.sum(x * x, axis=0, keepdims=True)


def own_kernel(take_own, pair, w1, w3, w2, b1, b3, b2, u1, u3, u2, sq13, sq2):
    dh, hidden = w1.shape
    block = min(hidden, 256)
    sq2[...] = jnp.broadcast_to(squares(w2[...]), sq2.shape)
    for j in range(0, hidden, block):
        js = slice(j, j + block)
        x1, x3, x2 = w1[:, js], w3[:, js], w2[js, :]
        b1[:, js], b3[:, js], b2[js, :] = x1.astype(BF), x3.astype(BF), x2.astype(BF)
        sq13[0:8, js] = jnp.broadcast_to(squares(x1), (8, block))
        sq13[8:16, js] = jnp.broadcast_to(squares(x3), (8, block))
        if take_own:
            d1, d3, d2 = gradients(pair[:, :dh], pair[:, dh:], b1[:, js], b3[:, js], b2[js, :])
            x1, x3, x2 = x1 + d1, x3 + d3, x2 + d2
        u1[:, js], u3[:, js], u2[js, :] = x1, x3, x2


def fast_kernel(n_pieces, near, *refs):
    pieces, refs = refs[:n_pieces], refs[n_pieces:]
    q, b1, b3, b2, u1, u3, u2, sq13, sq2, own_out, own_sq, send, ks, es, hp, qs = refs
    dh, hidden = b1.shape
    me = lax.axis_index("rep")
    at = 0
    for p in pieces:
        n = p.shape[0]
        ks[at : at + n, :] = p[:, :dh]
        es[at : at + n, :] = p[:, dh : 2 * dh]
        at += n
    tokens, step, block = at, min(at, 512), min(hidden, 256)
    n = q.shape[0]
    qs[:n, :] = q[...]
    if near > 1:
        mine, theirs = pieces[0], pieces[n_pieces // 2]
        rows = mine.shape[0]
        qs[pl.ds(pl.multiple_of(n + me * rows, rows), rows), :] = mine[:, 2 * dh : 3 * dh]
        qs[pl.ds(pl.multiple_of(n + (1 - me) * rows, rows), rows), :] = theirs[:, 2 * dh : 3 * dh]
    asked = qs[...]
    new_sq = jnp.zeros((1, dh), F32)
    for j in range(0, hidden, block):
        js = slice(j, j + block)

        def add(i, sums):
            rows = pl.ds(pl.multiple_of(i * step, step), step)
            parts = gradients(ks[rows, :], es[rows, :], b1[:, js], b3[:, js], b2[js, :])
            return tuple(s + p for s, p in zip(sums, parts))

        sums = (u1[:, js], u3[:, js], u2[js, :])
        sums = add(0, sums) if tokens == step else lax.fori_loop(0, tokens // step, add, sums)

        def normed(old_sq, new):
            return (new * (jnp.sqrt(old_sq) * lax.rsqrt(squares(new) + 1e-06))).astype(BF)

        new_sq = new_sq + squares(sums[2])
        qa = dot(asked, normed(sq13[0:1, js], sums[0]))
        qc = dot(asked, normed(sq13[8:9, js], sums[1]))
        part = dot((qa * jax.nn.sigmoid(qa) * qc).astype(BF), sums[2].astype(BF))
        hp[...] = part if j == 0 else hp[...] + part
    n, wide = own_out.shape
    own_out[...] = hp[:, window(me, wide)]
    send[:n, :] = hp[:, window(1 - me, wide)].astype(BF)
    row = lax.broadcasted_iota(jnp.int32, (8, dh), 0)
    hp[:8, :] = jnp.where(row == 0, sq2[...], jnp.where(row == 1, new_sq, 0.0))
    own_sq[...] = hp[:8, window(me, wide)]
    sq = hp[:8, window(1 - me, wide)]
    top = sq.astype(BF).astype(F32)
    send[n:, :] = jnp.concatenate([top, sq - top], axis=0).astype(BF)


def mix_kernel(own, own_sq, got, base, gains, *refs):
    *asks, mixed, low = refs
    n, wide = mixed.shape
    rows = own.shape[0]
    tail = got[rows:, :].astype(F32)
    sq = own_sq[...] + tail[:8] + tail[8:]
    y = (own[...] + got[:rows, :].astype(F32)) * (jnp.sqrt(sq[0:1]) * lax.rsqrt(sq[1:2] + 1e-06))
    mixed[...] = y[:n] + base[...].astype(F32)
    low[:n, :] = mixed[...].astype(BF)
    for message in asks:
        part = message.shape[0]
        for i in range(n // part):
            at, there = n + i * part, message.shape[1] - n // part * wide + i * wide
            low[at : at + part, :] = (y[at : at + part] + message[:, there : there + wide].astype(F32)).astype(BF)
    low[rows:, :] = gains[...]


def up_kernel(places, first, n_blocks, *refs):
    pieces, refs = refs[: len(places)], refs[len(places) :]
    blocks, (zs, total) = refs[:-2], refs[-2:]
    me_h, me_r, me_t = lax.axis_index("head"), lax.axis_index("rep"), lax.axis_index("tok")
    n_head = lax.axis_size("head")
    n, wide = pieces[0].shape[0] - 16, pieces[0].shape[1]
    width = zs.shape[1]
    for dg in range(lax.axis_size("groups")):
        here = [(p, dh, dr) for p, (g, dh, dr) in zip(pieces, places) if g == dg]
        norm = jnp.zeros((n, 1), F32)
        for p, _, _ in here:
            x = p[:n, :].astype(F32)
            norm = norm + jnp.sum(x * x, axis=1, keepdims=True)
        inv = lax.rsqrt(norm / width + 1e-06)
        for p, dh, dr in here:
            r = lax.rem(me_r + dr, 2)
            head = lax.rem(me_h + dh, n_head)
            gain = jnp.sum(p[n:, :].astype(F32), axis=0, keepdims=True)
            zs[dg * n : (dg + 1) * n, window(head * 2 + r, wide)] = (p[:n, :].astype(F32) * inv * gain).astype(BF)
    total[...] = up_terms(zs, first, n_blocks, blocks)


def up_terms(zs, first, n_blocks, blocks):
    deep = zs.shape[1] // n_blocks
    total = None
    for s, x in enumerate(blocks, first):
        z = zs[...] if n_blocks == 1 else zs[:, window(lax.bitwise_xor(lax.axis_index("tok"), s), deep)]
        term = dot(z, x[:deep, :])
        total = term if total is None else total + term
    return total


def down_kernel(n_late, n_blocks, zs, total, *refs):
    blocks, (own, send, os) = refs[:-3], refs[-3:]
    me_h, me_r, me_t = lax.axis_index("head"), lax.axis_index("rep"), lax.axis_index("tok")
    n_head = lax.axis_size("head")
    x = total[...]
    if n_late:
        x = x + up_terms(zs, n_blocks - n_late, n_blocks, blocks[n_blocks - n_late :])
    h = (0.5 * x * (1.0 + lax.erf(x * np.float32(0.5**0.5)))).astype(BF)
    units = h.shape[1]
    for s, x in enumerate(blocks):
        term = dot(h, x[x.shape[0] - units :, :])
        if n_blocks == 1:
            os[...] = term
        else:
            os[:, window(lax.bitwise_xor(me_t, s), term.shape[1])] = term
    rows, wide = own.shape[0], own.shape[1] // n_head
    for dh in range(n_head):
        there = slice(dh * wide, (dh + 1) * wide)
        cols = window(lax.rem(me_h + dh, n_head), wide)
        own[:, there] = os[window(me_r, rows), cols]
        send[:, there] = os[window(1 - me_r, rows), cols].astype(BF)


def pair_kernel(moves, own, got, *outs):
    n, wide = outs[0].shape
    for (dz, dh), out in zip(moves, outs):
        rows, cols = slice(dz * n, (dz + 1) * n), slice(dh * wide, (dh + 1) * wide)
        out[...] = (own[rows, cols] + got[rows, cols].astype(F32)).astype(BF)


def sum_kernel(*refs):
    *parts, mixed, keep, send, acc = refs
    total = parts[0][...].astype(F32)
    for p in parts[1:]:
        total = total + p[...].astype(F32)
    acc[...] = total
    me, wide = lax.axis_index("rep"), keep.shape[1]
    keep[...] = mixed[...] + acc[:, window(me, wide)]
    send[...] = acc[:, window(1 - me, wide)].astype(BF)


def dealt(x, tok, head):
    axes = ("groups", "tok", "head", "rep")
    sizes = [lax.axis_size(a) for a in axes]
    pairs = []
    for here in range(int(np.prod(sizes))):
        g, t, h, r = np.unravel_index(here, sizes)
        there = ((g + r) % sizes[0], t ^ tok, (h + head) % sizes[2], r)
        pairs.append((here, int(np.ravel_multi_index(there, sizes))))
    return lax.ppermute(x, axes, pairs)


def on_device(
    keys, values, rates, queries, stream, gain, counts, fw_one, fw_three, fw_two, mlp_up, mlp_down
):
    n_tok, n_head = lax.axis_size("tok"), lax.axis_size("head")
    groups, reps = lax.axis_size("groups"), lax.axis_size("rep")
    dh, n_key, n = keys.shape[1], keys.shape[0], queries.shape[0]
    hidden = fw_one.shape[2]
    wide = dh // reps
    paired = n_tok == 4 and n_key == n
    near = 2 if paired else 1
    units = mlp_up.shape[1] // groups // near
    barrier = lax.optimization_barrier

    rows = n_key // reps
    outs = [shape((n_key, 2 * dh), BF), shape((n, wide), BF), shape((16, wide), BF)]
    fetches = [((n_key, dh), BF), ((1, n_key), F32), ((n, dh), BF), ((1, dh), F32)]
    sources = [keys, values, rates.reshape(1, n_key), stream, gain[None, :]]
    if paired:
        outs += [shape((rows, 2 * dh), BF), shape((rows, 4 * dh), BF)]
        fetches = [((n, dh), BF), *fetches]
        sources += [queries]
    pair, base, gains, *messages = call(
        message_kernel,
        outs,
        sources,
        [*[pltpu.VMEM(*f) for f in fetches], pltpu.SemaphoreType.DMA((len(sources),))],
        fetched=len(sources),
    )
    square = [shape((dh, hidden), F32), shape((dh, hidden), F32), shape((hidden, dh), F32)]
    prepared = call(
        functools.partial(own_kernel, paired),
        [
            *[shape(x.shape, BF) for x in square],
            *square,
            shape((16, hidden), F32),
            shape((8, dh), F32),
        ],
        [pair, fw_one[0], fw_three[0], fw_two[0]],
    )
    asks = []
    if paired:
        share, full = messages
        others = [moved(full, tok=1), moved(share, tok=2), moved(share, tok=3)]
        same, other = call(
            pack_kernel, [shape((mlp_up.shape[0] + units, units), BF)] * 2, [mlp_up, mlp_down]
        )
        others, w_same, w_other, prepared = barrier((others, same, other, prepared))
        tokens = [*others, *[moved(x, rep=1) for x in others]]
        w_second, w_third, w_first = moved(w_same, tok=2), moved(w_other, tok=3), moved(w_other, tok=1)
        asks = others[:1]
    else:
        me_g = lax.axis_index("groups")
        up_own = lax.dynamic_slice_in_dim(mlp_up, me_g * units, units, 1)
        down_own = lax.dynamic_slice_in_dim(mlp_down, me_g * units, units, 0)
        tokens = [lax.all_gather(pair, "tok", axis=0, tiled=True)]
        up_blocks = [lax.all_gather(up_own, "tok", axis=0, tiled=True)]
        down_blocks = [lax.all_gather(down_own, "tok", axis=1, tiled=True)]
    n_all = sum(x.shape[0] for x in tokens)
    tokens = barrier(tokens)
    own, own_sq, send = call(
        functools.partial(fast_kernel, len(tokens), near),
        [shape((near * n, wide), F32), shape((8, wide), F32), shape((near * n + 16, wide), BF)],
        [*tokens, queries, *prepared],
        [pltpu.VMEM((n_all, dh), BF), pltpu.VMEM((n_all, dh), BF), pltpu.VMEM((near * n, dh), F32), pltpu.VMEM((near * n, dh), BF)],
    )
    got = moved(send, rep=1)
    mixed, low = call(
        mix_kernel,
        [shape((n, wide), F32), shape((near * n + 16, wide), BF)],
        [own, own_sq, got, base, gains, *asks],
    )
    across = {}
    for dg, h in itertools.product(range(groups), range(n_head)):
        x = low
        if paired and dg and h:
            x, w_first, w_second = barrier((x, w_first, w_second))
        across[dg, h] = moved(x, groups=dg, head=h)
    if paired:
        across, w_third = barrier((across, w_third))
    pieces, places = [], []
    for m, x in across.items():
        pieces += [x, moved(x, rep=1)]
        places += [(*m, 0), (*m, 1)]
    early, late = [], []
    if paired:
        early, late = [same, w_first, w_second], [w_third]
        up_blocks = down_blocks = [*early, *late]
    else:
        early = up_blocks
    count = len(up_blocks)
    model = n_head * dh
    zs, act = call(
        functools.partial(up_kernel, places, 0, count),
        [shape((groups * near * n, model), BF), shape((groups * near * n, units), F32)],
        [*pieces, *early],
    )
    own, send = call(
        functools.partial(down_kernel, len(late), count),
        [shape((near * n, model), F32), shape((near * n, model), BF)],
        [zs, act, *down_blocks],
        [pltpu.VMEM((groups * near * n, model), F32)],
    )
    got = moved(send, rep=1)
    moves = list(itertools.product(range(near), range(n_head)))
    parts = call(
        functools.partial(pair_kernel, moves), [shape((n, dh), BF)] * len(moves), [own, got]
    )
    parts = [dealt(x, *m) for m, x in zip(moves, parts)]
    keep, send = call(
        sum_kernel, [shape((n, wide), F32), shape((n, wide), BF)], [*parts, mixed], [pltpu.VMEM((n, dh), F32)]
    )
    total = keep + moved(send, rep=1).astype(F32)
    live = jnp.arange(n, dtype=jnp.int32) < counts[0]
    return jnp.where(live[:, None], total, 0.0).astype(BF)


def solution(mesh):
    placed = (
        P(("groups", "tok"), "head"),
        P(("groups", "tok"), "head"),
        P(("groups", "tok"), "head"),
        P(("groups", "tok"), "head"),
        P(("groups", "tok"), "head"),
        P("head"),
        P(("groups", "tok")),
        P("head", None, "rep"),
        P("head", None, "rep"),
        P("head", "rep", None),
        P("tok", ("head", "rep")),
        P(("head", "rep"), "tok"),
    )
    return jax.shard_map(
        on_device,
        mesh=mesh,
        in_specs=placed,
        out_specs=P(("groups", "tok"), ("head", "rep")),
        check_vma=False,
    )
```

time: 71.4 us -> 68.7 us (0.962)
  starting transfers between devices: 26.7 us -> 22 us
  waiting for transfers between devices: 31 us -> 33.6 us
    ppermute x25 -> x19, starting transfers between devices: 26.7 us -> 17.8 us  [moved(): return lax.ppermute(x, tuple(axes), pairs)]
    ppermute x0 -> x4, waiting for transfers between devices: none -> 4.58 us  [dealt(): return lax.ppermute(x, axes, pairs)]
    ppermute x0 -> x4, starting transfers between devices: none -> 4.22 us  [dealt(): return lax.ppermute(x, axes, pairs)]
    ppermute x25 -> x19, waiting for transfers between devices: 31 us -> 29 us  [moved(): return lax.ppermute(x, tuple(axes), pairs)]
    unnamed x16 -> x12, local copies, waits for them, and re-layouts: 4.18 us -> 3.5 us
    pallas_call x8 -> x9, Pallas kernels: 7.68 us -> 7.81 us  [call(): pl.pallas_call(kernel, out_shape=outs, in_specs=[pl.BlockSpec(memory_spac...]
  transfers between devices with their start and end apart: 25 -> 23, of which waited for: 11 -> 16; matrix products, arithmetic and copies ran while one was open for 0% -> 0% of each run, Pallas kernels for 6% -> 7%
where the time goes in v5:
time: 68.7 us; the launch traced here: 68.4 us
  waiting for transfers between devices  33.6 us (49%)
  starting transfers between devices  22 us (32%)
  Pallas kernels  7.81 us (11%)
  local copies, waits for them, and re-layouts  3.5 us (5%)
  between operations  0.78 us (1%)
  other arithmetic  0.72 us (1%)
    ppermute x19, waiting for transfers between devices, moved(): return lax.ppermute(x, tuple(axes), pairs)  29 us
    ppermute x19, starting transfers between devices, moved(): return lax.ppermute(x, tuple(axes), pairs)  17.8 us
    pallas_call x9, Pallas kernels, call(): pl.pallas_call(kernel, out_shape=outs, in_specs=[pl.BlockSpec(memory_spac...  7.81 us
    ppermute x4, waiting for transfers between devices, dealt(): return lax.ppermute(x, axes, pairs)  4.58 us
    ppermute x4, starting transfers between devices, dealt(): return lax.ppermute(x, axes, pairs)  4.22 us
    unnamed x12, local copies, waits for them, and re-layouts  3.5 us
  transfers between devices with their start and end apart: 23, of which 16 were waited for; matrix products, arithmetic and copies ran while one was open for 0% of the time, Pallas kernels for 7%

profile of v5, /device:TPU:0, one launch (start us, length us, event | category | flops | bytes accessed | tf_op | source)
XLA Modules:
  0.0 68.4 jit_solution(8536035461223000783)
XLA Ops:
  0.0 0.0 copy-start.4
  0.0 0.0 copy-start
  0.0 1.4 %shard_map.118 = (bf16[128,1024]{1,0:T(8,128)(2,1)S(1)}, bf16[128,256]{1,0:T(8,128)(2,1)S(1)}, bf16[16,256]{1,0:T(8,128)(2,1)S(1)}, bf16[64,1024]{1,0:T(8,128)(2,1)S(1)}, bf16[64,2048]{1,0:T(8,128)(2,1)S(1)}) custom-call(bf16[128,512]{1,0:T(8,128)(2,1)} %keys.1, bf16[128,512]{1,0:T(8,128)(2,1)} %values.1, f32[1,128]{1,0:T(1,128)} %bitcast.11, ...), custom_call_target="tpu_custom_call" | custom-call | flops 1 | bytes 1 | tf_op jit(solution)/shard_map/pallas_call | solution.py:41
  1.4 3.1 %collective-permute-start = (bf16[64,2048]{1,0:T(8,128)(2,1)S(1)}, bf16[64,2048]{1,0:T(8,128)(2,1)S(1)}, u32[]{:S(2)}, u32[]{:S(2)}) collective-permute-start(bf16[64,2048]{1,0:T(8,128)(2,1)S(1)} %get-tuple-element.62), channel_id=1, source_target_pairs={{4,0},{0,4},{12,8},{8,12},{5,1},{1,5},{13,9},{9,13},{6,2},{2,6},{1... | collective-permute-start | bytes 786440 | tf_op jit(solution)/shard_map/ppermute | solution.py:30
  4.5 2.6 %collective-permute-start.1 = (bf16[64,1024]{1,0:T(8,128)(2,1)S(1)}, bf16[64,1024]{1,0:T(8,128)(2,1)S(1)}, u32[]{:S(2)}, u32[]{:S(2)}) collective-permute-start(bf16[64,1024]{1,0:T(8,128)(2,1)S(1)} %get-tuple-element.63), channel_id=1, source_target_pairs={{8,0},{12,4},{0,8},{4,12},{9,1},{13,5},{1,9},{5,13},{10,2},{14,6},... | collective-permute-start | bytes 393224 | tf_op jit(solution)/shard_map/ppermute | solution.py:30
  7.1 0.0 collective-permute-start.2
  7.1 0.0 copy-done.4
  7.1 1.0 %copy-done.5 = bf16[1024,256]{1,0:T(8,128)(2,1)S(1)} copy-done((bf16[1024,256]{1,0:T(8,128)(2,1)S(1)}, bf16[1024,256]{1,0:T(8,128)(2,1)}, u32[]{:S(2)}) %copy-start.5) | copy-done | bytes 524312
  8.2 0.0 copy-done
  8.2 0.0 copy-start.1
  8.2 1.2 %copy-done.1 = f32[1,512,512]{2,1,0:T(8,128)S(1)} copy-done((f32[1,512,512]{2,1,0:T(8,128)S(1)}, f32[1,512,512]{2,1,0:T(8,128)}, u32[]{:S(2)}) %copy-start.1) | copy-done | bytes 1048600
  9.4 1.2 %copy-done.2 = f32[1,512,512]{2,1,0:T(8,128)S(1)} copy-done((f32[1,512,512]{2,1,0:T(8,128)S(1)}, f32[1,512,512]{2,1,0:T(8,128)}, u32[]{:S(2)}) %copy-start.2) | copy-done | bytes 1048600
  10.7 1.4 %shard_map.120 = (bf16[512,512]{1,0:T(8,128)(2,1)S(1)}, bf16[512,512]{1,0:T(8,128)(2,1)S(1)}, bf16[512,512]{1,0:T(8,128)(2,1)S(1)}, f32[512,512]{1,0:T(8,128)S(1...) custom-call(bf16[128,1024]{1,0:T(8,128)(2,1)S(1)} %get-tuple-element.66.pair,, ...), custom_call_target="tpu_custom_call" | custom-call | flops 1 | bytes 1 | tf_op jit(solution)/shard_map/pallas_call | solution.py:41
  12.1 2.0 %collective-permute-done.1.refs_1_ = bf16[64,1024]{1,0:T(8,128)(2,1)S(1)} collective-permute-done((bf16[64,1024]{1,0:T(8,128)(2,1)S(1)}, bf16[64,1024]{1,0:T(8,128)(2,1)S(1)}, u32[]{:S(2)}, u32[]{:S(2)}) %collective-permute-start.1) | collective-permute-done | bytes 131104 | tf_op jit(solution)/shard_map/ppermute | solution.py:30
  14.1 4.7 %collective-permute-done.2.refs_2_ = bf16[64,1024]{1,0:T(8,128)(2,1)S(1)} collective-permute-done((bf16[64,1024]{1,0:T(8,128)(2,1)S(1)}, bf16[64,1024]{1,0:T(8,128)(2,1)S(1)}, u32[]{:S(2)}, u32[]{:S(2)}) %collective-permute-start.2) | collective-permute-done | bytes 131104 | tf_op jit(solution)/shard_map/ppermute | solution.py:30
  18.7 0.0 collective-permute-done.refs_0_
  18.7 0.0 collective-permute-start.3
  18.8 0.5 collective-permute-start.4
  19.3 0.0 collective-permute-start.5
  19.3 0.7 collective-permute-start.9
  19.9 1.4 %collective-permute-start.10 = (bf16[512,256]{1,0:T(8,128)(2,1)S(1)}, bf16[512,256]{1,0:T(8,128)(2,1)S(1)}, u32[]{:S(2)}, u32[]{:S(2)}) collective-permute-start(bf16[512,256]{1,0:T(8,128)(2,1)S(1)} %get-tuple-element.99.refs_8_.refs_0_), channel_id=1, source_target_pairs={{8,0},{12,4},{0,8},{4,12},{9,1},{13,5},{1,9},{5,13},{10,2},{14,6},... | collective-permute-start | bytes 786440 | tf_op jit(solution)/shard_map/ppermute | solution.py:30
  21.3 0.0 collective-permute-done.4.refs_4_
  21.3 0.0 collective-permute-done.5.refs_5_
  21.3 0.0 collective-permute-done.3.refs_3_
  21.3 0.0 copy-done.3
  21.3 3.0 %shard_map.121 = (f32[256,256]{1,0:T(8,128)S(1)}, f32[8,256]{1,0:T(8,128)S(1)}, bf16[272,256]{1,0:T(8,128)(2,1)S(1)}) custom-call(bf16[64,2048]{1,0:T(8,128)(2,1)S(1)} %collective-permute-done.refs_0_, bf16[64,1024]{1,0:T(8,128)(2,1)S(1)} %collective-permute-done.1.refs_1_, bf16[64,1024]{1,0:T(8,128)(2,1)S(1)} %collective-permute-done.2.refs_2_, ...), custom_call_target="tpu_custom_call" | custom-call | flops 1 | bytes 1 | tf_op jit(solution)/shard_map/pallas_call | solution.py:41
  24.3 0.1 collective-permute-start.6
  24.4 2.4 %collective-permute-start.12 = (bf16[512,256]{1,0:T(8,128)(2,1)S(1)}, bf16[512,256]{1,0:T(8,128)(2,1)S(1)}, u32[]{:S(2)}, u32[]{:S(2)}) collective-permute-start(bf16[512,256]{1,0:T(8,128)(2,1)S(1)} %get-tuple-element.98), channel_id=1, source_target_pairs={{12,0},{8,4},{4,8},{0,12},{13,1},{9,5},{5,9},{1,13},{14,2},{10,6},... | collective-permute-start | bytes 786440 | tf_op jit(solution)/shard_map/ppermute | solution.py:30
  26.8 0.0 collective-permute-done.6.got
  26.8 0.1 shard_map.122
  26.9 6.3 %collective-permute-done.9.refs_9_.refs_1_ = bf16[512,256]{1,0:T(8,128)(2,1)S(1)} collective-permute-done((bf16[512,256]{1,0:T(8,128)(2,1)S(1)}, bf16[512,256]{1,0:T(8,128)(2,1)S(1)}, u32[]{:S(2)}, u32[]{:S(2)}) %collective-permute-start.9) | collective-permute-done | bytes 262176 | tf_op jit(solution)/shard_map/ppermute | solution.py:30
  33.2 7.9 %collective-permute-done.10.refs_10_.refs_2_ = bf16[512,256]{1,0:T(8,128)(2,1)S(1)} collective-permute-done((bf16[512,256]{1,0:T(8,128)(2,1)S(1)}, bf16[512,256]{1,0:T(8,128)(2,1)S(1)}, u32[]{:S(2)}, u32[]{:S(2)}) %collective-permute-start.10) | collective-permute-done | bytes 262176 | tf_op jit(solution)/shard_map/ppermute | solution.py:30
  41.2 2.4 %collective-permute-start.11 = (bf16[272,256]{1,0:T(8,128)(2,1)S(1)}, bf16[272,256]{1,0:T(8,128)(2,1)S(1)}, u32[]{:S(2)}, u32[]{:S(2)}) collective-permute-start(bf16[272,256]{1,0:T(8,128)(2,1)S(1)} %get-tuple-element.101.refs_0_), channel_id=1, source_target_pairs={{18,0},{16,2},{2,16},{0,18},{19,1},{17,3},{3,17},{1,19},{22,4},{20... | collective-permute-start | bytes 417800 | tf_op jit(solution)/shard_map/ppermute | solution.py:30
  43.6 0.5 collective-permute-start.7
  44.2 0.5 collective-permute-start.8
  44.7 0.0 collective-permute-done.12.refs_3_
  44.7 2.5 %collective-permute-done.11.refs_6_ = bf16[272,256]{1,0:T(8,128)(2,1)S(1)} collective-permute-done((bf16[272,256]{1,0:T(8,128)(2,1)S(1)}, bf16[272,256]{1,0:T(8,128)(2,1)S(1)}, u32[]{:S(2)}, u32[]{:S(2)}) %collective-permute-start.11) | collective-permute-done | bytes 139296 | tf_op jit(solution)/shard_map/ppermute | solution.py:30
  47.1 1.5 %collective-permute-done.7.refs_2_ = bf16[272,256]{1,0:T(8,128)(2,1)S(1)} collective-permute-done((bf16[272,256]{1,0:T(8,128)(2,1)S(1)}, bf16[272,256]{1,0:T(8,128)(2,1)S(1)}, u32[]{:S(2)}, u32[]{:S(2)}) %collective-permute-start.7) | collective-permute-done | bytes 139296 | tf_op jit(solution)/shard_map/ppermute | solution.py:30
  48.7 0.5 collective-permute-done.8.refs_4_
  49.2 0.0 collective-permute-start.13
  49.2 0.5 collective-permute-start.14
  49.7 0.0 collective-permute-start.15
  49.7 0.5 collective-permute-start.16
  50.2 0.3 collective-permute-done.13.refs_1_
  50.6 0.2 collective-permute-done.14.refs_3_
  50.8 0.3 collective-permute-done.15.refs_5_
  51.1 0.2 collective-permute-done.16.refs_7_
  51.3 0.9 %shard_map.123 = (bf16[512,1024]{1,0:T(8,128)(2,1)S(1)}, f32[512,256]{1,0:T(8,128)S(1)}) custom-call(bf16[272,256]{1,0:T(8,128)(2,1)S(1)} %get-tuple-element.101.refs_0_, bf16[272,256]{1,0:T(8,128)(2,1)S(1)} %collective-permute-done.13.refs_1_, bf16[272,256]{1,0:T(8,128)(2,1)S(1)} %collective-permute-done.7.refs_2_, ...), custom_call_target="tpu_custom_call" | custom-call | flops 1 | bytes 1 | tf_op jit(solution)/shard_map/pallas_call | solution.py:41
  52.1 0.8 %shard_map.124 = (f32[256,1024]{1,0:T(8,128)S(1)}, bf16[256,1024]{1,0:T(8,128)(2,1)S(1)}) custom-call(bf16[512,1024]{1,0:T(8,128)(2,1)S(1)} %get-tuple-element.107.zs, f32[512,256]{1,0:T(8,128)S(1)} %get-tuple-element.108.total, bf16[512,256]{1,0:T(8,128)(2,1)S(1)} %get-tuple-element.99.refs_8_.refs_0_, ...), custom_call_target="tpu_custom_call" | custom-call | flops 1 | bytes 1 | tf_op jit(solution)/shard_map/pallas_call | solution.py:41
  52.9 0.4 collective-permute-start.17
  53.3 1.6 %collective-permute-done.17.got = bf16[256,1024]{1,0:T(8,128)(2,1)S(1)} collective-permute-done((bf16[256,1024]{1,0:T(8,128)(2,1)S(1)}, bf16[256,1024]{1,0:T(8,128)(2,1)S(1)}, u32[]{:S(2)}, u32[]{:S(2)}) %collective-permute-start.17) | collective-permute-done | bytes 524320 | tf_op jit(solution)/shard_map/ppermute | solution.py:30
  54.9 0.1 shard_map.125
  55.0 0.7 collective-permute-start.18
  55.7 1.5 %collective-permute-start.19 = (bf16[128,512]{1,0:T(8,128)(2,1)S(1)}, bf16[128,512]{1,0:T(8,128)(2,1)S(1)}, u32[]{:S(2)}, u32[]{:S(2)}) collective-permute-start(bf16[128,512]{1,0:T(8,128)(2,1)S(1)} %get-tuple-element.113), channel_id=1, source_target_pairs={{0,2},{1,19},{2,0},{3,17},{4,6},{5,23},{6,4},{7,21},{8,10},{9,27},... | collective-permute-start | bytes 393224 | tf_op jit(solution)/shard_map/ppermute | solution.py:284
  57.2 0.0 collective-permute-start.20
  57.2 2.0 %collective-permute-start.21 = (bf16[128,512]{1,0:T(8,128)(2,1)S(1)}, bf16[128,512]{1,0:T(8,128)(2,1)S(1)}, u32[]{:S(2)}, u32[]{:S(2)}) collective-permute-start(bf16[128,512]{1,0:T(8,128)(2,1)S(1)} %get-tuple-element.115), channel_id=1, source_target_pairs={{0,6},{1,23},{2,4},{3,21},{4,2},{5,19},{6,0},{7,17},{8,14},{9,31},... | collective-permute-start | bytes 393224 | tf_op jit(solution)/shard_map/ppermute | solution.py:284
  59.9 0.0 collective-permute-done.18.refs_0_
  59.9 0.8 %collective-permute-done.19.refs_1_ = bf16[128,512]{1,0:T(8,128)(2,1)S(1)} collective-permute-done((bf16[128,512]{1,0:T(8,128)(2,1)S(1)}, bf16[128,512]{1,0:T(8,128)(2,1)S(1)}, u32[]{:S(2)}, u32[]{:S(2)}) %collective-permute-start.19) | collective-permute-done | bytes 131104 | tf_op jit(solution)/shard_map/ppermute | solution.py:284
  60.7 1.5 %collective-permute-done.20.refs_2_ = bf16[128,512]{1,0:T(8,128)(2,1)S(1)} collective-permute-done((bf16[128,512]{1,0:T(8,128)(2,1)S(1)}, bf16[128,512]{1,0:T(8,128)(2,1)S(1)}, u32[]{:S(2)}, u32[]{:S(2)}) %collective-permute-start.20) | collective-permute-done | bytes 131104 | tf_op jit(solution)/shard_map/ppermute | solution.py:284
  62.2 2.3 %collective-permute-done.21.refs_3_ = bf16[128,512]{1,0:T(8,128)(2,1)S(1)} collective-permute-done((bf16[128,512]{1,0:T(8,128)(2,1)S(1)}, bf16[128,512]{1,0:T(8,128)(2,1)S(1)}, u32[]{:S(2)}, u32[]{:S(2)}) %collective-permute-start.21) | collective-permute-done | bytes 131104 | tf_op jit(solution)/shard_map/ppermute | solution.py:284
  64.5 0.1 shard_map.126
  64.6 2.2 %collective-permute-start.22 = (bf16[128,256]{1,0:T(8,128)(2,1)S(1)}, bf16[128,256]{1,0:T(8,128)(2,1)S(1)}, u32[]{:S(2)}, u32[]{:S(2)}) collective-permute-start(bf16[128,256]{1,0:T(8,128)(2,1)S(1)} %get-tuple-element.118), channel_id=1, source_target_pairs={{1,0},{0,1},{3,2},{2,3},{5,4},{4,5},{7,6},{6,7},{9,8},{8,9},{11,10... | collective-permute-start | bytes 196616 | tf_op jit(solution)/shard_map/ppermute | solution.py:30
  66.8 0.9 %collective-permute-done.22 = bf16[128,256]{1,0:T(8,128)(2,1)S(1)} collective-permute-done((bf16[128,256]{1,0:T(8,128)(2,1)S(1)}, bf16[128,256]{1,0:T(8,128)(2,1)S(1)}, u32[]{:S(2)}, u32[]{:S(2)}) %collective-permute-start.22) | collective-permute-done | bytes 65568 | tf_op jit(solution)/shard_map/ppermute | solution.py:30
  67.7 0.7 %select_convert_fusion = bf16[128,256]{1,0:T(8,128)(2,1)} fusion(f32[128,256]{1,0:T(8,128)S(1)} %get-tuple-element.117, bf16[128,256]{1,0:T(8,128)(2,1)S(1)} %collective-permute-done.22, pred[128]{0:T(512)(128)(4,1)S(1)} %iota_compare_fusion), kind=kLoop, calls=%fused_computation | loop fusion | flops 131072 | bytes 262272 | tf_op jit(solution)/shard_map/convert_element_type | solution.py:400
  (5 shorter events, 0.1 us)
Async XLA Ops:
  0.0 7.1 %copy-start.4 = (bf16[256,1024]{1,0:T(8,128)(2,1)S(1)}, bf16[256,1024]{1,0:T(8,128)(2,1)}, u32[]{:S(2)}) copy-start(bf16[256,1024]{1,0:T(8,128)(2,1)} %up.1) | copy-start | bytes 1572868
  0.0 8.2 %copy-start = (f32[1,512,512]{2,1,0:T(8,128)S(1)}, f32[1,512,512]{2,1,0:T(8,128)}, u32[]{:S(2)}) copy-start(f32[1,512,512]{2,1,0:T(8,128)} %param.19) | copy-start | bytes 3145732
  1.4 17.3 %collective-permute-start = (bf16[64,2048]{1,0:T(8,128)(2,1)S(1)}, bf16[64,2048]{1,0:T(8,128)(2,1)S(1)}, u32[]{:S(2)}, u32[]{:S(2)}) collective-permute-start(bf16[64,2048]{1,0:T(8,128)(2,1)S(1)} %get-tuple-element.62), channel_id=1, source_target_pairs={{4,0},{0,4},{12,8},{8,12},{5,1},{1,5},{13,9},{9,13},{6,2},{2,6},{1... | collective-permute-start | bytes 786440 | tf_op jit(solution)/shard_map/ppermute | solution.py:30
  4.5 9.6 %collective-permute-start.1 = (bf16[64,1024]{1,0:T(8,128)(2,1)S(1)}, bf16[64,1024]{1,0:T(8,128)(2,1)S(1)}, u32[]{:S(2)}, u32[]{:S(2)}) collective-permute-start(bf16[64,1024]{1,0:T(8,128)(2,1)S(1)} %get-tuple-element.63), channel_id=1, source_target_pairs={{8,0},{12,4},{0,8},{4,12},{9,1},{13,5},{1,9},{5,13},{10,2},{14,6},... | collective-permute-start | bytes 393224 | tf_op jit(solution)/shard_map/ppermute | solution.py:30
  7.1 11.6 %collective-permute-start.2 = (bf16[64,1024]{1,0:T(8,128)(2,1)S(1)}, bf16[64,1024]{1,0:T(8,128)(2,1)S(1)}, u32[]{:S(2)}, u32[]{:S(2)}) collective-permute-start(bf16[64,1024]{1,0:T(8,128)(2,1)S(1)} %get-tuple-element.63), channel_id=1, source_target_pairs={{12,0},{8,4},{4,8},{0,12},{13,1},{9,5},{5,9},{1,13},{14,2},{10,6},... | collective-permute-start | bytes 393224 | tf_op jit(solution)/shard_map/ppermute | solution.py:30
  7.1 1.0 %copy-start.5 = (bf16[1024,256]{1,0:T(8,128)(2,1)S(1)}, bf16[1024,256]{1,0:T(8,128)(2,1)}, u32[]{:S(2)}) copy-start(bf16[1024,256]{1,0:T(8,128)(2,1)} %down.1) | copy-start | bytes 1572868
  8.2 1.2 %copy-start.1 = (f32[1,512,512]{2,1,0:T(8,128)S(1)}, f32[1,512,512]{2,1,0:T(8,128)}, u32[]{:S(2)}) copy-start(f32[1,512,512]{2,1,0:T(8,128)} %param.20) | copy-start | bytes 3145732
  9.4 1.2 %copy-start.2 = (f32[1,512,512]{2,1,0:T(8,128)S(1)}, f32[1,512,512]{2,1,0:T(8,128)}, u32[]{:S(2)}) copy-start(f32[1,512,512]{2,1,0:T(8,128)} %param.21) | copy-start | bytes 3145732
  10.7 10.6 %copy-start.3 = (bf16[128,512]{1,0:T(8,128)(2,1)S(1)}, bf16[128,512]{1,0:T(8,128)(2,1)}, u32[]{:S(2)}) copy-start(bf16[128,512]{1,0:T(8,128)(2,1)} %refs_6_.1) | copy-start | bytes 393220
  18.7 2.6 %collective-permute-start.3 = (bf16[64,2048]{1,0:T(8,128)(2,1)S(1)}, bf16[64,2048]{1,0:T(8,128)(2,1)S(1)}, u32[]{:S(2)}, u32[]{:S(2)}) collective-permute-start(bf16[64,2048]{1,0:T(8,128)(2,1)S(1)} %collective-permute-done.refs_0_), channel_id=1, source_target_pairs={{1,0},{0,1},{3,2},{2,3},{5,4},{4,5},{7,6},{6,7},{9,8},{8,9},{11,10... | collective-permute-start | bytes 786440 | tf_op jit(solution)/shard_map/ppermute | solution.py:30
  18.8 2.5 %collective-permute-start.4 = (bf16[64,1024]{1,0:T(8,128)(2,1)S(1)}, bf16[64,1024]{1,0:T(8,128)(2,1)S(1)}, u32[]{:S(2)}, u32[]{:S(2)}) collective-permute-start(bf16[64,1024]{1,0:T(8,128)(2,1)S(1)} %collective-permute-done.1.refs_1_), channel_id=1, source_target_pairs={{1,0},{0,1},{3,2},{2,3},{5,4},{4,5},{7,6},{6,7},{9,8},{8,9},{11,10... | collective-permute-start | bytes 393224 | tf_op jit(solution)/shard_map/ppermute | solution.py:30
  19.3 2.0 %collective-permute-start.5 = (bf16[64,1024]{1,0:T(8,128)(2,1)S(1)}, bf16[64,1024]{1,0:T(8,128)(2,1)S(1)}, u32[]{:S(2)}, u32[]{:S(2)}) collective-permute-start(bf16[64,1024]{1,0:T(8,128)(2,1)S(1)} %collective-permute-done.2.refs_2_), channel_id=1, source_target_pairs={{1,0},{0,1},{3,2},{2,3},{5,4},{4,5},{7,6},{6,7},{9,8},{8,9},{11,10... | collective-permute-start | bytes 393224 | tf_op jit(solution)/shard_map/ppermute | solution.py:30
  19.3 14.0 %collective-permute-start.9 = (bf16[512,256]{1,0:T(8,128)(2,1)S(1)}, bf16[512,256]{1,0:T(8,128)(2,1)S(1)}, u32[]{:S(2)}, u32[]{:S(2)}) collective-permute-start(bf16[512,256]{1,0:T(8,128)(2,1)S(1)} %get-tuple-element.98), channel_id=1, source_target_pairs={{4,0},{0,4},{12,8},{8,12},{5,1},{1,5},{13,9},{9,13},{6,2},{2,6},{1... | collective-permute-start | bytes 786440 | tf_op jit(solution)/shard_map/ppermute | solution.py:30
  19.9 21.2 %collective-permute-start.10 = (bf16[512,256]{1,0:T(8,128)(2,1)S(1)}, bf16[512,256]{1,0:T(8,128)(2,1)S(1)}, u32[]{:S(2)}, u32[]{:S(2)}) collective-permute-start(bf16[512,256]{1,0:T(8,128)(2,1)S(1)} %get-tuple-element.99.refs_8_.refs_0_), channel_id=1, source_target_pairs={{8,0},{12,4},{0,8},{4,12},{9,1},{13,5},{1,9},{5,13},{10,2},{14,6},... | collective-permute-start | bytes 786440 | tf_op jit(solution)/shard_map/ppermute | solution.py:30
  24.3 2.5 %collective-permute-start.6 = (bf16[272,256]{1,0:T(8,128)(2,1)S(1)}, bf16[272,256]{1,0:T(8,128)(2,1)S(1)}, u32[]{:S(2)}, u32[]{:S(2)}) collective-permute-start(bf16[272,256]{1,0:T(8,128)(2,1)S(1)} %get-tuple-element.94), channel_id=1, source_target_pairs={{1,0},{0,1},{3,2},{2,3},{5,4},{4,5},{7,6},{6,7},{9,8},{8,9},{11,10... | collective-permute-start | bytes 417800 | tf_op jit(solution)/shard_map/ppermute | solution.py:30
  24.4 20.2 %collective-permute-start.12 = (bf16[512,256]{1,0:T(8,128)(2,1)S(1)}, bf16[512,256]{1,0:T(8,128)(2,1)S(1)}, u32[]{:S(2)}, u32[]{:S(2)}) collective-permute-start(bf16[512,256]{1,0:T(8,128)(2,1)S(1)} %get-tuple-element.98), channel_id=1, source_target_pairs={{12,0},{8,4},{4,8},{0,12},{13,1},{9,5},{5,9},{1,13},{14,2},{10,6},... | collective-permute-start | bytes 786440 | tf_op jit(solution)/shard_map/ppermute | solution.py:30
  41.2 6.0 %collective-permute-start.11 = (bf16[272,256]{1,0:T(8,128)(2,1)S(1)}, bf16[272,256]{1,0:T(8,128)(2,1)S(1)}, u32[]{:S(2)}, u32[]{:S(2)}) collective-permute-start(bf16[272,256]{1,0:T(8,128)(2,1)S(1)} %get-tuple-element.101.refs_0_), channel_id=1, source_target_pairs={{18,0},{16,2},{2,16},{0,18},{19,1},{17,3},{3,17},{1,19},{22,4},{20... | collective-permute-start | bytes 417800 | tf_op jit(solution)/shard_map/ppermute | solution.py:30
  43.6 5.1 %collective-permute-start.7 = (bf16[272,256]{1,0:T(8,128)(2,1)S(1)}, bf16[272,256]{1,0:T(8,128)(2,1)S(1)}, u32[]{:S(2)}, u32[]{:S(2)}) collective-permute-start(bf16[272,256]{1,0:T(8,128)(2,1)S(1)} %get-tuple-element.101.refs_0_), channel_id=1, source_target_pairs={{2,0},{0,2},{3,1},{1,3},{6,4},{4,6},{7,5},{5,7},{10,8},{8,10},{11,... | collective-permute-start | bytes 417800 | tf_op jit(solution)/shard_map/ppermute | solution.py:30
  44.2 5.1 %collective-permute-start.8 = (bf16[272,256]{1,0:T(8,128)(2,1)S(1)}, bf16[272,256]{1,0:T(8,128)(2,1)S(1)}, u32[]{:S(2)}, u32[]{:S(2)}) collective-permute-start(bf16[272,256]{1,0:T(8,128)(2,1)S(1)} %get-tuple-element.101.refs_0_), channel_id=1, source_target_pairs={{16,0},{0,16},{17,1},{1,17},{18,2},{2,18},{19,3},{3,19},{20,4},{4,... | collective-permute-start | bytes 417800 | tf_op jit(solution)/shard_map/ppermute | solution.py:30
  49.2 1.4 %collective-permute-start.13 = (bf16[272,256]{1,0:T(8,128)(2,1)S(1)}, bf16[272,256]{1,0:T(8,128)(2,1)S(1)}, u32[]{:S(2)}, u32[]{:S(2)}) collective-permute-start(bf16[272,256]{1,0:T(8,128)(2,1)S(1)} %get-tuple-element.101.refs_0_), channel_id=1, source_target_pairs={{1,0},{0,1},{3,2},{2,3},{5,4},{4,5},{7,6},{6,7},{9,8},{8,9},{11,10... | collective-permute-start | bytes 417800 | tf_op jit(solution)/shard_map/ppermute | solution.py:30
  49.2 1.6 %collective-permute-start.14 = (bf16[272,256]{1,0:T(8,128)(2,1)S(1)}, bf16[272,256]{1,0:T(8,128)(2,1)S(1)}, u32[]{:S(2)}, u32[]{:S(2)}) collective-permute-start(bf16[272,256]{1,0:T(8,128)(2,1)S(1)} %collective-permute-done.7.refs_2_), channel_id=1, source_target_pairs={{1,0},{0,1},{3,2},{2,3},{5,4},{4,5},{7,6},{6,7},{9,8},{8,9},{11,10... | collective-permute-start | bytes 417800 | tf_op jit(solution)/shard_map/ppermute | solution.py:30
  49.7 1.4 %collective-permute-start.15 = (bf16[272,256]{1,0:T(8,128)(2,1)S(1)}, bf16[272,256]{1,0:T(8,128)(2,1)S(1)}, u32[]{:S(2)}, u32[]{:S(2)}) collective-permute-start(bf16[272,256]{1,0:T(8,128)(2,1)S(1)} %collective-permute-done.8.refs_4_), channel_id=1, source_target_pairs={{1,0},{0,1},{3,2},{2,3},{5,4},{4,5},{7,6},{6,7},{9,8},{8,9},{11,10... | collective-permute-start | bytes 417800 | tf_op jit(solution)/shard_map/ppermute | solution.py:30
  49.7 1.6 %collective-permute-start.16 = (bf16[272,256]{1,0:T(8,128)(2,1)S(1)}, bf16[272,256]{1,0:T(8,128)(2,1)S(1)}, u32[]{:S(2)}, u32[]{:S(2)}) collective-permute-start(bf16[272,256]{1,0:T(8,128)(2,1)S(1)} %collective-permute-done.11.refs_6_), channel_id=1, source_target_pairs={{1,0},{0,1},{3,2},{2,3},{5,4},{4,5},{7,6},{6,7},{9,8},{8,9},{11,10... | collective-permute-start | bytes 417800 | tf_op jit(solution)/shard_map/ppermute | solution.py:30
  52.9 2.0 %collective-permute-start.17 = (bf16[256,1024]{1,0:T(8,128)(2,1)S(1)}, bf16[256,1024]{1,0:T(8,128)(2,1)S(1)}, u32[]{:S(2)}, u32[]{:S(2)}) collective-permute-start(bf16[256,1024]{1,0:T(8,128)(2,1)S(1)} %get-tuple-element.111), channel_id=1, source_target_pairs={{1,0},{0,1},{3,2},{2,3},{5,4},{4,5},{7,6},{6,7},{9,8},{8,9},{11,10... | collective-permute-start | bytes 1572872 | tf_op jit(solution)/shard_map/ppermute | solution.py:30
  55.0 4.9 %collective-permute-start.18 = (bf16[128,512]{1,0:T(8,128)(2,1)S(1)}, bf16[128,512]{1,0:T(8,128)(2,1)S(1)}, u32[]{:S(2)}, u32[]{:S(2)}) collective-permute-start(bf16[128,512]{1,0:T(8,128)(2,1)S(1)} %get-tuple-element.112), channel_id=1, source_target_pairs={{0,0},{1,17},{2,2},{3,19},{4,4},{5,21},{6,6},{7,23},{8,8},{9,25},{... | collective-permute-start | bytes 393224 | tf_op jit(solution)/shard_map/ppermute | solution.py:284
  55.7 5.0 %collective-permute-start.19 = (bf16[128,512]{1,0:T(8,128)(2,1)S(1)}, bf16[128,512]{1,0:T(8,128)(2,1)S(1)}, u32[]{:S(2)}, u32[]{:S(2)}) collective-permute-start(bf16[128,512]{1,0:T(8,128)(2,1)S(1)} %get-tuple-element.113), channel_id=1, source_target_pairs={{0,2},{1,19},{2,0},{3,17},{4,6},{5,23},{6,4},{7,21},{8,10},{9,27},... | collective-permute-start | bytes 393224 | tf_op jit(solution)/shard_map/ppermute | solution.py:284
  57.2 5.0 %collective-permute-start.20 = (bf16[128,512]{1,0:T(8,128)(2,1)S(1)}, bf16[128,512]{1,0:T(8,128)(2,1)S(1)}, u32[]{:S(2)}, u32[]{:S(2)}) collective-permute-start(bf16[128,512]{1,0:T(8,128)(2,1)S(1)} %get-tuple-element.114), channel_id=1, source_target_pairs={{0,4},{1,21},{2,6},{3,23},{4,0},{5,17},{6,2},{7,19},{8,12},{9,29},... | collective-permute-start | bytes 393224 | tf_op jit(solution)/shard_map/ppermute | solution.py:284
  57.2 7.2 %collective-permute-start.21 = (bf16[128,512]{1,0:T(8,128)(2,1)S(1)}, bf16[128,512]{1,0:T(8,128)(2,1)S(1)}, u32[]{:S(2)}, u32[]{:S(2)}) collective-permute-start(bf16[128,512]{1,0:T(8,128)(2,1)S(1)} %get-tuple-element.115), channel_id=1, source_target_pairs={{0,6},{1,23},{2,4},{3,21},{4,2},{5,19},{6,0},{7,17},{8,14},{9,31},... | collective-permute-start | bytes 393224 | tf_op jit(solution)/shard_map/ppermute | solution.py:284
  64.6 3.1 %collective-permute-start.22 = (bf16[128,256]{1,0:T(8,128)(2,1)S(1)}, bf16[128,256]{1,0:T(8,128)(2,1)S(1)}, u32[]{:S(2)}, u32[]{:S(2)}) collective-permute-start(bf16[128,256]{1,0:T(8,128)(2,1)S(1)} %get-tuple-element.118), channel_id=1, source_target_pairs={{1,0},{0,1},{3,2},{2,3},{5,4},{4,5},{7,6},{6,7},{9,8},{8,9},{11,10... | collective-permute-start | bytes 196616 | tf_op jit(solution)/shard_map/ppermute | solution.py:30

commit v6 on v5

v6 whole, which is shorter than its diff:
```python
import functools
import itertools

import jax
import jax.numpy as jnp
import numpy as np
from jax import lax
from jax.experimental import pallas as pl
from jax.experimental.pallas import tpu as pltpu
from jax.sharding import PartitionSpec as P

BF, F32 = jnp.bfloat16, jnp.float32


def dot(a, b, dims=((1,), (0,))):
    return lax.dot_general(a, b, (dims, ((), ())), preferred_element_type=F32)


def moved(x, groups=0, tok=0, head=0, rep=0):
    shifts = {"groups": groups, "tok": tok, "head": head, "rep": rep}
    axes = [a for a, s in shifts.items() if s]
    if not axes:
        return x
    sizes = [lax.axis_size(a) for a in axes]
    pairs = []
    for here in range(int(np.prod(sizes))):
        at = np.unravel_index(here, sizes)
        there = [i ^ tok if a == "tok" else (i + shifts[a]) % n for a, i, n in zip(axes, at, sizes)]
        pairs.append((int(np.ravel_multi_index(there, sizes)), here))
    return lax.ppermute(x, tuple(axes), pairs)


def shape(dims, dtype):
    return jax.ShapeDtypeStruct(dims, dtype)


def call(kernel, outs, args, scratch=(), fetched=0, unmoved=0):
    touched = sum(int(np.prod(x.shape)) * x.dtype.itemsize for x in (*args, *outs))
    kept = sum(int(np.prod(x.shape)) * 4 for x in scratch if hasattr(x, "shape"))
    args = [pltpu.with_memory_space_constraint(x, pltpu.HBM) if i < fetched else x for i, x in enumerate(args)]
    return pl.pallas_call(
        kernel,
        out_shape=outs,
        in_specs=[pl.BlockSpec(memory_space=pltpu.HBM if i < fetched + unmoved else pltpu.VMEM) for i in range(len(args))],
        out_specs=[pl.BlockSpec(memory_space=pltpu.VMEM)] * len(outs),
        scratch_shapes=list(scratch),
        compiler_params=pltpu.CompilerParams(vmem_limit_bytes=touched + kept + (10 << 20)),
        cost_estimate=pl.CostEstimate(flops=1, bytes_accessed=1, transcendentals=0),
    )(*args)


def local(arrays):
    return [pltpu.VMEM(x.shape, x.dtype) for x in arrays]


def window(index, size):
    return pl.ds(pl.multiple_of(index * size, size), size)


def fetch(pairs, sems):
    copies = [pltpu.make_async_copy(src, dst, sems.at[i]) for i, (src, dst) in enumerate(pairs)]
    for c in copies:
        c.start()
    return copies


def side_by_side(pair, keys, values, rates):
    n, dh = keys.shape
    pair[:, :dh] = keys[...]
    rate = jnp.broadcast_to(rates[...], (128, n)).T
    for c in range(0, dh, 128):
        pair[:, dh + c : dh + c + 128] = (values[:, c : c + 128].astype(F32) * rate).astype(BF)


def message_kernel(n_far, *refs):
    far, refs = refs[:n_far], refs[n_far:]
    outs, near, (pair, sems) = refs[: -n_far - 2], refs[-n_far - 2 : -2], refs[-2:]
    for c in fetch(list(zip(far, near)), sems):
        c.wait()
    side_by_side(pair, *near[:3])
    if len(outs) == 1:
        outs[0][...] = pair[...]
        return
    share, full = outs
    q, s = near[3:]
    me, (rows, width) = lax.axis_index("rep"), share.shape
    part = pair[window(me, rows), :]
    share[...] = part
    full[:, :width] = part
    dh = width // 2
    full[:, width : width + dh] = q[window(me, rows), :]
    wide = dh // 2
    for i in range(q.shape[0] // rows):
        at = width + dh + i * wide
        full[:, at : at + wide] = s[i * rows : (i + 1) * rows, window(me, wide)]


def pack_kernel(up, down, out):
    deep, wide = up.shape[0], out.shape[2]
    for t in range(out.shape[0]):
        part = window(lax.axis_index("groups") * 2 + t % 2, wide)
        out[t, :deep, :] = up[:, part]
        out[t, deep:, :] = down[part, :]


def gradients(k, e, w1b, w3b, w2b):
    a1, a3, b = dot(k, w1b), dot(k, w3b), dot(e, w2b, ((1,), (1,)))
    sig = jax.nn.sigmoid(a1)
    act = a1 * sig
    g = (act * a3).astype(BF)
    r1 = (b * a3 * (sig * (1.0 + a1 * (1.0 - sig)))).astype(BF)
    r3 = (b * act).astype(BF)
    first = ((0,), (0,))
    return dot(k, r1, first), dot(k, r3, first), dot(g, e, first)


def squares(x):
    return jnp.sum(x * x, axis=0, keepdims=True)


def fast_kernel(n_pieces, near, *refs):
    far, refs = refs[:7], refs[7:]
    pieces, refs = refs[:n_pieces], refs[n_pieces:]
    own_out, own_sq, send, ks, es, hp, qs, pair, *local, sems = refs
    w1, w3, w2, keys, values, rates, q = local
    copies = fetch(list(zip(far, local)), sems)
    dh, hidden = w1.shape
    me = lax.axis_index("rep")
    n = q.shape[0]
    at = 0
    for p in pieces:
        rows = p.shape[0]
        ks[at : at + rows, :] = p[:, :dh]
        es[at : at + rows, :] = p[:, dh : 2 * dh]
        at += rows
    if near > 1:
        mine, theirs = pieces[0], pieces[n_pieces // 2]
        rows = mine.shape[0]
        qs[pl.ds(pl.multiple_of(n + me * rows, rows), rows), :] = mine[:, 2 * dh : 3 * dh]
        qs[pl.ds(pl.multiple_of(n + (1 - me) * rows, rows), rows), :] = theirs[:, 2 * dh : 3 * dh]
    for c in copies[3:]:
        c.wait()
    if near > 1:
        side_by_side(pair, keys, values, rates)
        ks[at : at + n, :] = pair[:, :dh]
        es[at : at + n, :] = pair[:, dh:]
        at += n
    qs[:n, :] = q[...]
    asked = qs[...]
    tokens, step, block = at, min(at, 512), min(hidden, 256)
    for c in copies[:3]:
        c.wait()
    old_sq = squares(w2[...])
    new_sq = jnp.zeros((1, dh), F32)
    for j in range(0, hidden, block):
        js = slice(j, j + block)
        x1, x3, x2 = w1[:, js], w3[:, js], w2[js, :]
        b1, b3, b2 = x1.astype(BF), x3.astype(BF), x2.astype(BF)

        def add(i, sums):
            rows = pl.ds(pl.multiple_of(i * step, step), step)
            return tuple(s + p for s, p in zip(sums, gradients(ks[rows, :], es[rows, :], b1, b3, b2)))

        sums = (x1, x3, x2)
        sums = add(0, sums) if tokens == step else lax.fori_loop(0, tokens // step, add, sums)

        def normed(old, new):
            return (new * (jnp.sqrt(squares(old)) * lax.rsqrt(squares(new) + 1e-06))).astype(BF)

        new_sq = new_sq + squares(sums[2])
        qa, qc = dot(asked, normed(x1, sums[0])), dot(asked, normed(x3, sums[1]))
        part = dot((qa * jax.nn.sigmoid(qa) * qc).astype(BF), sums[2].astype(BF))
        hp[...] = part if j == 0 else hp[...] + part
    rows, wide = own_out.shape
    own_out[...] = hp[:, window(me, wide)]
    send[:rows, :] = hp[:, window(1 - me, wide)].astype(BF)
    row = lax.broadcasted_iota(jnp.int32, (8, dh), 0)
    hp[:8, :] = jnp.where(row == 0, old_sq, jnp.where(row == 1, new_sq, 0.0))
    own_sq[...] = hp[:8, window(me, wide)]
    sq = hp[:8, window(1 - me, wide)]
    top = sq.astype(BF).astype(F32)
    send[rows:, :] = jnp.concatenate([top, sq - top], axis=0).astype(BF)


def mix_kernel(stream_far, gain_far, own, own_sq, got, *refs):
    *asks, mixed, low, stream, gain, sems = refs
    copies = fetch([(stream_far, stream), (gain_far, gain)], sems)
    n, wide = mixed.shape
    rows, me = own.shape[0], lax.axis_index("rep")
    tail = got[rows:, :].astype(F32)
    sq = own_sq[...] + tail[:8] + tail[8:]
    y = (own[...] + got[:rows, :].astype(F32)) * (jnp.sqrt(sq[0:1]) * lax.rsqrt(sq[1:2] + 1e-06))
    for c in copies:
        c.wait()
    mixed[...] = y[:n] + stream[:, window(me, wide)].astype(F32)
    low[:n, :] = mixed[...].astype(BF)
    for message in asks:
        part = message.shape[0]
        for i in range(n // part):
            at, there = n + i * part, message.shape[1] - n // part * wide + i * wide
            low[at : at + part, :] = (y[at : at + part] + message[:, there : there + wide].astype(F32)).astype(BF)
    x = jnp.broadcast_to(gain[:, window(me, wide)], (16, wide))
    row = lax.broadcasted_iota(jnp.int32, x.shape, 0)
    top = x.astype(BF).astype(F32)
    mid = (x - top).astype(BF).astype(F32)
    low[rows:, :] = jnp.where(row == 0, top, jnp.where(row == 1, mid, jnp.where(row == 2, x - top - mid, 0.0))).astype(BF)


def norm_kernel(places, *refs):
    pieces, zs = refs[:-1], refs[-1]
    me_h, me_r = lax.axis_index("head"), lax.axis_index("rep")
    n_head = lax.axis_size("head")
    n, wide = pieces[0].shape[0] - 16, pieces[0].shape[1]
    for dg in range(lax.axis_size("groups")):
        here = [(p, dh, dr) for p, (g, dh, dr) in zip(pieces, places) if g == dg]
        norm = jnp.zeros((n, 1), F32)
        for p, _, _ in here:
            x = p[:n, :].astype(F32)
            norm = norm + jnp.sum(x * x, axis=1, keepdims=True)
        inv = lax.rsqrt(norm / zs.shape[1] + 1e-06)
        for p, dh, dr in here:
            r = lax.rem(me_r + dr, 2)
            head = lax.rem(me_h + dh, n_head)
            gain = jnp.sum(p[n:, :].astype(F32), axis=0, keepdims=True)
            zs[dg * n : (dg + 1) * n, window(head * 2 + r, wide)] = (p[:n, :].astype(F32) * inv * gain).astype(BF)


def blocks_of(mlp, width):
    if len(mlp) > 1:
        return [mlp[0]], [mlp[1]]
    deep = width // mlp[0].shape[0]
    each = range(mlp[0].shape[0])
    return [mlp[0].at[t, :deep, :] for t in each], [mlp[0].at[t, deep:, :] for t in each]


def feed(z, ups, downs, os, wait=lambda: None):
    deep = z.shape[1] // len(ups)
    total = None
    for t, x in enumerate(ups):
        term = dot(z[:, t * deep : (t + 1) * deep], x[...])
        total = term if total is None else total + term
    h = (0.5 * total * (1.0 + lax.erf(total * np.float32(0.5**0.5)))).astype(BF)
    wait()
    for t, x in enumerate(downs):
        os[:, t * deep : (t + 1) * deep] = dot(h, x[...])


def turned(os, out):
    n_head = lax.axis_size("head")
    part = os.shape[1] // n_head
    for dh in range(n_head):
        cols = window(lax.rem(lax.axis_index("head") + dh, n_head), part)
        out[:, dh * part : (dh + 1) * part] = os[:, cols].astype(out.dtype)


def theirs_kernel(n_mlp, *refs):
    far, (zs, send, *near), (os, sems) = refs[:n_mlp], refs[n_mlp:-2], refs[-2:]
    width = zs.shape[1]
    pairs = [p for f, n in zip(blocks_of(far, width), blocks_of(near, width)) for p in zip(f, n)]
    copies = fetch(pairs, sems)
    ups, downs = blocks_of(near, width)
    for c in copies[: len(ups)]:
        c.wait()

    def rest():
        for c in copies[len(ups) :]:
            c.wait()

    rows = send.shape[0]
    feed(zs[window(1 - lax.axis_index("rep"), rows), :], ups, downs, os, rest)
    turned(os, send)


def ours_kernel(zs, *refs):
    *mlp, own, os = refs
    ups, downs = blocks_of(mlp, zs.shape[1])
    feed(zs[window(lax.axis_index("rep"), own.shape[0]), :], ups, downs, os)
    turned(os, own)


def pair_kernel(moves, own, got, *outs):
    n, wide = outs[0].shape
    for (dz, dh), out in zip(moves, outs):
        rows, cols = slice(dz * n, (dz + 1) * n), slice(dh * wide, (dh + 1) * wide)
        out[...] = (own[rows, cols] + got[rows, cols].astype(F32)).astype(BF)


def sum_kernel(*refs):
    *parts, mixed, keep, send, acc = refs
    total = parts[0][...].astype(F32)
    for p in parts[1:]:
        total = total + p[...].astype(F32)
    acc[...] = total
    me, wide = lax.axis_index("rep"), keep.shape[1]
    keep[...] = mixed[...] + acc[:, window(me, wide)]
    send[...] = acc[:, window(1 - me, wide)].astype(BF)


def dealt(x, tok, head):
    axes = ("groups", "tok", "head", "rep")
    sizes = [lax.axis_size(a) for a in axes]
    pairs = []
    for here in range(int(np.prod(sizes))):
        g, t, h, r = np.unravel_index(here, sizes)
        there = ((g + r) % sizes[0], t ^ tok, (h + head) % sizes[2], r)
        pairs.append((here, int(np.ravel_multi_index(there, sizes))))
    return lax.ppermute(x, axes, pairs)


def on_device(
    keys, values, rates, queries, stream, gain, counts, fw_one, fw_three, fw_two, mlp_up, mlp_down
):
    n_tok, n_head = lax.axis_size("tok"), lax.axis_size("head")
    groups, reps = lax.axis_size("groups"), lax.axis_size("rep")
    dh, n_key, n = keys.shape[1], keys.shape[0], queries.shape[0]
    wide = dh // reps
    paired = n_tok == 4 and n_key == n
    near = 2 if paired else 1
    units = mlp_up.shape[1] // groups // near
    barrier = lax.optimization_barrier

    rows = n_key // reps
    rate_row, gain = rates.reshape(1, n_key), gain[None, :]
    sources = [keys, values, rate_row]
    outs = [shape((n_key, 2 * dh), BF)]
    if paired:
        sources += [queries, stream]
        outs = [shape((rows, 2 * dh), BF), shape((rows, 4 * dh), BF)]
    messages = call(
        functools.partial(message_kernel, len(sources)),
        outs,
        sources,
        [*local(sources), pltpu.VMEM((n_key, 2 * dh), BF), pltpu.SemaphoreType.DMA((len(sources),))],
        fetched=len(sources),
    )
    asks = []
    if paired:
        share, full = messages
        others = [moved(full, tok=1), moved(share, tok=2), moved(share, tok=3)]
        (blocks,) = call(
            pack_kernel, [shape((n_tok, mlp_up.shape[0] + units, units), BF)], [mlp_up, mlp_down]
        )
        others, blocks = barrier((others, blocks))
        mlp = [lax.all_to_all(blocks, "tok", 0, 0)]
        tokens = [*others, *[moved(x, rep=1) for x in others]]
        asks = others[:1]
    else:
        me_g = lax.axis_index("groups")
        up_own = lax.dynamic_slice_in_dim(mlp_up, me_g * units, units, 1)
        down_own = lax.dynamic_slice_in_dim(mlp_down, me_g * units, units, 0)
        tokens = [lax.all_gather(messages[0], "tok", axis=0, tiled=True)]
        mlp = [
            lax.all_gather(up_own, "tok", axis=0, tiled=True),
            lax.all_gather(down_own, "tok", axis=1, tiled=True),
        ]

    n_all = sum(x.shape[0] for x in tokens) + (n_key if paired else 0)
    tokens = barrier(tokens)
    sources = [fw_one[0], fw_three[0], fw_two[0], keys, values, rate_row, queries]
    own, own_sq, send = call(
        functools.partial(fast_kernel, len(tokens), near),
        [shape((near * n, wide), F32), shape((8, wide), F32), shape((near * n + 16, wide), BF)],
        [*sources, *tokens],
        [
            pltpu.VMEM((n_all, dh), BF),
            pltpu.VMEM((n_all, dh), BF),
            pltpu.VMEM((near * n, dh), F32),
            pltpu.VMEM((near * n, dh), BF),
            pltpu.VMEM((n_key, 2 * dh), BF),
            *local(sources),
            pltpu.SemaphoreType.DMA((len(sources),)),
        ],
        fetched=len(sources),
    )
    got = moved(send, rep=1)
    sources = [stream, gain]
    mixed, low = call(
        mix_kernel,
        [shape((n, wide), F32), shape((near * n + 16, wide), BF)],
        [*sources, own, own_sq, got, *asks],
        [*local(sources), pltpu.SemaphoreType.DMA((2,))],
        fetched=2,
    )
    pieces, places = [], []
    for dg, h in itertools.product(range(groups), range(n_head)):
        x = moved(low, groups=dg, head=h)
        pieces += [x, moved(x, rep=1)]
        places += [(dg, h, 0), (dg, h, 1)]
    model = n_head * dh
    (zs,) = call(
        functools.partial(norm_kernel, places), [shape((groups * near * n, model), BF)], pieces
    )
    send, *mlp = call(
        functools.partial(theirs_kernel, len(mlp)),
        [shape((near * n, model), BF), *[shape(x.shape, BF) for x in mlp]],
        [*mlp, zs],
        [pltpu.VMEM((near * n, model), F32), pltpu.SemaphoreType.DMA((2 * n_tok if paired else 2,))],
        unmoved=len(mlp),
    )
    got = moved(send, rep=1)
    (own,) = call(
        ours_kernel, [shape((near * n, model), F32)], [zs, *mlp], [pltpu.VMEM((near * n, model), F32)]
    )
    moves = list(itertools.product(range(near), range(n_head)))
    parts = call(
        functools.partial(pair_kernel, moves), [shape((n, dh), BF)] * len(moves), [own, got]
    )
    parts = [dealt(x, *m) for m, x in zip(moves, parts)]
    keep, send = call(
        sum_kernel, [shape((n, wide), F32), shape((n, wide), BF)], [*parts, mixed], [pltpu.VMEM((n, dh), F32)]
    )
    total = keep + moved(send, rep=1).astype(F32)
    live = jnp.arange(n, dtype=jnp.int32) < counts[0]
    return jnp.where(live[:, None], total, 0.0).astype(BF)


def solution(mesh):
    placed = (
        P(("groups", "tok"), "head"),
        P(("groups", "tok"), "head"),
        P(("groups", "tok"), "head"),
        P(("groups", "tok"), "head"),
        P(("groups", "tok"), "head"),
        P("head"),
        P(("groups", "tok")),
        P("head", None, "rep"),
        P("head", None, "rep"),
        P("head", "rep", None),
        P("tok", ("head", "rep")),
        P(("head", "rep"), "tok"),
    )
    return jax.shard_map(
        on_device,
        mesh=mesh,
        in_specs=placed,
        out_specs=P(("groups", "tok"), ("head", "rep")),
        check_vma=False,
    )
```

time: 68.7 us -> 66 us (0.961)
  Pallas kernels: 7.81 us -> 12.8 us
  waiting for transfers between devices: 33.6 us -> 29.3 us
  local copies, waits for them, and re-layouts: 3.5 us -> 1.05 us
  starting transfers between devices: 22 us -> 21.1 us
    ppermute x19 -> x16, waiting for transfers between devices: 29 us -> 21.8 us  [moved(): return lax.ppermute(x, tuple(axes), pairs)]
    pallas_call x9, Pallas kernels: 7.81 us -> 12.8 us  [call(): pl.pallas_call(kernel, out_shape=outs, in_specs=[pl.BlockSpec(memory_spac...]
    ppermute x19 -> x16, starting transfers between devices: 17.8 us -> 13.3 us  [moved(): return lax.ppermute(x, tuple(axes), pairs)]
    all_to_all x0 -> x1, starting transfers between devices: none -> 3.52 us  [on_device(): mlp = [lax.all_to_all(blocks, 'tok', 0, 0)]]
    all_to_all x0 -> x1, waiting for transfers between devices: none -> 3.34 us  [on_device(): mlp = [lax.all_to_all(blocks, 'tok', 0, 0)]]
    unnamed x12 -> x4, local copies, waits for them, and re-layouts: 3.5 us -> 1.05 us
  transfers between devices with their start and end apart: 23 -> 21, of which waited for: 16 -> 16; matrix products, arithmetic and copies ran while one was open for 0% -> 0% of each run, Pallas kernels for 7% -> 13%
where the time goes in v6:
time: 66 us; the launch traced here: 65.7 us
  waiting for transfers between devices  29.3 us (44%)
  starting transfers between devices  21.1 us (32%)
  Pallas kernels  12.8 us (19%)
  local copies, waits for them, and re-layouts  1.05 us (2%)
  between operations  0.77 us (1%)
  other arithmetic  0.72 us (1%)
    ppermute x16, waiting for transfers between devices, moved(): return lax.ppermute(x, tuple(axes), pairs)  21.8 us
    ppermute x16, starting transfers between devices, moved(): return lax.ppermute(x, tuple(axes), pairs)  13.3 us
    pallas_call x9, Pallas kernels, call(): pl.pallas_call(kernel, out_shape=outs, in_specs=[pl.BlockSpec(memory_spac...  12.8 us
    ppermute x4, starting transfers between devices, dealt(): return lax.ppermute(x, axes, pairs)  4.22 us
    ppermute x4, waiting for transfers between devices, dealt(): return lax.ppermute(x, axes, pairs)  4.16 us
    all_to_all x1, starting transfers between devices, on_device(): mlp = [lax.all_to_all(blocks, 'tok', 0, 0)]  3.52 us
    all_to_all x1, waiting for transfers between devices, on_device(): mlp = [lax.all_to_all(blocks, 'tok', 0, 0)]  3.34 us
  transfers between devices with their start and end apart: 21, of which 16 were waited for; matrix products, arithmetic and copies ran while one was open for 0% of the time, Pallas kernels for 13%

profile of v6, /device:TPU:0, one launch (start us, length us, event | category | flops | bytes accessed | tf_op | source)
XLA Modules:
  0.0 65.7 jit_solution(15756395728740357903)
XLA Ops:
  0.0 0.0 copy-start
  0.0 1.3 %shard_map.118 = (bf16[64,1024]{1,0:T(8,128)(2,1)S(1)}, bf16[64,2048]{1,0:T(8,128)(2,1)S(1)}) custom-call(bf16[128,512]{1,0:T(8,128)(2,1)} %refs_3_.3, bf16[128,512]{1,0:T(8,128)(2,1)} %refs_4_.3, f32[1,128]{1,0:T(1,128)} %bitcast.11, bf16[128,512]{1,0:T(8,128)(2,1)} %refs_6_.1, bf16[128,512]{1,0:T(8,128)(2,1)} %stream_far.1), custom_call_target="tpu_custom_call" | custom-call | flops 1 | bytes 1 | tf_op jit(solution)/shard_map/pallas_call | solution.py:41
  1.3 3.1 %collective-permute-start = (bf16[64,2048]{1,0:T(8,128)(2,1)S(1)}, bf16[64,2048]{1,0:T(8,128)(2,1)S(1)}, u32[]{:S(2)}, u32[]{:S(2)}) collective-permute-start(bf16[64,2048]{1,0:T(8,128)(2,1)S(1)} %get-tuple-element.30), channel_id=1, source_target_pairs={{4,0},{0,4},{12,8},{8,12},{5,1},{1,5},{13,9},{9,13},{6,2},{2,6},{1... | collective-permute-start | bytes 786440 | tf_op jit(solution)/shard_map/ppermute | solution.py:30
  4.4 2.6 %collective-permute-start.1 = (bf16[64,1024]{1,0:T(8,128)(2,1)S(1)}, bf16[64,1024]{1,0:T(8,128)(2,1)S(1)}, u32[]{:S(2)}, u32[]{:S(2)}) collective-permute-start(bf16[64,1024]{1,0:T(8,128)(2,1)S(1)} %get-tuple-element.31), channel_id=1, source_target_pairs={{8,0},{12,4},{0,8},{4,12},{9,1},{13,5},{1,9},{5,13},{10,2},{14,6},... | collective-permute-start | bytes 393224 | tf_op jit(solution)/shard_map/ppermute | solution.py:30
  7.0 0.0 collective-permute-start.2
  7.0 0.0 copy-done
  7.0 0.0 copy-start.1
  7.0 1.0 %copy-done.1 = bf16[1024,256]{1,0:T(8,128)(2,1)S(1)} copy-done((bf16[1024,256]{1,0:T(8,128)(2,1)S(1)}, bf16[1024,256]{1,0:T(8,128)(2,1)}, u32[]{:S(2)}) %copy-start.1) | copy-done | bytes 524312
  8.1 1.1 %shard_map.119 = bf16[4,512,256]{2,1,0:T(8,128)(2,1)} custom-call(bf16[256,1024]{1,0:T(8,128)(2,1)S(1)} %copy-done, bf16[1024,256]{1,0:T(8,128)(2,1)S(1)} %copy-done.1), custom_call_target="tpu_custom_call" | custom-call | flops 1 | bytes 1 | tf_op jit(solution)/shard_map/pallas_call | solution.py:41
  9.1 4.9 %collective-permute-done.1.refs_8_ = bf16[64,1024]{1,0:T(8,128)(2,1)S(1)} collective-permute-done((bf16[64,1024]{1,0:T(8,128)(2,1)S(1)}, bf16[64,1024]{1,0:T(8,128)(2,1)S(1)}, u32[]{:S(2)}, u32[]{:S(2)}) %collective-permute-start.1) | collective-permute-done | bytes 131104 | tf_op jit(solution)/shard_map/ppermute | solution.py:30
  14.0 4.7 %collective-permute-done.2.refs_9_ = bf16[64,1024]{1,0:T(8,128)(2,1)S(1)} collective-permute-done((bf16[64,1024]{1,0:T(8,128)(2,1)S(1)}, bf16[64,1024]{1,0:T(8,128)(2,1)S(1)}, u32[]{:S(2)}, u32[]{:S(2)}) %collective-permute-start.2) | collective-permute-done | bytes 131104 | tf_op jit(solution)/shard_map/ppermute | solution.py:30
  18.7 0.0 collective-permute-done.refs_7_.refs_0_
  18.7 3.5 %all-to-all-start = ((bf16[4,512,256]{2,1,0:T(8,128)(2,1)}), bf16[4,512,256]{2,1,0:T(8,128)(2,1)S(1)}, u32[]{:S(2)}, u32[]{:S(2)}) async-start(bf16[4,512,256]{2,1,0:T(8,128)(2,1)} %shard_map.119), calls=%async_computation | async-start | bytes 2097152 | tf_op jit(solution)/shard_map/all_to_all | solution.py:344
  22.2 0.1 collective-permute-start.3
  22.3 0.5 collective-permute-start.4
  22.8 0.1 collective-permute-start.5
  22.8 1.1 %collective-permute-done.4.refs_11_ = bf16[64,1024]{1,0:T(8,128)(2,1)S(1)} collective-permute-done((bf16[64,1024]{1,0:T(8,128)(2,1)S(1)}, bf16[64,1024]{1,0:T(8,128)(2,1)S(1)}, u32[]{:S(2)}, u32[]{:S(2)}) %collective-permute-start.4) | collective-permute-done | bytes 131104 | tf_op jit(solution)/shard_map/ppermute | solution.py:30
  24.0 0.2 collective-permute-done.5.refs_12_
  24.2 0.0 collective-permute-done.3.refs_10_
  24.2 5.4 %shard_map.120 = (f32[256,256]{1,0:T(8,128)S(1)}, f32[8,256]{1,0:T(8,128)S(1)}, bf16[272,256]{1,0:T(8,128)(2,1)S(1)}) custom-call(f32[512,512]{1,0:T(8,128)} %bitcast.7, f32[512,512]{1,0:T(8,128)} %bitcast.8, f32[512,512]{1,0:T(8,128)} %bitcast.9, bf16[128,512]{1,0:T(8,128)(2,1)} %refs_3_.3, bf16[128,512]{1,0:T(8,128)(2,1)} %refs_4_.3, f32[1,128]{1,0:T(1,128)} %bitcast.12, ...), custom_call_target="tpu_custom_call" | custom-call | flops 1 | bytes 1 | tf_op jit(solution)/shard_map/pallas_call | solution.py:41
  29.6 0.2 collective-permute-start.6
  29.8 1.2 %collective-permute-done.6.got = bf16[272,256]{1,0:T(8,128)(2,1)S(1)} collective-permute-done((bf16[272,256]{1,0:T(8,128)(2,1)S(1)}, bf16[272,256]{1,0:T(8,128)(2,1)S(1)}, u32[]{:S(2)}, u32[]{:S(2)}) %collective-permute-start.6) | collective-permute-done | bytes 139296 | tf_op jit(solution)/shard_map/ppermute | solution.py:30
  31.0 1.0 %shard_map.121 = (f32[128,256]{1,0:T(8,128)S(1)}, bf16[272,256]{1,0:T(8,128)(2,1)S(1)}) custom-call(bf16[128,512]{1,0:T(8,128)(2,1)} %stream_far.1, f32[1,512]{1,0:T(1,128)} %bitcast.10, f32[256,256]{1,0:T(8,128)S(1)} %get-tuple-element.41.own, f32[8,256]{1,0:T(8,128)S(1)} %get-tuple-element.42.own_sq, bf16[272,256]{1,0:T(8,128)(2,1)S(1)} %collective-permute-done.6.got, ...), custom_call_target="tpu_custom_call" | custom-call | flops 1 | bytes 1 | tf_op jit(solution)/shard_map/pallas_call | solution.py:41
  32.0 1.6 %collective-permute-start.10 = (bf16[272,256]{1,0:T(8,128)(2,1)S(1)}, bf16[272,256]{1,0:T(8,128)(2,1)S(1)}, u32[]{:S(2)}, u32[]{:S(2)}) collective-permute-start(bf16[272,256]{1,0:T(8,128)(2,1)S(1)} %get-tuple-element.44.refs_0_), channel_id=1, source_target_pairs={{16,0},{0,16},{17,1},{1,17},{18,2},{2,18},{19,3},{3,19},{20,4},{4,... | collective-permute-start | bytes 417800 | tf_op jit(solution)/shard_map/ppermute | solution.py:30
  33.6 1.4 %collective-permute-start.12 = (bf16[272,256]{1,0:T(8,128)(2,1)S(1)}, bf16[272,256]{1,0:T(8,128)(2,1)S(1)}, u32[]{:S(2)}, u32[]{:S(2)}) collective-permute-start(bf16[272,256]{1,0:T(8,128)(2,1)S(1)} %get-tuple-element.44.refs_0_), channel_id=1, source_target_pairs={{18,0},{16,2},{2,16},{0,18},{19,1},{17,3},{3,17},{1,19},{22,4},{20... | collective-permute-start | bytes 417800 | tf_op jit(solution)/shard_map/ppermute | solution.py:30
  35.0 0.5 collective-permute-start.8
  35.5 0.0 collective-permute-start.7
  35.5 4.9 %collective-permute-done.10.refs_4_ = bf16[272,256]{1,0:T(8,128)(2,1)S(1)} collective-permute-done((bf16[272,256]{1,0:T(8,128)(2,1)S(1)}, bf16[272,256]{1,0:T(8,128)(2,1)S(1)}, u32[]{:S(2)}, u32[]{:S(2)}) %collective-permute-start.10) | collective-permute-done | bytes 139296 | tf_op jit(solution)/shard_map/ppermute | solution.py:30
  40.5 0.0 collective-permute-start.11
  40.5 0.5 collective-permute-done.12.refs_6_
  41.0 0.0 collective-permute-start.13
  41.0 1.0 %collective-permute-done.8.refs_2_ = bf16[272,256]{1,0:T(8,128)(2,1)S(1)} collective-permute-done((bf16[272,256]{1,0:T(8,128)(2,1)S(1)}, bf16[272,256]{1,0:T(8,128)(2,1)S(1)}, u32[]{:S(2)}, u32[]{:S(2)}) %collective-permute-start.8) | collective-permute-done | bytes 139296 | tf_op jit(solution)/shard_map/ppermute | solution.py:30
  42.0 0.0 collective-permute-start.9
  42.0 0.0 collective-permute-done.7.refs_1_
  42.0 0.0 collective-permute-done.11.refs_5_
  42.0 0.4 collective-permute-done.13.refs_7_
  42.4 1.0 %collective-permute-done.9.refs_3_ = bf16[272,256]{1,0:T(8,128)(2,1)S(1)} collective-permute-done((bf16[272,256]{1,0:T(8,128)(2,1)S(1)}, bf16[272,256]{1,0:T(8,128)(2,1)S(1)}, u32[]{:S(2)}, u32[]{:S(2)}) %collective-permute-start.9) | collective-permute-done | bytes 139296 | tf_op jit(solution)/shard_map/ppermute | solution.py:30
  43.3 0.5 shard_map.122.refs_1_.zs
  43.9 3.3 %all-to-all-done.refs_0_ = bf16[4,512,256]{2,1,0:T(8,128)(2,1)S(1)} async-done(((bf16[4,512,256]{2,1,0:T(8,128)(2,1)}), bf16[4,512,256]{2,1,0:T(8,128)(2,1)S(1)}, u32[]{:S(2)}, u32[]{:S(2)}) %all-to-all-start) | async-done | bytes 1048608 | tf_op jit(solution)/shard_map/all_to_all | solution.py:344
  47.2 2.4 %shard_map.123 = (bf16[256,1024]{1,0:T(8,128)(2,1)S(1)}, bf16[4,512,256]{2,1,0:T(8,128)(2,1)S(1)}) custom-call(bf16[4,512,256]{2,1,0:T(8,128)(2,1)S(1)} %all-to-all-done.refs_0_, bf16[512,1024]{1,0:T(8,128)(2,1)S(1)} %shard_map.122.refs_1_.zs), custom_call_target="tpu_custom_call" | custom-call | flops 1 | bytes 1 | tf_op jit(solution)/shard_map/pallas_call | solution.py:41
  49.6 0.1 collective-permute-start.14
  49.7 0.9 %shard_map.124.own = f32[256,1024]{1,0:T(8,128)S(1)} custom-call(bf16[512,1024]{1,0:T(8,128)(2,1)S(1)} %shard_map.122.refs_1_.zs, bf16[4,512,256]{2,1,0:T(8,128)(2,1)S(1)} %get-tuple-element.46.refs_0_), custom_call_target="tpu_custom_call" | custom-call | flops 1 | bytes 1 | tf_op jit(solution)/shard_map/pallas_call | solution.py:41
  50.6 1.0 %collective-permute-done.14.got = bf16[256,1024]{1,0:T(8,128)(2,1)S(1)} collective-permute-done((bf16[256,1024]{1,0:T(8,128)(2,1)S(1)}, bf16[256,1024]{1,0:T(8,128)(2,1)S(1)}, u32[]{:S(2)}, u32[]{:S(2)}) %collective-permute-start.14) | collective-permute-done | bytes 524320 | tf_op jit(solution)/shard_map/ppermute | solution.py:30
  51.6 0.1 shard_map.125
  51.7 0.7 %collective-permute-start.15 = (bf16[128,512]{1,0:T(8,128)(2,1)S(1)}, bf16[128,512]{1,0:T(8,128)(2,1)S(1)}, u32[]{:S(2)}, u32[]{:S(2)}) collective-permute-start(bf16[128,512]{1,0:T(8,128)(2,1)S(1)} %get-tuple-element.48), channel_id=1, source_target_pairs={{0,0},{1,17},{2,2},{3,19},{4,4},{5,21},{6,6},{7,23},{8,8},{9,25},{... | collective-permute-start | bytes 393224 | tf_op jit(solution)/shard_map/ppermute | solution.py:307
  52.4 1.6 %collective-permute-start.16 = (bf16[128,512]{1,0:T(8,128)(2,1)S(1)}, bf16[128,512]{1,0:T(8,128)(2,1)S(1)}, u32[]{:S(2)}, u32[]{:S(2)}) collective-permute-start(bf16[128,512]{1,0:T(8,128)(2,1)S(1)} %get-tuple-element.49), channel_id=1, source_target_pairs={{0,2},{1,19},{2,0},{3,17},{4,6},{5,23},{6,4},{7,21},{8,10},{9,27},... | collective-permute-start | bytes 393224 | tf_op jit(solution)/shard_map/ppermute | solution.py:307
  54.0 0.0 collective-permute-start.17
  54.0 2.0 %collective-permute-start.18 = (bf16[128,512]{1,0:T(8,128)(2,1)S(1)}, bf16[128,512]{1,0:T(8,128)(2,1)S(1)}, u32[]{:S(2)}, u32[]{:S(2)}) collective-permute-start(bf16[128,512]{1,0:T(8,128)(2,1)S(1)} %get-tuple-element.51), channel_id=1, source_target_pairs={{0,6},{1,23},{2,4},{3,21},{4,2},{5,19},{6,0},{7,17},{8,14},{9,31},... | collective-permute-start | bytes 393224 | tf_op jit(solution)/shard_map/ppermute | solution.py:307
  56.6 0.0 collective-permute-done.15.refs_0_
  56.6 0.8 %collective-permute-done.16.refs_1_ = bf16[128,512]{1,0:T(8,128)(2,1)S(1)} collective-permute-done((bf16[128,512]{1,0:T(8,128)(2,1)S(1)}, bf16[128,512]{1,0:T(8,128)(2,1)S(1)}, u32[]{:S(2)}, u32[]{:S(2)}) %collective-permute-start.16) | collective-permute-done | bytes 131104 | tf_op jit(solution)/shard_map/ppermute | solution.py:307
  57.4 1.5 %collective-permute-done.17.refs_2_ = bf16[128,512]{1,0:T(8,128)(2,1)S(1)} collective-permute-done((bf16[128,512]{1,0:T(8,128)(2,1)S(1)}, bf16[128,512]{1,0:T(8,128)(2,1)S(1)}, u32[]{:S(2)}, u32[]{:S(2)}) %collective-permute-start.17) | collective-permute-done | bytes 131104 | tf_op jit(solution)/shard_map/ppermute | solution.py:307
  58.9 1.8 %collective-permute-done.18.refs_3_ = bf16[128,512]{1,0:T(8,128)(2,1)S(1)} collective-permute-done((bf16[128,512]{1,0:T(8,128)(2,1)S(1)}, bf16[128,512]{1,0:T(8,128)(2,1)S(1)}, u32[]{:S(2)}, u32[]{:S(2)}) %collective-permute-start.18) | collective-permute-done | bytes 131104 | tf_op jit(solution)/shard_map/ppermute | solution.py:307
  60.8 0.1 shard_map.126
  60.9 3.2 %collective-permute-start.19 = (bf16[128,256]{1,0:T(8,128)(2,1)S(1)}, bf16[128,256]{1,0:T(8,128)(2,1)S(1)}, u32[]{:S(2)}, u32[]{:S(2)}) collective-permute-start(bf16[128,256]{1,0:T(8,128)(2,1)S(1)} %get-tuple-element.54), channel_id=1, source_target_pairs={{1,0},{0,1},{3,2},{2,3},{5,4},{4,5},{7,6},{6,7},{9,8},{8,9},{11,10... | collective-permute-start | bytes 196616 | tf_op jit(solution)/shard_map/ppermute | solution.py:30
  64.0 0.9 %collective-permute-done.19 = bf16[128,256]{1,0:T(8,128)(2,1)S(1)} collective-permute-done((bf16[128,256]{1,0:T(8,128)(2,1)S(1)}, bf16[128,256]{1,0:T(8,128)(2,1)S(1)}, u32[]{:S(2)}, u32[]{:S(2)}) %collective-permute-start.19) | collective-permute-done | bytes 65568 | tf_op jit(solution)/shard_map/ppermute | solution.py:30
  64.9 0.7 %select_convert_fusion = bf16[128,256]{1,0:T(8,128)(2,1)} fusion(f32[128,256]{1,0:T(8,128)S(1)} %get-tuple-element.53, bf16[128,256]{1,0:T(8,128)(2,1)S(1)} %collective-permute-done.19, pred[128]{0:T(512)(128)(4,1)S(1)} %iota_compare_fusion), kind=kLoop, calls=%fused_computation | loop fusion | flops 131072 | bytes 262272 | tf_op jit(solution)/shard_map/convert_element_type | solution.py:414
  (1 shorter events, 0.0 us)
Async XLA Ops:
  0.0 7.0 %copy-start = (bf16[256,1024]{1,0:T(8,128)(2,1)S(1)}, bf16[256,1024]{1,0:T(8,128)(2,1)}, u32[]{:S(2)}) copy-start(bf16[256,1024]{1,0:T(8,128)(2,1)} %up.1) | copy-start | bytes 1572868
  1.3 17.3 %collective-permute-start = (bf16[64,2048]{1,0:T(8,128)(2,1)S(1)}, bf16[64,2048]{1,0:T(8,128)(2,1)S(1)}, u32[]{:S(2)}, u32[]{:S(2)}) collective-permute-start(bf16[64,2048]{1,0:T(8,128)(2,1)S(1)} %get-tuple-element.30), channel_id=1, source_target_pairs={{4,0},{0,4},{12,8},{8,12},{5,1},{1,5},{13,9},{9,13},{6,2},{2,6},{1... | collective-permute-start | bytes 786440 | tf_op jit(solution)/shard_map/ppermute | solution.py:30
  4.4 9.6 %collective-permute-start.1 = (bf16[64,1024]{1,0:T(8,128)(2,1)S(1)}, bf16[64,1024]{1,0:T(8,128)(2,1)S(1)}, u32[]{:S(2)}, u32[]{:S(2)}) collective-permute-start(bf16[64,1024]{1,0:T(8,128)(2,1)S(1)} %get-tuple-element.31), channel_id=1, source_target_pairs={{8,0},{12,4},{0,8},{4,12},{9,1},{13,5},{1,9},{5,13},{10,2},{14,6},... | collective-permute-start | bytes 393224 | tf_op jit(solution)/shard_map/ppermute | solution.py:30
  7.0 11.6 %collective-permute-start.2 = (bf16[64,1024]{1,0:T(8,128)(2,1)S(1)}, bf16[64,1024]{1,0:T(8,128)(2,1)S(1)}, u32[]{:S(2)}, u32[]{:S(2)}) collective-permute-start(bf16[64,1024]{1,0:T(8,128)(2,1)S(1)} %get-tuple-element.31), channel_id=1, source_target_pairs={{12,0},{8,4},{4,8},{0,12},{13,1},{9,5},{5,9},{1,13},{14,2},{10,6},... | collective-permute-start | bytes 393224 | tf_op jit(solution)/shard_map/ppermute | solution.py:30
  7.0 1.0 %copy-start.1 = (bf16[1024,256]{1,0:T(8,128)(2,1)S(1)}, bf16[1024,256]{1,0:T(8,128)(2,1)}, u32[]{:S(2)}) copy-start(bf16[1024,256]{1,0:T(8,128)(2,1)} %down.1) | copy-start | bytes 1572868
  18.7 28.6 %all-to-all-start = ((bf16[4,512,256]{2,1,0:T(8,128)(2,1)}), bf16[4,512,256]{2,1,0:T(8,128)(2,1)S(1)}, u32[]{:S(2)}, u32[]{:S(2)}) async-start(bf16[4,512,256]{2,1,0:T(8,128)(2,1)} %shard_map.119), calls=%async_computation | async-start | bytes 2097152 | tf_op jit(solution)/shard_map/all_to_all | solution.py:344
  22.2 2.0 %collective-permute-start.3 = (bf16[64,2048]{1,0:T(8,128)(2,1)S(1)}, bf16[64,2048]{1,0:T(8,128)(2,1)S(1)}, u32[]{:S(2)}, u32[]{:S(2)}) collective-permute-start(bf16[64,2048]{1,0:T(8,128)(2,1)S(1)} %collective-permute-done.refs_7_.refs_0_), channel_id=1, source_target_pairs={{1,0},{0,1},{3,2},{2,3},{5,4},{4,5},{7,6},{6,7},{9,8},{8,9},{11,10... | collective-permute-start | bytes 786440 | tf_op jit(solution)/shard_map/ppermute | solution.py:30
  22.3 1.7 %collective-permute-start.4 = (bf16[64,1024]{1,0:T(8,128)(2,1)S(1)}, bf16[64,1024]{1,0:T(8,128)(2,1)S(1)}, u32[]{:S(2)}, u32[]{:S(2)}) collective-permute-start(bf16[64,1024]{1,0:T(8,128)(2,1)S(1)} %collective-permute-done.1.refs_8_), channel_id=1, source_target_pairs={{1,0},{0,1},{3,2},{2,3},{5,4},{4,5},{7,6},{6,7},{9,8},{8,9},{11,10... | collective-permute-start | bytes 393224 | tf_op jit(solution)/shard_map/ppermute | solution.py:30
  22.8 1.4 %collective-permute-start.5 = (bf16[64,1024]{1,0:T(8,128)(2,1)S(1)}, bf16[64,1024]{1,0:T(8,128)(2,1)S(1)}, u32[]{:S(2)}, u32[]{:S(2)}) collective-permute-start(bf16[64,1024]{1,0:T(8,128)(2,1)S(1)} %collective-permute-done.2.refs_9_), channel_id=1, source_target_pairs={{1,0},{0,1},{3,2},{2,3},{5,4},{4,5},{7,6},{6,7},{9,8},{8,9},{11,10... | collective-permute-start | bytes 393224 | tf_op jit(solution)/shard_map/ppermute | solution.py:30
  29.6 1.4 %collective-permute-start.6 = (bf16[272,256]{1,0:T(8,128)(2,1)S(1)}, bf16[272,256]{1,0:T(8,128)(2,1)S(1)}, u32[]{:S(2)}, u32[]{:S(2)}) collective-permute-start(bf16[272,256]{1,0:T(8,128)(2,1)S(1)} %get-tuple-element.43), channel_id=1, source_target_pairs={{1,0},{0,1},{3,2},{2,3},{5,4},{4,5},{7,6},{6,7},{9,8},{8,9},{11,10... | collective-permute-start | bytes 417800 | tf_op jit(solution)/shard_map/ppermute | solution.py:30
  32.0 8.5 %collective-permute-start.10 = (bf16[272,256]{1,0:T(8,128)(2,1)S(1)}, bf16[272,256]{1,0:T(8,128)(2,1)S(1)}, u32[]{:S(2)}, u32[]{:S(2)}) collective-permute-start(bf16[272,256]{1,0:T(8,128)(2,1)S(1)} %get-tuple-element.44.refs_0_), channel_id=1, source_target_pairs={{16,0},{0,16},{17,1},{1,17},{18,2},{2,18},{19,3},{3,19},{20,4},{4,... | collective-permute-start | bytes 417800 | tf_op jit(solution)/shard_map/ppermute | solution.py:30
  33.6 7.5 %collective-permute-start.12 = (bf16[272,256]{1,0:T(8,128)(2,1)S(1)}, bf16[272,256]{1,0:T(8,128)(2,1)S(1)}, u32[]{:S(2)}, u32[]{:S(2)}) collective-permute-start(bf16[272,256]{1,0:T(8,128)(2,1)S(1)} %get-tuple-element.44.refs_0_), channel_id=1, source_target_pairs={{18,0},{16,2},{2,16},{0,18},{19,1},{17,3},{3,17},{1,19},{22,4},{20... | collective-permute-start | bytes 417800 | tf_op jit(solution)/shard_map/ppermute | solution.py:30
  35.0 7.0 %collective-permute-start.8 = (bf16[272,256]{1,0:T(8,128)(2,1)S(1)}, bf16[272,256]{1,0:T(8,128)(2,1)S(1)}, u32[]{:S(2)}, u32[]{:S(2)}) collective-permute-start(bf16[272,256]{1,0:T(8,128)(2,1)S(1)} %get-tuple-element.44.refs_0_), channel_id=1, source_target_pairs={{2,0},{0,2},{3,1},{1,3},{6,4},{4,6},{7,5},{5,7},{10,8},{8,10},{11,... | collective-permute-start | bytes 417800 | tf_op jit(solution)/shard_map/ppermute | solution.py:30
  35.5 6.5 %collective-permute-start.7 = (bf16[272,256]{1,0:T(8,128)(2,1)S(1)}, bf16[272,256]{1,0:T(8,128)(2,1)S(1)}, u32[]{:S(2)}, u32[]{:S(2)}) collective-permute-start(bf16[272,256]{1,0:T(8,128)(2,1)S(1)} %get-tuple-element.44.refs_0_), channel_id=1, source_target_pairs={{1,0},{0,1},{3,2},{2,3},{5,4},{4,5},{7,6},{6,7},{9,8},{8,9},{11,10... | collective-permute-start | bytes 417800 | tf_op jit(solution)/shard_map/ppermute | solution.py:30
  40.5 1.5 %collective-permute-start.11 = (bf16[272,256]{1,0:T(8,128)(2,1)S(1)}, bf16[272,256]{1,0:T(8,128)(2,1)S(1)}, u32[]{:S(2)}, u32[]{:S(2)}) collective-permute-start(bf16[272,256]{1,0:T(8,128)(2,1)S(1)} %collective-permute-done.10.refs_4_), channel_id=1, source_target_pairs={{1,0},{0,1},{3,2},{2,3},{5,4},{4,5},{7,6},{6,7},{9,8},{8,9},{11,10... | collective-permute-start | bytes 417800 | tf_op jit(solution)/shard_map/ppermute | solution.py:30
  41.0 1.4 %collective-permute-start.13 = (bf16[272,256]{1,0:T(8,128)(2,1)S(1)}, bf16[272,256]{1,0:T(8,128)(2,1)S(1)}, u32[]{:S(2)}, u32[]{:S(2)}) collective-permute-start(bf16[272,256]{1,0:T(8,128)(2,1)S(1)} %collective-permute-done.12.refs_6_), channel_id=1, source_target_pairs={{1,0},{0,1},{3,2},{2,3},{5,4},{4,5},{7,6},{6,7},{9,8},{8,9},{11,10... | collective-permute-start | bytes 417800 | tf_op jit(solution)/shard_map/ppermute | solution.py:30
  42.0 1.4 %collective-permute-start.9 = (bf16[272,256]{1,0:T(8,128)(2,1)S(1)}, bf16[272,256]{1,0:T(8,128)(2,1)S(1)}, u32[]{:S(2)}, u32[]{:S(2)}) collective-permute-start(bf16[272,256]{1,0:T(8,128)(2,1)S(1)} %collective-permute-done.8.refs_2_), channel_id=1, source_target_pairs={{1,0},{0,1},{3,2},{2,3},{5,4},{4,5},{7,6},{6,7},{9,8},{8,9},{11,10... | collective-permute-start | bytes 417800 | tf_op jit(solution)/shard_map/ppermute | solution.py:30
  49.6 2.0 %collective-permute-start.14 = (bf16[256,1024]{1,0:T(8,128)(2,1)S(1)}, bf16[256,1024]{1,0:T(8,128)(2,1)S(1)}, u32[]{:S(2)}, u32[]{:S(2)}) collective-permute-start(bf16[256,1024]{1,0:T(8,128)(2,1)S(1)} %get-tuple-element.47), channel_id=1, source_target_pairs={{1,0},{0,1},{3,2},{2,3},{5,4},{4,5},{7,6},{6,7},{9,8},{8,9},{11,10... | collective-permute-start | bytes 1572872 | tf_op jit(solution)/shard_map/ppermute | solution.py:30
  51.7 4.9 %collective-permute-start.15 = (bf16[128,512]{1,0:T(8,128)(2,1)S(1)}, bf16[128,512]{1,0:T(8,128)(2,1)S(1)}, u32[]{:S(2)}, u32[]{:S(2)}) collective-permute-start(bf16[128,512]{1,0:T(8,128)(2,1)S(1)} %get-tuple-element.48), channel_id=1, source_target_pairs={{0,0},{1,17},{2,2},{3,19},{4,4},{5,21},{6,6},{7,23},{8,8},{9,25},{... | collective-permute-start | bytes 393224 | tf_op jit(solution)/shard_map/ppermute | solution.py:307
  52.4 5.0 %collective-permute-start.16 = (bf16[128,512]{1,0:T(8,128)(2,1)S(1)}, bf16[128,512]{1,0:T(8,128)(2,1)S(1)}, u32[]{:S(2)}, u32[]{:S(2)}) collective-permute-start(bf16[128,512]{1,0:T(8,128)(2,1)S(1)} %get-tuple-element.49), channel_id=1, source_target_pairs={{0,2},{1,19},{2,0},{3,17},{4,6},{5,23},{6,4},{7,21},{8,10},{9,27},... | collective-permute-start | bytes 393224 | tf_op jit(solution)/shard_map/ppermute | solution.py:307
  54.0 5.0 %collective-permute-start.17 = (bf16[128,512]{1,0:T(8,128)(2,1)S(1)}, bf16[128,512]{1,0:T(8,128)(2,1)S(1)}, u32[]{:S(2)}, u32[]{:S(2)}) collective-permute-start(bf16[128,512]{1,0:T(8,128)(2,1)S(1)} %get-tuple-element.50), channel_id=1, source_target_pairs={{0,4},{1,21},{2,6},{3,23},{4,0},{5,17},{6,2},{7,19},{8,12},{9,29},... | collective-permute-start | bytes 393224 | tf_op jit(solution)/shard_map/ppermute | solution.py:307
  54.0 6.8 %collective-permute-start.18 = (bf16[128,512]{1,0:T(8,128)(2,1)S(1)}, bf16[128,512]{1,0:T(8,128)(2,1)S(1)}, u32[]{:S(2)}, u32[]{:S(2)}) collective-permute-start(bf16[128,512]{1,0:T(8,128)(2,1)S(1)} %get-tuple-element.51), channel_id=1, source_target_pairs={{0,6},{1,23},{2,4},{3,21},{4,2},{5,19},{6,0},{7,17},{8,14},{9,31},... | collective-permute-start | bytes 393224 | tf_op jit(solution)/shard_map/ppermute | solution.py:307
  60.9 4.1 %collective-permute-start.19 = (bf16[128,256]{1,0:T(8,128)(2,1)S(1)}, bf16[128,256]{1,0:T(8,128)(2,1)S(1)}, u32[]{:S(2)}, u32[]{:S(2)}) collective-permute-start(bf16[128,256]{1,0:T(8,128)(2,1)S(1)} %get-tuple-element.54), channel_id=1, source_target_pairs={{1,0},{0,1},{3,2},{2,3},{5,4},{4,5},{7,6},{6,7},{9,8},{8,9},{11,10... | collective-permute-start | bytes 196616 | tf_op jit(solution)/shard_map/ppermute | solution.py:30

commit v7 on v6

--- a/solution.py
+++ b/solution.py
@@ -401,7 +401,7 @@
     (own,) = call(
         ours_kernel, [shape((near * n, model), F32)], [zs, *mlp], [pltpu.VMEM((near * n, model), F32)]
     )
-    moves = list(itertools.product(range(near), range(n_head)))
+    moves = sorted(itertools.product(range(near), range(n_head)), key=lambda m: (-m[0] - m[1], m[0]))
     parts = call(
         functools.partial(pair_kernel, moves), [shape((n, dh), BF)] * len(moves), [own, got]
     )

time: 66 us -> 64.3 us (0.974)
  starting transfers between devices: 21.1 us -> 18.4 us
  waiting for transfers between devices: 29.3 us -> 30.4 us
    ppermute x16, starting transfers between devices: 13.3 us -> 10.6 us  [moved(): return lax.ppermute(x, tuple(axes), pairs)]
    ppermute x4, waiting for transfers between devices: 4.16 us -> 5.24 us  [dealt(): return lax.ppermute(x, axes, pairs)]
  transfers between devices with their start and end apart: 21 -> 21, of which waited for: 16 -> 16; matrix products, arithmetic and copies ran while one was open for 0% -> 0% of each run, Pallas kernels for 13% -> 14%
where the time goes in v7:
time: 64.3 us; the launch traced here: 64 us
  waiting for transfers between devices  30.4 us (47%)
  starting transfers between devices  18.4 us (29%)
  Pallas kernels  12.8 us (20%)
  local copies, waits for them, and re-layouts  1.05 us (2%)
  between operations  0.76 us (1%)
  other arithmetic  0.72 us (1%)
    ppermute x16, waiting for transfers between devices, moved(): return lax.ppermute(x, tuple(axes), pairs)  21.8 us
    pallas_call x9, Pallas kernels, call(): pl.pallas_call(kernel, out_shape=outs, in_specs=[pl.BlockSpec(memory_spac...  12.8 us
    ppermute x16, starting transfers between devices, moved(): return lax.ppermute(x, tuple(axes), pairs)  10.6 us
    ppermute x4, waiting for transfers between devices, dealt(): return lax.ppermute(x, axes, pairs)  5.24 us
    ppermute x4, starting transfers between devices, dealt(): return lax.ppermute(x, axes, pairs)  4.2 us
    all_to_all x1, starting transfers between devices, on_device(): mlp = [lax.all_to_all(blocks, 'tok', 0, 0)]  3.52 us
    all_to_all x1, waiting for transfers between devices, on_device(): mlp = [lax.all_to_all(blocks, 'tok', 0, 0)]  3.34 us
  transfers between devices with their start and end apart: 21, of which 16 were waited for; matrix products, arithmetic and copies ran while one was open for 0% of the time, Pallas kernels for 14%

profile of v7, /device:TPU:0, one launch (start us, length us, event | category | flops | bytes accessed | tf_op | source)
XLA Modules:
  0.0 64.0 jit_solution(9297174624151576854)
XLA Ops:
  0.0 0.0 copy-start
  0.0 1.3 %shard_map.118 = (bf16[64,1024]{1,0:T(8,128)(2,1)S(1)}, bf16[64,2048]{1,0:T(8,128)(2,1)S(1)}) custom-call(bf16[128,512]{1,0:T(8,128)(2,1)} %refs_3_.3, bf16[128,512]{1,0:T(8,128)(2,1)} %refs_4_.3, f32[1,128]{1,0:T(1,128)} %bitcast.11, bf16[128,512]{1,0:T(8,128)(2,1)} %refs_6_.1, bf16[128,512]{1,0:T(8,128)(2,1)} %stream_far.1), custom_call_target="tpu_custom_call" | custom-call | flops 1 | bytes 1 | tf_op jit(solution)/shard_map/pallas_call | solution.py:41
  1.3 3.1 %collective-permute-start = (bf16[64,2048]{1,0:T(8,128)(2,1)S(1)}, bf16[64,2048]{1,0:T(8,128)(2,1)S(1)}, u32[]{:S(2)}, u32[]{:S(2)}) collective-permute-start(bf16[64,2048]{1,0:T(8,128)(2,1)S(1)} %get-tuple-element.30), channel_id=1, source_target_pairs={{4,0},{0,4},{12,8},{8,12},{5,1},{1,5},{13,9},{9,13},{6,2},{2,6},{1... | collective-permute-start | bytes 786440 | tf_op jit(solution)/shard_map/ppermute | solution.py:30
  4.4 2.6 %collective-permute-start.1 = (bf16[64,1024]{1,0:T(8,128)(2,1)S(1)}, bf16[64,1024]{1,0:T(8,128)(2,1)S(1)}, u32[]{:S(2)}, u32[]{:S(2)}) collective-permute-start(bf16[64,1024]{1,0:T(8,128)(2,1)S(1)} %get-tuple-element.31), channel_id=1, source_target_pairs={{8,0},{12,4},{0,8},{4,12},{9,1},{13,5},{1,9},{5,13},{10,2},{14,6},... | collective-permute-start | bytes 393224 | tf_op jit(solution)/shard_map/ppermute | solution.py:30
  7.0 0.0 collective-permute-start.2
  7.0 0.0 copy-done
  7.0 0.0 copy-start.1
  7.0 1.0 %copy-done.1 = bf16[1024,256]{1,0:T(8,128)(2,1)S(1)} copy-done((bf16[1024,256]{1,0:T(8,128)(2,1)S(1)}, bf16[1024,256]{1,0:T(8,128)(2,1)}, u32[]{:S(2)}) %copy-start.1) | copy-done | bytes 524312
  8.1 1.1 %shard_map.119 = bf16[4,512,256]{2,1,0:T(8,128)(2,1)} custom-call(bf16[256,1024]{1,0:T(8,128)(2,1)S(1)} %copy-done, bf16[1024,256]{1,0:T(8,128)(2,1)S(1)} %copy-done.1), custom_call_target="tpu_custom_call" | custom-call | flops 1 | bytes 1 | tf_op jit(solution)/shard_map/pallas_call | solution.py:41
  9.1 4.9 %collective-permute-done.1.refs_8_ = bf16[64,1024]{1,0:T(8,128)(2,1)S(1)} collective-permute-done((bf16[64,1024]{1,0:T(8,128)(2,1)S(1)}, bf16[64,1024]{1,0:T(8,128)(2,1)S(1)}, u32[]{:S(2)}, u32[]{:S(2)}) %collective-permute-start.1) | collective-permute-done | bytes 131104 | tf_op jit(solution)/shard_map/ppermute | solution.py:30
  14.0 4.7 %collective-permute-done.2.refs_9_ = bf16[64,1024]{1,0:T(8,128)(2,1)S(1)} collective-permute-done((bf16[64,1024]{1,0:T(8,128)(2,1)S(1)}, bf16[64,1024]{1,0:T(8,128)(2,1)S(1)}, u32[]{:S(2)}, u32[]{:S(2)}) %collective-permute-start.2) | collective-permute-done | bytes 131104 | tf_op jit(solution)/shard_map/ppermute | solution.py:30
  18.7 0.0 collective-permute-done.refs_7_.refs_0_
  18.7 3.5 %all-to-all-start = ((bf16[4,512,256]{2,1,0:T(8,128)(2,1)}), bf16[4,512,256]{2,1,0:T(8,128)(2,1)S(1)}, u32[]{:S(2)}, u32[]{:S(2)}) async-start(bf16[4,512,256]{2,1,0:T(8,128)(2,1)} %shard_map.119), calls=%async_computation | async-start | bytes 2097152 | tf_op jit(solution)/shard_map/all_to_all | solution.py:344
  22.2 0.1 collective-permute-start.3
  22.3 0.5 collective-permute-start.4
  22.8 0.1 collective-permute-start.5
  22.8 1.1 %collective-permute-done.4.refs_11_ = bf16[64,1024]{1,0:T(8,128)(2,1)S(1)} collective-permute-done((bf16[64,1024]{1,0:T(8,128)(2,1)S(1)}, bf16[64,1024]{1,0:T(8,128)(2,1)S(1)}, u32[]{:S(2)}, u32[]{:S(2)}) %collective-permute-start.4) | collective-permute-done | bytes 131104 | tf_op jit(solution)/shard_map/ppermute | solution.py:30
  24.0 0.2 collective-permute-done.5.refs_12_
  24.2 0.0 collective-permute-done.3.refs_10_
  24.2 5.4 %shard_map.120 = (f32[256,256]{1,0:T(8,128)S(1)}, f32[8,256]{1,0:T(8,128)S(1)}, bf16[272,256]{1,0:T(8,128)(2,1)S(1)}) custom-call(f32[512,512]{1,0:T(8,128)} %bitcast.7, f32[512,512]{1,0:T(8,128)} %bitcast.8, f32[512,512]{1,0:T(8,128)} %bitcast.9, bf16[128,512]{1,0:T(8,128)(2,1)} %refs_3_.3, bf16[128,512]{1,0:T(8,128)(2,1)} %refs_4_.3, f32[1,128]{1,0:T(1,128)} %bitcast.12, ...), custom_call_target="tpu_custom_call" | custom-call | flops 1 | bytes 1 | tf_op jit(solution)/shard_map/pallas_call | solution.py:41
  29.6 0.2 collective-permute-start.6
  29.8 1.2 %collective-permute-done.6.got = bf16[272,256]{1,0:T(8,128)(2,1)S(1)} collective-permute-done((bf16[272,256]{1,0:T(8,128)(2,1)S(1)}, bf16[272,256]{1,0:T(8,128)(2,1)S(1)}, u32[]{:S(2)}, u32[]{:S(2)}) %collective-permute-start.6) | collective-permute-done | bytes 139296 | tf_op jit(solution)/shard_map/ppermute | solution.py:30
  31.0 1.0 %shard_map.121 = (f32[128,256]{1,0:T(8,128)S(1)}, bf16[272,256]{1,0:T(8,128)(2,1)S(1)}) custom-call(bf16[128,512]{1,0:T(8,128)(2,1)} %stream_far.1, f32[1,512]{1,0:T(1,128)} %bitcast.10, f32[256,256]{1,0:T(8,128)S(1)} %get-tuple-element.41.own, f32[8,256]{1,0:T(8,128)S(1)} %get-tuple-element.42.own_sq, bf16[272,256]{1,0:T(8,128)(2,1)S(1)} %collective-permute-done.6.got, ...), custom_call_target="tpu_custom_call" | custom-call | flops 1 | bytes 1 | tf_op jit(solution)/shard_map/pallas_call | solution.py:41
  32.0 1.6 %collective-permute-start.10 = (bf16[272,256]{1,0:T(8,128)(2,1)S(1)}, bf16[272,256]{1,0:T(8,128)(2,1)S(1)}, u32[]{:S(2)}, u32[]{:S(2)}) collective-permute-start(bf16[272,256]{1,0:T(8,128)(2,1)S(1)} %get-tuple-element.44.refs_0_), channel_id=1, source_target_pairs={{16,0},{0,16},{17,1},{1,17},{18,2},{2,18},{19,3},{3,19},{20,4},{4,... | collective-permute-start | bytes 417800 | tf_op jit(solution)/shard_map/ppermute | solution.py:30
  33.6 1.4 %collective-permute-start.12 = (bf16[272,256]{1,0:T(8,128)(2,1)S(1)}, bf16[272,256]{1,0:T(8,128)(2,1)S(1)}, u32[]{:S(2)}, u32[]{:S(2)}) collective-permute-start(bf16[272,256]{1,0:T(8,128)(2,1)S(1)} %get-tuple-element.44.refs_0_), channel_id=1, source_target_pairs={{18,0},{16,2},{2,16},{0,18},{19,1},{17,3},{3,17},{1,19},{22,4},{20... | collective-permute-start | bytes 417800 | tf_op jit(solution)/shard_map/ppermute | solution.py:30
  35.0 0.5 collective-permute-start.8
  35.5 0.0 collective-permute-start.7
  35.5 4.9 %collective-permute-done.10.refs_4_ = bf16[272,256]{1,0:T(8,128)(2,1)S(1)} collective-permute-done((bf16[272,256]{1,0:T(8,128)(2,1)S(1)}, bf16[272,256]{1,0:T(8,128)(2,1)S(1)}, u32[]{:S(2)}, u32[]{:S(2)}) %collective-permute-start.10) | collective-permute-done | bytes 139296 | tf_op jit(solution)/shard_map/ppermute | solution.py:30
  40.5 0.0 collective-permute-start.11
  40.5 0.5 collective-permute-done.12.refs_6_
  41.0 0.0 collective-permute-start.13
  41.0 1.0 %collective-permute-done.8.refs_2_ = bf16[272,256]{1,0:T(8,128)(2,1)S(1)} collective-permute-done((bf16[272,256]{1,0:T(8,128)(2,1)S(1)}, bf16[272,256]{1,0:T(8,128)(2,1)S(1)}, u32[]{:S(2)}, u32[]{:S(2)}) %collective-permute-start.8) | collective-permute-done | bytes 139296 | tf_op jit(solution)/shard_map/ppermute | solution.py:30
  42.0 0.0 collective-permute-start.9
  42.0 0.0 collective-permute-done.7.refs_1_
  42.0 0.0 collective-permute-done.11.refs_5_
  42.0 0.4 collective-permute-done.13.refs_7_
  42.4 1.0 %collective-permute-done.9.refs_3_ = bf16[272,256]{1,0:T(8,128)(2,1)S(1)} collective-permute-done((bf16[272,256]{1,0:T(8,128)(2,1)S(1)}, bf16[272,256]{1,0:T(8,128)(2,1)S(1)}, u32[]{:S(2)}, u32[]{:S(2)}) %collective-permute-start.9) | collective-permute-done | bytes 139296 | tf_op jit(solution)/shard_map/ppermute | solution.py:30
  43.3 0.5 shard_map.122.refs_1_.zs
  43.9 3.3 %all-to-all-done.refs_0_ = bf16[4,512,256]{2,1,0:T(8,128)(2,1)S(1)} async-done(((bf16[4,512,256]{2,1,0:T(8,128)(2,1)}), bf16[4,512,256]{2,1,0:T(8,128)(2,1)S(1)}, u32[]{:S(2)}, u32[]{:S(2)}) %all-to-all-start) | async-done | bytes 1048608 | tf_op jit(solution)/shard_map/all_to_all | solution.py:344
  47.2 2.4 %shard_map.123 = (bf16[256,1024]{1,0:T(8,128)(2,1)S(1)}, bf16[4,512,256]{2,1,0:T(8,128)(2,1)S(1)}) custom-call(bf16[4,512,256]{2,1,0:T(8,128)(2,1)S(1)} %all-to-all-done.refs_0_, bf16[512,1024]{1,0:T(8,128)(2,1)S(1)} %shard_map.122.refs_1_.zs), custom_call_target="tpu_custom_call" | custom-call | flops 1 | bytes 1 | tf_op jit(solution)/shard_map/pallas_call | solution.py:41
  49.6 0.1 collective-permute-start.14
  49.7 0.9 %shard_map.124.own = f32[256,1024]{1,0:T(8,128)S(1)} custom-call(bf16[512,1024]{1,0:T(8,128)(2,1)S(1)} %shard_map.122.refs_1_.zs, bf16[4,512,256]{2,1,0:T(8,128)(2,1)S(1)} %get-tuple-element.46.refs_0_), custom_call_target="tpu_custom_call" | custom-call | flops 1 | bytes 1 | tf_op jit(solution)/shard_map/pallas_call | solution.py:41
  50.6 1.0 %collective-permute-done.14.got = bf16[256,1024]{1,0:T(8,128)(2,1)S(1)} collective-permute-done((bf16[256,1024]{1,0:T(8,128)(2,1)S(1)}, bf16[256,1024]{1,0:T(8,128)(2,1)S(1)}, u32[]{:S(2)}, u32[]{:S(2)}) %collective-permute-start.14) | collective-permute-done | bytes 524320 | tf_op jit(solution)/shard_map/ppermute | solution.py:30
  51.6 0.1 shard_map.125
  51.7 0.1 collective-permute-start.15
  51.8 1.6 %collective-permute-start.16 = (bf16[128,512]{1,0:T(8,128)(2,1)S(1)}, bf16[128,512]{1,0:T(8,128)(2,1)S(1)}, u32[]{:S(2)}, u32[]{:S(2)}) collective-permute-start(bf16[128,512]{1,0:T(8,128)(2,1)S(1)} %get-tuple-element.49), channel_id=1, source_target_pairs={{0,2},{1,19},{2,0},{3,17},{4,6},{5,23},{6,4},{7,21},{8,10},{9,27},... | collective-permute-start | bytes 393224 | tf_op jit(solution)/shard_map/ppermute | solution.py:307
  53.4 1.9 %collective-permute-start.17 = (bf16[128,512]{1,0:T(8,128)(2,1)S(1)}, bf16[128,512]{1,0:T(8,128)(2,1)S(1)}, u32[]{:S(2)}, u32[]{:S(2)}) collective-permute-start(bf16[128,512]{1,0:T(8,128)(2,1)S(1)} %get-tuple-element.50), channel_id=1, source_target_pairs={{0,4},{1,21},{2,6},{3,23},{4,0},{5,17},{6,2},{7,19},{8,12},{9,29},... | collective-permute-start | bytes 393224 | tf_op jit(solution)/shard_map/ppermute | solution.py:307
  55.3 0.7 %collective-permute-start.18 = (bf16[128,512]{1,0:T(8,128)(2,1)S(1)}, bf16[128,512]{1,0:T(8,128)(2,1)S(1)}, u32[]{:S(2)}, u32[]{:S(2)}) collective-permute-start(bf16[128,512]{1,0:T(8,128)(2,1)S(1)} %get-tuple-element.51), channel_id=1, source_target_pairs={{0,0},{1,17},{2,2},{3,19},{4,4},{5,21},{6,6},{7,23},{8,8},{9,25},{... | collective-permute-start | bytes 393224 | tf_op jit(solution)/shard_map/ppermute | solution.py:307
  56.6 2.4 %collective-permute-done.15.refs_0_ = bf16[128,512]{1,0:T(8,128)(2,1)S(1)} collective-permute-done((bf16[128,512]{1,0:T(8,128)(2,1)S(1)}, bf16[128,512]{1,0:T(8,128)(2,1)S(1)}, u32[]{:S(2)}, u32[]{:S(2)}) %collective-permute-start.15) | collective-permute-done | bytes 131104 | tf_op jit(solution)/shard_map/ppermute | solution.py:307
  59.0 1.9 %collective-permute-done.16.refs_1_ = bf16[128,512]{1,0:T(8,128)(2,1)S(1)} collective-permute-done((bf16[128,512]{1,0:T(8,128)(2,1)S(1)}, bf16[128,512]{1,0:T(8,128)(2,1)S(1)}, u32[]{:S(2)}, u32[]{:S(2)}) %collective-permute-start.16) | collective-permute-done | bytes 131104 | tf_op jit(solution)/shard_map/ppermute | solution.py:307
  60.9 0.9 %collective-permute-done.17.refs_2_ = bf16[128,512]{1,0:T(8,128)(2,1)S(1)} collective-permute-done((bf16[128,512]{1,0:T(8,128)(2,1)S(1)}, bf16[128,512]{1,0:T(8,128)(2,1)S(1)}, u32[]{:S(2)}, u32[]{:S(2)}) %collective-permute-start.17) | collective-permute-done | bytes 131104 | tf_op jit(solution)/shard_map/ppermute | solution.py:307
  61.8 0.0 collective-permute-done.18.refs_3_
  61.8 0.1 shard_map.126
  61.9 0.5 collective-permute-start.19
  62.4 0.9 %collective-permute-done.19 = bf16[128,256]{1,0:T(8,128)(2,1)S(1)} collective-permute-done((bf16[128,256]{1,0:T(8,128)(2,1)S(1)}, bf16[128,256]{1,0:T(8,128)(2,1)S(1)}, u32[]{:S(2)}, u32[]{:S(2)}) %collective-permute-start.19) | collective-permute-done | bytes 65568 | tf_op jit(solution)/shard_map/ppermute | solution.py:30
  63.3 0.7 %select_convert_fusion = bf16[128,256]{1,0:T(8,128)(2,1)} fusion(f32[128,256]{1,0:T(8,128)S(1)} %get-tuple-element.53, bf16[128,256]{1,0:T(8,128)(2,1)S(1)} %collective-permute-done.19, pred[128]{0:T(512)(128)(4,1)S(1)} %iota_compare_fusion), kind=kLoop, calls=%fused_computation | loop fusion | flops 131072 | bytes 262272 | tf_op jit(solution)/shard_map/convert_element_type | solution.py:414
  (1 shorter events, 0.0 us)
Async XLA Ops:
  0.0 7.0 %copy-start = (bf16[256,1024]{1,0:T(8,128)(2,1)S(1)}, bf16[256,1024]{1,0:T(8,128)(2,1)}, u32[]{:S(2)}) copy-start(bf16[256,1024]{1,0:T(8,128)(2,1)} %up.1) | copy-start | bytes 1572868
  1.3 17.3 %collective-permute-start = (bf16[64,2048]{1,0:T(8,128)(2,1)S(1)}, bf16[64,2048]{1,0:T(8,128)(2,1)S(1)}, u32[]{:S(2)}, u32[]{:S(2)}) collective-permute-start(bf16[64,2048]{1,0:T(8,128)(2,1)S(1)} %get-tuple-element.30), channel_id=1, source_target_pairs={{4,0},{0,4},{12,8},{8,12},{5,1},{1,5},{13,9},{9,13},{6,2},{2,6},{1... | collective-permute-start | bytes 786440 | tf_op jit(solution)/shard_map/ppermute | solution.py:30
  4.4 9.6 %collective-permute-start.1 = (bf16[64,1024]{1,0:T(8,128)(2,1)S(1)}, bf16[64,1024]{1,0:T(8,128)(2,1)S(1)}, u32[]{:S(2)}, u32[]{:S(2)}) collective-permute-start(bf16[64,1024]{1,0:T(8,128)(2,1)S(1)} %get-tuple-element.31), channel_id=1, source_target_pairs={{8,0},{12,4},{0,8},{4,12},{9,1},{13,5},{1,9},{5,13},{10,2},{14,6},... | collective-permute-start | bytes 393224 | tf_op jit(solution)/shard_map/ppermute | solution.py:30
  7.0 11.6 %collective-permute-start.2 = (bf16[64,1024]{1,0:T(8,128)(2,1)S(1)}, bf16[64,1024]{1,0:T(8,128)(2,1)S(1)}, u32[]{:S(2)}, u32[]{:S(2)}) collective-permute-start(bf16[64,1024]{1,0:T(8,128)(2,1)S(1)} %get-tuple-element.31), channel_id=1, source_target_pairs={{12,0},{8,4},{4,8},{0,12},{13,1},{9,5},{5,9},{1,13},{14,2},{10,6},... | collective-permute-start | bytes 393224 | tf_op jit(solution)/shard_map/ppermute | solution.py:30
  7.0 1.0 %copy-start.1 = (bf16[1024,256]{1,0:T(8,128)(2,1)S(1)}, bf16[1024,256]{1,0:T(8,128)(2,1)}, u32[]{:S(2)}) copy-start(bf16[1024,256]{1,0:T(8,128)(2,1)} %down.1) | copy-start | bytes 1572868
  18.7 28.6 %all-to-all-start = ((bf16[4,512,256]{2,1,0:T(8,128)(2,1)}), bf16[4,512,256]{2,1,0:T(8,128)(2,1)S(1)}, u32[]{:S(2)}, u32[]{:S(2)}) async-start(bf16[4,512,256]{2,1,0:T(8,128)(2,1)} %shard_map.119), calls=%async_computation | async-start | bytes 2097152 | tf_op jit(solution)/shard_map/all_to_all | solution.py:344
  22.2 2.0 %collective-permute-start.3 = (bf16[64,2048]{1,0:T(8,128)(2,1)S(1)}, bf16[64,2048]{1,0:T(8,128)(2,1)S(1)}, u32[]{:S(2)}, u32[]{:S(2)}) collective-permute-start(bf16[64,2048]{1,0:T(8,128)(2,1)S(1)} %collective-permute-done.refs_7_.refs_0_), channel_id=1, source_target_pairs={{1,0},{0,1},{3,2},{2,3},{5,4},{4,5},{7,6},{6,7},{9,8},{8,9},{11,10... | collective-permute-start | bytes 786440 | tf_op jit(solution)/shard_map/ppermute | solution.py:30
  22.3 1.7 %collective-permute-start.4 = (bf16[64,1024]{1,0:T(8,128)(2,1)S(1)}, bf16[64,1024]{1,0:T(8,128)(2,1)S(1)}, u32[]{:S(2)}, u32[]{:S(2)}) collective-permute-start(bf16[64,1024]{1,0:T(8,128)(2,1)S(1)} %collective-permute-done.1.refs_8_), channel_id=1, source_target_pairs={{1,0},{0,1},{3,2},{2,3},{5,4},{4,5},{7,6},{6,7},{9,8},{8,9},{11,10... | collective-permute-start | bytes 393224 | tf_op jit(solution)/shard_map/ppermute | solution.py:30
  22.8 1.4 %collective-permute-start.5 = (bf16[64,1024]{1,0:T(8,128)(2,1)S(1)}, bf16[64,1024]{1,0:T(8,128)(2,1)S(1)}, u32[]{:S(2)}, u32[]{:S(2)}) collective-permute-start(bf16[64,1024]{1,0:T(8,128)(2,1)S(1)} %collective-permute-done.2.refs_9_), channel_id=1, source_target_pairs={{1,0},{0,1},{3,2},{2,3},{5,4},{4,5},{7,6},{6,7},{9,8},{8,9},{11,10... | collective-permute-start | bytes 393224 | tf_op jit(solution)/shard_map/ppermute | solution.py:30
  29.6 1.4 %collective-permute-start.6 = (bf16[272,256]{1,0:T(8,128)(2,1)S(1)}, bf16[272,256]{1,0:T(8,128)(2,1)S(1)}, u32[]{:S(2)}, u32[]{:S(2)}) collective-permute-start(bf16[272,256]{1,0:T(8,128)(2,1)S(1)} %get-tuple-element.43), channel_id=1, source_target_pairs={{1,0},{0,1},{3,2},{2,3},{5,4},{4,5},{7,6},{6,7},{9,8},{8,9},{11,10... | collective-permute-start | bytes 417800 | tf_op jit(solution)/shard_map/ppermute | solution.py:30
  32.0 8.5 %collective-permute-start.10 = (bf16[272,256]{1,0:T(8,128)(2,1)S(1)}, bf16[272,256]{1,0:T(8,128)(2,1)S(1)}, u32[]{:S(2)}, u32[]{:S(2)}) collective-permute-start(bf16[272,256]{1,0:T(8,128)(2,1)S(1)} %get-tuple-element.44.refs_0_), channel_id=1, source_target_pairs={{16,0},{0,16},{17,1},{1,17},{18,2},{2,18},{19,3},{3,19},{20,4},{4,... | collective-permute-start | bytes 417800 | tf_op jit(solution)/shard_map/ppermute | solution.py:30
  33.6 7.5 %collective-permute-start.12 = (bf16[272,256]{1,0:T(8,128)(2,1)S(1)}, bf16[272,256]{1,0:T(8,128)(2,1)S(1)}, u32[]{:S(2)}, u32[]{:S(2)}) collective-permute-start(bf16[272,256]{1,0:T(8,128)(2,1)S(1)} %get-tuple-element.44.refs_0_), channel_id=1, source_target_pairs={{18,0},{16,2},{2,16},{0,18},{19,1},{17,3},{3,17},{1,19},{22,4},{20... | collective-permute-start | bytes 417800 | tf_op jit(solution)/shard_map/ppermute | solution.py:30
  35.0 7.0 %collective-permute-start.8 = (bf16[272,256]{1,0:T(8,128)(2,1)S(1)}, bf16[272,256]{1,0:T(8,128)(2,1)S(1)}, u32[]{:S(2)}, u32[]{:S(2)}) collective-permute-start(bf16[272,256]{1,0:T(8,128)(2,1)S(1)} %get-tuple-element.44.refs_0_), channel_id=1, source_target_pairs={{2,0},{0,2},{3,1},{1,3},{6,4},{4,6},{7,5},{5,7},{10,8},{8,10},{11,... | collective-permute-start | bytes 417800 | tf_op jit(solution)/shard_map/ppermute | solution.py:30
  35.5 6.5 %collective-permute-start.7 = (bf16[272,256]{1,0:T(8,128)(2,1)S(1)}, bf16[272,256]{1,0:T(8,128)(2,1)S(1)}, u32[]{:S(2)}, u32[]{:S(2)}) collective-permute-start(bf16[272,256]{1,0:T(8,128)(2,1)S(1)} %get-tuple-element.44.refs_0_), channel_id=1, source_target_pairs={{1,0},{0,1},{3,2},{2,3},{5,4},{4,5},{7,6},{6,7},{9,8},{8,9},{11,10... | collective-permute-start | bytes 417800 | tf_op jit(solution)/shard_map/ppermute | solution.py:30
  40.5 1.5 %collective-permute-start.11 = (bf16[272,256]{1,0:T(8,128)(2,1)S(1)}, bf16[272,256]{1,0:T(8,128)(2,1)S(1)}, u32[]{:S(2)}, u32[]{:S(2)}) collective-permute-start(bf16[272,256]{1,0:T(8,128)(2,1)S(1)} %collective-permute-done.10.refs_4_), channel_id=1, source_target_pairs={{1,0},{0,1},{3,2},{2,3},{5,4},{4,5},{7,6},{6,7},{9,8},{8,9},{11,10... | collective-permute-start | bytes 417800 | tf_op jit(solution)/shard_map/ppermute | solution.py:30
  41.0 1.4 %collective-permute-start.13 = (bf16[272,256]{1,0:T(8,128)(2,1)S(1)}, bf16[272,256]{1,0:T(8,128)(2,1)S(1)}, u32[]{:S(2)}, u32[]{:S(2)}) collective-permute-start(bf16[272,256]{1,0:T(8,128)(2,1)S(1)} %collective-permute-done.12.refs_6_), channel_id=1, source_target_pairs={{1,0},{0,1},{3,2},{2,3},{5,4},{4,5},{7,6},{6,7},{9,8},{8,9},{11,10... | collective-permute-start | bytes 417800 | tf_op jit(solution)/shard_map/ppermute | solution.py:30
  42.0 1.4 %collective-permute-start.9 = (bf16[272,256]{1,0:T(8,128)(2,1)S(1)}, bf16[272,256]{1,0:T(8,128)(2,1)S(1)}, u32[]{:S(2)}, u32[]{:S(2)}) collective-permute-start(bf16[272,256]{1,0:T(8,128)(2,1)S(1)} %collective-permute-done.8.refs_2_), channel_id=1, source_target_pairs={{1,0},{0,1},{3,2},{2,3},{5,4},{4,5},{7,6},{6,7},{9,8},{8,9},{11,10... | collective-permute-start | bytes 417800 | tf_op jit(solution)/shard_map/ppermute | solution.py:30
  49.6 2.0 %collective-permute-start.14 = (bf16[256,1024]{1,0:T(8,128)(2,1)S(1)}, bf16[256,1024]{1,0:T(8,128)(2,1)S(1)}, u32[]{:S(2)}, u32[]{:S(2)}) collective-permute-start(bf16[256,1024]{1,0:T(8,128)(2,1)S(1)} %get-tuple-element.47), channel_id=1, source_target_pairs={{1,0},{0,1},{3,2},{2,3},{5,4},{4,5},{7,6},{6,7},{9,8},{8,9},{11,10... | collective-permute-start | bytes 1572872 | tf_op jit(solution)/shard_map/ppermute | solution.py:30
  51.7 7.3 %collective-permute-start.15 = (bf16[128,512]{1,0:T(8,128)(2,1)S(1)}, bf16[128,512]{1,0:T(8,128)(2,1)S(1)}, u32[]{:S(2)}, u32[]{:S(2)}) collective-permute-start(bf16[128,512]{1,0:T(8,128)(2,1)S(1)} %get-tuple-element.48), channel_id=1, source_target_pairs={{0,6},{1,23},{2,4},{3,21},{4,2},{5,19},{6,0},{7,17},{8,14},{9,31},... | collective-permute-start | bytes 393224 | tf_op jit(solution)/shard_map/ppermute | solution.py:307
  51.8 9.1 %collective-permute-start.16 = (bf16[128,512]{1,0:T(8,128)(2,1)S(1)}, bf16[128,512]{1,0:T(8,128)(2,1)S(1)}, u32[]{:S(2)}, u32[]{:S(2)}) collective-permute-start(bf16[128,512]{1,0:T(8,128)(2,1)S(1)} %get-tuple-element.49), channel_id=1, source_target_pairs={{0,2},{1,19},{2,0},{3,17},{4,6},{5,23},{6,4},{7,21},{8,10},{9,27},... | collective-permute-start | bytes 393224 | tf_op jit(solution)/shard_map/ppermute | solution.py:307
  53.4 8.5 %collective-permute-start.17 = (bf16[128,512]{1,0:T(8,128)(2,1)S(1)}, bf16[128,512]{1,0:T(8,128)(2,1)S(1)}, u32[]{:S(2)}, u32[]{:S(2)}) collective-permute-start(bf16[128,512]{1,0:T(8,128)(2,1)S(1)} %get-tuple-element.50), channel_id=1, source_target_pairs={{0,4},{1,21},{2,6},{3,23},{4,0},{5,17},{6,2},{7,19},{8,12},{9,29},... | collective-permute-start | bytes 393224 | tf_op jit(solution)/shard_map/ppermute | solution.py:307
  55.3 6.6 %collective-permute-start.18 = (bf16[128,512]{1,0:T(8,128)(2,1)S(1)}, bf16[128,512]{1,0:T(8,128)(2,1)S(1)}, u32[]{:S(2)}, u32[]{:S(2)}) collective-permute-start(bf16[128,512]{1,0:T(8,128)(2,1)S(1)} %get-tuple-element.51), channel_id=1, source_target_pairs={{0,0},{1,17},{2,2},{3,19},{4,4},{5,21},{6,6},{7,23},{8,8},{9,25},{... | collective-permute-start | bytes 393224 | tf_op jit(solution)/shard_map/ppermute | solution.py:307
  61.9 1.4 %collective-permute-start.19 = (bf16[128,256]{1,0:T(8,128)(2,1)S(1)}, bf16[128,256]{1,0:T(8,128)(2,1)S(1)}, u32[]{:S(2)}, u32[]{:S(2)}) collective-permute-start(bf16[128,256]{1,0:T(8,128)(2,1)S(1)} %get-tuple-element.54), channel_id=1, source_target_pairs={{1,0},{0,1},{3,2},{2,3},{5,4},{4,5},{7,6},{6,7},{9,8},{8,9},{11,10... | collective-permute-start | bytes 196616 | tf_op jit(solution)/shard_map/ppermute | solution.py:30

commit v8 on v7

--- a/solution.py
+++ b/solution.py
@@ -119,10 +119,10 @@
 
 
 def fast_kernel(n_pieces, near, *refs):
-    far, refs = refs[:7], refs[7:]
+    far, refs = refs[:9], refs[9:]
     pieces, refs = refs[:n_pieces], refs[n_pieces:]
-    own_out, own_sq, send, ks, es, hp, qs, pair, *local, sems = refs
-    w1, w3, w2, keys, values, rates, q = local
+    own_out, own_sq, send, base, gains, ks, es, hp, qs, pair, *local, sems = refs
+    w1, w3, w2, keys, values, rates, q, stream, gain = local
     copies = fetch(list(zip(far, local)), sems)
     dh, hidden = w1.shape
     me = lax.axis_index("rep")
@@ -172,6 +172,12 @@
         part = dot((qa * jax.nn.sigmoid(qa) * qc).astype(BF), sums[2].astype(BF))
         hp[...] = part if j == 0 else hp[...] + part
     rows, wide = own_out.shape
+    base[...] = stream[:, window(me, wide)]
+    x = jnp.broadcast_to(gain[:, window(me, wide)], gains.shape)
+    row = lax.broadcasted_iota(jnp.int32, x.shape, 0)
+    top = x.astype(BF).astype(F32)
+    mid = (x - top).astype(BF).astype(F32)
+    gains[...] = jnp.where(row == 0, top, jnp.where(row == 1, mid, jnp.where(row == 2, x - top - mid, 0.0))).astype(BF)
     own_out[...] = hp[:, window(me, wide)]
     send[:rows, :] = hp[:, window(1 - me, wide)].astype(BF)
     row = lax.broadcasted_iota(jnp.int32, (8, dh), 0)
@@ -182,28 +188,21 @@
     send[rows:, :] = jnp.concatenate([top, sq - top], axis=0).astype(BF)
 
 
-def mix_kernel(stream_far, gain_far, own, own_sq, got, *refs):
-    *asks, mixed, low, stream, gain, sems = refs
-    copies = fetch([(stream_far, stream), (gain_far, gain)], sems)
+def mix_kernel(own, own_sq, got, base, gains, *refs):
+    *asks, mixed, low = refs
     n, wide = mixed.shape
-    rows, me = own.shape[0], lax.axis_index("rep")
+    rows = own.shape[0]
     tail = got[rows:, :].astype(F32)
     sq = own_sq[...] + tail[:8] + tail[8:]
     y = (own[...] + got[:rows, :].astype(F32)) * (jnp.sqrt(sq[0:1]) * lax.rsqrt(sq[1:2] + 1e-06))
-    for c in copies:
-        c.wait()
-    mixed[...] = y[:n] + stream[:, window(me, wide)].astype(F32)
+    mixed[...] = y[:n] + base[...].astype(F32)
     low[:n, :] = mixed[...].astype(BF)
     for message in asks:
         part = message.shape[0]
         for i in range(n // part):
             at, there = n + i * part, message.shape[1] - n // part * wide + i * wide
             low[at : at + part, :] = (y[at : at + part] + message[:, there : there + wide].astype(F32)).astype(BF)
-    x = jnp.broadcast_to(gain[:, window(me, wide)], (16, wide))
-    row = lax.broadcasted_iota(jnp.int32, x.shape, 0)
-    top = x.astype(BF).astype(F32)
-    mid = (x - top).astype(BF).astype(F32)
-    low[rows:, :] = jnp.where(row == 0, top, jnp.where(row == 1, mid, jnp.where(row == 2, x - top - mid, 0.0))).astype(BF)
+    low[rows:, :] = gains[...]
 
 
 def norm_kernel(places, *refs):
@@ -233,49 +232,28 @@
     return [mlp[0].at[t, :deep, :] for t in each], [mlp[0].at[t, deep:, :] for t in each]
 
 
-def feed(z, ups, downs, os, wait=lambda: None):
+def feed(z, ups, downs, out):
+    n_head = lax.axis_size("head")
+    part = z.shape[1] // n_head
     deep = z.shape[1] // len(ups)
+    wide = min(deep, part)
     total = None
     for t, x in enumerate(ups):
         term = dot(z[:, t * deep : (t + 1) * deep], x[...])
         total = term if total is None else total + term
     h = (0.5 * total * (1.0 + lax.erf(total * np.float32(0.5**0.5)))).astype(BF)
-    wait()
     for t, x in enumerate(downs):
-        os[:, t * deep : (t + 1) * deep] = dot(h, x[...])
-
-
-def turned(os, out):
-    n_head = lax.axis_size("head")
-    part = os.shape[1] // n_head
-    for dh in range(n_head):
-        cols = window(lax.rem(lax.axis_index("head") + dh, n_head), part)
-        out[:, dh * part : (dh + 1) * part] = os[:, cols].astype(out.dtype)
-
-
-def theirs_kernel(n_mlp, *refs):
-    far, (zs, send, *near), (os, sems) = refs[:n_mlp], refs[n_mlp:-2], refs[-2:]
-    width = zs.shape[1]
-    pairs = [p for f, n in zip(blocks_of(far, width), blocks_of(near, width)) for p in zip(f, n)]
-    copies = fetch(pairs, sems)
-    ups, downs = blocks_of(near, width)
-    for c in copies[: len(ups)]:
-        c.wait()
-
-    def rest():
-        for c in copies[len(ups) :]:
-            c.wait()
-
-    rows = send.shape[0]
-    feed(zs[window(1 - lax.axis_index("rep"), rows), :], ups, downs, os, rest)
-    turned(os, send)
-
-
-def ours_kernel(zs, *refs):
-    *mlp, own, os = refs
+        for c in range(0, deep, wide):
+            head, at = divmod(t * deep + c, part)
+            place = lax.rem(head - lax.axis_index("head") + n_head, n_head) * part + at
+            out[:, pl.ds(pl.multiple_of(place, wide), wide)] = dot(h, x[:, c : c + wide]).astype(out.dtype)
+
+
+def feed_kernel(ours, zs, *refs):
+    *mlp, out = refs
     ups, downs = blocks_of(mlp, zs.shape[1])
-    feed(zs[window(lax.axis_index("rep"), own.shape[0]), :], ups, downs, os)
-    turned(os, own)
+    me = lax.axis_index("rep")
+    feed(zs[window(me if ours else 1 - me, out.shape[0]), :], ups, downs, out)
 
 
 def pair_kernel(moves, own, got, *outs):
@@ -336,7 +314,8 @@
     asks = []
     if paired:
         share, full = messages
-        others = [moved(full, tok=1), moved(share, tok=2), moved(share, tok=3)]
+        others = [moved(share, tok=2), moved(full, tok=1)][::-1]
+        others.append(moved(others[1], tok=1))
         (blocks,) = call(
             pack_kernel, [shape((n_tok, mlp_up.shape[0] + units, units), BF)], [mlp_up, mlp_down]
         )
@@ -356,10 +335,16 @@
 
     n_all = sum(x.shape[0] for x in tokens) + (n_key if paired else 0)
     tokens = barrier(tokens)
-    sources = [fw_one[0], fw_three[0], fw_two[0], keys, values, rate_row, queries]
-    own, own_sq, send = call(
+    sources = [fw_one[0], fw_three[0], fw_two[0], keys, values, rate_row, queries, stream, gain]
+    own, own_sq, send, base, gains = call(
         functools.partial(fast_kernel, len(tokens), near),
-        [shape((near * n, wide), F32), shape((8, wide), F32), shape((near * n + 16, wide), BF)],
+        [
+            shape((near * n, wide), F32),
+            shape((8, wide), F32),
+            shape((near * n + 16, wide), BF),
+            shape((n, wide), BF),
+            shape((16, wide), BF),
+        ],
         [*sources, *tokens],
         [
             pltpu.VMEM((n_all, dh), BF),
@@ -373,13 +358,10 @@
         fetched=len(sources),
     )
     got = moved(send, rep=1)
-    sources = [stream, gain]
     mixed, low = call(
         mix_kernel,
         [shape((n, wide), F32), shape((near * n + 16, wide), BF)],
-        [*sources, own, own_sq, got, *asks],
-        [*local(sources), pltpu.SemaphoreType.DMA((2,))],
-        fetched=2,
+        [own, own_sq, got, base, gains, *asks],
     )
     pieces, places = [], []
     for dg, h in itertools.product(range(groups), range(n_head)):
@@ -390,16 +372,12 @@
     (zs,) = call(
         functools.partial(norm_kernel, places), [shape((groups * near * n, model), BF)], pieces
     )
-    send, *mlp = call(
-        functools.partial(theirs_kernel, len(mlp)),
-        [shape((near * n, model), BF), *[shape(x.shape, BF) for x in mlp]],
-        [*mlp, zs],
-        [pltpu.VMEM((near * n, model), F32), pltpu.SemaphoreType.DMA((2 * n_tok if paired else 2,))],
-        unmoved=len(mlp),
+    (send,) = call(
+        functools.partial(feed_kernel, False), [shape((near * n, model), BF)], [zs, *mlp]
     )
     got = moved(send, rep=1)
     (own,) = call(
-        ours_kernel, [shape((near * n, model), F32)], [zs, *mlp], [pltpu.VMEM((near * n, model), F32)]
+        functools.partial(feed_kernel, True), [shape((near * n, model), F32)], [zs, *mlp]
     )
     moves = sorted(itertools.product(range(near), range(n_head)), key=lambda m: (-m[0] - m[1], m[0]))
     parts = call(

time: 64.3 us -> 62.4 us (0.970)
  Pallas kernels: 12.8 us -> 10.2 us
  starting transfers between devices: 18.4 us -> 19.7 us
  waiting for transfers between devices: 30.4 us -> 29.7 us
    pallas_call x9, Pallas kernels: 12.8 us -> 10.2 us  [call(): pl.pallas_call(kernel, out_shape=outs, in_specs=[pl.BlockSpec(memory_spac...]
    ppermute x16, waiting for transfers between devices: 21.8 us -> 20.3 us  [moved(): return lax.ppermute(x, tuple(axes), pairs)]
    all_to_all x1, waiting for transfers between devices: 3.34 us -> 4.18 us  [on_device(): mlp = [lax.all_to_all(blocks, 'tok', 0, 0)]]
    all_to_all x1, starting transfers between devices: 3.52 us -> 4.36 us  [on_device(): mlp = [lax.all_to_all(blocks, 'tok', 0, 0)]]
  transfers between devices with their start and end apart: 21 -> 21, of which waited for: 16 -> 16; matrix products, arithmetic and copies ran while one was open for 0% -> 0% of each run, Pallas kernels for 14% -> 13%
where the time goes in v8:
time: 62.4 us; the launch traced here: 62.2 us
  waiting for transfers between devices  29.7 us (48%)
  starting transfers between devices  19.7 us (32%)
  Pallas kernels  10.2 us (16%)
  local copies, waits for them, and re-layouts  1.05 us (2%)
  between operations  0.74 us (1%)
  other arithmetic  0.72 us (1%)
    ppermute x16, waiting for transfers between devices, moved(): return lax.ppermute(x, tuple(axes), pairs)  20.3 us
    ppermute x16, starting transfers between devices, moved(): return lax.ppermute(x, tuple(axes), pairs)  11.2 us
    pallas_call x9, Pallas kernels, call(): pl.pallas_call(kernel, out_shape=outs, in_specs=[pl.BlockSpec(memory_spac...  10.2 us
    ppermute x4, waiting for transfers between devices, dealt(): return lax.ppermute(x, axes, pairs)  5.23 us
    all_to_all x1, starting transfers between devices, on_device(): mlp = [lax.all_to_all(blocks, 'tok', 0, 0)]  4.36 us
    ppermute x4, starting transfers between devices, dealt(): return lax.ppermute(x, axes, pairs)  4.2 us
    all_to_all x1, waiting for transfers between devices, on_device(): mlp = [lax.all_to_all(blocks, 'tok', 0, 0)]  4.18 us
  transfers between devices with their start and end apart: 21, of which 16 were waited for; matrix products, arithmetic and copies ran while one was open for 0% of the time, Pallas kernels for 13%

profile of v8, /device:TPU:0, one launch (start us, length us, event | category | flops | bytes accessed | tf_op | source)
XLA Modules:
  0.0 62.2 jit_solution(6984462418464114730)
XLA Ops:
  0.0 0.0 copy-start
  0.0 1.3 %shard_map.118 = (bf16[64,1024]{1,0:T(8,128)(2,1)S(1)}, bf16[64,2048]{1,0:T(8,128)(2,1)S(1)}) custom-call(bf16[128,512]{1,0:T(8,128)(2,1)} %refs_3_.3, bf16[128,512]{1,0:T(8,128)(2,1)} %refs_4_.3, f32[1,128]{1,0:T(1,128)} %bitcast.11, bf16[128,512]{1,0:T(8,128)(2,1)} %refs_6_.1, bf16[128,512]{1,0:T(8,128)(2,1)} %refs_7_.1), custom_call_target="tpu_custom_call" | custom-call | flops 1 | bytes 1 | tf_op jit(solution)/shard_map/pallas_call | solution.py:41
  1.3 4.1 %collective-permute-start.1 = (bf16[64,1024]{1,0:T(8,128)(2,1)S(1)}, bf16[64,1024]{1,0:T(8,128)(2,1)S(1)}, u32[]{:S(2)}, u32[]{:S(2)}) collective-permute-start(bf16[64,1024]{1,0:T(8,128)(2,1)S(1)} %get-tuple-element.31), channel_id=1, source_target_pairs={{8,0},{12,4},{0,8},{4,12},{9,1},{13,5},{1,9},{5,13},{10,2},{14,6},... | collective-permute-start | bytes 393224 | tf_op jit(solution)/shard_map/ppermute | solution.py:30
  5.4 1.6 %collective-permute-start = (bf16[64,2048]{1,0:T(8,128)(2,1)S(1)}, bf16[64,2048]{1,0:T(8,128)(2,1)S(1)}, u32[]{:S(2)}, u32[]{:S(2)}) collective-permute-start(bf16[64,2048]{1,0:T(8,128)(2,1)S(1)} %get-tuple-element.30), channel_id=1, source_target_pairs={{4,0},{0,4},{12,8},{8,12},{5,1},{1,5},{13,9},{9,13},{6,2},{2,6},{1... | collective-permute-start | bytes 786440 | tf_op jit(solution)/shard_map/ppermute | solution.py:30
  7.0 4.8 %collective-permute-done.1.refs_10_ = bf16[64,1024]{1,0:T(8,128)(2,1)S(1)} collective-permute-done((bf16[64,1024]{1,0:T(8,128)(2,1)S(1)}, bf16[64,1024]{1,0:T(8,128)(2,1)S(1)}, u32[]{:S(2)}, u32[]{:S(2)}) %collective-permute-start.1) | collective-permute-done | bytes 131104 | tf_op jit(solution)/shard_map/ppermute | solution.py:30
  11.9 0.7 %collective-permute-start.2 = (bf16[64,1024]{1,0:T(8,128)(2,1)S(1)}, bf16[64,1024]{1,0:T(8,128)(2,1)S(1)}, u32[]{:S(2)}, u32[]{:S(2)}) collective-permute-start(bf16[64,1024]{1,0:T(8,128)(2,1)S(1)} %collective-permute-done.1.refs_10_), channel_id=1, source_target_pairs={{4,0},{0,4},{12,8},{8,12},{5,1},{1,5},{13,9},{9,13},{6,2},{2,6},{1... | collective-permute-start | bytes 393224 | tf_op jit(solution)/shard_map/ppermute | solution.py:30
  12.5 0.0 copy-done
  12.5 0.0 copy-start.1
  12.5 1.0 %copy-done.1 = bf16[1024,256]{1,0:T(8,128)(2,1)S(1)} copy-done((bf16[1024,256]{1,0:T(8,128)(2,1)S(1)}, bf16[1024,256]{1,0:T(8,128)(2,1)}, u32[]{:S(2)}) %copy-start.1) | copy-done | bytes 524312
  13.6 1.1 %shard_map.119 = bf16[4,512,256]{2,1,0:T(8,128)(2,1)} custom-call(bf16[256,1024]{1,0:T(8,128)(2,1)S(1)} %copy-done, bf16[1024,256]{1,0:T(8,128)(2,1)S(1)} %copy-done.1), custom_call_target="tpu_custom_call" | custom-call | flops 1 | bytes 1 | tf_op jit(solution)/shard_map/pallas_call | solution.py:41
  14.7 3.0 %collective-permute-done.2.refs_11_ = bf16[64,1024]{1,0:T(8,128)(2,1)S(1)} collective-permute-done((bf16[64,1024]{1,0:T(8,128)(2,1)S(1)}, bf16[64,1024]{1,0:T(8,128)(2,1)S(1)}, u32[]{:S(2)}, u32[]{:S(2)}) %collective-permute-start.2) | collective-permute-done | bytes 131104 | tf_op jit(solution)/shard_map/ppermute | solution.py:30
  17.7 0.0 collective-permute-done.refs_9_.refs_0_
  17.7 4.4 %all-to-all-start = ((bf16[4,512,256]{2,1,0:T(8,128)(2,1)}), bf16[4,512,256]{2,1,0:T(8,128)(2,1)S(1)}, u32[]{:S(2)}, u32[]{:S(2)}) async-start(bf16[4,512,256]{2,1,0:T(8,128)(2,1)} %shard_map.119), calls=%async_computation | async-start | bytes 2097152 | tf_op jit(solution)/shard_map/all_to_all | solution.py:323
  22.0 0.0 collective-permute-start.3
  22.0 0.5 collective-permute-start.4
  22.5 0.0 collective-permute-start.5
  22.5 1.2 %collective-permute-done.4.refs_13_ = bf16[64,1024]{1,0:T(8,128)(2,1)S(1)} collective-permute-done((bf16[64,1024]{1,0:T(8,128)(2,1)S(1)}, bf16[64,1024]{1,0:T(8,128)(2,1)S(1)}, u32[]{:S(2)}, u32[]{:S(2)}) %collective-permute-start.4) | collective-permute-done | bytes 131104 | tf_op jit(solution)/shard_map/ppermute | solution.py:30
  23.8 0.2 collective-permute-done.5.refs_14_
  23.9 0.0 collective-permute-done.3.refs_12_
  23.9 5.5 %shard_map.120 = (f32[256,256]{1,0:T(8,128)S(1)}, f32[8,256]{1,0:T(8,128)S(1)}, bf16[272,256]{1,0:T(8,128)(2,1)S(1)}, bf16[128,256]{1,0:T(8,128)(2,1)S(1)}, bf16[16,256]{1,0:T(8,128)(2,1)S(1)}) custom-call(f32[512,512]{1,0:T(8,128)} %bitcast.7, f32[512,512]{1,0:T(8,128)} %bitcast.8, f32[512,512]{1,0:T(8,128)} %bitcast.9, bf16[128,512]{1,0:T(8,128)(2,1)} %refs_3_.3, ...), custom_call_target="tpu_custom_call" | custom-call | flops 1 | bytes 1 | tf_op jit(solution)/shard_map/pallas_call | solution.py:41
  29.4 0.2 collective-permute-start.6
  29.6 1.2 %collective-permute-done.6.got = bf16[272,256]{1,0:T(8,128)(2,1)S(1)} collective-permute-done((bf16[272,256]{1,0:T(8,128)(2,1)S(1)}, bf16[272,256]{1,0:T(8,128)(2,1)S(1)}, u32[]{:S(2)}, u32[]{:S(2)}) %collective-permute-start.6) | collective-permute-done | bytes 139296 | tf_op jit(solution)/shard_map/ppermute | solution.py:30
  30.9 0.1 shard_map.121
  30.9 1.6 %collective-permute-start.10 = (bf16[272,256]{1,0:T(8,128)(2,1)S(1)}, bf16[272,256]{1,0:T(8,128)(2,1)S(1)}, u32[]{:S(2)}, u32[]{:S(2)}) collective-permute-start(bf16[272,256]{1,0:T(8,128)(2,1)S(1)} %get-tuple-element.46.refs_0_), channel_id=1, source_target_pairs={{16,0},{0,16},{17,1},{1,17},{18,2},{2,18},{19,3},{3,19},{20,4},{4,... | collective-permute-start | bytes 417800 | tf_op jit(solution)/shard_map/ppermute | solution.py:30
  32.5 1.4 %collective-permute-start.12 = (bf16[272,256]{1,0:T(8,128)(2,1)S(1)}, bf16[272,256]{1,0:T(8,128)(2,1)S(1)}, u32[]{:S(2)}, u32[]{:S(2)}) collective-permute-start(bf16[272,256]{1,0:T(8,128)(2,1)S(1)} %get-tuple-element.46.refs_0_), channel_id=1, source_target_pairs={{18,0},{16,2},{2,16},{0,18},{19,1},{17,3},{3,17},{1,19},{22,4},{20... | collective-permute-start | bytes 417800 | tf_op jit(solution)/shard_map/ppermute | solution.py:30
  33.9 0.5 collective-permute-start.8
  34.5 0.0 collective-permute-start.7
  34.5 4.9 %collective-permute-done.10.refs_4_ = bf16[272,256]{1,0:T(8,128)(2,1)S(1)} collective-permute-done((bf16[272,256]{1,0:T(8,128)(2,1)S(1)}, bf16[272,256]{1,0:T(8,128)(2,1)S(1)}, u32[]{:S(2)}, u32[]{:S(2)}) %collective-permute-start.10) | collective-permute-done | bytes 139296 | tf_op jit(solution)/shard_map/ppermute | solution.py:30
  39.4 0.0 collective-permute-start.11
  39.4 0.5 collective-permute-done.12.refs_6_
  40.0 0.0 collective-permute-start.13
  40.0 1.0 %collective-permute-done.8.refs_2_ = bf16[272,256]{1,0:T(8,128)(2,1)S(1)} collective-permute-done((bf16[272,256]{1,0:T(8,128)(2,1)S(1)}, bf16[272,256]{1,0:T(8,128)(2,1)S(1)}, u32[]{:S(2)}, u32[]{:S(2)}) %collective-permute-start.8) | collective-permute-done | bytes 139296 | tf_op jit(solution)/shard_map/ppermute | solution.py:30
  40.9 0.0 collective-permute-start.9
  40.9 0.0 collective-permute-done.7.refs_1_
  40.9 0.0 collective-permute-done.11.refs_5_
  40.9 0.4 collective-permute-done.13.refs_7_
  41.3 1.0 %collective-permute-done.9.refs_3_ = bf16[272,256]{1,0:T(8,128)(2,1)S(1)} collective-permute-done((bf16[272,256]{1,0:T(8,128)(2,1)S(1)}, bf16[272,256]{1,0:T(8,128)(2,1)S(1)}, u32[]{:S(2)}, u32[]{:S(2)}) %collective-permute-start.9) | collective-permute-done | bytes 139296 | tf_op jit(solution)/shard_map/ppermute | solution.py:30
  42.3 0.5 shard_map.122.zs
  42.8 4.2 %all-to-all-done.refs_0_ = bf16[4,512,256]{2,1,0:T(8,128)(2,1)S(1)} async-done(((bf16[4,512,256]{2,1,0:T(8,128)(2,1)}), bf16[4,512,256]{2,1,0:T(8,128)(2,1)S(1)}, u32[]{:S(2)}, u32[]{:S(2)}) %all-to-all-start) | async-done | bytes 1048608 | tf_op jit(solution)/shard_map/all_to_all | solution.py:323
  47.0 0.7 %shard_map.124 = bf16[256,1024]{1,0:T(8,128)(2,1)S(1)} custom-call(bf16[512,1024]{1,0:T(8,128)(2,1)S(1)} %shard_map.122.zs, bf16[4,512,256]{2,1,0:T(8,128)(2,1)S(1)} %all-to-all-done.refs_0_), custom_call_target="tpu_custom_call" | custom-call | flops 1 | bytes 1 | tf_op jit(solution)/shard_map/pallas_call | solution.py:41
  47.8 0.1 collective-permute-start.14
  47.9 0.8 %shard_map.123.own = f32[256,1024]{1,0:T(8,128)S(1)} custom-call(bf16[512,1024]{1,0:T(8,128)(2,1)S(1)} %shard_map.122.zs, bf16[4,512,256]{2,1,0:T(8,128)(2,1)S(1)} %all-to-all-done.refs_0_), custom_call_target="tpu_custom_call" | custom-call | flops 1 | bytes 1 | tf_op jit(solution)/shard_map/pallas_call | solution.py:41
  48.6 1.1 %collective-permute-done.14.got = bf16[256,1024]{1,0:T(8,128)(2,1)S(1)} collective-permute-done((bf16[256,1024]{1,0:T(8,128)(2,1)S(1)}, bf16[256,1024]{1,0:T(8,128)(2,1)S(1)}, u32[]{:S(2)}, u32[]{:S(2)}) %collective-permute-start.14) | collective-permute-done | bytes 524320 | tf_op jit(solution)/shard_map/ppermute | solution.py:30
  49.8 0.1 shard_map.125
  49.8 0.1 collective-permute-start.15
  49.9 1.6 %collective-permute-start.16 = (bf16[128,512]{1,0:T(8,128)(2,1)S(1)}, bf16[128,512]{1,0:T(8,128)(2,1)S(1)}, u32[]{:S(2)}, u32[]{:S(2)}) collective-permute-start(bf16[128,512]{1,0:T(8,128)(2,1)S(1)} %get-tuple-element.49), channel_id=1, source_target_pairs={{0,2},{1,19},{2,0},{3,17},{4,6},{5,23},{6,4},{7,21},{8,10},{9,27},... | collective-permute-start | bytes 393224 | tf_op jit(solution)/shard_map/ppermute | solution.py:285
  51.5 1.9 %collective-permute-start.17 = (bf16[128,512]{1,0:T(8,128)(2,1)S(1)}, bf16[128,512]{1,0:T(8,128)(2,1)S(1)}, u32[]{:S(2)}, u32[]{:S(2)}) collective-permute-start(bf16[128,512]{1,0:T(8,128)(2,1)S(1)} %get-tuple-element.50), channel_id=1, source_target_pairs={{0,4},{1,21},{2,6},{3,23},{4,0},{5,17},{6,2},{7,19},{8,12},{9,29},... | collective-permute-start | bytes 393224 | tf_op jit(solution)/shard_map/ppermute | solution.py:285
  53.4 0.7 %collective-permute-start.18 = (bf16[128,512]{1,0:T(8,128)(2,1)S(1)}, bf16[128,512]{1,0:T(8,128)(2,1)S(1)}, u32[]{:S(2)}, u32[]{:S(2)}) collective-permute-start(bf16[128,512]{1,0:T(8,128)(2,1)S(1)} %get-tuple-element.51), channel_id=1, source_target_pairs={{0,0},{1,17},{2,2},{3,19},{4,4},{5,21},{6,6},{7,23},{8,8},{9,25},{... | collective-permute-start | bytes 393224 | tf_op jit(solution)/shard_map/ppermute | solution.py:285
  54.7 2.4 %collective-permute-done.15.refs_0_ = bf16[128,512]{1,0:T(8,128)(2,1)S(1)} collective-permute-done((bf16[128,512]{1,0:T(8,128)(2,1)S(1)}, bf16[128,512]{1,0:T(8,128)(2,1)S(1)}, u32[]{:S(2)}, u32[]{:S(2)}) %collective-permute-start.15) | collective-permute-done | bytes 131104 | tf_op jit(solution)/shard_map/ppermute | solution.py:285
  57.2 1.9 %collective-permute-done.16.refs_1_ = bf16[128,512]{1,0:T(8,128)(2,1)S(1)} collective-permute-done((bf16[128,512]{1,0:T(8,128)(2,1)S(1)}, bf16[128,512]{1,0:T(8,128)(2,1)S(1)}, u32[]{:S(2)}, u32[]{:S(2)}) %collective-permute-start.16) | collective-permute-done | bytes 131104 | tf_op jit(solution)/shard_map/ppermute | solution.py:285
  59.0 0.9 %collective-permute-done.17.refs_2_ = bf16[128,512]{1,0:T(8,128)(2,1)S(1)} collective-permute-done((bf16[128,512]{1,0:T(8,128)(2,1)S(1)}, bf16[128,512]{1,0:T(8,128)(2,1)S(1)}, u32[]{:S(2)}, u32[]{:S(2)}) %collective-permute-start.17) | collective-permute-done | bytes 131104 | tf_op jit(solution)/shard_map/ppermute | solution.py:285
  59.9 0.0 collective-permute-done.18.refs_3_
  59.9 0.1 shard_map.126
  60.1 0.5 collective-permute-start.19
  60.6 0.9 %collective-permute-done.19 = bf16[128,256]{1,0:T(8,128)(2,1)S(1)} collective-permute-done((bf16[128,256]{1,0:T(8,128)(2,1)S(1)}, bf16[128,256]{1,0:T(8,128)(2,1)S(1)}, u32[]{:S(2)}, u32[]{:S(2)}) %collective-permute-start.19) | collective-permute-done | bytes 65568 | tf_op jit(solution)/shard_map/ppermute | solution.py:30
  61.5 0.7 %select_convert_fusion = bf16[128,256]{1,0:T(8,128)(2,1)} fusion(f32[128,256]{1,0:T(8,128)S(1)} %get-tuple-element.53, bf16[128,256]{1,0:T(8,128)(2,1)S(1)} %collective-permute-done.19, pred[128]{0:T(512)(128)(4,1)S(1)} %iota_compare_fusion), kind=kLoop, calls=%fused_computation | loop fusion | flops 131072 | bytes 262272 | tf_op jit(solution)/shard_map/convert_element_type | solution.py:392
  (1 shorter events, 0.0 us)
Async XLA Ops:
  0.0 12.5 %copy-start = (bf16[256,1024]{1,0:T(8,128)(2,1)S(1)}, bf16[256,1024]{1,0:T(8,128)(2,1)}, u32[]{:S(2)}) copy-start(bf16[256,1024]{1,0:T(8,128)(2,1)} %up.1) | copy-start | bytes 1572868
  1.3 10.5 %collective-permute-start.1 = (bf16[64,1024]{1,0:T(8,128)(2,1)S(1)}, bf16[64,1024]{1,0:T(8,128)(2,1)S(1)}, u32[]{:S(2)}, u32[]{:S(2)}) collective-permute-start(bf16[64,1024]{1,0:T(8,128)(2,1)S(1)} %get-tuple-element.31), channel_id=1, source_target_pairs={{8,0},{12,4},{0,8},{4,12},{9,1},{13,5},{1,9},{5,13},{10,2},{14,6},... | collective-permute-start | bytes 393224 | tf_op jit(solution)/shard_map/ppermute | solution.py:30
  5.4 12.2 %collective-permute-start = (bf16[64,2048]{1,0:T(8,128)(2,1)S(1)}, bf16[64,2048]{1,0:T(8,128)(2,1)S(1)}, u32[]{:S(2)}, u32[]{:S(2)}) collective-permute-start(bf16[64,2048]{1,0:T(8,128)(2,1)S(1)} %get-tuple-element.30), channel_id=1, source_target_pairs={{4,0},{0,4},{12,8},{8,12},{5,1},{1,5},{13,9},{9,13},{6,2},{2,6},{1... | collective-permute-start | bytes 786440 | tf_op jit(solution)/shard_map/ppermute | solution.py:30
  11.9 5.8 %collective-permute-start.2 = (bf16[64,1024]{1,0:T(8,128)(2,1)S(1)}, bf16[64,1024]{1,0:T(8,128)(2,1)S(1)}, u32[]{:S(2)}, u32[]{:S(2)}) collective-permute-start(bf16[64,1024]{1,0:T(8,128)(2,1)S(1)} %collective-permute-done.1.refs_10_), channel_id=1, source_target_pairs={{4,0},{0,4},{12,8},{8,12},{5,1},{1,5},{13,9},{9,13},{6,2},{2,6},{1... | collective-permute-start | bytes 393224 | tf_op jit(solution)/shard_map/ppermute | solution.py:30
  12.5 1.0 %copy-start.1 = (bf16[1024,256]{1,0:T(8,128)(2,1)S(1)}, bf16[1024,256]{1,0:T(8,128)(2,1)}, u32[]{:S(2)}) copy-start(bf16[1024,256]{1,0:T(8,128)(2,1)} %down.1) | copy-start | bytes 1572868
  17.7 29.3 %all-to-all-start = ((bf16[4,512,256]{2,1,0:T(8,128)(2,1)}), bf16[4,512,256]{2,1,0:T(8,128)(2,1)S(1)}, u32[]{:S(2)}, u32[]{:S(2)}) async-start(bf16[4,512,256]{2,1,0:T(8,128)(2,1)} %shard_map.119), calls=%async_computation | async-start | bytes 2097152 | tf_op jit(solution)/shard_map/all_to_all | solution.py:323
  22.0 1.9 %collective-permute-start.3 = (bf16[64,2048]{1,0:T(8,128)(2,1)S(1)}, bf16[64,2048]{1,0:T(8,128)(2,1)S(1)}, u32[]{:S(2)}, u32[]{:S(2)}) collective-permute-start(bf16[64,2048]{1,0:T(8,128)(2,1)S(1)} %collective-permute-done.refs_9_.refs_0_), channel_id=1, source_target_pairs={{1,0},{0,1},{3,2},{2,3},{5,4},{4,5},{7,6},{6,7},{9,8},{8,9},{11,10... | collective-permute-start | bytes 786440 | tf_op jit(solution)/shard_map/ppermute | solution.py:30
  22.0 1.7 %collective-permute-start.4 = (bf16[64,1024]{1,0:T(8,128)(2,1)S(1)}, bf16[64,1024]{1,0:T(8,128)(2,1)S(1)}, u32[]{:S(2)}, u32[]{:S(2)}) collective-permute-start(bf16[64,1024]{1,0:T(8,128)(2,1)S(1)} %collective-permute-done.1.refs_10_), channel_id=1, source_target_pairs={{1,0},{0,1},{3,2},{2,3},{5,4},{4,5},{7,6},{6,7},{9,8},{8,9},{11,10... | collective-permute-start | bytes 393224 | tf_op jit(solution)/shard_map/ppermute | solution.py:30
  22.5 1.4 %collective-permute-start.5 = (bf16[64,1024]{1,0:T(8,128)(2,1)S(1)}, bf16[64,1024]{1,0:T(8,128)(2,1)S(1)}, u32[]{:S(2)}, u32[]{:S(2)}) collective-permute-start(bf16[64,1024]{1,0:T(8,128)(2,1)S(1)} %collective-permute-done.2.refs_11_), channel_id=1, source_target_pairs={{1,0},{0,1},{3,2},{2,3},{5,4},{4,5},{7,6},{6,7},{9,8},{8,9},{11,10... | collective-permute-start | bytes 393224 | tf_op jit(solution)/shard_map/ppermute | solution.py:30
  29.4 1.4 %collective-permute-start.6 = (bf16[272,256]{1,0:T(8,128)(2,1)S(1)}, bf16[272,256]{1,0:T(8,128)(2,1)S(1)}, u32[]{:S(2)}, u32[]{:S(2)}) collective-permute-start(bf16[272,256]{1,0:T(8,128)(2,1)S(1)} %get-tuple-element.43), channel_id=1, source_target_pairs={{1,0},{0,1},{3,2},{2,3},{5,4},{4,5},{7,6},{6,7},{9,8},{8,9},{11,10... | collective-permute-start | bytes 417800 | tf_op jit(solution)/shard_map/ppermute | solution.py:30
  30.9 8.5 %collective-permute-start.10 = (bf16[272,256]{1,0:T(8,128)(2,1)S(1)}, bf16[272,256]{1,0:T(8,128)(2,1)S(1)}, u32[]{:S(2)}, u32[]{:S(2)}) collective-permute-start(bf16[272,256]{1,0:T(8,128)(2,1)S(1)} %get-tuple-element.46.refs_0_), channel_id=1, source_target_pairs={{16,0},{0,16},{17,1},{1,17},{18,2},{2,18},{19,3},{3,19},{20,4},{4,... | collective-permute-start | bytes 417800 | tf_op jit(solution)/shard_map/ppermute | solution.py:30
  32.5 7.5 %collective-permute-start.12 = (bf16[272,256]{1,0:T(8,128)(2,1)S(1)}, bf16[272,256]{1,0:T(8,128)(2,1)S(1)}, u32[]{:S(2)}, u32[]{:S(2)}) collective-permute-start(bf16[272,256]{1,0:T(8,128)(2,1)S(1)} %get-tuple-element.46.refs_0_), channel_id=1, source_target_pairs={{18,0},{16,2},{2,16},{0,18},{19,1},{17,3},{3,17},{1,19},{22,4},{20... | collective-permute-start | bytes 417800 | tf_op jit(solution)/shard_map/ppermute | solution.py:30
  33.9 7.0 %collective-permute-start.8 = (bf16[272,256]{1,0:T(8,128)(2,1)S(1)}, bf16[272,256]{1,0:T(8,128)(2,1)S(1)}, u32[]{:S(2)}, u32[]{:S(2)}) collective-permute-start(bf16[272,256]{1,0:T(8,128)(2,1)S(1)} %get-tuple-element.46.refs_0_), channel_id=1, source_target_pairs={{2,0},{0,2},{3,1},{1,3},{6,4},{4,6},{7,5},{5,7},{10,8},{8,10},{11,... | collective-permute-start | bytes 417800 | tf_op jit(solution)/shard_map/ppermute | solution.py:30
  34.5 6.5 %collective-permute-start.7 = (bf16[272,256]{1,0:T(8,128)(2,1)S(1)}, bf16[272,256]{1,0:T(8,128)(2,1)S(1)}, u32[]{:S(2)}, u32[]{:S(2)}) collective-permute-start(bf16[272,256]{1,0:T(8,128)(2,1)S(1)} %get-tuple-element.46.refs_0_), channel_id=1, source_target_pairs={{1,0},{0,1},{3,2},{2,3},{5,4},{4,5},{7,6},{6,7},{9,8},{8,9},{11,10... | collective-permute-start | bytes 417800 | tf_op jit(solution)/shard_map/ppermute | solution.py:30
  39.4 1.5 %collective-permute-start.11 = (bf16[272,256]{1,0:T(8,128)(2,1)S(1)}, bf16[272,256]{1,0:T(8,128)(2,1)S(1)}, u32[]{:S(2)}, u32[]{:S(2)}) collective-permute-start(bf16[272,256]{1,0:T(8,128)(2,1)S(1)} %collective-permute-done.10.refs_4_), channel_id=1, source_target_pairs={{1,0},{0,1},{3,2},{2,3},{5,4},{4,5},{7,6},{6,7},{9,8},{8,9},{11,10... | collective-permute-start | bytes 417800 | tf_op jit(solution)/shard_map/ppermute | solution.py:30
  40.0 1.4 %collective-permute-start.13 = (bf16[272,256]{1,0:T(8,128)(2,1)S(1)}, bf16[272,256]{1,0:T(8,128)(2,1)S(1)}, u32[]{:S(2)}, u32[]{:S(2)}) collective-permute-start(bf16[272,256]{1,0:T(8,128)(2,1)S(1)} %collective-permute-done.12.refs_6_), channel_id=1, source_target_pairs={{1,0},{0,1},{3,2},{2,3},{5,4},{4,5},{7,6},{6,7},{9,8},{8,9},{11,10... | collective-permute-start | bytes 417800 | tf_op jit(solution)/shard_map/ppermute | solution.py:30
  40.9 1.4 %collective-permute-start.9 = (bf16[272,256]{1,0:T(8,128)(2,1)S(1)}, bf16[272,256]{1,0:T(8,128)(2,1)S(1)}, u32[]{:S(2)}, u32[]{:S(2)}) collective-permute-start(bf16[272,256]{1,0:T(8,128)(2,1)S(1)} %collective-permute-done.8.refs_2_), channel_id=1, source_target_pairs={{1,0},{0,1},{3,2},{2,3},{5,4},{4,5},{7,6},{6,7},{9,8},{8,9},{11,10... | collective-permute-start | bytes 417800 | tf_op jit(solution)/shard_map/ppermute | solution.py:30
  47.8 2.0 %collective-permute-start.14 = (bf16[256,1024]{1,0:T(8,128)(2,1)S(1)}, bf16[256,1024]{1,0:T(8,128)(2,1)S(1)}, u32[]{:S(2)}, u32[]{:S(2)}) collective-permute-start(bf16[256,1024]{1,0:T(8,128)(2,1)S(1)} %shard_map.124), channel_id=1, source_target_pairs={{1,0},{0,1},{3,2},{2,3},{5,4},{4,5},{7,6},{6,7},{9,8},{8,9},{11,10... | collective-permute-start | bytes 1572872 | tf_op jit(solution)/shard_map/ppermute | solution.py:30
  49.8 7.3 %collective-permute-start.15 = (bf16[128,512]{1,0:T(8,128)(2,1)S(1)}, bf16[128,512]{1,0:T(8,128)(2,1)S(1)}, u32[]{:S(2)}, u32[]{:S(2)}) collective-permute-start(bf16[128,512]{1,0:T(8,128)(2,1)S(1)} %get-tuple-element.48), channel_id=1, source_target_pairs={{0,6},{1,23},{2,4},{3,21},{4,2},{5,19},{6,0},{7,17},{8,14},{9,31},... | collective-permute-start | bytes 393224 | tf_op jit(solution)/shard_map/ppermute | solution.py:285
  49.9 9.1 %collective-permute-start.16 = (bf16[128,512]{1,0:T(8,128)(2,1)S(1)}, bf16[128,512]{1,0:T(8,128)(2,1)S(1)}, u32[]{:S(2)}, u32[]{:S(2)}) collective-permute-start(bf16[128,512]{1,0:T(8,128)(2,1)S(1)} %get-tuple-element.49), channel_id=1, source_target_pairs={{0,2},{1,19},{2,0},{3,17},{4,6},{5,23},{6,4},{7,21},{8,10},{9,27},... | collective-permute-start | bytes 393224 | tf_op jit(solution)/shard_map/ppermute | solution.py:285
  51.5 8.5 %collective-permute-start.17 = (bf16[128,512]{1,0:T(8,128)(2,1)S(1)}, bf16[128,512]{1,0:T(8,128)(2,1)S(1)}, u32[]{:S(2)}, u32[]{:S(2)}) collective-permute-start(bf16[128,512]{1,0:T(8,128)(2,1)S(1)} %get-tuple-element.50), channel_id=1, source_target_pairs={{0,4},{1,21},{2,6},{3,23},{4,0},{5,17},{6,2},{7,19},{8,12},{9,29},... | collective-permute-start | bytes 393224 | tf_op jit(solution)/shard_map/ppermute | solution.py:285
  53.4 6.5 %collective-permute-start.18 = (bf16[128,512]{1,0:T(8,128)(2,1)S(1)}, bf16[128,512]{1,0:T(8,128)(2,1)S(1)}, u32[]{:S(2)}, u32[]{:S(2)}) collective-permute-start(bf16[128,512]{1,0:T(8,128)(2,1)S(1)} %get-tuple-element.51), channel_id=1, source_target_pairs={{0,0},{1,17},{2,2},{3,19},{4,4},{5,21},{6,6},{7,23},{8,8},{9,25},{... | collective-permute-start | bytes 393224 | tf_op jit(solution)/shard_map/ppermute | solution.py:285
  60.1 1.4 %collective-permute-start.19 = (bf16[128,256]{1,0:T(8,128)(2,1)S(1)}, bf16[128,256]{1,0:T(8,128)(2,1)S(1)}, u32[]{:S(2)}, u32[]{:S(2)}) collective-permute-start(bf16[128,256]{1,0:T(8,128)(2,1)S(1)} %get-tuple-element.54), channel_id=1, source_target_pairs={{1,0},{0,1},{3,2},{2,3},{5,4},{4,5},{7,6},{6,7},{9,8},{8,9},{11,10... | collective-permute-start | bytes 196616 | tf_op jit(solution)/shard_map/ppermute | solution.py:30

commit v9 on v8

--- a/solution.py
+++ b/solution.py
@@ -72,27 +72,34 @@
         pair[:, dh + c : dh + c + 128] = (values[:, c : c + 128].astype(F32) * rate).astype(BF)
 
 
-def message_kernel(n_far, *refs):
-    far, refs = refs[:n_far], refs[n_far:]
-    outs, near, (pair, sems) = refs[: -n_far - 2], refs[-n_far - 2 : -2], refs[-2:]
-    for c in fetch(list(zip(far, near)), sems):
+def message_kernel(keys, values, rates, *refs):
+    out, *near, sems = refs
+    for c in fetch(list(zip((keys, values, rates), near)), sems):
         c.wait()
-    side_by_side(pair, *near[:3])
-    if len(outs) == 1:
-        outs[0][...] = pair[...]
-        return
-    share, full = outs
-    q, s = near[3:]
-    me, (rows, width) = lax.axis_index("rep"), share.shape
-    part = pair[window(me, rows), :]
-    share[...] = part
-    full[:, :width] = part
-    dh = width // 2
-    full[:, width : width + dh] = q[window(me, rows), :]
+    side_by_side(out, *near)
+
+
+def share_kernel(keys, values, rates, queries, stream, share, full, v, rate_row, rate, sems):
+    rows, width = share.shape
+    dh, n = width // 2, queries.shape[0]
     wide = dh // 2
-    for i in range(q.shape[0] // rows):
+    me = lax.axis_index("rep")
+    mine = window(me, rows)
+    pairs = [(keys.at[mine, :], share.at[:, :dh]), (values.at[mine, :], v), (rates, rate_row)]
+    pairs.append((queries.at[mine, :], full.at[:, width : width + dh]))
+    for i in range(n // rows):
         at = width + dh + i * wide
-        full[:, at : at + wide] = s[i * rows : (i + 1) * rows, window(me, wide)]
+        pairs.append((stream.at[i * rows : (i + 1) * rows, window(me, wide)], full.at[:, at : at + wide]))
+    copies = fetch(pairs, sems)
+    for c in copies[:3]:
+        c.wait()
+    rate[...] = jnp.broadcast_to(rate_row[...], (128, rate.shape[0])).T
+    by_row = rate[mine, :]
+    for c in range(0, dh, 128):
+        share[:, dh + c : dh + c + 128] = (v[:, c : c + 128].astype(F32) * by_row).astype(BF)
+    full[:, :width] = share[...]
+    for c in copies[3:]:
+        c.wait()
 
 
 def pack_kernel(up, down, out):
@@ -300,17 +307,28 @@
     rows = n_key // reps
     rate_row, gain = rates.reshape(1, n_key), gain[None, :]
     sources = [keys, values, rate_row]
-    outs = [shape((n_key, 2 * dh), BF)]
     if paired:
         sources += [queries, stream]
-        outs = [shape((rows, 2 * dh), BF), shape((rows, 4 * dh), BF)]
-    messages = call(
-        functools.partial(message_kernel, len(sources)),
-        outs,
-        sources,
-        [*local(sources), pltpu.VMEM((n_key, 2 * dh), BF), pltpu.SemaphoreType.DMA((len(sources),))],
-        fetched=len(sources),
-    )
+        messages = call(
+            share_kernel,
+            [shape((rows, 2 * dh), BF), shape((rows, 4 * dh), BF)],
+            sources,
+            [
+                pltpu.VMEM((rows, dh), BF),
+                pltpu.VMEM((1, n_key), F32),
+                pltpu.VMEM((n_key, 128), F32),
+                pltpu.SemaphoreType.DMA((4 + n // rows,)),
+            ],
+            fetched=len(sources),
+        )
+    else:
+        messages = call(
+            message_kernel,
+            [shape((n_key, 2 * dh), BF)],
+            sources,
+            [*local(sources), pltpu.SemaphoreType.DMA((len(sources),))],
+            fetched=len(sources),
+        )
     asks = []
     if paired:
         share, full = messages

time: 62.4 us -> 62.2 us (level)
  no operation moved by 1% of the time
where the time goes in v9:
time: 62.2 us; the launch traced here: 62 us
  waiting for transfers between devices  29.7 us (48%)
  starting transfers between devices  19.7 us (32%)
  Pallas kernels  9.99 us (16%)
  local copies, waits for them, and re-layouts  1.05 us (2%)
  between operations  0.74 us (1%)
  other arithmetic  0.72 us (1%)
    ppermute x16, waiting for transfers between devices, moved(): return lax.ppermute(x, tuple(axes), pairs)  20.3 us
    ppermute x16, starting transfers between devices, moved(): return lax.ppermute(x, tuple(axes), pairs)  11.2 us
    pallas_call x9, Pallas kernels, call(): pl.pallas_call(kernel, out_shape=outs, in_specs=[pl.BlockSpec(memory_spac...  9.99 us
    ppermute x4, waiting for transfers between devices, dealt(): return lax.ppermute(x, axes, pairs)  5.23 us
    all_to_all x1, starting transfers between devices, on_device(): mlp = [lax.all_to_all(blocks, 'tok', 0, 0)]  4.36 us
    ppermute x4, starting transfers between devices, dealt(): return lax.ppermute(x, axes, pairs)  4.2 us
    all_to_all x1, waiting for transfers between devices, on_device(): mlp = [lax.all_to_all(blocks, 'tok', 0, 0)]  4.19 us
  transfers between devices with their start and end apart: 21, of which 16 were waited for; matrix products, arithmetic and copies ran while one was open for 0% of the time, Pallas kernels for 13%

profile of v9, /device:TPU:0, one launch (start us, length us, event | category | flops | bytes accessed | tf_op | source)
XLA Modules:
  0.0 62.0 jit_solution(9182256351647710952)
XLA Ops:
  0.0 0.0 copy-start
  0.0 1.1 %shard_map.118 = (bf16[64,1024]{1,0:T(8,128)(2,1)S(1)}, bf16[64,2048]{1,0:T(8,128)(2,1)S(1)}) custom-call(bf16[128,512]{1,0:T(8,128)(2,1)} %refs_3_.1, bf16[128,512]{1,0:T(8,128)(2,1)} %refs_4_.1, f32[1,128]{1,0:T(1,128)} %bitcast.11, bf16[128,512]{1,0:T(8,128)(2,1)} %refs_6_.1, bf16[128,512]{1,0:T(8,128)(2,1)} %refs_7_.1), custom_call_target="tpu_custom_call" | custom-call | flops 1 | bytes 1 | tf_op jit(solution)/shard_map/pallas_call | solution.py:41
  1.1 4.1 %collective-permute-start.1 = (bf16[64,1024]{1,0:T(8,128)(2,1)S(1)}, bf16[64,1024]{1,0:T(8,128)(2,1)S(1)}, u32[]{:S(2)}, u32[]{:S(2)}) collective-permute-start(bf16[64,1024]{1,0:T(8,128)(2,1)S(1)} %get-tuple-element.31), channel_id=1, source_target_pairs={{8,0},{12,4},{0,8},{4,12},{9,1},{13,5},{1,9},{5,13},{10,2},{14,6},... | collective-permute-start | bytes 393224 | tf_op jit(solution)/shard_map/ppermute | solution.py:30
  5.2 1.6 %collective-permute-start = (bf16[64,2048]{1,0:T(8,128)(2,1)S(1)}, bf16[64,2048]{1,0:T(8,128)(2,1)S(1)}, u32[]{:S(2)}, u32[]{:S(2)}) collective-permute-start(bf16[64,2048]{1,0:T(8,128)(2,1)S(1)} %get-tuple-element.30), channel_id=1, source_target_pairs={{4,0},{0,4},{12,8},{8,12},{5,1},{1,5},{13,9},{9,13},{6,2},{2,6},{1... | collective-permute-start | bytes 786440 | tf_op jit(solution)/shard_map/ppermute | solution.py:30
  6.8 4.8 %collective-permute-done.1.refs_10_ = bf16[64,1024]{1,0:T(8,128)(2,1)S(1)} collective-permute-done((bf16[64,1024]{1,0:T(8,128)(2,1)S(1)}, bf16[64,1024]{1,0:T(8,128)(2,1)S(1)}, u32[]{:S(2)}, u32[]{:S(2)}) %collective-permute-start.1) | collective-permute-done | bytes 131104 | tf_op jit(solution)/shard_map/ppermute | solution.py:30
  11.7 0.7 %collective-permute-start.2 = (bf16[64,1024]{1,0:T(8,128)(2,1)S(1)}, bf16[64,1024]{1,0:T(8,128)(2,1)S(1)}, u32[]{:S(2)}, u32[]{:S(2)}) collective-permute-start(bf16[64,1024]{1,0:T(8,128)(2,1)S(1)} %collective-permute-done.1.refs_10_), channel_id=1, source_target_pairs={{4,0},{0,4},{12,8},{8,12},{5,1},{1,5},{13,9},{9,13},{6,2},{2,6},{1... | collective-permute-start | bytes 393224 | tf_op jit(solution)/shard_map/ppermute | solution.py:30
  12.3 0.0 copy-done
  12.3 0.0 copy-start.1
  12.3 1.0 %copy-done.1 = bf16[1024,256]{1,0:T(8,128)(2,1)S(1)} copy-done((bf16[1024,256]{1,0:T(8,128)(2,1)S(1)}, bf16[1024,256]{1,0:T(8,128)(2,1)}, u32[]{:S(2)}) %copy-start.1) | copy-done | bytes 524312
  13.4 1.1 %shard_map.119 = bf16[4,512,256]{2,1,0:T(8,128)(2,1)} custom-call(bf16[256,1024]{1,0:T(8,128)(2,1)S(1)} %copy-done, bf16[1024,256]{1,0:T(8,128)(2,1)S(1)} %copy-done.1), custom_call_target="tpu_custom_call" | custom-call | flops 1 | bytes 1 | tf_op jit(solution)/shard_map/pallas_call | solution.py:41
  14.4 3.0 %collective-permute-done.2.refs_11_ = bf16[64,1024]{1,0:T(8,128)(2,1)S(1)} collective-permute-done((bf16[64,1024]{1,0:T(8,128)(2,1)S(1)}, bf16[64,1024]{1,0:T(8,128)(2,1)S(1)}, u32[]{:S(2)}, u32[]{:S(2)}) %collective-permute-start.2) | collective-permute-done | bytes 131104 | tf_op jit(solution)/shard_map/ppermute | solution.py:30
  17.5 0.0 collective-permute-done.refs_9_.refs_0_
  17.5 4.4 %all-to-all-start = ((bf16[4,512,256]{2,1,0:T(8,128)(2,1)}), bf16[4,512,256]{2,1,0:T(8,128)(2,1)S(1)}, u32[]{:S(2)}, u32[]{:S(2)}) async-start(bf16[4,512,256]{2,1,0:T(8,128)(2,1)} %shard_map.119), calls=%async_computation | async-start | bytes 2097152 | tf_op jit(solution)/shard_map/all_to_all | solution.py:341
  21.8 0.0 collective-permute-start.3
  21.8 0.5 collective-permute-start.4
  22.3 0.0 collective-permute-start.5
  22.3 1.2 %collective-permute-done.4.refs_13_ = bf16[64,1024]{1,0:T(8,128)(2,1)S(1)} collective-permute-done((bf16[64,1024]{1,0:T(8,128)(2,1)S(1)}, bf16[64,1024]{1,0:T(8,128)(2,1)S(1)}, u32[]{:S(2)}, u32[]{:S(2)}) %collective-permute-start.4) | collective-permute-done | bytes 131104 | tf_op jit(solution)/shard_map/ppermute | solution.py:30
  23.5 0.2 collective-permute-done.5.refs_14_
  23.7 0.0 collective-permute-done.3.refs_12_
  23.7 5.5 %shard_map.120 = (f32[256,256]{1,0:T(8,128)S(1)}, f32[8,256]{1,0:T(8,128)S(1)}, bf16[272,256]{1,0:T(8,128)(2,1)S(1)}, bf16[128,256]{1,0:T(8,128)(2,1)S(1)}, bf16[16,256]{1,0:T(8,128)(2,1)S(1)}) custom-call(f32[512,512]{1,0:T(8,128)} %bitcast.7, f32[512,512]{1,0:T(8,128)} %bitcast.8, f32[512,512]{1,0:T(8,128)} %bitcast.9, bf16[128,512]{1,0:T(8,128)(2,1)} %refs_3_.1, ...), custom_call_target="tpu_custom_call" | custom-call | flops 1 | bytes 1 | tf_op jit(solution)/shard_map/pallas_call | solution.py:41
  29.2 0.2 collective-permute-start.6
  29.4 1.2 %collective-permute-done.6.got = bf16[272,256]{1,0:T(8,128)(2,1)S(1)} collective-permute-done((bf16[272,256]{1,0:T(8,128)(2,1)S(1)}, bf16[272,256]{1,0:T(8,128)(2,1)S(1)}, u32[]{:S(2)}, u32[]{:S(2)}) %collective-permute-start.6) | collective-permute-done | bytes 139296 | tf_op jit(solution)/shard_map/ppermute | solution.py:30
  30.7 0.1 shard_map.121
  30.7 1.6 %collective-permute-start.10 = (bf16[272,256]{1,0:T(8,128)(2,1)S(1)}, bf16[272,256]{1,0:T(8,128)(2,1)S(1)}, u32[]{:S(2)}, u32[]{:S(2)}) collective-permute-start(bf16[272,256]{1,0:T(8,128)(2,1)S(1)} %get-tuple-element.46.refs_0_), channel_id=1, source_target_pairs={{16,0},{0,16},{17,1},{1,17},{18,2},{2,18},{19,3},{3,19},{20,4},{4,... | collective-permute-start | bytes 417800 | tf_op jit(solution)/shard_map/ppermute | solution.py:30
  32.3 1.4 %collective-permute-start.12 = (bf16[272,256]{1,0:T(8,128)(2,1)S(1)}, bf16[272,256]{1,0:T(8,128)(2,1)S(1)}, u32[]{:S(2)}, u32[]{:S(2)}) collective-permute-start(bf16[272,256]{1,0:T(8,128)(2,1)S(1)} %get-tuple-element.46.refs_0_), channel_id=1, source_target_pairs={{18,0},{16,2},{2,16},{0,18},{19,1},{17,3},{3,17},{1,19},{22,4},{20... | collective-permute-start | bytes 417800 | tf_op jit(solution)/shard_map/ppermute | solution.py:30
  33.7 0.5 collective-permute-start.8
  34.3 0.0 collective-permute-start.7
  34.3 4.9 %collective-permute-done.10.refs_4_ = bf16[272,256]{1,0:T(8,128)(2,1)S(1)} collective-permute-done((bf16[272,256]{1,0:T(8,128)(2,1)S(1)}, bf16[272,256]{1,0:T(8,128)(2,1)S(1)}, u32[]{:S(2)}, u32[]{:S(2)}) %collective-permute-start.10) | collective-permute-done | bytes 139296 | tf_op jit(solution)/shard_map/ppermute | solution.py:30
  39.2 0.0 collective-permute-start.11
  39.2 0.5 collective-permute-done.12.refs_6_
  39.8 0.0 collective-permute-start.13
  39.8 1.0 %collective-permute-done.8.refs_2_ = bf16[272,256]{1,0:T(8,128)(2,1)S(1)} collective-permute-done((bf16[272,256]{1,0:T(8,128)(2,1)S(1)}, bf16[272,256]{1,0:T(8,128)(2,1)S(1)}, u32[]{:S(2)}, u32[]{:S(2)}) %collective-permute-start.8) | collective-permute-done | bytes 139296 | tf_op jit(solution)/shard_map/ppermute | solution.py:30
  40.7 0.0 collective-permute-start.9
  40.7 0.0 collective-permute-done.7.refs_1_
  40.7 0.0 collective-permute-done.11.refs_5_
  40.7 0.4 collective-permute-done.13.refs_7_
  41.1 1.0 %collective-permute-done.9.refs_3_ = bf16[272,256]{1,0:T(8,128)(2,1)S(1)} collective-permute-done((bf16[272,256]{1,0:T(8,128)(2,1)S(1)}, bf16[272,256]{1,0:T(8,128)(2,1)S(1)}, u32[]{:S(2)}, u32[]{:S(2)}) %collective-permute-start.9) | collective-permute-done | bytes 139296 | tf_op jit(solution)/shard_map/ppermute | solution.py:30
  42.1 0.5 shard_map.122.zs
  42.6 4.2 %all-to-all-done.refs_0_ = bf16[4,512,256]{2,1,0:T(8,128)(2,1)S(1)} async-done(((bf16[4,512,256]{2,1,0:T(8,128)(2,1)}), bf16[4,512,256]{2,1,0:T(8,128)(2,1)S(1)}, u32[]{:S(2)}, u32[]{:S(2)}) %all-to-all-start) | async-done | bytes 1048608 | tf_op jit(solution)/shard_map/all_to_all | solution.py:341
  46.8 0.7 %shard_map.124 = bf16[256,1024]{1,0:T(8,128)(2,1)S(1)} custom-call(bf16[512,1024]{1,0:T(8,128)(2,1)S(1)} %shard_map.122.zs, bf16[4,512,256]{2,1,0:T(8,128)(2,1)S(1)} %all-to-all-done.refs_0_), custom_call_target="tpu_custom_call" | custom-call | flops 1 | bytes 1 | tf_op jit(solution)/shard_map/pallas_call | solution.py:41
  47.6 0.1 collective-permute-start.14
  47.6 0.8 %shard_map.123.own = f32[256,1024]{1,0:T(8,128)S(1)} custom-call(bf16[512,1024]{1,0:T(8,128)(2,1)S(1)} %shard_map.122.zs, bf16[4,512,256]{2,1,0:T(8,128)(2,1)S(1)} %all-to-all-done.refs_0_), custom_call_target="tpu_custom_call" | custom-call | flops 1 | bytes 1 | tf_op jit(solution)/shard_map/pallas_call | solution.py:41
  48.4 1.1 %collective-permute-done.14.got = bf16[256,1024]{1,0:T(8,128)(2,1)S(1)} collective-permute-done((bf16[256,1024]{1,0:T(8,128)(2,1)S(1)}, bf16[256,1024]{1,0:T(8,128)(2,1)S(1)}, u32[]{:S(2)}, u32[]{:S(2)}) %collective-permute-start.14) | collective-permute-done | bytes 524320 | tf_op jit(solution)/shard_map/ppermute | solution.py:30
  49.5 0.1 shard_map.125
  49.6 0.1 collective-permute-start.15
  49.7 1.6 %collective-permute-start.16 = (bf16[128,512]{1,0:T(8,128)(2,1)S(1)}, bf16[128,512]{1,0:T(8,128)(2,1)S(1)}, u32[]{:S(2)}, u32[]{:S(2)}) collective-permute-start(bf16[128,512]{1,0:T(8,128)(2,1)S(1)} %get-tuple-element.49), channel_id=1, source_target_pairs={{0,2},{1,19},{2,0},{3,17},{4,6},{5,23},{6,4},{7,21},{8,10},{9,27},... | collective-permute-start | bytes 393224 | tf_op jit(solution)/shard_map/ppermute | solution.py:292
  51.3 1.9 %collective-permute-start.17 = (bf16[128,512]{1,0:T(8,128)(2,1)S(1)}, bf16[128,512]{1,0:T(8,128)(2,1)S(1)}, u32[]{:S(2)}, u32[]{:S(2)}) collective-permute-start(bf16[128,512]{1,0:T(8,128)(2,1)S(1)} %get-tuple-element.50), channel_id=1, source_target_pairs={{0,4},{1,21},{2,6},{3,23},{4,0},{5,17},{6,2},{7,19},{8,12},{9,29},... | collective-permute-start | bytes 393224 | tf_op jit(solution)/shard_map/ppermute | solution.py:292
  53.2 0.7 %collective-permute-start.18 = (bf16[128,512]{1,0:T(8,128)(2,1)S(1)}, bf16[128,512]{1,0:T(8,128)(2,1)S(1)}, u32[]{:S(2)}, u32[]{:S(2)}) collective-permute-start(bf16[128,512]{1,0:T(8,128)(2,1)S(1)} %get-tuple-element.51), channel_id=1, source_target_pairs={{0,0},{1,17},{2,2},{3,19},{4,4},{5,21},{6,6},{7,23},{8,8},{9,25},{... | collective-permute-start | bytes 393224 | tf_op jit(solution)/shard_map/ppermute | solution.py:292
  54.5 2.4 %collective-permute-done.15.refs_0_ = bf16[128,512]{1,0:T(8,128)(2,1)S(1)} collective-permute-done((bf16[128,512]{1,0:T(8,128)(2,1)S(1)}, bf16[128,512]{1,0:T(8,128)(2,1)S(1)}, u32[]{:S(2)}, u32[]{:S(2)}) %collective-permute-start.15) | collective-permute-done | bytes 131104 | tf_op jit(solution)/shard_map/ppermute | solution.py:292
  56.9 1.9 %collective-permute-done.16.refs_1_ = bf16[128,512]{1,0:T(8,128)(2,1)S(1)} collective-permute-done((bf16[128,512]{1,0:T(8,128)(2,1)S(1)}, bf16[128,512]{1,0:T(8,128)(2,1)S(1)}, u32[]{:S(2)}, u32[]{:S(2)}) %collective-permute-start.16) | collective-permute-done | bytes 131104 | tf_op jit(solution)/shard_map/ppermute | solution.py:292
  58.8 0.9 %collective-permute-done.17.refs_2_ = bf16[128,512]{1,0:T(8,128)(2,1)S(1)} collective-permute-done((bf16[128,512]{1,0:T(8,128)(2,1)S(1)}, bf16[128,512]{1,0:T(8,128)(2,1)S(1)}, u32[]{:S(2)}, u32[]{:S(2)}) %collective-permute-start.17) | collective-permute-done | bytes 131104 | tf_op jit(solution)/shard_map/ppermute | solution.py:292
  59.7 0.0 collective-permute-done.18.refs_3_
  59.7 0.1 shard_map.126
  59.8 0.5 collective-permute-start.19
  60.3 0.9 %collective-permute-done.19 = bf16[128,256]{1,0:T(8,128)(2,1)S(1)} collective-permute-done((bf16[128,256]{1,0:T(8,128)(2,1)S(1)}, bf16[128,256]{1,0:T(8,128)(2,1)S(1)}, u32[]{:S(2)}, u32[]{:S(2)}) %collective-permute-start.19) | collective-permute-done | bytes 65568 | tf_op jit(solution)/shard_map/ppermute | solution.py:30
  61.2 0.7 %select_convert_fusion = bf16[128,256]{1,0:T(8,128)(2,1)} fusion(f32[128,256]{1,0:T(8,128)S(1)} %get-tuple-element.53, bf16[128,256]{1,0:T(8,128)(2,1)S(1)} %collective-permute-done.19, pred[128]{0:T(512)(128)(4,1)S(1)} %iota_compare_fusion), kind=kLoop, calls=%fused_computation | loop fusion | flops 131072 | bytes 262272 | tf_op jit(solution)/shard_map/convert_element_type | solution.py:410
  (1 shorter events, 0.0 us)
Async XLA Ops:
  0.0 12.3 %copy-start = (bf16[256,1024]{1,0:T(8,128)(2,1)S(1)}, bf16[256,1024]{1,0:T(8,128)(2,1)}, u32[]{:S(2)}) copy-start(bf16[256,1024]{1,0:T(8,128)(2,1)} %up.1) | copy-start | bytes 1572868
  1.1 10.5 %collective-permute-start.1 = (bf16[64,1024]{1,0:T(8,128)(2,1)S(1)}, bf16[64,1024]{1,0:T(8,128)(2,1)S(1)}, u32[]{:S(2)}, u32[]{:S(2)}) collective-permute-start(bf16[64,1024]{1,0:T(8,128)(2,1)S(1)} %get-tuple-element.31), channel_id=1, source_target_pairs={{8,0},{12,4},{0,8},{4,12},{9,1},{13,5},{1,9},{5,13},{10,2},{14,6},... | collective-permute-start | bytes 393224 | tf_op jit(solution)/shard_map/ppermute | solution.py:30
  5.2 12.2 %collective-permute-start = (bf16[64,2048]{1,0:T(8,128)(2,1)S(1)}, bf16[64,2048]{1,0:T(8,128)(2,1)S(1)}, u32[]{:S(2)}, u32[]{:S(2)}) collective-permute-start(bf16[64,2048]{1,0:T(8,128)(2,1)S(1)} %get-tuple-element.30), channel_id=1, source_target_pairs={{4,0},{0,4},{12,8},{8,12},{5,1},{1,5},{13,9},{9,13},{6,2},{2,6},{1... | collective-permute-start | bytes 786440 | tf_op jit(solution)/shard_map/ppermute | solution.py:30
  11.7 5.8 %collective-permute-start.2 = (bf16[64,1024]{1,0:T(8,128)(2,1)S(1)}, bf16[64,1024]{1,0:T(8,128)(2,1)S(1)}, u32[]{:S(2)}, u32[]{:S(2)}) collective-permute-start(bf16[64,1024]{1,0:T(8,128)(2,1)S(1)} %collective-permute-done.1.refs_10_), channel_id=1, source_target_pairs={{4,0},{0,4},{12,8},{8,12},{5,1},{1,5},{13,9},{9,13},{6,2},{2,6},{1... | collective-permute-start | bytes 393224 | tf_op jit(solution)/shard_map/ppermute | solution.py:30
  12.3 1.0 %copy-start.1 = (bf16[1024,256]{1,0:T(8,128)(2,1)S(1)}, bf16[1024,256]{1,0:T(8,128)(2,1)}, u32[]{:S(2)}) copy-start(bf16[1024,256]{1,0:T(8,128)(2,1)} %down.1) | copy-start | bytes 1572868
  17.5 29.3 %all-to-all-start = ((bf16[4,512,256]{2,1,0:T(8,128)(2,1)}), bf16[4,512,256]{2,1,0:T(8,128)(2,1)S(1)}, u32[]{:S(2)}, u32[]{:S(2)}) async-start(bf16[4,512,256]{2,1,0:T(8,128)(2,1)} %shard_map.119), calls=%async_computation | async-start | bytes 2097152 | tf_op jit(solution)/shard_map/all_to_all | solution.py:341
  21.8 1.9 %collective-permute-start.3 = (bf16[64,2048]{1,0:T(8,128)(2,1)S(1)}, bf16[64,2048]{1,0:T(8,128)(2,1)S(1)}, u32[]{:S(2)}, u32[]{:S(2)}) collective-permute-start(bf16[64,2048]{1,0:T(8,128)(2,1)S(1)} %collective-permute-done.refs_9_.refs_0_), channel_id=1, source_target_pairs={{1,0},{0,1},{3,2},{2,3},{5,4},{4,5},{7,6},{6,7},{9,8},{8,9},{11,10... | collective-permute-start | bytes 786440 | tf_op jit(solution)/shard_map/ppermute | solution.py:30
  21.8 1.7 %collective-permute-start.4 = (bf16[64,1024]{1,0:T(8,128)(2,1)S(1)}, bf16[64,1024]{1,0:T(8,128)(2,1)S(1)}, u32[]{:S(2)}, u32[]{:S(2)}) collective-permute-start(bf16[64,1024]{1,0:T(8,128)(2,1)S(1)} %collective-permute-done.1.refs_10_), channel_id=1, source_target_pairs={{1,0},{0,1},{3,2},{2,3},{5,4},{4,5},{7,6},{6,7},{9,8},{8,9},{11,10... | collective-permute-start | bytes 393224 | tf_op jit(solution)/shard_map/ppermute | solution.py:30
  22.3 1.4 %collective-permute-start.5 = (bf16[64,1024]{1,0:T(8,128)(2,1)S(1)}, bf16[64,1024]{1,0:T(8,128)(2,1)S(1)}, u32[]{:S(2)}, u32[]{:S(2)}) collective-permute-start(bf16[64,1024]{1,0:T(8,128)(2,1)S(1)} %collective-permute-done.2.refs_11_), channel_id=1, source_target_pairs={{1,0},{0,1},{3,2},{2,3},{5,4},{4,5},{7,6},{6,7},{9,8},{8,9},{11,10... | collective-permute-start | bytes 393224 | tf_op jit(solution)/shard_map/ppermute | solution.py:30
  29.2 1.4 %collective-permute-start.6 = (bf16[272,256]{1,0:T(8,128)(2,1)S(1)}, bf16[272,256]{1,0:T(8,128)(2,1)S(1)}, u32[]{:S(2)}, u32[]{:S(2)}) collective-permute-start(bf16[272,256]{1,0:T(8,128)(2,1)S(1)} %get-tuple-element.43), channel_id=1, source_target_pairs={{1,0},{0,1},{3,2},{2,3},{5,4},{4,5},{7,6},{6,7},{9,8},{8,9},{11,10... | collective-permute-start | bytes 417800 | tf_op jit(solution)/shard_map/ppermute | solution.py:30
  30.7 8.5 %collective-permute-start.10 = (bf16[272,256]{1,0:T(8,128)(2,1)S(1)}, bf16[272,256]{1,0:T(8,128)(2,1)S(1)}, u32[]{:S(2)}, u32[]{:S(2)}) collective-permute-start(bf16[272,256]{1,0:T(8,128)(2,1)S(1)} %get-tuple-element.46.refs_0_), channel_id=1, source_target_pairs={{16,0},{0,16},{17,1},{1,17},{18,2},{2,18},{19,3},{3,19},{20,4},{4,... | collective-permute-start | bytes 417800 | tf_op jit(solution)/shard_map/ppermute | solution.py:30
  32.3 7.5 %collective-permute-start.12 = (bf16[272,256]{1,0:T(8,128)(2,1)S(1)}, bf16[272,256]{1,0:T(8,128)(2,1)S(1)}, u32[]{:S(2)}, u32[]{:S(2)}) collective-permute-start(bf16[272,256]{1,0:T(8,128)(2,1)S(1)} %get-tuple-element.46.refs_0_), channel_id=1, source_target_pairs={{18,0},{16,2},{2,16},{0,18},{19,1},{17,3},{3,17},{1,19},{22,4},{20... | collective-permute-start | bytes 417800 | tf_op jit(solution)/shard_map/ppermute | solution.py:30
  33.7 7.0 %collective-permute-start.8 = (bf16[272,256]{1,0:T(8,128)(2,1)S(1)}, bf16[272,256]{1,0:T(8,128)(2,1)S(1)}, u32[]{:S(2)}, u32[]{:S(2)}) collective-permute-start(bf16[272,256]{1,0:T(8,128)(2,1)S(1)} %get-tuple-element.46.refs_0_), channel_id=1, source_target_pairs={{2,0},{0,2},{3,1},{1,3},{6,4},{4,6},{7,5},{5,7},{10,8},{8,10},{11,... | collective-permute-start | bytes 417800 | tf_op jit(solution)/shard_map/ppermute | solution.py:30
  34.3 6.5 %collective-permute-start.7 = (bf16[272,256]{1,0:T(8,128)(2,1)S(1)}, bf16[272,256]{1,0:T(8,128)(2,1)S(1)}, u32[]{:S(2)}, u32[]{:S(2)}) collective-permute-start(bf16[272,256]{1,0:T(8,128)(2,1)S(1)} %get-tuple-element.46.refs_0_), channel_id=1, source_target_pairs={{1,0},{0,1},{3,2},{2,3},{5,4},{4,5},{7,6},{6,7},{9,8},{8,9},{11,10... | collective-permute-start | bytes 417800 | tf_op jit(solution)/shard_map/ppermute | solution.py:30
  39.2 1.5 %collective-permute-start.11 = (bf16[272,256]{1,0:T(8,128)(2,1)S(1)}, bf16[272,256]{1,0:T(8,128)(2,1)S(1)}, u32[]{:S(2)}, u32[]{:S(2)}) collective-permute-start(bf16[272,256]{1,0:T(8,128)(2,1)S(1)} %collective-permute-done.10.refs_4_), channel_id=1, source_target_pairs={{1,0},{0,1},{3,2},{2,3},{5,4},{4,5},{7,6},{6,7},{9,8},{8,9},{11,10... | collective-permute-start | bytes 417800 | tf_op jit(solution)/shard_map/ppermute | solution.py:30
  39.8 1.4 %collective-permute-start.13 = (bf16[272,256]{1,0:T(8,128)(2,1)S(1)}, bf16[272,256]{1,0:T(8,128)(2,1)S(1)}, u32[]{:S(2)}, u32[]{:S(2)}) collective-permute-start(bf16[272,256]{1,0:T(8,128)(2,1)S(1)} %collective-permute-done.12.refs_6_), channel_id=1, source_target_pairs={{1,0},{0,1},{3,2},{2,3},{5,4},{4,5},{7,6},{6,7},{9,8},{8,9},{11,10... | collective-permute-start | bytes 417800 | tf_op jit(solution)/shard_map/ppermute | solution.py:30
  40.7 1.4 %collective-permute-start.9 = (bf16[272,256]{1,0:T(8,128)(2,1)S(1)}, bf16[272,256]{1,0:T(8,128)(2,1)S(1)}, u32[]{:S(2)}, u32[]{:S(2)}) collective-permute-start(bf16[272,256]{1,0:T(8,128)(2,1)S(1)} %collective-permute-done.8.refs_2_), channel_id=1, source_target_pairs={{1,0},{0,1},{3,2},{2,3},{5,4},{4,5},{7,6},{6,7},{9,8},{8,9},{11,10... | collective-permute-start | bytes 417800 | tf_op jit(solution)/shard_map/ppermute | solution.py:30
  47.6 2.0 %collective-permute-start.14 = (bf16[256,1024]{1,0:T(8,128)(2,1)S(1)}, bf16[256,1024]{1,0:T(8,128)(2,1)S(1)}, u32[]{:S(2)}, u32[]{:S(2)}) collective-permute-start(bf16[256,1024]{1,0:T(8,128)(2,1)S(1)} %shard_map.124), channel_id=1, source_target_pairs={{1,0},{0,1},{3,2},{2,3},{5,4},{4,5},{7,6},{6,7},{9,8},{8,9},{11,10... | collective-permute-start | bytes 1572872 | tf_op jit(solution)/shard_map/ppermute | solution.py:30
  49.6 7.3 %collective-permute-start.15 = (bf16[128,512]{1,0:T(8,128)(2,1)S(1)}, bf16[128,512]{1,0:T(8,128)(2,1)S(1)}, u32[]{:S(2)}, u32[]{:S(2)}) collective-permute-start(bf16[128,512]{1,0:T(8,128)(2,1)S(1)} %get-tuple-element.48), channel_id=1, source_target_pairs={{0,6},{1,23},{2,4},{3,21},{4,2},{5,19},{6,0},{7,17},{8,14},{9,31},... | collective-permute-start | bytes 393224 | tf_op jit(solution)/shard_map/ppermute | solution.py:292
  49.7 9.1 %collective-permute-start.16 = (bf16[128,512]{1,0:T(8,128)(2,1)S(1)}, bf16[128,512]{1,0:T(8,128)(2,1)S(1)}, u32[]{:S(2)}, u32[]{:S(2)}) collective-permute-start(bf16[128,512]{1,0:T(8,128)(2,1)S(1)} %get-tuple-element.49), channel_id=1, source_target_pairs={{0,2},{1,19},{2,0},{3,17},{4,6},{5,23},{6,4},{7,21},{8,10},{9,27},... | collective-permute-start | bytes 393224 | tf_op jit(solution)/shard_map/ppermute | solution.py:292
  51.3 8.5 %collective-permute-start.17 = (bf16[128,512]{1,0:T(8,128)(2,1)S(1)}, bf16[128,512]{1,0:T(8,128)(2,1)S(1)}, u32[]{:S(2)}, u32[]{:S(2)}) collective-permute-start(bf16[128,512]{1,0:T(8,128)(2,1)S(1)} %get-tuple-element.50), channel_id=1, source_target_pairs={{0,4},{1,21},{2,6},{3,23},{4,0},{5,17},{6,2},{7,19},{8,12},{9,29},... | collective-permute-start | bytes 393224 | tf_op jit(solution)/shard_map/ppermute | solution.py:292
  53.2 6.5 %collective-permute-start.18 = (bf16[128,512]{1,0:T(8,128)(2,1)S(1)}, bf16[128,512]{1,0:T(8,128)(2,1)S(1)}, u32[]{:S(2)}, u32[]{:S(2)}) collective-permute-start(bf16[128,512]{1,0:T(8,128)(2,1)S(1)} %get-tuple-element.51), channel_id=1, source_target_pairs={{0,0},{1,17},{2,2},{3,19},{4,4},{5,21},{6,6},{7,23},{8,8},{9,25},{... | collective-permute-start | bytes 393224 | tf_op jit(solution)/shard_map/ppermute | solution.py:292
  59.8 1.4 %collective-permute-start.19 = (bf16[128,256]{1,0:T(8,128)(2,1)S(1)}, bf16[128,256]{1,0:T(8,128)(2,1)S(1)}, u32[]{:S(2)}, u32[]{:S(2)}) collective-permute-start(bf16[128,256]{1,0:T(8,128)(2,1)S(1)} %get-tuple-element.54), channel_id=1, source_target_pairs={{1,0},{0,1},{3,2},{2,3},{5,4},{4,5},{7,6},{6,7},{9,8},{8,9},{11,10... | collective-permute-start | bytes 196616 | tf_op jit(solution)/shard_map/ppermute | solution.py:30

commit v10 on v9

--- a/solution.py
+++ b/solution.py
@@ -271,12 +271,13 @@
 
 
 def sum_kernel(*refs):
-    *parts, mixed, keep, send, acc = refs
-    total = parts[0][...].astype(F32)
-    for p in parts[1:]:
+    *parts, own, mixed, keep, send, acc = refs
+    me = lax.axis_index("rep")
+    total = jnp.where(me == 0, own[...].astype(F32), 0.0)
+    for p in parts:
         total = total + p[...].astype(F32)
     acc[...] = total
-    me, wide = lax.axis_index("rep"), keep.shape[1]
+    wide = keep.shape[1]
     keep[...] = mixed[...] + acc[:, window(me, wide)]
     send[...] = acc[:, window(1 - me, wide)].astype(BF)
 
@@ -289,7 +290,7 @@
         g, t, h, r = np.unravel_index(here, sizes)
         there = ((g + r) % sizes[0], t ^ tok, (h + head) % sizes[2], r)
         pairs.append((here, int(np.ravel_multi_index(there, sizes))))
-    return lax.ppermute(x, axes, pairs)
+    return lax.ppermute(x, axes, [p for p in pairs if p[0] != p[1]])
 
 
 def on_device(
@@ -397,13 +398,14 @@
     (own,) = call(
         functools.partial(feed_kernel, True), [shape((near * n, model), F32)], [zs, *mlp]
     )
-    moves = sorted(itertools.product(range(near), range(n_head)), key=lambda m: (-m[0] - m[1], m[0]))
+    moves = sorted(itertools.product(range(near), range(n_head)), key=lambda m: (m[0] + m[1] < 2, m[0], -m[1]))
     parts = call(
         functools.partial(pair_kernel, moves), [shape((n, dh), BF)] * len(moves), [own, got]
     )
+    own = parts[moves.index((0, 0))]
     parts = [dealt(x, *m) for m, x in zip(moves, parts)]
     keep, send = call(
-        sum_kernel, [shape((n, wide), F32), shape((n, wide), BF)], [*parts, mixed], [pltpu.VMEM((n, dh), F32)]
+        sum_kernel, [shape((n, wide), F32), shape((n, wide), BF)], [*parts, own, mixed], [pltpu.VMEM((n, dh), F32)]
     )
     total = keep + moved(send, rep=1).astype(F32)
     live = jnp.arange(n, dtype=jnp.int32) < counts[0]

time: 62.2 us -> 62.1 us (level)
  waiting for transfers between devices: 29.7 us -> 28.9 us
  starting transfers between devices: 19.7 us -> 20.4 us
    ppermute x4, waiting for transfers between devices: 5.23 us -> 4.43 us  [dealt(): return lax.ppermute(x, axes, [p for p in pairs if p[0] != p[1]])]
where the time goes in v10:
time: 62.1 us; the launch traced here: 61.8 us
  waiting for transfers between devices  28.9 us (47%)
  starting transfers between devices  20.4 us (33%)
  Pallas kernels  10 us (16%)
  local copies, waits for them, and re-layouts  1.05 us (2%)
  between operations  0.74 us (1%)
  other arithmetic  0.72 us (1%)
    ppermute x16, waiting for transfers between devices, moved(): return lax.ppermute(x, tuple(axes), pairs)  20.3 us
    ppermute x16, starting transfers between devices, moved(): return lax.ppermute(x, tuple(axes), pairs)  11.7 us
    pallas_call x9, Pallas kernels, call(): pl.pallas_call(kernel, out_shape=outs, in_specs=[pl.BlockSpec(memory_spac...  10 us
    ppermute x4, waiting for transfers between devices, dealt(): return lax.ppermute(x, axes, [p for p in pairs if p[0] != p[1]])  4.43 us
    all_to_all x1, starting transfers between devices, on_device(): mlp = [lax.all_to_all(blocks, 'tok', 0, 0)]  4.36 us
    ppermute x4, starting transfers between devices, dealt(): return lax.ppermute(x, axes, [p for p in pairs if p[0] != p[1]])  4.27 us
    all_to_all x1, waiting for transfers between devices, on_device(): mlp = [lax.all_to_all(blocks, 'tok', 0, 0)]  4.19 us
  transfers between devices with their start and end apart: 21, of which 16 were waited for; matrix products, arithmetic and copies ran while one was open for 0% of the time, Pallas kernels for 13%

profile of v10, /device:TPU:0, one launch (start us, length us, event | category | flops | bytes accessed | tf_op | source)
XLA Modules:
  0.0 61.8 jit_solution(16841893096985949512)
XLA Ops:
  0.0 0.0 copy-start
  0.0 1.1 %shard_map.118 = (bf16[64,1024]{1,0:T(8,128)(2,1)S(1)}, bf16[64,2048]{1,0:T(8,128)(2,1)S(1)}) custom-call(bf16[128,512]{1,0:T(8,128)(2,1)} %refs_3_.1, bf16[128,512]{1,0:T(8,128)(2,1)} %refs_4_.1, f32[1,128]{1,0:T(1,128)} %bitcast.11, bf16[128,512]{1,0:T(8,128)(2,1)} %refs_6_.1, bf16[128,512]{1,0:T(8,128)(2,1)} %refs_7_.1), custom_call_target="tpu_custom_call" | custom-call | flops 1 | bytes 1 | tf_op jit(solution)/shard_map/pallas_call | solution.py:41
  1.1 4.1 %collective-permute-start.1 = (bf16[64,1024]{1,0:T(8,128)(2,1)S(1)}, bf16[64,1024]{1,0:T(8,128)(2,1)S(1)}, u32[]{:S(2)}, u32[]{:S(2)}) collective-permute-start(bf16[64,1024]{1,0:T(8,128)(2,1)S(1)} %get-tuple-element.31), channel_id=1, source_target_pairs={{8,0},{12,4},{0,8},{4,12},{9,1},{13,5},{1,9},{5,13},{10,2},{14,6},... | collective-permute-start | bytes 393224 | tf_op jit(solution)/shard_map/ppermute | solution.py:30
  5.2 1.6 %collective-permute-start = (bf16[64,2048]{1,0:T(8,128)(2,1)S(1)}, bf16[64,2048]{1,0:T(8,128)(2,1)S(1)}, u32[]{:S(2)}, u32[]{:S(2)}) collective-permute-start(bf16[64,2048]{1,0:T(8,128)(2,1)S(1)} %get-tuple-element.30), channel_id=1, source_target_pairs={{4,0},{0,4},{12,8},{8,12},{5,1},{1,5},{13,9},{9,13},{6,2},{2,6},{1... | collective-permute-start | bytes 786440 | tf_op jit(solution)/shard_map/ppermute | solution.py:30
  6.8 4.8 %collective-permute-done.1.refs_10_ = bf16[64,1024]{1,0:T(8,128)(2,1)S(1)} collective-permute-done((bf16[64,1024]{1,0:T(8,128)(2,1)S(1)}, bf16[64,1024]{1,0:T(8,128)(2,1)S(1)}, u32[]{:S(2)}, u32[]{:S(2)}) %collective-permute-start.1) | collective-permute-done | bytes 131104 | tf_op jit(solution)/shard_map/ppermute | solution.py:30
  11.7 0.7 %collective-permute-start.2 = (bf16[64,1024]{1,0:T(8,128)(2,1)S(1)}, bf16[64,1024]{1,0:T(8,128)(2,1)S(1)}, u32[]{:S(2)}, u32[]{:S(2)}) collective-permute-start(bf16[64,1024]{1,0:T(8,128)(2,1)S(1)} %collective-permute-done.1.refs_10_), channel_id=1, source_target_pairs={{4,0},{0,4},{12,8},{8,12},{5,1},{1,5},{13,9},{9,13},{6,2},{2,6},{1... | collective-permute-start | bytes 393224 | tf_op jit(solution)/shard_map/ppermute | solution.py:30
  12.3 0.0 copy-done
  12.3 0.0 copy-start.1
  12.3 1.0 %copy-done.1 = bf16[1024,256]{1,0:T(8,128)(2,1)S(1)} copy-done((bf16[1024,256]{1,0:T(8,128)(2,1)S(1)}, bf16[1024,256]{1,0:T(8,128)(2,1)}, u32[]{:S(2)}) %copy-start.1) | copy-done | bytes 524312
  13.4 1.1 %shard_map.119 = bf16[4,512,256]{2,1,0:T(8,128)(2,1)} custom-call(bf16[256,1024]{1,0:T(8,128)(2,1)S(1)} %copy-done, bf16[1024,256]{1,0:T(8,128)(2,1)S(1)} %copy-done.1), custom_call_target="tpu_custom_call" | custom-call | flops 1 | bytes 1 | tf_op jit(solution)/shard_map/pallas_call | solution.py:41
  14.4 3.0 %collective-permute-done.2.refs_11_ = bf16[64,1024]{1,0:T(8,128)(2,1)S(1)} collective-permute-done((bf16[64,1024]{1,0:T(8,128)(2,1)S(1)}, bf16[64,1024]{1,0:T(8,128)(2,1)S(1)}, u32[]{:S(2)}, u32[]{:S(2)}) %collective-permute-start.2) | collective-permute-done | bytes 131104 | tf_op jit(solution)/shard_map/ppermute | solution.py:30
  17.5 0.0 collective-permute-done.refs_9_.refs_0_
  17.5 4.4 %all-to-all-start = ((bf16[4,512,256]{2,1,0:T(8,128)(2,1)}), bf16[4,512,256]{2,1,0:T(8,128)(2,1)S(1)}, u32[]{:S(2)}, u32[]{:S(2)}) async-start(bf16[4,512,256]{2,1,0:T(8,128)(2,1)} %shard_map.119), calls=%async_computation | async-start | bytes 2097152 | tf_op jit(solution)/shard_map/all_to_all | solution.py:342
  21.8 0.0 collective-permute-start.3
  21.8 0.5 collective-permute-start.4
  22.3 0.0 collective-permute-start.5
  22.3 1.2 %collective-permute-done.4.refs_13_ = bf16[64,1024]{1,0:T(8,128)(2,1)S(1)} collective-permute-done((bf16[64,1024]{1,0:T(8,128)(2,1)S(1)}, bf16[64,1024]{1,0:T(8,128)(2,1)S(1)}, u32[]{:S(2)}, u32[]{:S(2)}) %collective-permute-start.4) | collective-permute-done | bytes 131104 | tf_op jit(solution)/shard_map/ppermute | solution.py:30
  23.5 0.2 collective-permute-done.5.refs_14_
  23.7 0.0 collective-permute-done.3.refs_12_
  23.7 5.5 %shard_map.120 = (f32[256,256]{1,0:T(8,128)S(1)}, f32[8,256]{1,0:T(8,128)S(1)}, bf16[272,256]{1,0:T(8,128)(2,1)S(1)}, bf16[128,256]{1,0:T(8,128)(2,1)S(1)}, bf16[16,256]{1,0:T(8,128)(2,1)S(1)}) custom-call(f32[512,512]{1,0:T(8,128)} %bitcast.7, f32[512,512]{1,0:T(8,128)} %bitcast.8, f32[512,512]{1,0:T(8,128)} %bitcast.9, bf16[128,512]{1,0:T(8,128)(2,1)} %refs_3_.1, ...), custom_call_target="tpu_custom_call" | custom-call | flops 1 | bytes 1 | tf_op jit(solution)/shard_map/pallas_call | solution.py:41
  29.2 0.2 collective-permute-start.6
  29.4 1.2 %collective-permute-done.6.got = bf16[272,256]{1,0:T(8,128)(2,1)S(1)} collective-permute-done((bf16[272,256]{1,0:T(8,128)(2,1)S(1)}, bf16[272,256]{1,0:T(8,128)(2,1)S(1)}, u32[]{:S(2)}, u32[]{:S(2)}) %collective-permute-start.6) | collective-permute-done | bytes 139296 | tf_op jit(solution)/shard_map/ppermute | solution.py:30
  30.7 0.1 shard_map.121
  30.7 1.6 %collective-permute-start.10 = (bf16[272,256]{1,0:T(8,128)(2,1)S(1)}, bf16[272,256]{1,0:T(8,128)(2,1)S(1)}, u32[]{:S(2)}, u32[]{:S(2)}) collective-permute-start(bf16[272,256]{1,0:T(8,128)(2,1)S(1)} %get-tuple-element.46.refs_0_), channel_id=1, source_target_pairs={{16,0},{0,16},{17,1},{1,17},{18,2},{2,18},{19,3},{3,19},{20,4},{4,... | collective-permute-start | bytes 417800 | tf_op jit(solution)/shard_map/ppermute | solution.py:30
  32.3 1.4 %collective-permute-start.12 = (bf16[272,256]{1,0:T(8,128)(2,1)S(1)}, bf16[272,256]{1,0:T(8,128)(2,1)S(1)}, u32[]{:S(2)}, u32[]{:S(2)}) collective-permute-start(bf16[272,256]{1,0:T(8,128)(2,1)S(1)} %get-tuple-element.46.refs_0_), channel_id=1, source_target_pairs={{18,0},{16,2},{2,16},{0,18},{19,1},{17,3},{3,17},{1,19},{22,4},{20... | collective-permute-start | bytes 417800 | tf_op jit(solution)/shard_map/ppermute | solution.py:30
  33.7 0.5 collective-permute-start.8
  34.3 0.0 collective-permute-start.7
  34.3 4.9 %collective-permute-done.10.refs_4_ = bf16[272,256]{1,0:T(8,128)(2,1)S(1)} collective-permute-done((bf16[272,256]{1,0:T(8,128)(2,1)S(1)}, bf16[272,256]{1,0:T(8,128)(2,1)S(1)}, u32[]{:S(2)}, u32[]{:S(2)}) %collective-permute-start.10) | collective-permute-done | bytes 139296 | tf_op jit(solution)/shard_map/ppermute | solution.py:30
  39.2 0.0 collective-permute-start.11
  39.2 0.5 collective-permute-done.12.refs_6_
  39.8 0.0 collective-permute-start.13
  39.8 1.0 %collective-permute-done.8.refs_2_ = bf16[272,256]{1,0:T(8,128)(2,1)S(1)} collective-permute-done((bf16[272,256]{1,0:T(8,128)(2,1)S(1)}, bf16[272,256]{1,0:T(8,128)(2,1)S(1)}, u32[]{:S(2)}, u32[]{:S(2)}) %collective-permute-start.8) | collective-permute-done | bytes 139296 | tf_op jit(solution)/shard_map/ppermute | solution.py:30
  40.7 0.0 collective-permute-start.9
  40.7 0.0 collective-permute-done.7.refs_1_
  40.7 0.0 collective-permute-done.11.refs_5_
  40.7 0.4 collective-permute-done.13.refs_7_
  41.1 1.0 %collective-permute-done.9.refs_3_ = bf16[272,256]{1,0:T(8,128)(2,1)S(1)} collective-permute-done((bf16[272,256]{1,0:T(8,128)(2,1)S(1)}, bf16[272,256]{1,0:T(8,128)(2,1)S(1)}, u32[]{:S(2)}, u32[]{:S(2)}) %collective-permute-start.9) | collective-permute-done | bytes 139296 | tf_op jit(solution)/shard_map/ppermute | solution.py:30
  42.1 0.5 shard_map.122.zs
  42.6 4.2 %all-to-all-done.refs_0_ = bf16[4,512,256]{2,1,0:T(8,128)(2,1)S(1)} async-done(((bf16[4,512,256]{2,1,0:T(8,128)(2,1)}), bf16[4,512,256]{2,1,0:T(8,128)(2,1)S(1)}, u32[]{:S(2)}, u32[]{:S(2)}) %all-to-all-start) | async-done | bytes 1048608 | tf_op jit(solution)/shard_map/all_to_all | solution.py:342
  46.8 0.7 %shard_map.124 = bf16[256,1024]{1,0:T(8,128)(2,1)S(1)} custom-call(bf16[512,1024]{1,0:T(8,128)(2,1)S(1)} %shard_map.122.zs, bf16[4,512,256]{2,1,0:T(8,128)(2,1)S(1)} %all-to-all-done.refs_0_), custom_call_target="tpu_custom_call" | custom-call | flops 1 | bytes 1 | tf_op jit(solution)/shard_map/pallas_call | solution.py:41
  47.6 0.1 collective-permute-start.14
  47.6 0.8 %shard_map.123.own = f32[256,1024]{1,0:T(8,128)S(1)} custom-call(bf16[512,1024]{1,0:T(8,128)(2,1)S(1)} %shard_map.122.zs, bf16[4,512,256]{2,1,0:T(8,128)(2,1)S(1)} %all-to-all-done.refs_0_), custom_call_target="tpu_custom_call" | custom-call | flops 1 | bytes 1 | tf_op jit(solution)/shard_map/pallas_call | solution.py:41
  48.4 1.1 %collective-permute-done.14.got = bf16[256,1024]{1,0:T(8,128)(2,1)S(1)} collective-permute-done((bf16[256,1024]{1,0:T(8,128)(2,1)S(1)}, bf16[256,1024]{1,0:T(8,128)(2,1)S(1)}, u32[]{:S(2)}, u32[]{:S(2)}) %collective-permute-start.14) | collective-permute-done | bytes 524320 | tf_op jit(solution)/shard_map/ppermute | solution.py:30
  49.5 0.1 shard_map.125
  49.6 0.1 collective-permute-start.15
  49.7 1.6 %collective-permute-start.16 = (bf16[128,512]{1,0:T(8,128)(2,1)S(1)}, bf16[128,512]{1,0:T(8,128)(2,1)S(1)}, u32[]{:S(2)}, u32[]{:S(2)}) collective-permute-start(bf16[128,512]{1,0:T(8,128)(2,1)S(1)} %get-tuple-element.49), channel_id=1, source_target_pairs={{0,2},{1,19},{2,0},{3,17},{4,6},{5,23},{6,4},{7,21},{8,10},{9,27},... | collective-permute-start | bytes 393224 | tf_op jit(solution)/shard_map/ppermute | solution.py:293
  51.3 0.7 %collective-permute-start.17 = (bf16[128,512]{1,0:T(8,128)(2,1)S(1)}, bf16[128,512]{1,0:T(8,128)(2,1)S(1)}, u32[]{:S(2)}, u32[]{:S(2)}) collective-permute-start(bf16[128,512]{1,0:T(8,128)(2,1)S(1)} %get-tuple-element.50.refs_4_), channel_id=1, source_target_pairs={{1,17},{3,19},{5,21},{7,23},{9,25},{11,27},{13,29},{15,31},{17,1},... | collective-permute-start | bytes 393224 | tf_op jit(solution)/shard_map/ppermute | solution.py:293
  51.9 2.0 %collective-permute-start.18 = (bf16[128,512]{1,0:T(8,128)(2,1)S(1)}, bf16[128,512]{1,0:T(8,128)(2,1)S(1)}, u32[]{:S(2)}, u32[]{:S(2)}) collective-permute-start(bf16[128,512]{1,0:T(8,128)(2,1)S(1)} %get-tuple-element.51), channel_id=1, source_target_pairs={{0,4},{1,21},{2,6},{3,23},{4,0},{5,17},{6,2},{7,19},{8,12},{9,29},... | collective-permute-start | bytes 393224 | tf_op jit(solution)/shard_map/ppermute | solution.py:293
  54.6 2.4 %collective-permute-done.15.refs_0_ = bf16[128,512]{1,0:T(8,128)(2,1)S(1)} collective-permute-done((bf16[128,512]{1,0:T(8,128)(2,1)S(1)}, bf16[128,512]{1,0:T(8,128)(2,1)S(1)}, u32[]{:S(2)}, u32[]{:S(2)}) %collective-permute-start.15) | collective-permute-done | bytes 131104 | tf_op jit(solution)/shard_map/ppermute | solution.py:293
  56.9 1.9 %collective-permute-done.16.refs_1_ = bf16[128,512]{1,0:T(8,128)(2,1)S(1)} collective-permute-done((bf16[128,512]{1,0:T(8,128)(2,1)S(1)}, bf16[128,512]{1,0:T(8,128)(2,1)S(1)}, u32[]{:S(2)}, u32[]{:S(2)}) %collective-permute-start.16) | collective-permute-done | bytes 131104 | tf_op jit(solution)/shard_map/ppermute | solution.py:293
  58.8 0.0 collective-permute-done.17.refs_2_
  58.8 0.2 collective-permute-done.18.refs_3_
  59.0 0.1 shard_map.126
  59.2 1.0 %collective-permute-start.19 = (bf16[128,256]{1,0:T(8,128)(2,1)S(1)}, bf16[128,256]{1,0:T(8,128)(2,1)S(1)}, u32[]{:S(2)}, u32[]{:S(2)}) collective-permute-start(bf16[128,256]{1,0:T(8,128)(2,1)S(1)} %get-tuple-element.54), channel_id=1, source_target_pairs={{1,0},{0,1},{3,2},{2,3},{5,4},{4,5},{7,6},{6,7},{9,8},{8,9},{11,10... | collective-permute-start | bytes 196616 | tf_op jit(solution)/shard_map/ppermute | solution.py:30
  60.2 0.9 %collective-permute-done.19 = bf16[128,256]{1,0:T(8,128)(2,1)S(1)} collective-permute-done((bf16[128,256]{1,0:T(8,128)(2,1)S(1)}, bf16[128,256]{1,0:T(8,128)(2,1)S(1)}, u32[]{:S(2)}, u32[]{:S(2)}) %collective-permute-start.19) | collective-permute-done | bytes 65568 | tf_op jit(solution)/shard_map/ppermute | solution.py:30
  61.1 0.7 %select_convert_fusion = bf16[128,256]{1,0:T(8,128)(2,1)} fusion(f32[128,256]{1,0:T(8,128)S(1)} %get-tuple-element.53, bf16[128,256]{1,0:T(8,128)(2,1)S(1)} %collective-permute-done.19, pred[128]{0:T(512)(128)(4,1)S(1)} %iota_compare_fusion), kind=kLoop, calls=%fused_computation | loop fusion | flops 131072 | bytes 262272 | tf_op jit(solution)/shard_map/convert_element_type | solution.py:412
  (1 shorter events, 0.0 us)
Async XLA Ops:
  0.0 12.3 %copy-start = (bf16[256,1024]{1,0:T(8,128)(2,1)S(1)}, bf16[256,1024]{1,0:T(8,128)(2,1)}, u32[]{:S(2)}) copy-start(bf16[256,1024]{1,0:T(8,128)(2,1)} %up.1) | copy-start | bytes 1572868
  1.1 10.5 %collective-permute-start.1 = (bf16[64,1024]{1,0:T(8,128)(2,1)S(1)}, bf16[64,1024]{1,0:T(8,128)(2,1)S(1)}, u32[]{:S(2)}, u32[]{:S(2)}) collective-permute-start(bf16[64,1024]{1,0:T(8,128)(2,1)S(1)} %get-tuple-element.31), channel_id=1, source_target_pairs={{8,0},{12,4},{0,8},{4,12},{9,1},{13,5},{1,9},{5,13},{10,2},{14,6},... | collective-permute-start | bytes 393224 | tf_op jit(solution)/shard_map/ppermute | solution.py:30
  5.2 12.2 %collective-permute-start = (bf16[64,2048]{1,0:T(8,128)(2,1)S(1)}, bf16[64,2048]{1,0:T(8,128)(2,1)S(1)}, u32[]{:S(2)}, u32[]{:S(2)}) collective-permute-start(bf16[64,2048]{1,0:T(8,128)(2,1)S(1)} %get-tuple-element.30), channel_id=1, source_target_pairs={{4,0},{0,4},{12,8},{8,12},{5,1},{1,5},{13,9},{9,13},{6,2},{2,6},{1... | collective-permute-start | bytes 786440 | tf_op jit(solution)/shard_map/ppermute | solution.py:30
  11.7 5.8 %collective-permute-start.2 = (bf16[64,1024]{1,0:T(8,128)(2,1)S(1)}, bf16[64,1024]{1,0:T(8,128)(2,1)S(1)}, u32[]{:S(2)}, u32[]{:S(2)}) collective-permute-start(bf16[64,1024]{1,0:T(8,128)(2,1)S(1)} %collective-permute-done.1.refs_10_), channel_id=1, source_target_pairs={{4,0},{0,4},{12,8},{8,12},{5,1},{1,5},{13,9},{9,13},{6,2},{2,6},{1... | collective-permute-start | bytes 393224 | tf_op jit(solution)/shard_map/ppermute | solution.py:30
  12.3 1.0 %copy-start.1 = (bf16[1024,256]{1,0:T(8,128)(2,1)S(1)}, bf16[1024,256]{1,0:T(8,128)(2,1)}, u32[]{:S(2)}) copy-start(bf16[1024,256]{1,0:T(8,128)(2,1)} %down.1) | copy-start | bytes 1572868
  17.5 29.3 %all-to-all-start = ((bf16[4,512,256]{2,1,0:T(8,128)(2,1)}), bf16[4,512,256]{2,1,0:T(8,128)(2,1)S(1)}, u32[]{:S(2)}, u32[]{:S(2)}) async-start(bf16[4,512,256]{2,1,0:T(8,128)(2,1)} %shard_map.119), calls=%async_computation | async-start | bytes 2097152 | tf_op jit(solution)/shard_map/all_to_all | solution.py:342
  21.8 1.9 %collective-permute-start.3 = (bf16[64,2048]{1,0:T(8,128)(2,1)S(1)}, bf16[64,2048]{1,0:T(8,128)(2,1)S(1)}, u32[]{:S(2)}, u32[]{:S(2)}) collective-permute-start(bf16[64,2048]{1,0:T(8,128)(2,1)S(1)} %collective-permute-done.refs_9_.refs_0_), channel_id=1, source_target_pairs={{1,0},{0,1},{3,2},{2,3},{5,4},{4,5},{7,6},{6,7},{9,8},{8,9},{11,10... | collective-permute-start | bytes 786440 | tf_op jit(solution)/shard_map/ppermute | solution.py:30
  21.8 1.7 %collective-permute-start.4 = (bf16[64,1024]{1,0:T(8,128)(2,1)S(1)}, bf16[64,1024]{1,0:T(8,128)(2,1)S(1)}, u32[]{:S(2)}, u32[]{:S(2)}) collective-permute-start(bf16[64,1024]{1,0:T(8,128)(2,1)S(1)} %collective-permute-done.1.refs_10_), channel_id=1, source_target_pairs={{1,0},{0,1},{3,2},{2,3},{5,4},{4,5},{7,6},{6,7},{9,8},{8,9},{11,10... | collective-permute-start | bytes 393224 | tf_op jit(solution)/shard_map/ppermute | solution.py:30
  22.3 1.4 %collective-permute-start.5 = (bf16[64,1024]{1,0:T(8,128)(2,1)S(1)}, bf16[64,1024]{1,0:T(8,128)(2,1)S(1)}, u32[]{:S(2)}, u32[]{:S(2)}) collective-permute-start(bf16[64,1024]{1,0:T(8,128)(2,1)S(1)} %collective-permute-done.2.refs_11_), channel_id=1, source_target_pairs={{1,0},{0,1},{3,2},{2,3},{5,4},{4,5},{7,6},{6,7},{9,8},{8,9},{11,10... | collective-permute-start | bytes 393224 | tf_op jit(solution)/shard_map/ppermute | solution.py:30
  29.2 1.4 %collective-permute-start.6 = (bf16[272,256]{1,0:T(8,128)(2,1)S(1)}, bf16[272,256]{1,0:T(8,128)(2,1)S(1)}, u32[]{:S(2)}, u32[]{:S(2)}) collective-permute-start(bf16[272,256]{1,0:T(8,128)(2,1)S(1)} %get-tuple-element.43), channel_id=1, source_target_pairs={{1,0},{0,1},{3,2},{2,3},{5,4},{4,5},{7,6},{6,7},{9,8},{8,9},{11,10... | collective-permute-start | bytes 417800 | tf_op jit(solution)/shard_map/ppermute | solution.py:30
  30.7 8.5 %collective-permute-start.10 = (bf16[272,256]{1,0:T(8,128)(2,1)S(1)}, bf16[272,256]{1,0:T(8,128)(2,1)S(1)}, u32[]{:S(2)}, u32[]{:S(2)}) collective-permute-start(bf16[272,256]{1,0:T(8,128)(2,1)S(1)} %get-tuple-element.46.refs_0_), channel_id=1, source_target_pairs={{16,0},{0,16},{17,1},{1,17},{18,2},{2,18},{19,3},{3,19},{20,4},{4,... | collective-permute-start | bytes 417800 | tf_op jit(solution)/shard_map/ppermute | solution.py:30
  32.3 7.5 %collective-permute-start.12 = (bf16[272,256]{1,0:T(8,128)(2,1)S(1)}, bf16[272,256]{1,0:T(8,128)(2,1)S(1)}, u32[]{:S(2)}, u32[]{:S(2)}) collective-permute-start(bf16[272,256]{1,0:T(8,128)(2,1)S(1)} %get-tuple-element.46.refs_0_), channel_id=1, source_target_pairs={{18,0},{16,2},{2,16},{0,18},{19,1},{17,3},{3,17},{1,19},{22,4},{20... | collective-permute-start | bytes 417800 | tf_op jit(solution)/shard_map/ppermute | solution.py:30
  33.7 7.0 %collective-permute-start.8 = (bf16[272,256]{1,0:T(8,128)(2,1)S(1)}, bf16[272,256]{1,0:T(8,128)(2,1)S(1)}, u32[]{:S(2)}, u32[]{:S(2)}) collective-permute-start(bf16[272,256]{1,0:T(8,128)(2,1)S(1)} %get-tuple-element.46.refs_0_), channel_id=1, source_target_pairs={{2,0},{0,2},{3,1},{1,3},{6,4},{4,6},{7,5},{5,7},{10,8},{8,10},{11,... | collective-permute-start | bytes 417800 | tf_op jit(solution)/shard_map/ppermute | solution.py:30
  34.3 6.5 %collective-permute-start.7 = (bf16[272,256]{1,0:T(8,128)(2,1)S(1)}, bf16[272,256]{1,0:T(8,128)(2,1)S(1)}, u32[]{:S(2)}, u32[]{:S(2)}) collective-permute-start(bf16[272,256]{1,0:T(8,128)(2,1)S(1)} %get-tuple-element.46.refs_0_), channel_id=1, source_target_pairs={{1,0},{0,1},{3,2},{2,3},{5,4},{4,5},{7,6},{6,7},{9,8},{8,9},{11,10... | collective-permute-start | bytes 417800 | tf_op jit(solution)/shard_map/ppermute | solution.py:30
  39.2 1.5 %collective-permute-start.11 = (bf16[272,256]{1,0:T(8,128)(2,1)S(1)}, bf16[272,256]{1,0:T(8,128)(2,1)S(1)}, u32[]{:S(2)}, u32[]{:S(2)}) collective-permute-start(bf16[272,256]{1,0:T(8,128)(2,1)S(1)} %collective-permute-done.10.refs_4_), channel_id=1, source_target_pairs={{1,0},{0,1},{3,2},{2,3},{5,4},{4,5},{7,6},{6,7},{9,8},{8,9},{11,10... | collective-permute-start | bytes 417800 | tf_op jit(solution)/shard_map/ppermute | solution.py:30
  39.8 1.4 %collective-permute-start.13 = (bf16[272,256]{1,0:T(8,128)(2,1)S(1)}, bf16[272,256]{1,0:T(8,128)(2,1)S(1)}, u32[]{:S(2)}, u32[]{:S(2)}) collective-permute-start(bf16[272,256]{1,0:T(8,128)(2,1)S(1)} %collective-permute-done.12.refs_6_), channel_id=1, source_target_pairs={{1,0},{0,1},{3,2},{2,3},{5,4},{4,5},{7,6},{6,7},{9,8},{8,9},{11,10... | collective-permute-start | bytes 417800 | tf_op jit(solution)/shard_map/ppermute | solution.py:30
  40.7 1.4 %collective-permute-start.9 = (bf16[272,256]{1,0:T(8,128)(2,1)S(1)}, bf16[272,256]{1,0:T(8,128)(2,1)S(1)}, u32[]{:S(2)}, u32[]{:S(2)}) collective-permute-start(bf16[272,256]{1,0:T(8,128)(2,1)S(1)} %collective-permute-done.8.refs_2_), channel_id=1, source_target_pairs={{1,0},{0,1},{3,2},{2,3},{5,4},{4,5},{7,6},{6,7},{9,8},{8,9},{11,10... | collective-permute-start | bytes 417800 | tf_op jit(solution)/shard_map/ppermute | solution.py:30
  47.6 2.0 %collective-permute-start.14 = (bf16[256,1024]{1,0:T(8,128)(2,1)S(1)}, bf16[256,1024]{1,0:T(8,128)(2,1)S(1)}, u32[]{:S(2)}, u32[]{:S(2)}) collective-permute-start(bf16[256,1024]{1,0:T(8,128)(2,1)S(1)} %shard_map.124), channel_id=1, source_target_pairs={{1,0},{0,1},{3,2},{2,3},{5,4},{4,5},{7,6},{6,7},{9,8},{8,9},{11,10... | collective-permute-start | bytes 1572872 | tf_op jit(solution)/shard_map/ppermute | solution.py:30
  49.6 7.3 %collective-permute-start.15 = (bf16[128,512]{1,0:T(8,128)(2,1)S(1)}, bf16[128,512]{1,0:T(8,128)(2,1)S(1)}, u32[]{:S(2)}, u32[]{:S(2)}) collective-permute-start(bf16[128,512]{1,0:T(8,128)(2,1)S(1)} %get-tuple-element.48), channel_id=1, source_target_pairs={{0,6},{1,23},{2,4},{3,21},{4,2},{5,19},{6,0},{7,17},{8,14},{9,31},... | collective-permute-start | bytes 393224 | tf_op jit(solution)/shard_map/ppermute | solution.py:293
  49.7 9.1 %collective-permute-start.16 = (bf16[128,512]{1,0:T(8,128)(2,1)S(1)}, bf16[128,512]{1,0:T(8,128)(2,1)S(1)}, u32[]{:S(2)}, u32[]{:S(2)}) collective-permute-start(bf16[128,512]{1,0:T(8,128)(2,1)S(1)} %get-tuple-element.49), channel_id=1, source_target_pairs={{0,2},{1,19},{2,0},{3,17},{4,6},{5,23},{6,4},{7,21},{8,10},{9,27},... | collective-permute-start | bytes 393224 | tf_op jit(solution)/shard_map/ppermute | solution.py:293
  51.3 7.6 %collective-permute-start.17 = (bf16[128,512]{1,0:T(8,128)(2,1)S(1)}, bf16[128,512]{1,0:T(8,128)(2,1)S(1)}, u32[]{:S(2)}, u32[]{:S(2)}) collective-permute-start(bf16[128,512]{1,0:T(8,128)(2,1)S(1)} %get-tuple-element.50.refs_4_), channel_id=1, source_target_pairs={{1,17},{3,19},{5,21},{7,23},{9,25},{11,27},{13,29},{15,31},{17,1},... | collective-permute-start | bytes 393224 | tf_op jit(solution)/shard_map/ppermute | solution.py:293
  51.9 7.1 %collective-permute-start.18 = (bf16[128,512]{1,0:T(8,128)(2,1)S(1)}, bf16[128,512]{1,0:T(8,128)(2,1)S(1)}, u32[]{:S(2)}, u32[]{:S(2)}) collective-permute-start(bf16[128,512]{1,0:T(8,128)(2,1)S(1)} %get-tuple-element.51), channel_id=1, source_target_pairs={{0,4},{1,21},{2,6},{3,23},{4,0},{5,17},{6,2},{7,19},{8,12},{9,29},... | collective-permute-start | bytes 393224 | tf_op jit(solution)/shard_map/ppermute | solution.py:293
  59.2 1.9 %collective-permute-start.19 = (bf16[128,256]{1,0:T(8,128)(2,1)S(1)}, bf16[128,256]{1,0:T(8,128)(2,1)S(1)}, u32[]{:S(2)}, u32[]{:S(2)}) collective-permute-start(bf16[128,256]{1,0:T(8,128)(2,1)S(1)} %get-tuple-element.54), channel_id=1, source_target_pairs={{1,0},{0,1},{3,2},{2,3},{5,4},{4,5},{7,6},{6,7},{9,8},{8,9},{11,10... | collective-permute-start | bytes 196616 | tf_op jit(solution)/shard_map/ppermute | solution.py:30

commit v11 on v10

--- a/solution.py
+++ b/solution.py
@@ -333,7 +333,7 @@
     asks = []
     if paired:
         share, full = messages
-        others = [moved(share, tok=2), moved(full, tok=1)][::-1]
+        others = [moved(full, tok=1), moved(share, tok=2)]
         others.append(moved(others[1], tok=1))
         (blocks,) = call(
             pack_kernel, [shape((n_tok, mlp_up.shape[0] + units, units), BF)], [mlp_up, mlp_down]

time: 62.1 us -> 62.1 us (level)
  no operation moved by 1% of the time
where the time goes in v11:
time: 62.1 us; the launch traced here: 61.8 us
  waiting for transfers between devices  28.9 us (47%)
  starting transfers between devices  20.4 us (33%)
  Pallas kernels  10 us (16%)
  local copies, waits for them, and re-layouts  1.05 us (2%)
  between operations  0.74 us (1%)
  other arithmetic  0.72 us (1%)
    ppermute x16, waiting for transfers between devices, moved(): return lax.ppermute(x, tuple(axes), pairs)  20.3 us
    ppermute x16, starting transfers between devices, moved(): return lax.ppermute(x, tuple(axes), pairs)  11.7 us
    pallas_call x9, Pallas kernels, call(): pl.pallas_call(kernel, out_shape=outs, in_specs=[pl.BlockSpec(memory_spac...  10 us
    ppermute x4, waiting for transfers between devices, dealt(): return lax.ppermute(x, axes, [p for p in pairs if p[0] != p[1]])  4.43 us
    all_to_all x1, starting transfers between devices, on_device(): mlp = [lax.all_to_all(blocks, 'tok', 0, 0)]  4.36 us
    ppermute x4, starting transfers between devices, dealt(): return lax.ppermute(x, axes, [p for p in pairs if p[0] != p[1]])  4.27 us
    all_to_all x1, waiting for transfers between devices, on_device(): mlp = [lax.all_to_all(blocks, 'tok', 0, 0)]  4.19 us
  transfers between devices with their start and end apart: 21, of which 16 were waited for; matrix products, arithmetic and copies ran while one was open for 0% of the time, Pallas kernels for 13%

profile of v11, /device:TPU:0, one launch (start us, length us, event | category | flops | bytes accessed | tf_op | source)
XLA Modules:
  0.0 61.8 jit_solution(16841893096985949512)
XLA Ops:
  0.0 0.0 copy-start
  0.0 1.1 %shard_map.118 = (bf16[64,1024]{1,0:T(8,128)(2,1)S(1)}, bf16[64,2048]{1,0:T(8,128)(2,1)S(1)}) custom-call(bf16[128,512]{1,0:T(8,128)(2,1)} %refs_3_.1, bf16[128,512]{1,0:T(8,128)(2,1)} %refs_4_.1, f32[1,128]{1,0:T(1,128)} %bitcast.11, bf16[128,512]{1,0:T(8,128)(2,1)} %refs_6_.1, bf16[128,512]{1,0:T(8,128)(2,1)} %refs_7_.1), custom_call_target="tpu_custom_call" | custom-call | flops 1 | bytes 1 | tf_op jit(solution)/shard_map/pallas_call | solution.py:41
  1.1 4.1 %collective-permute-start.1 = (bf16[64,1024]{1,0:T(8,128)(2,1)S(1)}, bf16[64,1024]{1,0:T(8,128)(2,1)S(1)}, u32[]{:S(2)}, u32[]{:S(2)}) collective-permute-start(bf16[64,1024]{1,0:T(8,128)(2,1)S(1)} %get-tuple-element.31), channel_id=1, source_target_pairs={{8,0},{12,4},{0,8},{4,12},{9,1},{13,5},{1,9},{5,13},{10,2},{14,6},... | collective-permute-start | bytes 393224 | tf_op jit(solution)/shard_map/ppermute | solution.py:30
  5.2 1.6 %collective-permute-start = (bf16[64,2048]{1,0:T(8,128)(2,1)S(1)}, bf16[64,2048]{1,0:T(8,128)(2,1)S(1)}, u32[]{:S(2)}, u32[]{:S(2)}) collective-permute-start(bf16[64,2048]{1,0:T(8,128)(2,1)S(1)} %get-tuple-element.30), channel_id=1, source_target_pairs={{4,0},{0,4},{12,8},{8,12},{5,1},{1,5},{13,9},{9,13},{6,2},{2,6},{1... | collective-permute-start | bytes 786440 | tf_op jit(solution)/shard_map/ppermute | solution.py:30
  6.8 4.8 %collective-permute-done.1.refs_10_ = bf16[64,1024]{1,0:T(8,128)(2,1)S(1)} collective-permute-done((bf16[64,1024]{1,0:T(8,128)(2,1)S(1)}, bf16[64,1024]{1,0:T(8,128)(2,1)S(1)}, u32[]{:S(2)}, u32[]{:S(2)}) %collective-permute-start.1) | collective-permute-done | bytes 131104 | tf_op jit(solution)/shard_map/ppermute | solution.py:30
  11.7 0.7 %collective-permute-start.2 = (bf16[64,1024]{1,0:T(8,128)(2,1)S(1)}, bf16[64,1024]{1,0:T(8,128)(2,1)S(1)}, u32[]{:S(2)}, u32[]{:S(2)}) collective-permute-start(bf16[64,1024]{1,0:T(8,128)(2,1)S(1)} %collective-permute-done.1.refs_10_), channel_id=1, source_target_pairs={{4,0},{0,4},{12,8},{8,12},{5,1},{1,5},{13,9},{9,13},{6,2},{2,6},{1... | collective-permute-start | bytes 393224 | tf_op jit(solution)/shard_map/ppermute | solution.py:30
  12.3 0.0 copy-done
  12.3 0.0 copy-start.1
  12.3 1.0 %copy-done.1 = bf16[1024,256]{1,0:T(8,128)(2,1)S(1)} copy-done((bf16[1024,256]{1,0:T(8,128)(2,1)S(1)}, bf16[1024,256]{1,0:T(8,128)(2,1)}, u32[]{:S(2)}) %copy-start.1) | copy-done | bytes 524312
  13.4 1.1 %shard_map.119 = bf16[4,512,256]{2,1,0:T(8,128)(2,1)} custom-call(bf16[256,1024]{1,0:T(8,128)(2,1)S(1)} %copy-done, bf16[1024,256]{1,0:T(8,128)(2,1)S(1)} %copy-done.1), custom_call_target="tpu_custom_call" | custom-call | flops 1 | bytes 1 | tf_op jit(solution)/shard_map/pallas_call | solution.py:41
  14.4 3.0 %collective-permute-done.2.refs_11_ = bf16[64,1024]{1,0:T(8,128)(2,1)S(1)} collective-permute-done((bf16[64,1024]{1,0:T(8,128)(2,1)S(1)}, bf16[64,1024]{1,0:T(8,128)(2,1)S(1)}, u32[]{:S(2)}, u32[]{:S(2)}) %collective-permute-start.2) | collective-permute-done | bytes 131104 | tf_op jit(solution)/shard_map/ppermute | solution.py:30
  17.5 0.0 collective-permute-done.refs_9_.refs_0_
  17.5 4.4 %all-to-all-start = ((bf16[4,512,256]{2,1,0:T(8,128)(2,1)}), bf16[4,512,256]{2,1,0:T(8,128)(2,1)S(1)}, u32[]{:S(2)}, u32[]{:S(2)}) async-start(bf16[4,512,256]{2,1,0:T(8,128)(2,1)} %shard_map.119), calls=%async_computation | async-start | bytes 2097152 | tf_op jit(solution)/shard_map/all_to_all | solution.py:342
  21.8 0.0 collective-permute-start.3
  21.8 0.5 collective-permute-start.4
  22.3 0.0 collective-permute-start.5
  22.3 1.2 %collective-permute-done.4.refs_13_ = bf16[64,1024]{1,0:T(8,128)(2,1)S(1)} collective-permute-done((bf16[64,1024]{1,0:T(8,128)(2,1)S(1)}, bf16[64,1024]{1,0:T(8,128)(2,1)S(1)}, u32[]{:S(2)}, u32[]{:S(2)}) %collective-permute-start.4) | collective-permute-done | bytes 131104 | tf_op jit(solution)/shard_map/ppermute | solution.py:30
  23.5 0.2 collective-permute-done.5.refs_14_
  23.7 0.0 collective-permute-done.3.refs_12_
  23.7 5.5 %shard_map.120 = (f32[256,256]{1,0:T(8,128)S(1)}, f32[8,256]{1,0:T(8,128)S(1)}, bf16[272,256]{1,0:T(8,128)(2,1)S(1)}, bf16[128,256]{1,0:T(8,128)(2,1)S(1)}, bf16[16,256]{1,0:T(8,128)(2,1)S(1)}) custom-call(f32[512,512]{1,0:T(8,128)} %bitcast.7, f32[512,512]{1,0:T(8,128)} %bitcast.8, f32[512,512]{1,0:T(8,128)} %bitcast.9, bf16[128,512]{1,0:T(8,128)(2,1)} %refs_3_.1, ...), custom_call_target="tpu_custom_call" | custom-call | flops 1 | bytes 1 | tf_op jit(solution)/shard_map/pallas_call | solution.py:41
  29.2 0.2 collective-permute-start.6
  29.4 1.2 %collective-permute-done.6.got = bf16[272,256]{1,0:T(8,128)(2,1)S(1)} collective-permute-done((bf16[272,256]{1,0:T(8,128)(2,1)S(1)}, bf16[272,256]{1,0:T(8,128)(2,1)S(1)}, u32[]{:S(2)}, u32[]{:S(2)}) %collective-permute-start.6) | collective-permute-done | bytes 139296 | tf_op jit(solution)/shard_map/ppermute | solution.py:30
  30.7 0.1 shard_map.121
  30.7 1.6 %collective-permute-start.10 = (bf16[272,256]{1,0:T(8,128)(2,1)S(1)}, bf16[272,256]{1,0:T(8,128)(2,1)S(1)}, u32[]{:S(2)}, u32[]{:S(2)}) collective-permute-start(bf16[272,256]{1,0:T(8,128)(2,1)S(1)} %get-tuple-element.46.refs_0_), channel_id=1, source_target_pairs={{16,0},{0,16},{17,1},{1,17},{18,2},{2,18},{19,3},{3,19},{20,4},{4,... | collective-permute-start | bytes 417800 | tf_op jit(solution)/shard_map/ppermute | solution.py:30
  32.3 1.4 %collective-permute-start.12 = (bf16[272,256]{1,0:T(8,128)(2,1)S(1)}, bf16[272,256]{1,0:T(8,128)(2,1)S(1)}, u32[]{:S(2)}, u32[]{:S(2)}) collective-permute-start(bf16[272,256]{1,0:T(8,128)(2,1)S(1)} %get-tuple-element.46.refs_0_), channel_id=1, source_target_pairs={{18,0},{16,2},{2,16},{0,18},{19,1},{17,3},{3,17},{1,19},{22,4},{20... | collective-permute-start | bytes 417800 | tf_op jit(solution)/shard_map/ppermute | solution.py:30
  33.7 0.5 collective-permute-start.8
  34.3 0.0 collective-permute-start.7
  34.3 4.9 %collective-permute-done.10.refs_4_ = bf16[272,256]{1,0:T(8,128)(2,1)S(1)} collective-permute-done((bf16[272,256]{1,0:T(8,128)(2,1)S(1)}, bf16[272,256]{1,0:T(8,128)(2,1)S(1)}, u32[]{:S(2)}, u32[]{:S(2)}) %collective-permute-start.10) | collective-permute-done | bytes 139296 | tf_op jit(solution)/shard_map/ppermute | solution.py:30
  39.2 0.0 collective-permute-start.11
  39.2 0.5 collective-permute-done.12.refs_6_
  39.8 0.0 collective-permute-start.13
  39.8 1.0 %collective-permute-done.8.refs_2_ = bf16[272,256]{1,0:T(8,128)(2,1)S(1)} collective-permute-done((bf16[272,256]{1,0:T(8,128)(2,1)S(1)}, bf16[272,256]{1,0:T(8,128)(2,1)S(1)}, u32[]{:S(2)}, u32[]{:S(2)}) %collective-permute-start.8) | collective-permute-done | bytes 139296 | tf_op jit(solution)/shard_map/ppermute | solution.py:30
  40.7 0.0 collective-permute-start.9
  40.7 0.0 collective-permute-done.7.refs_1_
  40.7 0.0 collective-permute-done.11.refs_5_
  40.7 0.4 collective-permute-done.13.refs_7_
  41.1 1.0 %collective-permute-done.9.refs_3_ = bf16[272,256]{1,0:T(8,128)(2,1)S(1)} collective-permute-done((bf16[272,256]{1,0:T(8,128)(2,1)S(1)}, bf16[272,256]{1,0:T(8,128)(2,1)S(1)}, u32[]{:S(2)}, u32[]{:S(2)}) %collective-permute-start.9) | collective-permute-done | bytes 139296 | tf_op jit(solution)/shard_map/ppermute | solution.py:30
  42.1 0.5 shard_map.122.zs
  42.6 4.2 %all-to-all-done.refs_0_ = bf16[4,512,256]{2,1,0:T(8,128)(2,1)S(1)} async-done(((bf16[4,512,256]{2,1,0:T(8,128)(2,1)}), bf16[4,512,256]{2,1,0:T(8,128)(2,1)S(1)}, u32[]{:S(2)}, u32[]{:S(2)}) %all-to-all-start) | async-done | bytes 1048608 | tf_op jit(solution)/shard_map/all_to_all | solution.py:342
  46.8 0.7 %shard_map.124 = bf16[256,1024]{1,0:T(8,128)(2,1)S(1)} custom-call(bf16[512,1024]{1,0:T(8,128)(2,1)S(1)} %shard_map.122.zs, bf16[4,512,256]{2,1,0:T(8,128)(2,1)S(1)} %all-to-all-done.refs_0_), custom_call_target="tpu_custom_call" | custom-call | flops 1 | bytes 1 | tf_op jit(solution)/shard_map/pallas_call | solution.py:41
  47.6 0.1 collective-permute-start.14
  47.6 0.8 %shard_map.123.own = f32[256,1024]{1,0:T(8,128)S(1)} custom-call(bf16[512,1024]{1,0:T(8,128)(2,1)S(1)} %shard_map.122.zs, bf16[4,512,256]{2,1,0:T(8,128)(2,1)S(1)} %all-to-all-done.refs_0_), custom_call_target="tpu_custom_call" | custom-call | flops 1 | bytes 1 | tf_op jit(solution)/shard_map/pallas_call | solution.py:41
  48.4 1.1 %collective-permute-done.14.got = bf16[256,1024]{1,0:T(8,128)(2,1)S(1)} collective-permute-done((bf16[256,1024]{1,0:T(8,128)(2,1)S(1)}, bf16[256,1024]{1,0:T(8,128)(2,1)S(1)}, u32[]{:S(2)}, u32[]{:S(2)}) %collective-permute-start.14) | collective-permute-done | bytes 524320 | tf_op jit(solution)/shard_map/ppermute | solution.py:30
  49.5 0.1 shard_map.125
  49.6 0.1 collective-permute-start.15
  49.7 1.6 %collective-permute-start.16 = (bf16[128,512]{1,0:T(8,128)(2,1)S(1)}, bf16[128,512]{1,0:T(8,128)(2,1)S(1)}, u32[]{:S(2)}, u32[]{:S(2)}) collective-permute-start(bf16[128,512]{1,0:T(8,128)(2,1)S(1)} %get-tuple-element.49), channel_id=1, source_target_pairs={{0,2},{1,19},{2,0},{3,17},{4,6},{5,23},{6,4},{7,21},{8,10},{9,27},... | collective-permute-start | bytes 393224 | tf_op jit(solution)/shard_map/ppermute | solution.py:293
  51.3 0.7 %collective-permute-start.17 = (bf16[128,512]{1,0:T(8,128)(2,1)S(1)}, bf16[128,512]{1,0:T(8,128)(2,1)S(1)}, u32[]{:S(2)}, u32[]{:S(2)}) collective-permute-start(bf16[128,512]{1,0:T(8,128)(2,1)S(1)} %get-tuple-element.50.refs_4_), channel_id=1, source_target_pairs={{1,17},{3,19},{5,21},{7,23},{9,25},{11,27},{13,29},{15,31},{17,1},... | collective-permute-start | bytes 393224 | tf_op jit(solution)/shard_map/ppermute | solution.py:293
  51.9 2.0 %collective-permute-start.18 = (bf16[128,512]{1,0:T(8,128)(2,1)S(1)}, bf16[128,512]{1,0:T(8,128)(2,1)S(1)}, u32[]{:S(2)}, u32[]{:S(2)}) collective-permute-start(bf16[128,512]{1,0:T(8,128)(2,1)S(1)} %get-tuple-element.51), channel_id=1, source_target_pairs={{0,4},{1,21},{2,6},{3,23},{4,0},{5,17},{6,2},{7,19},{8,12},{9,29},... | collective-permute-start | bytes 393224 | tf_op jit(solution)/shard_map/ppermute | solution.py:293
  54.6 2.4 %collective-permute-done.15.refs_0_ = bf16[128,512]{1,0:T(8,128)(2,1)S(1)} collective-permute-done((bf16[128,512]{1,0:T(8,128)(2,1)S(1)}, bf16[128,512]{1,0:T(8,128)(2,1)S(1)}, u32[]{:S(2)}, u32[]{:S(2)}) %collective-permute-start.15) | collective-permute-done | bytes 131104 | tf_op jit(solution)/shard_map/ppermute | solution.py:293
  56.9 1.9 %collective-permute-done.16.refs_1_ = bf16[128,512]{1,0:T(8,128)(2,1)S(1)} collective-permute-done((bf16[128,512]{1,0:T(8,128)(2,1)S(1)}, bf16[128,512]{1,0:T(8,128)(2,1)S(1)}, u32[]{:S(2)}, u32[]{:S(2)}) %collective-permute-start.16) | collective-permute-done | bytes 131104 | tf_op jit(solution)/shard_map/ppermute | solution.py:293
  58.8 0.0 collective-permute-done.17.refs_2_
  58.8 0.2 collective-permute-done.18.refs_3_
  59.0 0.1 shard_map.126
  59.2 1.0 %collective-permute-start.19 = (bf16[128,256]{1,0:T(8,128)(2,1)S(1)}, bf16[128,256]{1,0:T(8,128)(2,1)S(1)}, u32[]{:S(2)}, u32[]{:S(2)}) collective-permute-start(bf16[128,256]{1,0:T(8,128)(2,1)S(1)} %get-tuple-element.54), channel_id=1, source_target_pairs={{1,0},{0,1},{3,2},{2,3},{5,4},{4,5},{7,6},{6,7},{9,8},{8,9},{11,10... | collective-permute-start | bytes 196616 | tf_op jit(solution)/shard_map/ppermute | solution.py:30
  60.2 0.9 %collective-permute-done.19 = bf16[128,256]{1,0:T(8,128)(2,1)S(1)} collective-permute-done((bf16[128,256]{1,0:T(8,128)(2,1)S(1)}, bf16[128,256]{1,0:T(8,128)(2,1)S(1)}, u32[]{:S(2)}, u32[]{:S(2)}) %collective-permute-start.19) | collective-permute-done | bytes 65568 | tf_op jit(solution)/shard_map/ppermute | solution.py:30
  61.1 0.7 %select_convert_fusion = bf16[128,256]{1,0:T(8,128)(2,1)} fusion(f32[128,256]{1,0:T(8,128)S(1)} %get-tuple-element.53, bf16[128,256]{1,0:T(8,128)(2,1)S(1)} %collective-permute-done.19, pred[128]{0:T(512)(128)(4,1)S(1)} %iota_compare_fusion), kind=kLoop, calls=%fused_computation | loop fusion | flops 131072 | bytes 262272 | tf_op jit(solution)/shard_map/convert_element_type | solution.py:412
  (1 shorter events, 0.0 us)
Async XLA Ops:
  0.0 12.3 %copy-start = (bf16[256,1024]{1,0:T(8,128)(2,1)S(1)}, bf16[256,1024]{1,0:T(8,128)(2,1)}, u32[]{:S(2)}) copy-start(bf16[256,1024]{1,0:T(8,128)(2,1)} %up.1) | copy-start | bytes 1572868
  1.1 10.5 %collective-permute-start.1 = (bf16[64,1024]{1,0:T(8,128)(2,1)S(1)}, bf16[64,1024]{1,0:T(8,128)(2,1)S(1)}, u32[]{:S(2)}, u32[]{:S(2)}) collective-permute-start(bf16[64,1024]{1,0:T(8,128)(2,1)S(1)} %get-tuple-element.31), channel_id=1, source_target_pairs={{8,0},{12,4},{0,8},{4,12},{9,1},{13,5},{1,9},{5,13},{10,2},{14,6},... | collective-permute-start | bytes 393224 | tf_op jit(solution)/shard_map/ppermute | solution.py:30
  5.2 12.2 %collective-permute-start = (bf16[64,2048]{1,0:T(8,128)(2,1)S(1)}, bf16[64,2048]{1,0:T(8,128)(2,1)S(1)}, u32[]{:S(2)}, u32[]{:S(2)}) collective-permute-start(bf16[64,2048]{1,0:T(8,128)(2,1)S(1)} %get-tuple-element.30), channel_id=1, source_target_pairs={{4,0},{0,4},{12,8},{8,12},{5,1},{1,5},{13,9},{9,13},{6,2},{2,6},{1... | collective-permute-start | bytes 786440 | tf_op jit(solution)/shard_map/ppermute | solution.py:30
  11.7 5.8 %collective-permute-start.2 = (bf16[64,1024]{1,0:T(8,128)(2,1)S(1)}, bf16[64,1024]{1,0:T(8,128)(2,1)S(1)}, u32[]{:S(2)}, u32[]{:S(2)}) collective-permute-start(bf16[64,1024]{1,0:T(8,128)(2,1)S(1)} %collective-permute-done.1.refs_10_), channel_id=1, source_target_pairs={{4,0},{0,4},{12,8},{8,12},{5,1},{1,5},{13,9},{9,13},{6,2},{2,6},{1... | collective-permute-start | bytes 393224 | tf_op jit(solution)/shard_map/ppermute | solution.py:30
  12.3 1.0 %copy-start.1 = (bf16[1024,256]{1,0:T(8,128)(2,1)S(1)}, bf16[1024,256]{1,0:T(8,128)(2,1)}, u32[]{:S(2)}) copy-start(bf16[1024,256]{1,0:T(8,128)(2,1)} %down.1) | copy-start | bytes 1572868
  17.5 29.3 %all-to-all-start = ((bf16[4,512,256]{2,1,0:T(8,128)(2,1)}), bf16[4,512,256]{2,1,0:T(8,128)(2,1)S(1)}, u32[]{:S(2)}, u32[]{:S(2)}) async-start(bf16[4,512,256]{2,1,0:T(8,128)(2,1)} %shard_map.119), calls=%async_computation | async-start | bytes 2097152 | tf_op jit(solution)/shard_map/all_to_all | solution.py:342
  21.8 1.9 %collective-permute-start.3 = (bf16[64,2048]{1,0:T(8,128)(2,1)S(1)}, bf16[64,2048]{1,0:T(8,128)(2,1)S(1)}, u32[]{:S(2)}, u32[]{:S(2)}) collective-permute-start(bf16[64,2048]{1,0:T(8,128)(2,1)S(1)} %collective-permute-done.refs_9_.refs_0_), channel_id=1, source_target_pairs={{1,0},{0,1},{3,2},{2,3},{5,4},{4,5},{7,6},{6,7},{9,8},{8,9},{11,10... | collective-permute-start | bytes 786440 | tf_op jit(solution)/shard_map/ppermute | solution.py:30
  21.8 1.7 %collective-permute-start.4 = (bf16[64,1024]{1,0:T(8,128)(2,1)S(1)}, bf16[64,1024]{1,0:T(8,128)(2,1)S(1)}, u32[]{:S(2)}, u32[]{:S(2)}) collective-permute-start(bf16[64,1024]{1,0:T(8,128)(2,1)S(1)} %collective-permute-done.1.refs_10_), channel_id=1, source_target_pairs={{1,0},{0,1},{3,2},{2,3},{5,4},{4,5},{7,6},{6,7},{9,8},{8,9},{11,10... | collective-permute-start | bytes 393224 | tf_op jit(solution)/shard_map/ppermute | solution.py:30
  22.3 1.4 %collective-permute-start.5 = (bf16[64,1024]{1,0:T(8,128)(2,1)S(1)}, bf16[64,1024]{1,0:T(8,128)(2,1)S(1)}, u32[]{:S(2)}, u32[]{:S(2)}) collective-permute-start(bf16[64,1024]{1,0:T(8,128)(2,1)S(1)} %collective-permute-done.2.refs_11_), channel_id=1, source_target_pairs={{1,0},{0,1},{3,2},{2,3},{5,4},{4,5},{7,6},{6,7},{9,8},{8,9},{11,10... | collective-permute-start | bytes 393224 | tf_op jit(solution)/shard_map/ppermute | solution.py:30
  29.2 1.4 %collective-permute-start.6 = (bf16[272,256]{1,0:T(8,128)(2,1)S(1)}, bf16[272,256]{1,0:T(8,128)(2,1)S(1)}, u32[]{:S(2)}, u32[]{:S(2)}) collective-permute-start(bf16[272,256]{1,0:T(8,128)(2,1)S(1)} %get-tuple-element.43), channel_id=1, source_target_pairs={{1,0},{0,1},{3,2},{2,3},{5,4},{4,5},{7,6},{6,7},{9,8},{8,9},{11,10... | collective-permute-start | bytes 417800 | tf_op jit(solution)/shard_map/ppermute | solution.py:30
  30.7 8.5 %collective-permute-start.10 = (bf16[272,256]{1,0:T(8,128)(2,1)S(1)}, bf16[272,256]{1,0:T(8,128)(2,1)S(1)}, u32[]{:S(2)}, u32[]{:S(2)}) collective-permute-start(bf16[272,256]{1,0:T(8,128)(2,1)S(1)} %get-tuple-element.46.refs_0_), channel_id=1, source_target_pairs={{16,0},{0,16},{17,1},{1,17},{18,2},{2,18},{19,3},{3,19},{20,4},{4,... | collective-permute-start | bytes 417800 | tf_op jit(solution)/shard_map/ppermute | solution.py:30
  32.3 7.5 %collective-permute-start.12 = (bf16[272,256]{1,0:T(8,128)(2,1)S(1)}, bf16[272,256]{1,0:T(8,128)(2,1)S(1)}, u32[]{:S(2)}, u32[]{:S(2)}) collective-permute-start(bf16[272,256]{1,0:T(8,128)(2,1)S(1)} %get-tuple-element.46.refs_0_), channel_id=1, source_target_pairs={{18,0},{16,2},{2,16},{0,18},{19,1},{17,3},{3,17},{1,19},{22,4},{20... | collective-permute-start | bytes 417800 | tf_op jit(solution)/shard_map/ppermute | solution.py:30
  33.7 7.0 %collective-permute-start.8 = (bf16[272,256]{1,0:T(8,128)(2,1)S(1)}, bf16[272,256]{1,0:T(8,128)(2,1)S(1)}, u32[]{:S(2)}, u32[]{:S(2)}) collective-permute-start(bf16[272,256]{1,0:T(8,128)(2,1)S(1)} %get-tuple-element.46.refs_0_), channel_id=1, source_target_pairs={{2,0},{0,2},{3,1},{1,3},{6,4},{4,6},{7,5},{5,7},{10,8},{8,10},{11,... | collective-permute-start | bytes 417800 | tf_op jit(solution)/shard_map/ppermute | solution.py:30
  34.3 6.5 %collective-permute-start.7 = (bf16[272,256]{1,0:T(8,128)(2,1)S(1)}, bf16[272,256]{1,0:T(8,128)(2,1)S(1)}, u32[]{:S(2)}, u32[]{:S(2)}) collective-permute-start(bf16[272,256]{1,0:T(8,128)(2,1)S(1)} %get-tuple-element.46.refs_0_), channel_id=1, source_target_pairs={{1,0},{0,1},{3,2},{2,3},{5,4},{4,5},{7,6},{6,7},{9,8},{8,9},{11,10... | collective-permute-start | bytes 417800 | tf_op jit(solution)/shard_map/ppermute | solution.py:30
  39.2 1.5 %collective-permute-start.11 = (bf16[272,256]{1,0:T(8,128)(2,1)S(1)}, bf16[272,256]{1,0:T(8,128)(2,1)S(1)}, u32[]{:S(2)}, u32[]{:S(2)}) collective-permute-start(bf16[272,256]{1,0:T(8,128)(2,1)S(1)} %collective-permute-done.10.refs_4_), channel_id=1, source_target_pairs={{1,0},{0,1},{3,2},{2,3},{5,4},{4,5},{7,6},{6,7},{9,8},{8,9},{11,10... | collective-permute-start | bytes 417800 | tf_op jit(solution)/shard_map/ppermute | solution.py:30
  39.8 1.4 %collective-permute-start.13 = (bf16[272,256]{1,0:T(8,128)(2,1)S(1)}, bf16[272,256]{1,0:T(8,128)(2,1)S(1)}, u32[]{:S(2)}, u32[]{:S(2)}) collective-permute-start(bf16[272,256]{1,0:T(8,128)(2,1)S(1)} %collective-permute-done.12.refs_6_), channel_id=1, source_target_pairs={{1,0},{0,1},{3,2},{2,3},{5,4},{4,5},{7,6},{6,7},{9,8},{8,9},{11,10... | collective-permute-start | bytes 417800 | tf_op jit(solution)/shard_map/ppermute | solution.py:30
  40.7 1.4 %collective-permute-start.9 = (bf16[272,256]{1,0:T(8,128)(2,1)S(1)}, bf16[272,256]{1,0:T(8,128)(2,1)S(1)}, u32[]{:S(2)}, u32[]{:S(2)}) collective-permute-start(bf16[272,256]{1,0:T(8,128)(2,1)S(1)} %collective-permute-done.8.refs_2_), channel_id=1, source_target_pairs={{1,0},{0,1},{3,2},{2,3},{5,4},{4,5},{7,6},{6,7},{9,8},{8,9},{11,10... | collective-permute-start | bytes 417800 | tf_op jit(solution)/shard_map/ppermute | solution.py:30
  47.6 2.0 %collective-permute-start.14 = (bf16[256,1024]{1,0:T(8,128)(2,1)S(1)}, bf16[256,1024]{1,0:T(8,128)(2,1)S(1)}, u32[]{:S(2)}, u32[]{:S(2)}) collective-permute-start(bf16[256,1024]{1,0:T(8,128)(2,1)S(1)} %shard_map.124), channel_id=1, source_target_pairs={{1,0},{0,1},{3,2},{2,3},{5,4},{4,5},{7,6},{6,7},{9,8},{8,9},{11,10... | collective-permute-start | bytes 1572872 | tf_op jit(solution)/shard_map/ppermute | solution.py:30
  49.6 7.3 %collective-permute-start.15 = (bf16[128,512]{1,0:T(8,128)(2,1)S(1)}, bf16[128,512]{1,0:T(8,128)(2,1)S(1)}, u32[]{:S(2)}, u32[]{:S(2)}) collective-permute-start(bf16[128,512]{1,0:T(8,128)(2,1)S(1)} %get-tuple-element.48), channel_id=1, source_target_pairs={{0,6},{1,23},{2,4},{3,21},{4,2},{5,19},{6,0},{7,17},{8,14},{9,31},... | collective-permute-start | bytes 393224 | tf_op jit(solution)/shard_map/ppermute | solution.py:293
  49.7 9.1 %collective-permute-start.16 = (bf16[128,512]{1,0:T(8,128)(2,1)S(1)}, bf16[128,512]{1,0:T(8,128)(2,1)S(1)}, u32[]{:S(2)}, u32[]{:S(2)}) collective-permute-start(bf16[128,512]{1,0:T(8,128)(2,1)S(1)} %get-tuple-element.49), channel_id=1, source_target_pairs={{0,2},{1,19},{2,0},{3,17},{4,6},{5,23},{6,4},{7,21},{8,10},{9,27},... | collective-permute-start | bytes 393224 | tf_op jit(solution)/shard_map/ppermute | solution.py:293
  51.3 7.6 %collective-permute-start.17 = (bf16[128,512]{1,0:T(8,128)(2,1)S(1)}, bf16[128,512]{1,0:T(8,128)(2,1)S(1)}, u32[]{:S(2)}, u32[]{:S(2)}) collective-permute-start(bf16[128,512]{1,0:T(8,128)(2,1)S(1)} %get-tuple-element.50.refs_4_), channel_id=1, source_target_pairs={{1,17},{3,19},{5,21},{7,23},{9,25},{11,27},{13,29},{15,31},{17,1},... | collective-permute-start | bytes 393224 | tf_op jit(solution)/shard_map/ppermute | solution.py:293
  51.9 7.1 %collective-permute-start.18 = (bf16[128,512]{1,0:T(8,128)(2,1)S(1)}, bf16[128,512]{1,0:T(8,128)(2,1)S(1)}, u32[]{:S(2)}, u32[]{:S(2)}) collective-permute-start(bf16[128,512]{1,0:T(8,128)(2,1)S(1)} %get-tuple-element.51), channel_id=1, source_target_pairs={{0,4},{1,21},{2,6},{3,23},{4,0},{5,17},{6,2},{7,19},{8,12},{9,29},... | collective-permute-start | bytes 393224 | tf_op jit(solution)/shard_map/ppermute | solution.py:293
  59.2 1.9 %collective-permute-start.19 = (bf16[128,256]{1,0:T(8,128)(2,1)S(1)}, bf16[128,256]{1,0:T(8,128)(2,1)S(1)}, u32[]{:S(2)}, u32[]{:S(2)}) collective-permute-start(bf16[128,256]{1,0:T(8,128)(2,1)S(1)} %get-tuple-element.54), channel_id=1, source_target_pairs={{1,0},{0,1},{3,2},{2,3},{5,4},{4,5},{7,6},{6,7},{9,8},{8,9},{11,10... | collective-permute-start | bytes 196616 | tf_op jit(solution)/shard_map/ppermute | solution.py:30
